TPU v7x, 128 devices: a whole 4x4x4 slice. The times are simulated.
128 devices in a mesh: layer: 4 (over y_hi, core), lat: 32 (over x, y_lo, z).
Axes of the slice: x: 4, y: 4 (y_hi: 2, y_lo: 2; y = y_hi * 2 + y_lo), z: 4, core: 2. Of those that a mesh axis runs over, the one named last changes fastest.
Arguments:
- resid_halves: bfloat16 [4, 1024, 4096], P('layer'), may hold values from -6 to 6
- enc_weight: bfloat16 [4, 4096, 16384], P('layer', None, 'lat'), may hold values from -0.0625 to 0.0625
- enc_bias: float32 [2, 16384], P(None, 'lat'), may hold values from -3 to 3
- jump_threshold: float32 [2, 16384], P(None, 'lat'), may hold values from 0.1 to 1
- dec_weight: bfloat16 [4, 2, 16384, 8192], P('layer', None, 'lat'), may hold values from -0.03125 to 0.03125
- dec_bias: float32 [4, 8192], P('layer'), may hold values from -3 to 3
- clamp_rows: int32 [2, 1024], replicated, may hold values from 0 to 1023, each once within a row
- clamp_feats: int32 [2, 1024], replicated, may hold values from 0 to 16383
- clamp_slots: int32 [2, 1024], replicated, may hold values from 0 to 15
- clamp_values: float32 [16], replicated, may hold values from 5 to 15
Outputs:
- recon: bfloat16 [4, 1024, 8192], P('layer', 'lat')
Inputs may be any that keep to these rules, and one draw needn't show every extreme that they name: Each row of clamp_rows names every token row once.
All inputs are finite; a program needn't handle non-finite values.
Results may differ from a plain program's by a relative error of at most 0.0042.
Values may be sent and summed in bfloat16 or wider, within the bound.
No kernel may reach another device: no remote copies, remote signals or barrier semaphores. Data moves between devices by JAX's collectives and lax.ppermute only.
A program may use at most 192 MiB of HBM per device.

v0:
```python
import jax
import jax.numpy as jnp
from jax import lax
from jax.sharding import PartitionSpec as P


def swapped(value, axis, distance):
    mask = 2**distance
    pairs = [(source, source ^ mask) for source in range(lax.axis_size(axis))]
    return lax.ppermute(value, axis, pairs)


def clamp_codes(activity, feat_ids, slot_ids, row_ids, clamp_values, lat_first):
    n_rows = activity.shape[0]
    width = activity.shape[1]
    row_hot = (row_ids[:, None] == jnp.arange(n_rows, dtype=jnp.int32)[None, :]).astype(jnp.float32)
    slot_hot = (
        slot_ids[:, None] == jnp.arange(clamp_values.shape[0], dtype=jnp.int32)[None, :]
    ).astype(jnp.float32)
    chosen = jnp.dot(slot_hot, clamp_values, precision=lax.Precision.HIGHEST)
    feat_row = jnp.dot(feat_ids.astype(jnp.float32), row_hot, precision=lax.Precision.HIGHEST)
    value_row = jnp.dot(chosen, row_hot, precision=lax.Precision.HIGHEST)
    target_col = feat_row.astype(jnp.int32) - lat_first
    hit = target_col[:, None] == jnp.arange(width, dtype=jnp.int32)[None, :]
    return jnp.where(hit, value_row[:, None], activity)


def shards(
    resid_halves,
    enc_weight,
    enc_bias,
    jump_threshold,
    dec_weight,
    dec_bias,
    clamp_rows,
    clamp_feats,
    clamp_slots,
    clamp_values,
):
    group = lax.axis_index("layer")
    source = group // 2
    shard_width = enc_weight.shape[2]
    lat_first = lax.axis_index("lat") * shard_width
    my_bias = lax.dynamic_index_in_dim(enc_bias, source, 0, keepdims=False)
    my_thresh = lax.dynamic_index_in_dim(jump_threshold, source, 0, keepdims=False)
    my_feats = lax.dynamic_index_in_dim(clamp_feats, source, 0, keepdims=False)
    my_slots = lax.dynamic_index_in_dim(clamp_slots, source, 0, keepdims=False)
    my_rows = lax.dynamic_index_in_dim(clamp_rows, source, 0, keepdims=False)
    partial_pre = jnp.dot(resid_halves[0], enc_weight[0], preferred_element_type=jnp.float32)
    partner = swapped(partial_pre, "layer", 0)
    pre_act = partial_pre + partner + my_bias[None, :]
    ramp = jnp.clip((pre_act - my_thresh[None, :]) / 0.25 + 1.0, 0.0, 1.0)
    clamped = clamp_codes(pre_act * ramp, my_feats, my_slots, my_rows, clamp_values, lat_first)
    own_codes = clamped.astype(jnp.bfloat16)
    other_codes = swapped(own_codes, "layer", 1)
    both_codes = jnp.where(
        source == 0, jnp.stack([own_codes, other_codes]), jnp.stack([other_codes, own_codes])
    )
    total = jnp.dot(both_codes[0], dec_weight[0, 0], preferred_element_type=jnp.float32)
    summed = lax.psum_scatter(
        total + jnp.dot(both_codes[1], dec_weight[0, 1], preferred_element_type=jnp.float32),
        "lat",
        scatter_dimension=0,
        tiled=True,
    )
    result = (summed + dec_bias[0][None, :]).astype(jnp.bfloat16)
    return result[None, :, :]


def solution(mesh):
    return jax.shard_map(
        shards,
        mesh=mesh,
        in_specs=(
            P("layer", None, None),
            P("layer", None, "lat"),
            P(None, "lat"),
            P(None, "lat"),
            P("layer", None, "lat", None),
            P("layer", None),
            P(),
            P(),
            P(),
            P(),
        ),
        out_specs=P("layer", "lat", None),
        check_vma=False,
    )
```

profile of v0, /device:TPU:0, one launch (start us, length us, event | category | flops | bytes accessed | tf_op | source)
XLA Modules:
  0.0 473.8 jit_solution(14954663480901401410)
XLA Ops:
  6.5 0.0 copy-start
  6.5 0.0 copy-start.6
  6.5 0.0 copy-start.7
  6.5 0.0 copy-start.4
  6.5 0.0 copy-start.5
  6.5 0.0 copy-start.8
  6.6 0.0 reduce-scatter.2.cloned.1.call-start
  6.6 8.2 %fusion.3 = f32[1024,512]{1,0:T(8,128)S(1)} fusion(bf16[1,1024,4096]{2,1,0:T(8,128)(2,1)} %param.10, bf16[1,4096,512]{2,1,0:T(8,128)(2,1)} %param.11), kind=kOutput, calls=%fused_computation.4 | convolution fusion | flops 4294967296 | bytes 14680064 | tf_op jit(solution)/shard_map/dot_general | solution.py:49
  14.8 0.1 collective-permute-start
  14.9 0.0 copy-done.6
  14.9 0.0 copy-done.7
  14.9 0.0 copy-done.4
  14.9 0.0 copy-done.5
  15.0 0.0 copy-done.8
  15.0 1.5 fusion.9
  16.4 0.0 copy-done
  16.5 0.4 convolution_bitcast_fusion
  16.9 1.5 fusion.8
  18.4 0.8 collective-permute-done
  19.1 2.3 select_convert_fusion
  21.5 3.4 collective-permute-start.1
  24.8 23.5 %collective-permute-done.1 = bf16[1024,512]{1,0:T(8,128)(2,1)S(1)} collective-permute-done((bf16[1024,512]{1,0:T(8,128)(2,1)S(1)}, bf16[1024,512]{1,0:T(8,128)(2,1)S(1)}, u32[]{:S(2)}, u32[]{:S(2)}) %collective-permute-start.1) | collective-permute-done | bytes 1048608 | tf_op jit(solution)/shard_map/ppermute | solution.py:10
  48.3 0.0 copy-start.2
  48.3 1.0 copy-done.2
  49.3 2.0 maximum_select_fusion
  51.2 17.9 %fusion.1 = f32[1024,8192]{1,0:T(8,128)} fusion(bf16[1,2,512,8192]{3,2,1,0:T(8,128)(2,1)} %param.14, bf16[2,1024,512]{2,1,0:T(8,128)(2,1)S(1)} %maximum_select_fusion), kind=kOutput, calls=%fused_computation.2 | convolution fusion | flops 8589934592 | bytes 42991616 | tf_op jit(solution)/shard_map/dot_general | solution.py:59
  69.1 28.5 %convolution_add_fusion = f32[1024,8192]{1,0:T(8,128)} fusion(f32[1024,8192]{1,0:T(8,128)} %fusion.1, bf16[1,2,512,8192]{3,2,1,0:T(8,128)(2,1)} %param.14, bf16[2,1024,512]{2,1,0:T(8,128)(2,1)S(1)} %maximum_select_fusion), kind=kOutput, calls=%fused_computation | convolution fusion | flops 8598323200 | bytes 76546048 | tf_op jit(solution)/shard_map/dot_general | solution.py:61
  97.6 0.0 copy-start.3
  97.6 0.0 reduce-scatter.2.cloned.1.call-update
  97.6 0.0 copy-start.1
  97.7 367.2 %reduce-scatter.2.cloned.1.call-done = f32[32,8192]{1,0:T(8,128)} async-done(((f32[1024,8192]{1,0:T(8,128)}), f32[32,8192]{1,0:T(8,128)}) %reduce-scatter.2.cloned.1.call-update) | async-done | bytes 1048592 | tf_op jit(solution)/shard_map/reduce_scatter | solution.py:60
  464.9 0.0 copy-done.3
  464.9 2.1 fusion.12
  467.0 0.0 copy-done.1
  (3 shorter events, 0.0 us)
Async XLA Ops:
  6.5 9.9 %copy-start = (f32[16]{0:T(128)S(1)}, f32[16]{0:T(128)}, u32[]{:S(2)}) copy-start(f32[16]{0:T(128)} %param.19) | copy-start | bytes 196
  6.5 8.4 %copy-start.6 = (f32[2,512]{1,0:T(2,128)S(1)}, f32[2,512]{1,0:T(2,128)}, u32[]{:S(2)}) copy-start(f32[2,512]{1,0:T(2,128)} %param.13) | copy-start | bytes 12292
  6.5 8.4 %copy-start.7 = (f32[2,512]{1,0:T(2,128)S(1)}, f32[2,512]{1,0:T(2,128)}, u32[]{:S(2)}) copy-start(f32[2,512]{1,0:T(2,128)} %param.12) | copy-start | bytes 12292
  6.5 8.4 %copy-start.4 = (s32[2,1024]{1,0:T(2,128)S(1)}, s32[2,1024]{1,0:T(2,128)}, u32[]{:S(2)}) copy-start(s32[2,1024]{1,0:T(2,128)} %param.18) | copy-start | bytes 24580
  6.5 8.4 %copy-start.5 = (s32[2,1024]{1,0:T(2,128)S(1)}, s32[2,1024]{1,0:T(2,128)}, u32[]{:S(2)}) copy-start(s32[2,1024]{1,0:T(2,128)} %param.16) | copy-start | bytes 24580
  6.5 8.4 %copy-start.8 = (s32[2,1024]{1,0:T(2,128)S(1)}, s32[2,1024]{1,0:T(2,128)}, u32[]{:S(2)}) copy-start(s32[2,1024]{1,0:T(2,128)} %param.17) | copy-start | bytes 24580
  6.6 458.3 %reduce-scatter.2.cloned.1.call-start = ((), (), s32[]{:S(2)}) async-start(), calls=%async_computation.1 | async-start | bytes 34603008 | tf_op jit(solution)/shard_map/reduce_scatter | solution.py:60
  14.8 4.4 collective-permute-start
  21.5 26.8 %collective-permute-start.1 = (bf16[1024,512]{1,0:T(8,128)(2,1)S(1)}, bf16[1024,512]{1,0:T(8,128)(2,1)S(1)}, u32[]{:S(2)}, u32[]{:S(2)}) collective-permute-start(bf16[1024,512]{1,0:T(8,128)(2,1)S(1)} %select_convert_fusion), channel_id=1, source_target_pairs={{0,64},{32,96},{64,0},{96,32},{1,65},{33,97},{65,1},{97,33},{2,66}... | collective-permute-start | bytes 3145736 | tf_op jit(solution)/shard_map/ppermute | solution.py:10
  48.3 1.0 copy-start.2
  97.6 367.3 %copy-start.3 = (f32[1,8192]{1,0:T(1,128)S(1)}, f32[1,8192]{1,0:T(1,128)}, u32[]{:S(2)}) copy-start(f32[1,8192]{1,0:T(1,128)} %param.15) | copy-start | bytes 98308
  97.6 369.3 %copy-start.1 = (f32[16]{0:T(128)S(1)}, f32[16]{0:T(128)}, u32[]{:S(2)}) copy-start(f32[16]{0:T(128)} %param.19) | copy-start | bytes 196
Sparse Core Ops, SparseCore 0:
  97.8 367.0 reduce-scatter.1
where the time goes:
time: 475 us; the launch traced here: 474 us
  waiting for transfers between devices  391 us (82%)
  matrix products  57.9 us (12%)
  between operations  13.5 us (3%)
  other arithmetic  6.38 us (1%)
    reduce_scatter x1, waiting for transfers between devices, shards(): lax.psum_scatter(total + jnp.dot(both_codes[1], dec_weight[0, 1], preferr...  367 us
    dot_general x1, matrix products, shards(): jnp.dot(both_codes[1], dec_weight[0, 1], preferred_element_type=jnp.float32)  28.5 us
    ppermute x2, waiting for transfers between devices, swapped(): return lax.ppermute(value, axis, pairs)  24.2 us
    dot_general x1, matrix products, shards(): jnp.dot(both_codes[0], dec_weight[0, 0], preferred_element_type=jnp.float32)  17.9 us
  transfers between devices with their start and end apart: 3, of which 3 were waited for; matrix products, arithmetic and copies ran while one was open for 1% of the time, Pallas kernels for 0%

commit v1 on v0

v1 whole, which is shorter than its diff:
```python
import functools

import jax
import jax.numpy as jnp
from jax import lax
from jax.experimental import pallas as pl
from jax.experimental.pallas import tpu as pltpu
from jax.sharding import PartitionSpec as P

BF16, F32 = jnp.bfloat16, jnp.float32
LINKS = (8, 1, 4, 24, 3)
STEPS = len(LINKS)
TILE = 256
PARTS = tuple((p, t) for p, t in zip((0, 1, 2, 3, 4), (7, 7, 6, 6, 6)))


def xor_swap(value, axis, mask):
    return lax.ppermute(value, axis, [(i, i ^ mask) for i in range(lax.axis_size(axis))])


def block_masks():
    n = 1 << STEPS
    out = []
    for j in range(n):
        m = 0
        for k in range(STEPS):
            if (j >> (STEPS - 1 - k)) & 1:
                m ^= LINKS[k]
        out.append(m)
    return out


def part_blocks(first):
    out = []
    for j in range(1 << STEPS):
        base = 0
        for i in range(STEPS):
            if (j >> (STEPS - 1 - i)) & 1:
                base |= 1 << (STEPS - 1 - (first + i) % STEPS)
        out.append(base)
    return out


def encode_kernel(x_hbm, w_hbm, keep_ref, send_ref, xbuf, wbuf, xsem, wsem, *, masks, rows, tile):
    me = lax.axis_index("lat")
    core = lax.axis_index("layer") % 2
    width = w_hbm.shape[2] // 2
    wcopy = pltpu.make_async_copy(w_hbm.at[0], wbuf, wsem)
    wcopy.start()
    copies = []
    for j, mask in enumerate(masks):
        src = jnp.bitwise_xor(me, mask)
        copies.append(
            pltpu.make_async_copy(
                x_hbm.at[0, pl.ds(pl.multiple_of(src * rows, rows), rows)],
                xbuf.at[pl.ds(j * rows, rows)],
                xsem.at[j],
            )
        )
    for c in copies:
        c.start()
    wcopy.wait()
    mine = pl.ds(pl.multiple_of(core * width, width), width)
    other = pl.ds(pl.multiple_of((1 - core) * width, width), width)
    per = tile // rows
    for t in range(len(masks) // per):
        for c in copies[t * per : (t + 1) * per]:
            c.wait()
        at = pl.ds(t * tile, tile)
        send_ref[at, :] = jnp.dot(xbuf[at, :], wbuf[:, other], preferred_element_type=F32)
        keep_ref[at, :] = jnp.dot(xbuf[at, :], wbuf[:, mine], preferred_element_type=F32)


def encode(x, w):
    tokens, depth = x.shape[1], x.shape[2]
    width = w.shape[2] // 2
    masks = block_masks()
    rows = tokens // len(masks)
    half = jax.ShapeDtypeStruct((tokens, width), F32)
    return pl.pallas_call(
        functools.partial(encode_kernel, masks=masks, rows=rows, tile=256),
        out_shape=(half, half),
        in_specs=[pl.BlockSpec(memory_space=pl.ANY)] * 2,
        out_specs=[pl.BlockSpec(memory_space=pltpu.VMEM)] * 2,
        scratch_shapes=[
            pltpu.VMEM((tokens, depth), BF16),
            pltpu.VMEM((depth, 2 * width), BF16),
            pltpu.SemaphoreType.DMA((len(masks),)),
            pltpu.SemaphoreType.DMA,
        ],
        compiler_params=pltpu.CompilerParams(vmem_limit_bytes=28 << 20),
        cost_estimate=pl.CostEstimate(
            flops=4 * tokens * depth * width,
            bytes_accessed=2 * (tokens * depth + 2 * depth * width) + 8 * tokens * width,
            transcendentals=0,
        ),
        name="encode",
    )(x, w)


def decode_kernel(codes_ref, w_ref, keep_ref, send_ref, lhs, *, blocks, rows):
    half = len(blocks) // 2

    @pl.when(pl.program_id(0) == 0)
    def _():
        for j, b in enumerate(blocks):
            lhs[pl.ds(j * rows, rows), :] = codes_ref[pl.ds(b * rows, rows), :]

    n = half * rows
    w = jnp.concatenate([w_ref[0, 0], w_ref[0, 1]], axis=0)
    send_ref[...] = jnp.dot(lhs[n:, :], w, preferred_element_type=F32).astype(BF16)
    keep_ref[...] = jnp.dot(lhs[:n, :], w, preferred_element_type=F32)


def decode(codes, w, first, at, tiles):
    tokens, depth = codes.shape
    blocks = part_blocks(first)
    rows = tokens // len(blocks)
    n = tokens // 2
    wide = tiles * TILE
    return pl.pallas_call(
        functools.partial(decode_kernel, blocks=blocks, rows=rows),
        out_shape=(jax.ShapeDtypeStruct((n, wide), F32), jax.ShapeDtypeStruct((n, wide), BF16)),
        grid=(tiles,),
        in_specs=[
            pl.BlockSpec((tokens, depth), lambda j: (0, 0)),
            pl.BlockSpec((1, 2, depth // 2, TILE), lambda j: (0, 0, 0, at + j)),
        ],
        out_specs=[
            pl.BlockSpec((n, TILE), lambda j: (0, j)),
            pl.BlockSpec((n, TILE), lambda j: (0, j)),
        ],
        scratch_shapes=[pltpu.VMEM((tokens, depth), BF16)],
        compiler_params=pltpu.CompilerParams(vmem_limit_bytes=20 << 20),
        cost_estimate=pl.CostEstimate(
            flops=2 * tokens * depth * wide,
            bytes_accessed=2 * tokens * depth + 2 * depth * wide + 6 * n * wide,
            transcendentals=0,
        ),
        name=f"decode{first}",
    )(codes, w)


def shards(
    resid_halves,
    enc_weight,
    enc_bias,
    jump_threshold,
    dec_weight,
    dec_bias,
    clamp_rows,
    clamp_feats,
    clamp_slots,
    clamp_values,
):
    group = lax.axis_index("layer")
    me = lax.axis_index("lat")
    source, core = group // 2, group % 2
    tokens = resid_halves.shape[1]
    width = enc_weight.shape[2]
    hw = width // 2
    masks = jnp.array(block_masks(), jnp.int32)
    rows = tokens // masks.shape[0]

    keep, send = encode(resid_halves, enc_weight)
    recv = xor_swap(send, "layer", 1)

    row_token = (
        jnp.bitwise_xor(masks, me)[:, None] * rows + jnp.arange(rows, dtype=jnp.int32)[None, :]
    ).reshape(tokens)
    my_rows = lax.dynamic_index_in_dim(clamp_rows, source, 0, keepdims=False)
    my_pick = lax.dynamic_index_in_dim(
        clamp_feats * clamp_values.shape[0] + clamp_slots, source, 0, keepdims=False
    )
    row_hot = (my_rows[:, None] == row_token[None, :]).astype(F32)
    pick = jnp.dot(my_pick.astype(F32), row_hot, precision=lax.Precision.HIGHEST).astype(jnp.int32)
    feat, slot = pick // clamp_values.shape[0], pick % clamp_values.shape[0]
    slot_hot = slot[:, None] == jnp.arange(clamp_values.shape[0], dtype=jnp.int32)[None, :]
    value = jnp.sum(jnp.where(slot_hot, clamp_values[None, :], 0.0), axis=1)
    first = core * hw
    column = feat - me * width - first

    my_bias = lax.dynamic_slice(enc_bias, (source, first), (1, hw))
    my_thresh = lax.dynamic_slice(jump_threshold, (source, first), (1, hw))
    pre = keep + recv + my_bias
    ramp = jnp.clip((pre - my_thresh) / 0.25 + 1.0, 0.0, 1.0)
    hit = column[:, None] == jnp.arange(hw, dtype=jnp.int32)[None, :]
    own = jnp.where(hit, value[:, None], pre * ramp).astype(BF16)

    own_far = xor_swap(own, "layer", 2)
    own_sib = xor_swap(own, "layer", 1)
    far_sib = xor_swap(own_far, "layer", 1)

    def joined(mine, sib):
        return jnp.where(
            core == 0, jnp.concatenate([mine, sib], 1), jnp.concatenate([sib, mine], 1)
        )

    here, there = joined(own, own_sib), joined(own_far, far_sib)
    codes = jnp.where(
        source == 0, jnp.concatenate([here, there], 1), jnp.concatenate([there, here], 1)
    )

    outs, at = [], 0
    for first_link, tiles in PARTS:
        kept, out = decode(codes, dec_weight, first_link, at, tiles)
        for i in range(STEPS):
            got = xor_swap(out, "lat", LINKS[(first_link + i) % STEPS])
            total = kept + got.astype(F32)
            n = total.shape[0] // 2
            kept, out = total[:n], total[n:].astype(BF16)
            if i == STEPS - 1:
                outs.append(total)
        at += tiles
    summed = jnp.concatenate(outs, axis=1)
    return (summed + dec_bias).astype(BF16)[None]


def solution(mesh):
    return jax.shard_map(
        shards,
        mesh=mesh,
        in_specs=(
            P("layer", None, None),
            P("layer", None, "lat"),
            P(None, "lat"),
            P(None, "lat"),
            P("layer", None, "lat", None),
            P("layer", None),
            P(),
            P(),
            P(),
            P(),
        ),
        out_specs=P("layer", "lat", None),
        check_vma=False,
    )
```

time: 475 us -> 174 us (0.37)
  waiting for transfers between devices: 391 us -> 83.2 us
  matrix products: 57.9 us -> 1.34 us
  Pallas kernels: 0 us -> 33.9 us
  starting transfers between devices: 3.47 us -> 29.9 us
  between operations: 13.5 us -> 0.57 us
  local copies, waits for them, and re-layouts: 1.03 us -> 13.8 us
    reduce_scatter x1 -> x0, waiting for transfers between devices: 367 us -> none  [shards(): lax.psum_scatter(total + jnp.dot(both_codes[1], dec_weight[0, 1], preferr...]
    ppermute x2 -> x29, waiting for transfers between devices: 24.2 us -> 83.2 us  [xor_swap(): lax.ppermute(value, axis, [(i, i ^ mask) for i in range(lax.axis_size(axi...]
    dot_general x6 -> x1, matrix products: 57.9 us -> 1.34 us  [shards(): jnp.dot(my_pick.astype(F32), row_hot, precision=lax.Precision.HIGHEST)]
    pallas_call x0 -> x6, Pallas kernels: none -> 33.9 us  [the longest x5 27.5 us: decode(): pl.pallas_call(functools.partial(decode_kernel, blocks=blocks, rows=rows)...]
    ppermute x2 -> x29, starting transfers between devices: 3.44 us -> 29.9 us  [xor_swap(): lax.ppermute(value, axis, [(i, i ^ mask) for i in range(lax.axis_size(axi...]
    unnamed x18 -> x20, local copies, waits for them, and re-layouts: 1 us -> 11.4 us
    add x0 -> x21, other arithmetic: none -> 7.81 us  [the longest x20 7.73 us: shards(): total = kept + got.astype(F32)]
  transfers between devices with their start and end apart: 3 -> 29, of which waited for: 3 -> 16; matrix products, arithmetic and copies ran while one was open for 1% -> 7% of each run, Pallas kernels for 0% -> 13%
where the time goes in v1:
time: 174 us; the launch traced here: 173 us
  waiting for transfers between devices  83.2 us (48%)
  Pallas kernels  33.9 us (19%)
  starting transfers between devices  29.9 us (17%)
  local copies, waits for them, and re-layouts  13.8 us (8%)
  other arithmetic  10.5 us (6%)
    ppermute x29, waiting for transfers between devices, xor_swap(): lax.ppermute(value, axis, [(i, i ^ mask) for i in range(lax.axis_size(axi...  83.2 us
    ppermute x29, starting transfers between devices, xor_swap(): lax.ppermute(value, axis, [(i, i ^ mask) for i in range(lax.axis_size(axi...  29.9 us
    pallas_call x5, Pallas kernels, decode(): pl.pallas_call(functools.partial(decode_kernel, blocks=blocks, rows=rows)...  27.5 us
    unnamed x20, local copies, waits for them, and re-layouts  11.4 us
    add x20, other arithmetic, shards(): total = kept + got.astype(F32)  7.73 us
    pallas_call x1, Pallas kernels, encode(): pl.pallas_call(functools.partial(encode_kernel, masks=masks, rows=rows, t...  6.39 us
  transfers between devices with their start and end apart: 29, of which 16 were waited for; matrix products, arithmetic and copies ran while one was open for 7% of the time, Pallas kernels for 13%

profile of v1, /device:TPU:0, one launch (start us, length us, event | category | flops | bytes accessed | tf_op | source)
XLA Modules:
  0.0 173.3 jit_solution(18270748979302566122)
XLA Ops:
  0.0 3.4 %copy-done.3 = bf16[1,1024,4096]{2,1,0:T(8,128)(2,1)S(1)} copy-done((bf16[1,1024,4096]{2,1,0:T(8,128)(2,1)S(1)}, bf16[1,1024,4096]{2,1,0:T(8,128)(2,1)}, u32[]{:S(2)}) %copy-start.3) | copy-done | bytes 8388632
  3.4 2.2 %copy-done.4 = bf16[1,4096,512]{2,1,0:T(8,128)(2,1)S(1)} copy-done((bf16[1,4096,512]{2,1,0:T(8,128)(2,1)S(1)}, bf16[1,4096,512]{2,1,0:T(8,128)(2,1)}, u32[]{:S(2)}) %copy-start.4) | copy-done | bytes 4194328
  5.6 6.4 %encode.1 = (f32[1024,256]{1,0:T(8,128)S(1)}, f32[1024,256]{1,0:T(8,128)S(1)}) custom-call(bf16[1,1024,4096]{2,1,0:T(8,128)(2,1)S(1)} %copy-done.3, bf16[1,4096,512]{2,1,0:T(8,128)(2,1)S(1)} %copy-done.4), custom_call_target="tpu_custom_call" | custom-call | flops 4294967296 | bytes 14680064 | tf_op jit(solution)/shard_map/encode/pallas_call | solution.py:80
  12.1 0.8 dynamic_slice.16
  12.9 0.8 dynamic_slice.15
  13.8 1.3 fusion
  15.7 3.4 %collective-permute-start.2 = (bf16[1024,256]{1,0:T(8,128)(2,1)S(1)}, bf16[1024,256]{1,0:T(8,128)(2,1)S(1)}, u32[]{:S(2)}, u32[]{:S(2)}) collective-permute-start(bf16[1024,256]{1,0:T(8,128)(2,1)S(1)} %select_convert_fusion), channel_id=1, source_target_pairs={{0,64},{32,96},{64,0},{96,32},{1,65},{33,97},{65,1},{97,33},{2,66}... | collective-permute-start | bytes 1572872 | tf_op jit(solution)/shard_map/ppermute | solution.py:18
  19.2 12.4 %collective-permute-done.2 = bf16[1024,256]{1,0:T(8,128)(2,1)S(1)} collective-permute-done((bf16[1024,256]{1,0:T(8,128)(2,1)S(1)}, bf16[1024,256]{1,0:T(8,128)(2,1)S(1)}, u32[]{:S(2)}, u32[]{:S(2)}) %collective-permute-start.2) | collective-permute-done | bytes 524320 | tf_op jit(solution)/shard_map/ppermute | solution.py:18
  31.9 1.6 collective-permute-done.3
  33.8 0.6 maximum_select_fusion.codes_ref
  34.4 5.8 %copy-done.2 = bf16[1,2,512,8192]{3,2,1,0:T(8,128)(2,1)S(1)} copy-done((bf16[1,2,512,8192]{3,2,1,0:T(8,128)(2,1)S(1)}, bf16[1,2,512,8192]{3,2,1,0:T(8,128)(2,1)}, u32[]{:S(2)}) %copy-start.2) | copy-done | bytes 16777240
  40.2 5.2 %decode2.1 = (f32[512,1536]{1,0:T(8,128)S(1)}, bf16[512,1536]{1,0:T(8,128)(2,1)S(1)}) custom-call(bf16[1024,1024]{1,0:T(8,128)(2,1)S(1)} %maximum_select_fusion.codes_ref, bf16[1,2,512,8192]{3,2,1,0:T(8,128)(2,1)S(1)} %copy-done.2), custom_call_target="tpu_custom_call" | custom-call | flops 3221225472 | bytes 9961472 | tf_op jit(solution)/shard_map/decode2/pallas_call | solution.py:121
  45.4 1.7 collective-permute-start.14
  47.1 5.2 %decode3.1 = (f32[512,1536]{1,0:T(8,128)S(1)}, bf16[512,1536]{1,0:T(8,128)(2,1)S(1)}) custom-call(bf16[1024,1024]{1,0:T(8,128)(2,1)S(1)} %maximum_select_fusion.codes_ref, bf16[1,2,512,8192]{3,2,1,0:T(8,128)(2,1)S(1)} %copy-done.2), custom_call_target="tpu_custom_call" | custom-call | flops 3221225472 | bytes 9961472 | tf_op jit(solution)/shard_map/decode3/pallas_call | solution.py:121
  52.3 2.8 %collective-permute-start.19 = (bf16[512,1536]{1,0:T(8,128)(2,1)S(1)}, bf16[512,1536]{1,0:T(8,128)(2,1)}, u32[]{:S(2)}, u32[]{:S(2)}) collective-permute-start(bf16[512,1536]{1,0:T(8,128)(2,1)S(1)} %get-tuple-element.26), channel_id=1, source_target_pairs={{0,24},{1,25},{2,26},{3,27},{4,28},{5,29},{6,30},{7,31},{8,16},{9,... | collective-permute-start | bytes 4718600 | tf_op jit(solution)/shard_map/ppermute | solution.py:18
  55.1 5.2 %decode4.1 = (f32[512,1536]{1,0:T(8,128)S(1)}, bf16[512,1536]{1,0:T(8,128)(2,1)S(1)}) custom-call(bf16[1024,1024]{1,0:T(8,128)(2,1)S(1)} %maximum_select_fusion.codes_ref, bf16[1,2,512,8192]{3,2,1,0:T(8,128)(2,1)S(1)} %copy-done.2), custom_call_target="tpu_custom_call" | custom-call | flops 3221225472 | bytes 9961472 | tf_op jit(solution)/shard_map/decode4/pallas_call | solution.py:121
  60.3 4.3 %collective-permute-start.24 = (bf16[512,1536]{1,0:T(8,128)(2,1)S(1)}, bf16[512,1536]{1,0:T(8,128)(2,1)}, u32[]{:S(2)}, u32[]{:S(2)}) collective-permute-start(bf16[512,1536]{1,0:T(8,128)(2,1)S(1)} %get-tuple-element.28), channel_id=1, source_target_pairs={{0,3},{1,2},{2,1},{3,0},{4,7},{5,6},{6,5},{7,4},{8,11},{9,10},{10,... | collective-permute-start | bytes 4718600 | tf_op jit(solution)/shard_map/ppermute | solution.py:18
  64.6 6.0 %decode0.1 = (f32[512,1792]{1,0:T(8,128)S(1)}, bf16[512,1792]{1,0:T(8,128)(2,1)S(1)}) custom-call(bf16[1024,1024]{1,0:T(8,128)(2,1)S(1)} %maximum_select_fusion.codes_ref, bf16[1,2,512,8192]{3,2,1,0:T(8,128)(2,1)S(1)} %copy-done.2), custom_call_target="tpu_custom_call" | custom-call | flops 3758096384 | bytes 11272192 | tf_op jit(solution)/shard_map/decode0/pallas_call | solution.py:121
  70.6 6.0 %decode1.1 = (f32[512,1792]{1,0:T(8,128)S(1)}, bf16[512,1792]{1,0:T(8,128)(2,1)S(1)}) custom-call(bf16[1024,1024]{1,0:T(8,128)(2,1)S(1)} %maximum_select_fusion.codes_ref, bf16[1,2,512,8192]{3,2,1,0:T(8,128)(2,1)S(1)} %copy-done.2), custom_call_target="tpu_custom_call" | custom-call | flops 3758096384 | bytes 11272192 | tf_op jit(solution)/shard_map/decode1/pallas_call | solution.py:121
  76.9 5.1 %collective-permute-done.14 = bf16[512,1536]{1,0:T(8,128)(2,1)} collective-permute-done((bf16[512,1536]{1,0:T(8,128)(2,1)S(1)}, bf16[512,1536]{1,0:T(8,128)(2,1)}, u32[]{:S(2)}, u32[]{:S(2)}) %collective-permute-start.14) | collective-permute-done | bytes 1572896 | tf_op jit(solution)/shard_map/ppermute | solution.py:18
  82.0 1.9 %convert_add_fusion.4 = f32[512,1536]{1,0:T(8,128)S(1)} fusion(f32[512,1536]{1,0:T(8,128)S(1)} %get-tuple-element.23, bf16[512,1536]{1,0:T(8,128)(2,1)} %collective-permute-done.14), kind=kLoop, calls=%fused_computation.6 | loop fusion | flops 1572864 | bytes 7864320 | tf_op jit(solution)/shard_map/add | solution.py:209
  84.0 2.9 %collective-permute-start.15 = (bf16[256,1536]{1,0:T(8,128)(2,1)S(1)}, bf16[256,1536]{1,0:T(8,128)(2,1)S(1)}, u32[]{:S(2)}, u32[]{:S(2)}) collective-permute-start(bf16[256,1536]{1,0:T(8,128)(2,1)S(1)} %slice.284), channel_id=1, source_target_pairs={{0,24},{1,25},{2,26},{3,27},{4,28},{5,29},{6,30},{7,31},{8,16},{9,... | collective-permute-start | bytes 2359304 | tf_op jit(solution)/shard_map/ppermute | solution.py:18
  86.8 4.1 %collective-permute-done.19 = bf16[512,1536]{1,0:T(8,128)(2,1)} collective-permute-done((bf16[512,1536]{1,0:T(8,128)(2,1)S(1)}, bf16[512,1536]{1,0:T(8,128)(2,1)}, u32[]{:S(2)}, u32[]{:S(2)}) %collective-permute-start.19) | collective-permute-done | bytes 1572896 | tf_op jit(solution)/shard_map/ppermute | solution.py:18
  91.0 1.9 %convert_add_fusion.3 = f32[512,1536]{1,0:T(8,128)S(1)} fusion(f32[512,1536]{1,0:T(8,128)S(1)} %get-tuple-element.25, bf16[512,1536]{1,0:T(8,128)(2,1)} %collective-permute-done.19), kind=kLoop, calls=%fused_computation.5 | loop fusion | flops 1572864 | bytes 7864320 | tf_op jit(solution)/shard_map/add | solution.py:209
  92.9 4.1 %collective-permute-start.20 = (bf16[256,1536]{1,0:T(8,128)(2,1)S(1)}, bf16[256,1536]{1,0:T(8,128)(2,1)S(1)}, u32[]{:S(2)}, u32[]{:S(2)}) collective-permute-start(bf16[256,1536]{1,0:T(8,128)(2,1)S(1)} %slice.283), channel_id=1, source_target_pairs={{0,3},{1,2},{2,1},{3,0},{4,7},{5,6},{6,5},{7,4},{8,11},{9,10},{10,... | collective-permute-start | bytes 2359304 | tf_op jit(solution)/shard_map/ppermute | solution.py:18
  97.0 2.9 %collective-permute-done.24 = bf16[512,1536]{1,0:T(8,128)(2,1)} collective-permute-done((bf16[512,1536]{1,0:T(8,128)(2,1)S(1)}, bf16[512,1536]{1,0:T(8,128)(2,1)}, u32[]{:S(2)}, u32[]{:S(2)}) %collective-permute-start.24) | collective-permute-done | bytes 1572896 | tf_op jit(solution)/shard_map/ppermute | solution.py:18
  100.0 1.9 %convert_add_fusion.2 = f32[512,1536]{1,0:T(8,128)S(1)} fusion(f32[512,1536]{1,0:T(8,128)S(1)} %get-tuple-element.27, bf16[512,1536]{1,0:T(8,128)(2,1)} %collective-permute-done.24), kind=kLoop, calls=%fused_computation.4 | loop fusion | flops 1572864 | bytes 7864320 | tf_op jit(solution)/shard_map/add | solution.py:209
  102.2 17.4 %collective-permute-done.4 = bf16[512,1792]{1,0:T(8,128)(2,1)S(1)} collective-permute-done((bf16[512,1792]{1,0:T(8,128)(2,1)S(1)}, bf16[512,1792]{1,0:T(8,128)(2,1)S(1)}, u32[]{:S(2)}, u32[]{:S(2)}) %collective-permute-start.4) | collective-permute-done | bytes 1835040 | tf_op jit(solution)/shard_map/ppermute | solution.py:18
  121.4 0.6 collective-permute-start.16
  122.5 14.0 %collective-permute-done.25 = bf16[256,1536]{1,0:T(8,128)(2,1)S(1)} collective-permute-done((bf16[256,1536]{1,0:T(8,128)(2,1)S(1)}, bf16[256,1536]{1,0:T(8,128)(2,1)S(1)}, u32[]{:S(2)}, u32[]{:S(2)}) %collective-permute-start.25) | collective-permute-done | bytes 786464 | tf_op jit(solution)/shard_map/ppermute | solution.py:18
  136.8 5.2 %collective-permute-done.5 = bf16[256,1792]{1,0:T(8,128)(2,1)S(1)} collective-permute-done((bf16[256,1792]{1,0:T(8,128)(2,1)S(1)}, bf16[256,1792]{1,0:T(8,128)(2,1)S(1)}, u32[]{:S(2)}, u32[]{:S(2)}) %collective-permute-start.5) | collective-permute-done | bytes 917536 | tf_op jit(solution)/shard_map/ppermute | solution.py:18
  142.2 0.5 collective-permute-start.6
  143.0 0.5 collective-permute-start.11
  144.0 0.9 collective-permute-done.21
  145.0 0.8 collective-permute-start.22
  145.8 4.6 %collective-permute-done.26 = bf16[128,1536]{1,0:T(8,128)(2,1)S(1)} collective-permute-done((bf16[128,1536]{1,0:T(8,128)(2,1)S(1)}, bf16[128,1536]{1,0:T(8,128)(2,1)S(1)}, u32[]{:S(2)}, u32[]{:S(2)}) %collective-permute-start.26) | collective-permute-done | bytes 393248 | tf_op jit(solution)/shard_map/ppermute | solution.py:18
  151.3 1.4 collective-permute-done.22
  152.8 0.5 collective-permute-start.23
  153.4 2.9 %collective-permute-done.27 = bf16[64,1536]{1,0:T(8,128)(2,1)S(1)} collective-permute-done((bf16[64,1536]{1,0:T(8,128)(2,1)S(1)}, bf16[64,1536]{1,0:T(8,128)(2,1)S(1)}, u32[]{:S(2)}, u32[]{:S(2)}) %collective-permute-start.27) | collective-permute-done | bytes 196640 | tf_op jit(solution)/shard_map/ppermute | solution.py:18
  156.4 0.6 collective-permute-start.28
  157.0 2.8 %collective-permute-start.7 = (bf16[64,1792]{1,0:T(8,128)(2,1)S(1)}, bf16[64,1792]{1,0:T(8,128)(2,1)S(1)}, u32[]{:S(2)}, u32[]{:S(2)}) collective-permute-start(bf16[64,1792]{1,0:T(8,128)(2,1)S(1)} %slice.291), channel_id=1, source_target_pairs={{0,24},{1,25},{2,26},{3,27},{4,28},{5,29},{6,30},{7,31},{8,16},{9,... | collective-permute-start | bytes 688136 | tf_op jit(solution)/shard_map/ppermute | solution.py:18
  160.0 0.7 collective-permute-start.12
  160.7 4.1 %collective-permute-done.7 = bf16[64,1792]{1,0:T(8,128)(2,1)S(1)} collective-permute-done((bf16[64,1792]{1,0:T(8,128)(2,1)S(1)}, bf16[64,1792]{1,0:T(8,128)(2,1)S(1)}, u32[]{:S(2)}, u32[]{:S(2)}) %collective-permute-start.7) | collective-permute-done | bytes 229408 | tf_op jit(solution)/shard_map/ppermute | solution.py:18
  164.8 0.7 collective-permute-start.8
  165.5 1.8 %collective-permute-done.12 = bf16[64,1792]{1,0:T(8,128)(2,1)S(1)} collective-permute-done((bf16[64,1792]{1,0:T(8,128)(2,1)S(1)}, bf16[64,1792]{1,0:T(8,128)(2,1)S(1)}, u32[]{:S(2)}, u32[]{:S(2)}) %collective-permute-start.12) | collective-permute-done | bytes 229408 | tf_op jit(solution)/shard_map/ppermute | solution.py:18
  167.5 3.4 %collective-permute-done.8 = bf16[32,1792]{1,0:T(8,128)(2,1)S(1)} collective-permute-done((bf16[32,1792]{1,0:T(8,128)(2,1)S(1)}, bf16[32,1792]{1,0:T(8,128)(2,1)S(1)}, u32[]{:S(2)}, u32[]{:S(2)}) %collective-permute-start.8) | collective-permute-done | bytes 114720 | tf_op jit(solution)/shard_map/ppermute | solution.py:18
  170.9 1.4 collective-permute-done.13
  172.4 0.9 add_convert_fusion
  (95 shorter events, 7.4 us)
Async XLA Ops:
  0.0 13.8 %copy-start = (s32[2,1024]{1,0:T(2,128)S(1)}, s32[2,1024]{1,0:T(2,128)}, u32[]{:S(2)}) copy-start(s32[2,1024]{1,0:T(2,128)} %param.17) | copy-start | bytes 24580
  0.0 3.4 %copy-start.3 = (bf16[1,1024,4096]{2,1,0:T(8,128)(2,1)S(1)}, bf16[1,1024,4096]{2,1,0:T(8,128)(2,1)}, u32[]{:S(2)}) copy-start(bf16[1,1024,4096]{2,1,0:T(8,128)(2,1)} %x_hbm.1) | copy-start | bytes 25165828
  3.4 2.2 %copy-start.4 = (bf16[1,4096,512]{2,1,0:T(8,128)(2,1)S(1)}, bf16[1,4096,512]{2,1,0:T(8,128)(2,1)}, u32[]{:S(2)}) copy-start(bf16[1,4096,512]{2,1,0:T(8,128)(2,1)} %w_hbm.1) | copy-start | bytes 12582916
  5.6 8.1 %copy-start.9 = (s32[32]{0:T(128)S(1)}, s32[32]{0:T(128)}, u32[]{:S(2)}) copy-start(s32[32]{0:T(128)} %constant.82.clone) | copy-start | bytes 388
  5.6 8.2 %copy-start.7 = (s32[2,1024]{1,0:T(2,128)S(1)}, s32[2,1024]{1,0:T(2,128)}, u32[]{:S(2)}) copy-start(s32[2,1024]{1,0:T(2,128)} %param.19) | copy-start | bytes 24580
  5.6 8.2 %copy-start.8 = (s32[2,1024]{1,0:T(2,128)S(1)}, s32[2,1024]{1,0:T(2,128)}, u32[]{:S(2)}) copy-start(s32[2,1024]{1,0:T(2,128)} %param.18) | copy-start | bytes 24580
  5.6 9.6 %copy-start.6 = (f32[16]{0:T(128)S(1)}, f32[16]{0:T(128)}, u32[]{:S(2)}) copy-start(f32[16]{0:T(128)} %param.20) | copy-start | bytes 196
  12.0 3.3 %collective-permute-start = (f32[1024,256]{1,0:T(8,128)S(1)}, f32[1024,256]{1,0:T(8,128)S(1)}, u32[]{:S(2)}, u32[]{:S(2)}) collective-permute-start(f32[1024,256]{1,0:T(8,128)S(1)} %get-tuple-element.18), channel_id=1, source_target_pairs={{0,32},{32,0},{64,96},{96,64},{1,33},{33,1},{65,97},{97,65},{2,34}... | collective-permute-start | bytes 3145736 | tf_op jit(solution)/shard_map/ppermute | solution.py:18
  15.7 15.9 %collective-permute-start.2 = (bf16[1024,256]{1,0:T(8,128)(2,1)S(1)}, bf16[1024,256]{1,0:T(8,128)(2,1)S(1)}, u32[]{:S(2)}, u32[]{:S(2)}) collective-permute-start(bf16[1024,256]{1,0:T(8,128)(2,1)S(1)} %select_convert_fusion), channel_id=1, source_target_pairs={{0,64},{32,96},{64,0},{96,32},{1,65},{33,97},{65,1},{97,33},{2,66}... | collective-permute-start | bytes 1572872 | tf_op jit(solution)/shard_map/ppermute | solution.py:18
  19.0 12.6 %collective-permute-start.1 = (bf16[1024,256]{1,0:T(8,128)(2,1)S(1)}, bf16[1024,256]{1,0:T(8,128)(2,1)S(1)}, u32[]{:S(2)}, u32[]{:S(2)}) collective-permute-start(bf16[1024,256]{1,0:T(8,128)(2,1)S(1)} %select_convert_fusion), channel_id=1, source_target_pairs={{0,32},{32,0},{64,96},{96,64},{1,33},{33,1},{65,97},{97,65},{2,34}... | collective-permute-start | bytes 1572872 | tf_op jit(solution)/shard_map/ppermute | solution.py:18
  31.6 1.9 %collective-permute-start.3 = (bf16[1024,256]{1,0:T(8,128)(2,1)S(1)}, bf16[1024,256]{1,0:T(8,128)(2,1)S(1)}, u32[]{:S(2)}, u32[]{:S(2)}) collective-permute-start(bf16[1024,256]{1,0:T(8,128)(2,1)S(1)} %collective-permute-done.2), channel_id=1, source_target_pairs={{0,32},{32,0},{64,96},{96,64},{1,33},{33,1},{65,97},{97,65},{2,34}... | collective-permute-start | bytes 1572872 | tf_op jit(solution)/shard_map/ppermute | solution.py:18
  34.4 5.8 %copy-start.2 = (bf16[1,2,512,8192]{3,2,1,0:T(8,128)(2,1)S(1)}, bf16[1,2,512,8192]{3,2,1,0:T(8,128)(2,1)}, u32[]{:S(2)}) copy-start(bf16[1,2,512,8192]{3,2,1,0:T(8,128)(2,1)} %w_ref.9) | copy-start | bytes 50331652
  45.4 36.6 %collective-permute-start.14 = (bf16[512,1536]{1,0:T(8,128)(2,1)S(1)}, bf16[512,1536]{1,0:T(8,128)(2,1)}, u32[]{:S(2)}, u32[]{:S(2)}) collective-permute-start(bf16[512,1536]{1,0:T(8,128)(2,1)S(1)} %get-tuple-element.24), channel_id=1, source_target_pairs={{0,4},{1,5},{2,6},{3,7},{4,0},{5,1},{6,2},{7,3},{8,12},{9,13},{10,... | collective-permute-start | bytes 4718600 | tf_op jit(solution)/shard_map/ppermute | solution.py:18
  52.3 38.7 %collective-permute-start.19 = (bf16[512,1536]{1,0:T(8,128)(2,1)S(1)}, bf16[512,1536]{1,0:T(8,128)(2,1)}, u32[]{:S(2)}, u32[]{:S(2)}) collective-permute-start(bf16[512,1536]{1,0:T(8,128)(2,1)S(1)} %get-tuple-element.26), channel_id=1, source_target_pairs={{0,24},{1,25},{2,26},{3,27},{4,28},{5,29},{6,30},{7,31},{8,16},{9,... | collective-permute-start | bytes 4718600 | tf_op jit(solution)/shard_map/ppermute | solution.py:18
  60.3 39.7 %collective-permute-start.24 = (bf16[512,1536]{1,0:T(8,128)(2,1)S(1)}, bf16[512,1536]{1,0:T(8,128)(2,1)}, u32[]{:S(2)}, u32[]{:S(2)}) collective-permute-start(bf16[512,1536]{1,0:T(8,128)(2,1)S(1)} %get-tuple-element.28), channel_id=1, source_target_pairs={{0,3},{1,2},{2,1},{3,0},{4,7},{5,6},{6,5},{7,4},{8,11},{9,10},{10,... | collective-permute-start | bytes 4718600 | tf_op jit(solution)/shard_map/ppermute | solution.py:18
  76.6 43.0 %collective-permute-start.4 = (bf16[512,1792]{1,0:T(8,128)(2,1)S(1)}, bf16[512,1792]{1,0:T(8,128)(2,1)S(1)}, u32[]{:S(2)}, u32[]{:S(2)}) collective-permute-start(bf16[512,1792]{1,0:T(8,128)(2,1)S(1)} %get-tuple-element.20), channel_id=1, source_target_pairs={{0,8},{1,9},{2,10},{3,11},{4,12},{5,13},{6,14},{7,15},{8,0},{9,1},... | collective-permute-start | bytes 5505032 | tf_op jit(solution)/shard_map/ppermute | solution.py:18
  76.9 43.3 %collective-permute-start.9 = (bf16[512,1792]{1,0:T(8,128)(2,1)S(1)}, bf16[512,1792]{1,0:T(8,128)(2,1)S(1)}, u32[]{:S(2)}, u32[]{:S(2)}) collective-permute-start(bf16[512,1792]{1,0:T(8,128)(2,1)S(1)} %get-tuple-element.22), channel_id=1, source_target_pairs={{0,1},{1,0},{2,3},{3,2},{4,5},{5,4},{6,7},{7,6},{8,9},{9,8},{10,11... | collective-permute-start | bytes 5505032 | tf_op jit(solution)/shard_map/ppermute | solution.py:18
  84.0 37.2 %collective-permute-start.15 = (bf16[256,1536]{1,0:T(8,128)(2,1)S(1)}, bf16[256,1536]{1,0:T(8,128)(2,1)S(1)}, u32[]{:S(2)}, u32[]{:S(2)}) collective-permute-start(bf16[256,1536]{1,0:T(8,128)(2,1)S(1)} %slice.284), channel_id=1, source_target_pairs={{0,24},{1,25},{2,26},{3,27},{4,28},{5,29},{6,30},{7,31},{8,16},{9,... | collective-permute-start | bytes 2359304 | tf_op jit(solution)/shard_map/ppermute | solution.py:18
  92.9 29.1 %collective-permute-start.20 = (bf16[256,1536]{1,0:T(8,128)(2,1)S(1)}, bf16[256,1536]{1,0:T(8,128)(2,1)S(1)}, u32[]{:S(2)}, u32[]{:S(2)}) collective-permute-start(bf16[256,1536]{1,0:T(8,128)(2,1)S(1)} %slice.283), channel_id=1, source_target_pairs={{0,3},{1,2},{2,1},{3,0},{4,7},{5,6},{6,5},{7,4},{8,11},{9,10},{10,... | collective-permute-start | bytes 2359304 | tf_op jit(solution)/shard_map/ppermute | solution.py:18
  101.9 34.6 %collective-permute-start.25 = (bf16[256,1536]{1,0:T(8,128)(2,1)S(1)}, bf16[256,1536]{1,0:T(8,128)(2,1)S(1)}, u32[]{:S(2)}, u32[]{:S(2)}) collective-permute-start(bf16[256,1536]{1,0:T(8,128)(2,1)S(1)} %slice.282), channel_id=1, source_target_pairs={{0,8},{1,9},{2,10},{3,11},{4,12},{5,13},{6,14},{7,15},{8,0},{9,1},... | collective-permute-start | bytes 2359304 | tf_op jit(solution)/shard_map/ppermute | solution.py:18
  120.1 21.9 %collective-permute-start.5 = (bf16[256,1792]{1,0:T(8,128)(2,1)S(1)}, bf16[256,1792]{1,0:T(8,128)(2,1)S(1)}, u32[]{:S(2)}, u32[]{:S(2)}) collective-permute-start(bf16[256,1792]{1,0:T(8,128)(2,1)S(1)} %slice.281), channel_id=1, source_target_pairs={{0,1},{1,0},{2,3},{3,2},{4,5},{5,4},{6,7},{7,6},{8,9},{9,8},{10,11... | collective-permute-start | bytes 2752520 | tf_op jit(solution)/shard_map/ppermute | solution.py:18
  120.6 22.1 %collective-permute-start.10 = (bf16[256,1792]{1,0:T(8,128)(2,1)S(1)}, bf16[256,1792]{1,0:T(8,128)(2,1)S(1)}, u32[]{:S(2)}, u32[]{:S(2)}) collective-permute-start(bf16[256,1792]{1,0:T(8,128)(2,1)S(1)} %slice.280), channel_id=1, source_target_pairs={{0,4},{1,5},{2,6},{3,7},{4,0},{5,1},{6,2},{7,3},{8,12},{9,13},{10,... | collective-permute-start | bytes 2752520 | tf_op jit(solution)/shard_map/ppermute | solution.py:18
  121.4 22.1 %collective-permute-start.16 = (bf16[128,1536]{1,0:T(8,128)(2,1)S(1)}, bf16[128,1536]{1,0:T(8,128)(2,1)S(1)}, u32[]{:S(2)}, u32[]{:S(2)}) collective-permute-start(bf16[128,1536]{1,0:T(8,128)(2,1)S(1)} %slice.289), channel_id=1, source_target_pairs={{0,3},{1,2},{2,1},{3,0},{4,7},{5,6},{6,5},{7,4},{8,11},{9,10},{10,... | collective-permute-start | bytes 1179656 | tf_op jit(solution)/shard_map/ppermute | solution.py:18
  122.2 22.7 %collective-permute-start.21 = (bf16[128,1536]{1,0:T(8,128)(2,1)S(1)}, bf16[128,1536]{1,0:T(8,128)(2,1)S(1)}, u32[]{:S(2)}, u32[]{:S(2)}) collective-permute-start(bf16[128,1536]{1,0:T(8,128)(2,1)S(1)} %slice.288), channel_id=1, source_target_pairs={{0,8},{1,9},{2,10},{3,11},{4,12},{5,13},{6,14},{7,15},{8,0},{9,1},... | collective-permute-start | bytes 1179656 | tf_op jit(solution)/shard_map/ppermute | solution.py:18
  136.7 13.7 %collective-permute-start.26 = (bf16[128,1536]{1,0:T(8,128)(2,1)S(1)}, bf16[128,1536]{1,0:T(8,128)(2,1)S(1)}, u32[]{:S(2)}, u32[]{:S(2)}) collective-permute-start(bf16[128,1536]{1,0:T(8,128)(2,1)S(1)} %slice.287), channel_id=1, source_target_pairs={{0,1},{1,0},{2,3},{3,2},{4,5},{5,4},{6,7},{7,6},{8,9},{9,8},{10,11... | collective-permute-start | bytes 1179656 | tf_op jit(solution)/shard_map/ppermute | solution.py:18
  142.2 14.7 %collective-permute-start.6 = (bf16[128,1792]{1,0:T(8,128)(2,1)S(1)}, bf16[128,1792]{1,0:T(8,128)(2,1)S(1)}, u32[]{:S(2)}, u32[]{:S(2)}) collective-permute-start(bf16[128,1792]{1,0:T(8,128)(2,1)S(1)} %slice.286), channel_id=1, source_target_pairs={{0,4},{1,5},{2,6},{3,7},{4,0},{5,1},{6,2},{7,3},{8,12},{9,13},{10,... | collective-permute-start | bytes 1376264 | tf_op jit(solution)/shard_map/ppermute | solution.py:18
  143.0 16.9 %collective-permute-start.11 = (bf16[128,1792]{1,0:T(8,128)(2,1)S(1)}, bf16[128,1792]{1,0:T(8,128)(2,1)S(1)}, u32[]{:S(2)}, u32[]{:S(2)}) collective-permute-start(bf16[128,1792]{1,0:T(8,128)(2,1)S(1)} %slice.285), channel_id=1, source_target_pairs={{0,24},{1,25},{2,26},{3,27},{4,28},{5,29},{6,30},{7,31},{8,16},{9,... | collective-permute-start | bytes 1376264 | tf_op jit(solution)/shard_map/ppermute | solution.py:18
  143.6 7.3 %collective-permute-start.17 = (bf16[64,1536]{1,0:T(8,128)(2,1)S(1)}, bf16[64,1536]{1,0:T(8,128)(2,1)S(1)}, u32[]{:S(2)}, u32[]{:S(2)}) collective-permute-start(bf16[64,1536]{1,0:T(8,128)(2,1)S(1)} %slice.294), channel_id=1, source_target_pairs={{0,8},{1,9},{2,10},{3,11},{4,12},{5,13},{6,14},{7,15},{8,0},{9,1},... | collective-permute-start | bytes 589832 | tf_op jit(solution)/shard_map/ppermute | solution.py:18
  145.0 7.7 %collective-permute-start.22 = (bf16[64,1536]{1,0:T(8,128)(2,1)S(1)}, bf16[64,1536]{1,0:T(8,128)(2,1)S(1)}, u32[]{:S(2)}, u32[]{:S(2)}) collective-permute-start(bf16[64,1536]{1,0:T(8,128)(2,1)S(1)} %slice.293), channel_id=1, source_target_pairs={{0,1},{1,0},{2,3},{3,2},{4,5},{5,4},{6,7},{7,6},{8,9},{9,8},{10,11... | collective-permute-start | bytes 589832 | tf_op jit(solution)/shard_map/ppermute | solution.py:18
  150.6 5.7 %collective-permute-start.27 = (bf16[64,1536]{1,0:T(8,128)(2,1)S(1)}, bf16[64,1536]{1,0:T(8,128)(2,1)S(1)}, u32[]{:S(2)}, u32[]{:S(2)}) collective-permute-start(bf16[64,1536]{1,0:T(8,128)(2,1)S(1)} %slice.292), channel_id=1, source_target_pairs={{0,4},{1,5},{2,6},{3,7},{4,0},{5,1},{6,2},{7,3},{8,12},{9,13},{10,... | collective-permute-start | bytes 589832 | tf_op jit(solution)/shard_map/ppermute | solution.py:18
  151.0 21.3 %collective-permute-start.18 = (bf16[32,1536]{1,0:T(8,128)(2,1)S(1)}, bf16[32,1536]{1,0:T(8,128)(2,1)S(1)}, u32[]{:S(2)}, u32[]{:S(2)}) collective-permute-start(bf16[32,1536]{1,0:T(8,128)(2,1)S(1)} %slice.299), channel_id=1, source_target_pairs={{0,1},{1,0},{2,3},{3,2},{4,5},{5,4},{6,7},{7,6},{8,9},{9,8},{10,11... | collective-permute-start | bytes 294920 | tf_op jit(solution)/shard_map/ppermute | solution.py:18
  152.8 19.5 %collective-permute-start.23 = (bf16[32,1536]{1,0:T(8,128)(2,1)S(1)}, bf16[32,1536]{1,0:T(8,128)(2,1)S(1)}, u32[]{:S(2)}, u32[]{:S(2)}) collective-permute-start(bf16[32,1536]{1,0:T(8,128)(2,1)S(1)} %slice.298), channel_id=1, source_target_pairs={{0,4},{1,5},{2,6},{3,7},{4,0},{5,1},{6,2},{7,3},{8,12},{9,13},{10,... | collective-permute-start | bytes 294920 | tf_op jit(solution)/shard_map/ppermute | solution.py:18
  156.4 16.0 %collective-permute-start.28 = (bf16[32,1536]{1,0:T(8,128)(2,1)S(1)}, bf16[32,1536]{1,0:T(8,128)(2,1)S(1)}, u32[]{:S(2)}, u32[]{:S(2)}) collective-permute-start(bf16[32,1536]{1,0:T(8,128)(2,1)S(1)} %slice.297), channel_id=1, source_target_pairs={{0,24},{1,25},{2,26},{3,27},{4,28},{5,29},{6,30},{7,31},{8,16},{9,... | collective-permute-start | bytes 294920 | tf_op jit(solution)/shard_map/ppermute | solution.py:18
  157.0 7.7 %collective-permute-start.7 = (bf16[64,1792]{1,0:T(8,128)(2,1)S(1)}, bf16[64,1792]{1,0:T(8,128)(2,1)S(1)}, u32[]{:S(2)}, u32[]{:S(2)}) collective-permute-start(bf16[64,1792]{1,0:T(8,128)(2,1)S(1)} %slice.291), channel_id=1, source_target_pairs={{0,24},{1,25},{2,26},{3,27},{4,28},{5,29},{6,30},{7,31},{8,16},{9,... | collective-permute-start | bytes 688136 | tf_op jit(solution)/shard_map/ppermute | solution.py:18
  160.0 7.3 %collective-permute-start.12 = (bf16[64,1792]{1,0:T(8,128)(2,1)S(1)}, bf16[64,1792]{1,0:T(8,128)(2,1)S(1)}, u32[]{:S(2)}, u32[]{:S(2)}) collective-permute-start(bf16[64,1792]{1,0:T(8,128)(2,1)S(1)} %slice.290), channel_id=1, source_target_pairs={{0,3},{1,2},{2,1},{3,0},{4,7},{5,6},{6,5},{7,4},{8,11},{9,10},{10,... | collective-permute-start | bytes 688136 | tf_op jit(solution)/shard_map/ppermute | solution.py:18
  164.8 7.6 %copy-start.5 = (f32[1,8192]{1,0:T(1,128)S(1)}, f32[1,8192]{1,0:T(1,128)}, u32[]{:S(2)}) copy-start(f32[1,8192]{1,0:T(1,128)} %param.16) | copy-start | bytes 98308
  164.8 6.1 %collective-permute-start.8 = (bf16[32,1792]{1,0:T(8,128)(2,1)S(1)}, bf16[32,1792]{1,0:T(8,128)(2,1)S(1)}, u32[]{:S(2)}, u32[]{:S(2)}) collective-permute-start(bf16[32,1792]{1,0:T(8,128)(2,1)S(1)} %slice.296), channel_id=1, source_target_pairs={{0,3},{1,2},{2,1},{3,0},{4,7},{5,6},{6,5},{7,4},{8,11},{9,10},{10,... | collective-permute-start | bytes 344072 | tf_op jit(solution)/shard_map/ppermute | solution.py:18
  167.4 5.9 %copy-start.1 = (s32[2,1024]{1,0:T(2,128)S(1)}, s32[2,1024]{1,0:T(2,128)}, u32[]{:S(2)}) copy-start(s32[2,1024]{1,0:T(2,128)} %param.17) | copy-start | bytes 24580
  167.4 4.9 %collective-permute-start.13 = (bf16[32,1792]{1,0:T(8,128)(2,1)S(1)}, bf16[32,1792]{1,0:T(8,128)(2,1)S(1)}, u32[]{:S(2)}, u32[]{:S(2)}) collective-permute-start(bf16[32,1792]{1,0:T(8,128)(2,1)S(1)} %slice.295), channel_id=1, source_target_pairs={{0,8},{1,9},{2,10},{3,11},{4,12},{5,13},{6,14},{7,15},{8,0},{9,1},... | collective-permute-start | bytes 344072 | tf_op jit(solution)/shard_map/ppermute | solution.py:18

commit v2 on v1

v2 whole, which is shorter than its diff:
```python
import functools

import jax
import jax.numpy as jnp
from jax import lax
from jax.experimental import pallas as pl
from jax.experimental.pallas import tpu as pltpu
from jax.sharding import PartitionSpec as P

BF16, F32 = jnp.bfloat16, jnp.float32
LINKS = (8, 1, 4, 24, 3)
STEPS = len(LINKS)
TILE = 256
PARTS = ((7, 6, 7, 6, 6), (6, 7, 6, 6, 7))
WAVES = len(PARTS)
VMEM = pl.BlockSpec(memory_space=pltpu.VMEM)
HBM = pl.BlockSpec(memory_space=pltpu.HBM)
MIB = 1 << 20


def xor_swap(value, axis, mask):
    return lax.ppermute(value, axis, [(i, i ^ mask) for i in range(lax.axis_size(axis))])


def block_masks():
    n = 1 << STEPS
    out = []
    for j in range(n):
        m = 0
        for k in range(STEPS):
            if (j >> (STEPS - 1 - k)) & 1:
                m ^= LINKS[k]
        out.append(m)
    return out


def part_blocks(first):
    out = []
    for j in range(1 << STEPS):
        base = 0
        for i in range(STEPS):
            if (j >> (STEPS - 1 - i)) & 1:
                base |= 1 << (STEPS - 1 - (first + i) % STEPS)
        out.append(base)
    return out


def encode_kernel(x_hbm, w_hbm, keep_ref, send_ref, xbuf, wbuf, xsem, wsem, *, masks, rows, chunks):
    me = lax.axis_index("lat")
    core = lax.axis_index("layer") % 2
    width = w_hbm.shape[2] // 2
    depth = w_hbm.shape[1] // chunks
    n = len(masks)
    part = rows // WAVES
    wcopies, xcopies = [], []
    for k in range(chunks):
        at = pl.ds(k * depth, depth)
        wcopies.append(pltpu.make_async_copy(w_hbm.at[0, at], wbuf.at[at], wsem.at[k]))
    for h in range(WAVES):
        for j, mask in enumerate(masks):
            src = jnp.bitwise_xor(me, mask) * rows + h * part
            to = (h * n + j) * part
            xcopies.append(
                pltpu.make_async_copy(
                    x_hbm.at[0, pl.ds(pl.multiple_of(src, part), part)],
                    xbuf.at[pl.ds(to, part)],
                    xsem.at[h * n + j],
                )
            )
    for c in wcopies[:1] + xcopies[:n] + wcopies[1:] + xcopies[n:]:
        c.start()
    mine = pl.ds(pl.multiple_of(core * width, width), width)
    other = pl.ds(pl.multiple_of((1 - core) * width, width), width)
    for h in range(WAVES):
        for c in xcopies[h * n : (h + 1) * n]:
            c.wait()
        rs = pl.ds(h * n * part, n * part)
        for k in range(chunks):
            if h == 0:
                wcopies[k].wait()
            at = pl.ds(k * depth, depth)
            x = xbuf[rs, at]
            for ref, cols in ((send_ref, other), (keep_ref, mine)):
                d = jnp.dot(x, wbuf[at, cols], preferred_element_type=F32)
                ref[rs, :] = d if k == 0 else ref[rs, :] + d


def encode(x, w):
    tokens, depth = x.shape[1], x.shape[2]
    width = w.shape[2] // 2
    masks = block_masks()
    rows = tokens // len(masks)
    half = jax.ShapeDtypeStruct((tokens, width), F32)
    return pl.pallas_call(
        functools.partial(encode_kernel, masks=masks, rows=rows, chunks=4),
        out_shape=(half, half),
        in_specs=[HBM, HBM],
        out_specs=[VMEM, VMEM],
        scratch_shapes=[
            pltpu.VMEM((tokens, depth), BF16),
            pltpu.VMEM((depth, 2 * width), BF16),
            pltpu.SemaphoreType.DMA((len(masks) * WAVES,)),
            pltpu.SemaphoreType.DMA((4,)),
        ],
        compiler_params=pltpu.CompilerParams(vmem_limit_bytes=56 * MIB),
        cost_estimate=pl.CostEstimate(
            flops=4 * tokens * depth * width,
            bytes_accessed=2 * (tokens * depth + 2 * depth * width) + 8 * tokens * width,
            transcendentals=0,
        ),
        name="encode",
    )(x, w)


def load_kernel(w_hbm, out, sem, *, pieces):
    step = w_hbm.shape[2] // pieces
    copies = [
        pltpu.make_async_copy(
            w_hbm.at[0, s, pl.ds(q * step, step)], out.at[s, pl.ds(q * step, step)], sem.at[s * pieces + q]
        )
        for s in range(2)
        for q in range(pieces)
    ]
    for c in copies:
        c.start()
    for c in copies:
        c.wait()


def load(w):
    _, sources, depth, wide = w.shape
    return pl.pallas_call(
        functools.partial(load_kernel, pieces=4),
        out_shape=pltpu.VMEM((sources, depth, wide), BF16),
        in_specs=[HBM],
        out_specs=VMEM,
        scratch_shapes=[pltpu.SemaphoreType.DMA((8,))],
        compiler_params=pltpu.CompilerParams(vmem_limit_bytes=40 * MIB),
        cost_estimate=pl.CostEstimate(
            flops=0, bytes_accessed=4 * sources * depth * wide, transcendentals=0
        ),
        name="load",
    )(w)


def assemble_kernel(own_ref, own_sib_ref, far_ref, far_sib_ref, out_ref):
    group = lax.axis_index("layer")
    source, core = group // 2, group % 2
    hw = own_ref.shape[1]
    for ref, s, c in (
        (own_ref, source, core),
        (own_sib_ref, source, 1 - core),
        (far_ref, 1 - source, core),
        (far_sib_ref, 1 - source, 1 - core),
    ):
        out_ref[:, pl.ds(pl.multiple_of((s * 2 + c) * hw, hw), hw)] = ref[...]


def assemble(*pieces):
    n, hw = pieces[0].shape
    return pl.pallas_call(
        assemble_kernel,
        out_shape=pltpu.VMEM((n, 4 * hw), BF16),
        in_specs=[VMEM] * 4,
        out_specs=VMEM,
        compiler_params=pltpu.CompilerParams(vmem_limit_bytes=8 * MIB),
        name="assemble",
    )(*pieces)


def gather_rows(codes_ref, lhs, blocks):
    rows = lhs.shape[0] // len(blocks)
    for j, b in enumerate(blocks):
        lhs[pl.ds(j * rows, rows), :] = codes_ref[pl.ds(b * rows, rows), :]


def tile_product(lhs, w_ref, at, t):
    w = w_ref[:, :, pl.ds(pl.multiple_of(at + t * TILE, TILE), TILE)]
    return jnp.dot(lhs[...], w.reshape(lhs.shape[1], TILE), preferred_element_type=F32)


def send_kernel(codes_ref, w_ref, send_ref, lhs, *, blocks, at):
    gather_rows(codes_ref, lhs, blocks)

    @pl.loop(0, send_ref.shape[1] // TILE)
    def _(t):
        cols = pl.ds(pl.multiple_of(t * TILE, TILE), TILE)
        send_ref[:, cols] = tile_product(lhs, w_ref, at, t).astype(BF16)


def keep_kernel(codes_ref, w_ref, got_ref, keep_ref, send_ref, lhs, *, blocks, at):
    gather_rows(codes_ref, lhs, blocks)
    n2 = lhs.shape[0] // 2

    @pl.loop(0, send_ref.shape[1] // TILE)
    def _(t):
        cols = pl.ds(pl.multiple_of(t * TILE, TILE), TILE)
        total = tile_product(lhs, w_ref, at, t) + got_ref[:, cols].astype(F32)
        keep_ref[:, cols] = total[:n2]
        send_ref[:, cols] = total[n2:].astype(BF16)


def decode_send(codes, w, first, at, wide):
    tokens, depth = codes.shape
    blocks = part_blocks(first)
    n = tokens // 2
    return pl.pallas_call(
        functools.partial(send_kernel, blocks=blocks[len(blocks) // 2 :], at=at),
        out_shape=jax.ShapeDtypeStruct((n, wide), BF16),
        in_specs=[VMEM, VMEM],
        out_specs=VMEM,
        scratch_shapes=[pltpu.VMEM((n, depth), BF16)],
        compiler_params=pltpu.CompilerParams(vmem_limit_bytes=8 * MIB),
        cost_estimate=pl.CostEstimate(flops=1000, bytes_accessed=1000, transcendentals=0),
        name=f"send{first}",
    )(codes, w)


def decode_keep(codes, w, got, first, at, wide):
    tokens, depth = codes.shape
    blocks = part_blocks(first)
    n = tokens // 2
    return pl.pallas_call(
        functools.partial(keep_kernel, blocks=blocks[: len(blocks) // 2], at=at),
        out_shape=(
            jax.ShapeDtypeStruct((n // 2, wide), F32),
            jax.ShapeDtypeStruct((n // 2, wide), BF16),
        ),
        in_specs=[VMEM, VMEM, VMEM],
        out_specs=[VMEM, VMEM],
        scratch_shapes=[pltpu.VMEM((n, depth), BF16)],
        compiler_params=pltpu.CompilerParams(vmem_limit_bytes=8 * MIB),
        cost_estimate=pl.CostEstimate(flops=1000, bytes_accessed=1000, transcendentals=0),
        name=f"keep{first}",
    )(codes, w, got)

def shards(
    resid_halves,
    enc_weight,
    enc_bias,
    jump_threshold,
    dec_weight,
    dec_bias,
    clamp_rows,
    clamp_feats,
    clamp_slots,
    clamp_values,
):
    group = lax.axis_index("layer")
    me = lax.axis_index("lat")
    source, core = group // 2, group % 2
    tokens = resid_halves.shape[1]
    width = enc_weight.shape[2]
    hw = width // 2
    masks = jnp.array(block_masks(), jnp.int32)
    rows = tokens // masks.shape[0]

    keep, send = encode(resid_halves, enc_weight)
    recv = xor_swap(send, "layer", 1)

    part = rows // WAVES
    within = jnp.arange(part, dtype=jnp.int32)
    row_token = (
        (jnp.bitwise_xor(masks, me) * rows)[None, :, None]
        + (jnp.arange(WAVES, dtype=jnp.int32) * part)[:, None, None]
        + within[None, None, :]
    ).reshape(tokens)
    my_rows = lax.dynamic_index_in_dim(clamp_rows, source, 0, keepdims=False)
    my_pick = lax.dynamic_index_in_dim(
        clamp_feats * clamp_values.shape[0] + clamp_slots, source, 0, keepdims=False
    )
    row_hot = (my_rows[:, None] == row_token[None, :]).astype(F32)
    pick = jnp.dot(my_pick.astype(F32), row_hot, precision=lax.Precision.HIGHEST).astype(jnp.int32)
    feat, slot = pick // clamp_values.shape[0], pick % clamp_values.shape[0]
    slot_hot = slot[:, None] == jnp.arange(clamp_values.shape[0], dtype=jnp.int32)[None, :]
    value = jnp.sum(jnp.where(slot_hot, clamp_values[None, :], 0.0), axis=1)
    first = core * hw
    column = feat - me * width - first

    my_bias = lax.dynamic_slice(enc_bias, (source, first), (1, hw))
    my_thresh = lax.dynamic_slice(jump_threshold, (source, first), (1, hw))
    pre = keep + recv + my_bias
    ramp = jnp.clip((pre - my_thresh) / 0.25 + 1.0, 0.0, 1.0)
    hit = column[:, None] == jnp.arange(hw, dtype=jnp.int32)[None, :]
    own = jnp.where(hit, value[:, None], pre * ramp).astype(BF16)

    own_sib = xor_swap(own, "layer", 1)
    weights = load(lax.optimization_barrier((dec_weight, own))[0])
    n = tokens // WAVES
    codes, far = [], None
    for h in range(WAVES):
        mine = own[h * n : (h + 1) * n]
        sent = mine if far is None else lax.optimization_barrier((mine, far, weights))[0]
        far = xor_swap(sent, "layer", 2)
        codes.append(
            assemble(mine, own_sib[h * n : (h + 1) * n], far, xor_swap(far, "layer", 1))
        )

    starts = [[sum(wave[:p]) * TILE for p in range(STEPS)] for wave in PARTS]
    out, kept = {}, {}
    for h in range(WAVES):
        for p in range(STEPS):
            out[h, p] = decode_send(codes[h], weights, p, starts[h][p], PARTS[h][p] * TILE)
    last = [None] * STEPS
    for i in range(STEPS):
        for h in range(WAVES):
            for p in range(STEPS):
                link = (p + i) % STEPS
                data = out[h, p]
                if last[link] is not None:
                    data = lax.optimization_barrier((data, last[link]))[0]
                got = last[link] = xor_swap(data, "lat", LINKS[link])
                if i == 0:
                    kept[h, p], out[h, p] = decode_keep(
                        codes[h], weights, got, p, starts[h][p], PARTS[h][p] * TILE
                    )
                else:
                    total = kept[h, p] + got.astype(F32)
                    m = total.shape[0] // 2
                    kept[h, p] = total[:m] if i < STEPS - 1 else total
                    out[h, p] = total[m:].astype(BF16)
    summed = [jnp.concatenate([kept[h, p] for p in range(STEPS)], axis=1) for h in range(WAVES)]
    return (jnp.concatenate(summed, axis=0) + dec_bias).astype(BF16)[None]


def solution(mesh):
    return jax.shard_map(
        shards,
        mesh=mesh,
        in_specs=(
            P("layer", None, None),
            P("layer", None, "lat"),
            P(None, "lat"),
            P(None, "lat"),
            P("layer", None, "lat", None),
            P("layer", None),
            P(),
            P(),
            P(),
            P(),
        ),
        out_specs=P("layer", "lat", None),
        check_vma=False,
    )
```

time: 174 us -> 169 us (0.971)
  waiting for transfers between devices: 83.2 us -> 30.1 us
  starting transfers between devices: 29.9 us -> 71.5 us
  Pallas kernels: 33.9 us -> 58.4 us
  local copies, waits for them, and re-layouts: 13.8 us -> 2.18 us
  other arithmetic: 10.5 us -> 4.19 us
    ppermute x29 -> x56, waiting for transfers between devices: 83.2 us -> 30.1 us  [xor_swap(): lax.ppermute(value, axis, [(i, i ^ mask) for i in range(lax.axis_size(axi...]
    ppermute x29 -> x56, starting transfers between devices: 29.9 us -> 71.5 us  [xor_swap(): lax.ppermute(value, axis, [(i, i ^ mask) for i in range(lax.axis_size(axi...]
    pallas_call x6 -> x24, Pallas kernels: 33.9 us -> 58.4 us  [the longest x10 20.8 us: decode_keep(): pl.pallas_call(functools.partial(keep_kernel, blocks=blocks[:len(blocks)...]
    unnamed x20 -> x14, local copies, waits for them, and re-layouts: 11.4 us -> 0.03 us
    add x21 -> x32, other arithmetic: 7.81 us -> 1.49 us  [the longest x30 1.34 us: shards(): total = kept[h, p] + got.astype(F32)]
  transfers between devices with their start and end apart: 29 -> 56, of which waited for: 16 -> 18; matrix products, arithmetic and copies ran while one was open for 7% -> 3% of each run, Pallas kernels for 13% -> 28%
where the time goes in v2:
time: 169 us
  starting transfers between devices  71.5 us (42%)
  Pallas kernels  58.4 us (35%)
  waiting for transfers between devices  30.1 us (18%)
  other arithmetic  4.19 us (2%)
  local copies, waits for them, and re-layouts  2.18 us (1%)
    ppermute x56, starting transfers between devices, xor_swap(): lax.ppermute(value, axis, [(i, i ^ mask) for i in range(lax.axis_size(axi...  71.5 us
    ppermute x56, waiting for transfers between devices, xor_swap(): lax.ppermute(value, axis, [(i, i ^ mask) for i in range(lax.axis_size(axi...  30.1 us
    pallas_call x10, Pallas kernels, decode_keep(): pl.pallas_call(functools.partial(keep_kernel, blocks=blocks[:len(blocks)...  20.8 us
    pallas_call x10, Pallas kernels, decode_send(): pl.pallas_call(functools.partial(send_kernel, blocks=blocks[len(blocks) /...  20.7 us
    pallas_call x1, Pallas kernels, encode(): pl.pallas_call(functools.partial(encode_kernel, masks=masks, rows=rows, c...  10.6 us
    pallas_call x1, Pallas kernels, load(): pl.pallas_call(functools.partial(load_kernel, pieces=4), out_shape=pltpu....  5.92 us
  transfers between devices with their start and end apart: 56, of which 18 were waited for; matrix products, arithmetic and copies ran while one was open for 3% of the time, Pallas kernels for 28%

profile of v2, /device:TPU:0, one launch (start us, length us, event | category | flops | bytes accessed | tf_op | source)
XLA Modules:
  0.0 168.8 jit_solution(6935515963168993937)
XLA Ops:
  0.0 10.6 %encode.1 = (f32[1024,256]{1,0:T(8,128)}, f32[1024,256]{1,0:T(8,128)}) custom-call(bf16[1,1024,4096]{2,1,0:T(8,128)(2,1)} %x_hbm.1, bf16[1,4096,512]{2,1,0:T(8,128)(2,1)} %w_hbm.1), custom_call_target="tpu_custom_call" | custom-call | flops 4294967296 | bytes 14680064 | tf_op jit(solution)/shard_map/encode/pallas_call | solution.py:94
  16.2 3.4 %collective-permute-start.2 = (bf16[512,256]{1,0:T(8,128)(2,1)S(1)}, bf16[512,256]{1,0:T(8,128)(2,1)S(1)}, u32[]{:S(2)}, u32[]{:S(2)}) collective-permute-start(bf16[512,256]{1,0:T(8,128)(2,1)S(1)} %get-tuple-element.145.own_ref), channel_id=1, source_target_pairs={{0,64},{32,96},{64,0},{96,32},{1,65},{33,97},{65,1},{97,33},{2,66}... | collective-permute-start | bytes 786440 | tf_op jit(solution)/shard_map/ppermute | solution.py:22
  19.6 6.5 %collective-permute-done.2.far_ref = bf16[512,256]{1,0:T(8,128)(2,1)S(1)} collective-permute-done((bf16[512,256]{1,0:T(8,128)(2,1)S(1)}, bf16[512,256]{1,0:T(8,128)(2,1)S(1)}, u32[]{:S(2)}, u32[]{:S(2)}) %collective-permute-start.2) | collective-permute-done | bytes 262176 | tf_op jit(solution)/shard_map/ppermute | solution.py:22
  26.1 5.9 %load.1.w_ref = bf16[2,512,8192]{2,1,0:T(8,128)(2,1)S(1)} custom-call(bf16[1,2,512,8192]{3,2,1,0:T(8,128)(2,1)} %w_hbm.2), custom_call_target="tpu_custom_call" | custom-call | bytes 33554432 | tf_op jit(solution)/shard_map/load/pallas_call | solution.py:132
  32.1 3.3 %collective-permute-start.5 = (bf16[512,256]{1,0:T(8,128)(2,1)S(1)}, bf16[512,256]{1,0:T(8,128)(2,1)S(1)}, u32[]{:S(2)}, u32[]{:S(2)}) collective-permute-start(bf16[512,256]{1,0:T(8,128)(2,1)S(1)} %get-tuple-element.79.own_ref), channel_id=1, source_target_pairs={{0,64},{32,96},{64,0},{96,32},{1,65},{33,97},{65,1},{97,33},{2,66}... | collective-permute-start | bytes 786440 | tf_op jit(solution)/shard_map/ppermute | solution.py:22
  35.6 1.9 %send3.3 = bf16[256,1536]{1,0:T(8,128)(2,1)S(1)} custom-call(bf16[512,1024]{1,0:T(8,128)(2,1)S(1)} %assemble.2.codes_ref, bf16[2,512,8192]{2,1,0:T(8,128)(2,1)S(1)} %load.1.w_ref), custom_call_target="tpu_custom_call" | custom-call | flops 1000 | bytes 1000 | tf_op jit(solution)/shard_map/send3/pallas_call | solution.py:207
  37.6 2.8 %collective-permute-start.15 = (bf16[256,1536]{1,0:T(8,128)(2,1)S(1)}, bf16[256,1536]{1,0:T(8,128)(2,1)S(1)}, u32[]{:S(2)}, u32[]{:S(2)}) collective-permute-start(bf16[256,1536]{1,0:T(8,128)(2,1)S(1)} %send3.3), channel_id=1, source_target_pairs={{0,24},{1,25},{2,26},{3,27},{4,28},{5,29},{6,30},{7,31},{8,16},{9,... | collective-permute-start | bytes 2359304 | tf_op jit(solution)/shard_map/ppermute | solution.py:22
  40.4 2.0 %collective-permute-done.5.far_ref = bf16[512,256]{1,0:T(8,128)(2,1)S(1)} collective-permute-done((bf16[512,256]{1,0:T(8,128)(2,1)S(1)}, bf16[512,256]{1,0:T(8,128)(2,1)S(1)}, u32[]{:S(2)}, u32[]{:S(2)}) %collective-permute-start.5) | collective-permute-done | bytes 262176 | tf_op jit(solution)/shard_map/ppermute | solution.py:22
  42.4 1.9 %send1.3 = bf16[256,1536]{1,0:T(8,128)(2,1)S(1)} custom-call(bf16[512,1024]{1,0:T(8,128)(2,1)S(1)} %assemble.2.codes_ref, bf16[2,512,8192]{2,1,0:T(8,128)(2,1)S(1)} %load.1.w_ref), custom_call_target="tpu_custom_call" | custom-call | flops 1000 | bytes 1000 | tf_op jit(solution)/shard_map/send1/pallas_call | solution.py:207
  44.3 2.0 %collective-permute-start.7 = (bf16[256,1536]{1,0:T(8,128)(2,1)S(1)}, bf16[256,1536]{1,0:T(8,128)(2,1)S(1)}, u32[]{:S(2)}, u32[]{:S(2)}) collective-permute-start(bf16[256,1536]{1,0:T(8,128)(2,1)S(1)} %send1.3), channel_id=1, source_target_pairs={{0,1},{1,0},{2,3},{3,2},{4,5},{5,4},{6,7},{7,6},{8,9},{9,8},{10,11... | collective-permute-start | bytes 2359304 | tf_op jit(solution)/shard_map/ppermute | solution.py:22
  46.4 2.3 %send2.3 = bf16[256,1792]{1,0:T(8,128)(2,1)S(1)} custom-call(bf16[512,1024]{1,0:T(8,128)(2,1)S(1)} %assemble.2.codes_ref, bf16[2,512,8192]{2,1,0:T(8,128)(2,1)S(1)} %load.1.w_ref), custom_call_target="tpu_custom_call" | custom-call | flops 1000 | bytes 1000 | tf_op jit(solution)/shard_map/send2/pallas_call | solution.py:207
  50.3 2.0 %send4.3 = bf16[256,1536]{1,0:T(8,128)(2,1)S(1)} custom-call(bf16[512,1024]{1,0:T(8,128)(2,1)S(1)} %assemble.2.codes_ref, bf16[2,512,8192]{2,1,0:T(8,128)(2,1)S(1)} %load.1.w_ref), custom_call_target="tpu_custom_call" | custom-call | flops 1000 | bytes 1000 | tf_op jit(solution)/shard_map/send4/pallas_call | solution.py:207
  52.3 2.6 %collective-permute-start.22 = (bf16[256,1536]{1,0:T(8,128)(2,1)S(1)}, bf16[256,1536]{1,0:T(8,128)(2,1)S(1)}, u32[]{:S(2)}, u32[]{:S(2)}) collective-permute-start(bf16[256,1536]{1,0:T(8,128)(2,1)S(1)} %send4.3), channel_id=1, source_target_pairs={{0,3},{1,2},{2,1},{3,0},{4,7},{5,6},{6,5},{7,4},{8,11},{9,10},{10,... | collective-permute-start | bytes 2359304 | tf_op jit(solution)/shard_map/ppermute | solution.py:22
  54.9 2.3 %send0.2 = bf16[256,1792]{1,0:T(8,128)(2,1)S(1)} custom-call(bf16[512,1024]{1,0:T(8,128)(2,1)S(1)} %assemble.2.codes_ref, bf16[2,512,8192]{2,1,0:T(8,128)(2,1)S(1)} %load.1.w_ref), custom_call_target="tpu_custom_call" | custom-call | flops 1000 | bytes 1000 | tf_op jit(solution)/shard_map/send0/pallas_call | solution.py:207
  58.9 1.9 %send3.2 = bf16[256,1536]{1,0:T(8,128)(2,1)S(1)} custom-call(bf16[512,1024]{1,0:T(8,128)(2,1)S(1)} %assemble.3.codes_ref, bf16[2,512,8192]{2,1,0:T(8,128)(2,1)S(1)} %load.1.w_ref), custom_call_target="tpu_custom_call" | custom-call | flops 1000 | bytes 1000 | tf_op jit(solution)/shard_map/send3/pallas_call | solution.py:207
  60.8 2.2 %collective-permute-start.16 = (bf16[256,1536]{1,0:T(8,128)(2,1)S(1)}, bf16[256,1536]{1,0:T(8,128)(2,1)S(1)}, u32[]{:S(2)}, u32[]{:S(2)}) collective-permute-start(bf16[256,1536]{1,0:T(8,128)(2,1)S(1)} %send3.2), channel_id=1, source_target_pairs={{0,24},{1,25},{2,26},{3,27},{4,28},{5,29},{6,30},{7,31},{8,16},{9,... | collective-permute-start | bytes 2359304 | tf_op jit(solution)/shard_map/ppermute | solution.py:22
  63.0 2.3 %send1.2 = bf16[256,1792]{1,0:T(8,128)(2,1)S(1)} custom-call(bf16[512,1024]{1,0:T(8,128)(2,1)S(1)} %assemble.3.codes_ref, bf16[2,512,8192]{2,1,0:T(8,128)(2,1)S(1)} %load.1.w_ref), custom_call_target="tpu_custom_call" | custom-call | flops 1000 | bytes 1000 | tf_op jit(solution)/shard_map/send1/pallas_call | solution.py:207
  66.4 2.3 %send4.2 = bf16[256,1792]{1,0:T(8,128)(2,1)S(1)} custom-call(bf16[512,1024]{1,0:T(8,128)(2,1)S(1)} %assemble.3.codes_ref, bf16[2,512,8192]{2,1,0:T(8,128)(2,1)S(1)} %load.1.w_ref), custom_call_target="tpu_custom_call" | custom-call | flops 1000 | bytes 1000 | tf_op jit(solution)/shard_map/send4/pallas_call | solution.py:207
  68.7 4.3 %collective-permute-done.22.got_ref = bf16[256,1536]{1,0:T(8,128)(2,1)S(1)} collective-permute-done((bf16[256,1536]{1,0:T(8,128)(2,1)S(1)}, bf16[256,1536]{1,0:T(8,128)(2,1)S(1)}, u32[]{:S(2)}, u32[]{:S(2)}) %collective-permute-start.22) | collective-permute-done | bytes 786464 | tf_op jit(solution)/shard_map/ppermute | solution.py:22
  73.0 2.5 %collective-permute-start.23 = (bf16[256,1792]{1,0:T(8,128)(2,1)S(1)}, bf16[256,1792]{1,0:T(8,128)(2,1)S(1)}, u32[]{:S(2)}, u32[]{:S(2)}) collective-permute-start(bf16[256,1792]{1,0:T(8,128)(2,1)S(1)} %send4.2), channel_id=1, source_target_pairs={{0,3},{1,2},{2,1},{3,0},{4,7},{5,6},{6,5},{7,4},{8,11},{9,10},{10,... | collective-permute-start | bytes 2752520 | tf_op jit(solution)/shard_map/ppermute | solution.py:22
  75.5 2.0 %send2.2 = bf16[256,1536]{1,0:T(8,128)(2,1)S(1)} custom-call(bf16[512,1024]{1,0:T(8,128)(2,1)S(1)} %assemble.3.codes_ref, bf16[2,512,8192]{2,1,0:T(8,128)(2,1)S(1)} %load.1.w_ref), custom_call_target="tpu_custom_call" | custom-call | flops 1000 | bytes 1000 | tf_op jit(solution)/shard_map/send2/pallas_call | solution.py:207
  78.2 1.9 %send0.3 = bf16[256,1536]{1,0:T(8,128)(2,1)S(1)} custom-call(bf16[512,1024]{1,0:T(8,128)(2,1)S(1)} %assemble.3.codes_ref, bf16[2,512,8192]{2,1,0:T(8,128)(2,1)S(1)} %load.1.w_ref), custom_call_target="tpu_custom_call" | custom-call | flops 1000 | bytes 1000 | tf_op jit(solution)/shard_map/send0/pallas_call | solution.py:207
  81.7 2.3 %keep2.3 = (f32[128,1792]{1,0:T(8,128)S(1)}, bf16[128,1792]{1,0:T(8,128)(2,1)S(1)}) custom-call(bf16[512,1024]{1,0:T(8,128)(2,1)S(1)} %assemble.2.codes_ref, bf16[2,512,8192]{2,1,0:T(8,128)(2,1)S(1)} %load.1.w_ref, bf16[256,1792]{1,0:T(8,128)(2,1)S(1)} %collective-permute-done.10.got_ref), custom_call_target="tpu_custom_call" | custom-call | flops 1000 | bytes 1000 | tf_op jit(solution)/shard_map/keep2/pallas_call | solution.py:223
  84.0 2.2 %collective-permute-start.17 = (bf16[128,1792]{1,0:T(8,128)(2,1)S(1)}, bf16[128,1792]{1,0:T(8,128)(2,1)S(1)}, u32[]{:S(2)}, u32[]{:S(2)}) collective-permute-start(bf16[128,1792]{1,0:T(8,128)(2,1)S(1)} %get-tuple-element.93), channel_id=1, source_target_pairs={{0,24},{1,25},{2,26},{3,27},{4,28},{5,29},{6,30},{7,31},{8,16},{9,... | collective-permute-start | bytes 1376264 | tf_op jit(solution)/shard_map/ppermute | solution.py:22
  86.2 2.0 %keep1.3 = (f32[128,1536]{1,0:T(8,128)S(1)}, bf16[128,1536]{1,0:T(8,128)(2,1)S(1)}) custom-call(bf16[512,1024]{1,0:T(8,128)(2,1)S(1)} %assemble.2.codes_ref, bf16[2,512,8192]{2,1,0:T(8,128)(2,1)S(1)} %load.1.w_ref, bf16[256,1536]{1,0:T(8,128)(2,1)S(1)} %collective-permute-done.7.got_ref), custom_call_target="tpu_custom_call" | custom-call | flops 1000 | bytes 1000 | tf_op jit(solution)/shard_map/keep1/pallas_call | solution.py:223
  88.1 2.0 %keep3.3 = (f32[128,1536]{1,0:T(8,128)S(1)}, bf16[128,1536]{1,0:T(8,128)(2,1)S(1)}) custom-call(bf16[512,1024]{1,0:T(8,128)(2,1)S(1)} %assemble.2.codes_ref, bf16[2,512,8192]{2,1,0:T(8,128)(2,1)S(1)} %load.1.w_ref, bf16[256,1536]{1,0:T(8,128)(2,1)S(1)} %collective-permute-done.15.got_ref), custom_call_target="tpu_custom_call" | custom-call | flops 1000 | bytes 1000 | tf_op jit(solution)/shard_map/keep3/pallas_call | solution.py:223
  90.1 2.0 %keep4.3 = (f32[128,1536]{1,0:T(8,128)S(1)}, bf16[128,1536]{1,0:T(8,128)(2,1)S(1)}) custom-call(bf16[512,1024]{1,0:T(8,128)(2,1)S(1)} %assemble.2.codes_ref, bf16[2,512,8192]{2,1,0:T(8,128)(2,1)S(1)} %load.1.w_ref, bf16[256,1536]{1,0:T(8,128)(2,1)S(1)} %collective-permute-done.22.got_ref), custom_call_target="tpu_custom_call" | custom-call | flops 1000 | bytes 1000 | tf_op jit(solution)/shard_map/keep4/pallas_call | solution.py:223
  92.0 2.3 %keep0.2 = (f32[128,1792]{1,0:T(8,128)S(1)}, bf16[128,1792]{1,0:T(8,128)(2,1)S(1)}) custom-call(bf16[512,1024]{1,0:T(8,128)(2,1)S(1)} %assemble.2.codes_ref, bf16[2,512,8192]{2,1,0:T(8,128)(2,1)S(1)} %load.1.w_ref, bf16[256,1792]{1,0:T(8,128)(2,1)S(1)} %collective-permute-done.4.got_ref), custom_call_target="tpu_custom_call" | custom-call | flops 1000 | bytes 1000 | tf_op jit(solution)/shard_map/keep0/pallas_call | solution.py:223
  94.3 2.0 %keep3.2 = (f32[128,1536]{1,0:T(8,128)S(1)}, bf16[128,1536]{1,0:T(8,128)(2,1)S(1)}) custom-call(bf16[512,1024]{1,0:T(8,128)(2,1)S(1)} %assemble.3.codes_ref, bf16[2,512,8192]{2,1,0:T(8,128)(2,1)S(1)} %load.1.w_ref, bf16[256,1536]{1,0:T(8,128)(2,1)S(1)} %collective-permute-done.16.got_ref), custom_call_target="tpu_custom_call" | custom-call | flops 1000 | bytes 1000 | tf_op jit(solution)/shard_map/keep3/pallas_call | solution.py:223
  99.7 1.9 %keep0.3 = (f32[128,1536]{1,0:T(8,128)S(1)}, bf16[128,1536]{1,0:T(8,128)(2,1)S(1)}) custom-call(bf16[512,1024]{1,0:T(8,128)(2,1)S(1)} %assemble.3.codes_ref, bf16[2,512,8192]{2,1,0:T(8,128)(2,1)S(1)} %load.1.w_ref, bf16[256,1536]{1,0:T(8,128)(2,1)S(1)} %collective-permute-done.31.got_ref), custom_call_target="tpu_custom_call" | custom-call | flops 1000 | bytes 1000 | tf_op jit(solution)/shard_map/keep0/pallas_call | solution.py:223
  101.6 2.3 %keep1.2 = (f32[128,1792]{1,0:T(8,128)S(1)}, bf16[128,1792]{1,0:T(8,128)(2,1)S(1)}) custom-call(bf16[512,1024]{1,0:T(8,128)(2,1)S(1)} %assemble.3.codes_ref, bf16[2,512,8192]{2,1,0:T(8,128)(2,1)S(1)} %load.1.w_ref, bf16[256,1792]{1,0:T(8,128)(2,1)S(1)} %collective-permute-done.8.got_ref), custom_call_target="tpu_custom_call" | custom-call | flops 1000 | bytes 1000 | tf_op jit(solution)/shard_map/keep1/pallas_call | solution.py:223
  103.9 2.0 %keep2.2 = (f32[128,1536]{1,0:T(8,128)S(1)}, bf16[128,1536]{1,0:T(8,128)(2,1)S(1)}) custom-call(bf16[512,1024]{1,0:T(8,128)(2,1)S(1)} %assemble.3.codes_ref, bf16[2,512,8192]{2,1,0:T(8,128)(2,1)S(1)} %load.1.w_ref, bf16[256,1536]{1,0:T(8,128)(2,1)S(1)} %collective-permute-done.11.got_ref), custom_call_target="tpu_custom_call" | custom-call | flops 1000 | bytes 1000 | tf_op jit(solution)/shard_map/keep2/pallas_call | solution.py:223
  105.9 2.3 %keep4.2 = (f32[128,1792]{1,0:T(8,128)S(1)}, bf16[128,1792]{1,0:T(8,128)(2,1)S(1)}) custom-call(bf16[512,1024]{1,0:T(8,128)(2,1)S(1)} %assemble.3.codes_ref, bf16[2,512,8192]{2,1,0:T(8,128)(2,1)S(1)} %load.1.w_ref, bf16[256,1792]{1,0:T(8,128)(2,1)S(1)} %collective-permute-done.23.got_ref), custom_call_target="tpu_custom_call" | custom-call | flops 1000 | bytes 1000 | tf_op jit(solution)/shard_map/keep4/pallas_call | solution.py:223
  108.2 2.2 %collective-permute-start.18 = (bf16[128,1536]{1,0:T(8,128)(2,1)S(1)}, bf16[128,1536]{1,0:T(8,128)(2,1)S(1)}, u32[]{:S(2)}, u32[]{:S(2)}) collective-permute-start(bf16[128,1536]{1,0:T(8,128)(2,1)S(1)} %get-tuple-element.94), channel_id=1, source_target_pairs={{0,24},{1,25},{2,26},{3,27},{4,28},{5,29},{6,30},{7,31},{8,16},{9,... | collective-permute-start | bytes 1179656 | tf_op jit(solution)/shard_map/ppermute | solution.py:22
  110.4 1.7 collective-permute-start.13
  114.9 3.0 %collective-permute-done.18 = bf16[128,1536]{1,0:T(8,128)(2,1)S(1)} collective-permute-done((bf16[128,1536]{1,0:T(8,128)(2,1)S(1)}, bf16[128,1536]{1,0:T(8,128)(2,1)S(1)}, u32[]{:S(2)}, u32[]{:S(2)}) %collective-permute-start.18) | collective-permute-done | bytes 393248 | tf_op jit(solution)/shard_map/ppermute | solution.py:22
  118.0 2.1 %collective-permute-start.19 = (bf16[64,1536]{1,0:T(8,128)(2,1)S(1)}, bf16[64,1536]{1,0:T(8,128)(2,1)S(1)}, u32[]{:S(2)}, u32[]{:S(2)}) collective-permute-start(bf16[64,1536]{1,0:T(8,128)(2,1)S(1)} %slice.439), channel_id=1, source_target_pairs={{0,24},{1,25},{2,26},{3,27},{4,28},{5,29},{6,30},{7,31},{8,16},{9,... | collective-permute-start | bytes 589832 | tf_op jit(solution)/shard_map/ppermute | solution.py:22
  121.5 1.7 %collective-permute-start.26 = (bf16[64,1792]{1,0:T(8,128)(2,1)S(1)}, bf16[64,1792]{1,0:T(8,128)(2,1)S(1)}, u32[]{:S(2)}, u32[]{:S(2)}) collective-permute-start(bf16[64,1792]{1,0:T(8,128)(2,1)S(1)} %slice.431), channel_id=1, source_target_pairs={{0,3},{1,2},{2,1},{3,0},{4,7},{5,6},{6,5},{7,4},{8,11},{9,10},{10,... | collective-permute-start | bytes 688136 | tf_op jit(solution)/shard_map/ppermute | solution.py:22
  126.0 2.3 %collective-permute-start.20 = (bf16[64,1792]{1,0:T(8,128)(2,1)S(1)}, bf16[64,1792]{1,0:T(8,128)(2,1)S(1)}, u32[]{:S(2)}, u32[]{:S(2)}) collective-permute-start(bf16[64,1792]{1,0:T(8,128)(2,1)S(1)} %slice.432), channel_id=1, source_target_pairs={{0,24},{1,25},{2,26},{3,27},{4,28},{5,29},{6,30},{7,31},{8,16},{9,... | collective-permute-start | bytes 688136 | tf_op jit(solution)/shard_map/ppermute | solution.py:22
  129.8 2.0 %collective-permute-start.27 = (bf16[64,1536]{1,0:T(8,128)(2,1)S(1)}, bf16[64,1536]{1,0:T(8,128)(2,1)S(1)}, u32[]{:S(2)}, u32[]{:S(2)}) collective-permute-start(bf16[64,1536]{1,0:T(8,128)(2,1)S(1)} %slice.438), channel_id=1, source_target_pairs={{0,3},{1,2},{2,1},{3,0},{4,7},{5,6},{6,5},{7,4},{8,11},{9,10},{10,... | collective-permute-start | bytes 589832 | tf_op jit(solution)/shard_map/ppermute | solution.py:22
  134.4 2.3 %collective-permute-start.21 = (bf16[32,1792]{1,0:T(8,128)(2,1)S(1)}, bf16[32,1792]{1,0:T(8,128)(2,1)S(1)}, u32[]{:S(2)}, u32[]{:S(2)}) collective-permute-start(bf16[32,1792]{1,0:T(8,128)(2,1)S(1)} %slice.443), channel_id=1, source_target_pairs={{0,24},{1,25},{2,26},{3,27},{4,28},{5,29},{6,30},{7,31},{8,16},{9,... | collective-permute-start | bytes 344072 | tf_op jit(solution)/shard_map/ppermute | solution.py:22
  137.7 2.0 %collective-permute-start.28 = (bf16[32,1536]{1,0:T(8,128)(2,1)S(1)}, bf16[32,1536]{1,0:T(8,128)(2,1)S(1)}, u32[]{:S(2)}, u32[]{:S(2)}) collective-permute-start(bf16[32,1536]{1,0:T(8,128)(2,1)S(1)} %slice.449), channel_id=1, source_target_pairs={{0,3},{1,2},{2,1},{3,0},{4,7},{5,6},{6,5},{7,4},{8,11},{9,10},{10,... | collective-permute-start | bytes 294920 | tf_op jit(solution)/shard_map/ppermute | solution.py:22
  140.8 2.0 %collective-permute-start.49 = (bf16[32,1536]{1,0:T(8,128)(2,1)S(1)}, bf16[32,1536]{1,0:T(8,128)(2,1)S(1)}, u32[]{:S(2)}, u32[]{:S(2)}) collective-permute-start(bf16[32,1536]{1,0:T(8,128)(2,1)S(1)} %slice.444), channel_id=1, source_target_pairs={{0,24},{1,25},{2,26},{3,27},{4,28},{5,29},{6,30},{7,31},{8,16},{9,... | collective-permute-start | bytes 294920 | tf_op jit(solution)/shard_map/ppermute | solution.py:22
  142.9 1.7 %collective-permute-start.42 = (bf16[32,1536]{1,0:T(8,128)(2,1)S(1)}, bf16[32,1536]{1,0:T(8,128)(2,1)S(1)}, u32[]{:S(2)}, u32[]{:S(2)}) collective-permute-start(bf16[32,1536]{1,0:T(8,128)(2,1)S(1)} %slice.446), channel_id=1, source_target_pairs={{0,1},{1,0},{2,3},{3,2},{4,5},{5,4},{6,7},{7,6},{8,9},{9,8},{10,11... | collective-permute-start | bytes 294920 | tf_op jit(solution)/shard_map/ppermute | solution.py:22
  150.4 2.0 %collective-permute-start.50 = (bf16[16,1536]{1,0:T(8,128)(2,1)S(1)}, bf16[16,1536]{1,0:T(8,128)(2,1)S(1)}, u32[]{:S(2)}, u32[]{:S(2)}) collective-permute-start(bf16[16,1536]{1,0:T(8,128)(2,1)S(1)} %slice.457), channel_id=1, source_target_pairs={{0,24},{1,25},{2,26},{3,27},{4,28},{5,29},{6,30},{7,31},{8,16},{9,... | collective-permute-start | bytes 147464 | tf_op jit(solution)/shard_map/ppermute | solution.py:22
  152.4 1.8 %collective-permute-start.30 = (bf16[16,1792]{1,0:T(8,128)(2,1)S(1)}, bf16[16,1792]{1,0:T(8,128)(2,1)S(1)}, u32[]{:S(2)}, u32[]{:S(2)}) collective-permute-start(bf16[16,1792]{1,0:T(8,128)(2,1)S(1)} %slice.453), channel_id=1, source_target_pairs={{0,3},{1,2},{2,1},{3,0},{4,7},{5,6},{6,5},{7,4},{8,11},{9,10},{10,... | collective-permute-start | bytes 172040 | tf_op jit(solution)/shard_map/ppermute | solution.py:22
  155.1 2.7 %collective-permute-done.30 = bf16[16,1792]{1,0:T(8,128)(2,1)S(1)} collective-permute-done((bf16[16,1792]{1,0:T(8,128)(2,1)S(1)}, bf16[16,1792]{1,0:T(8,128)(2,1)S(1)}, u32[]{:S(2)}, u32[]{:S(2)}) %collective-permute-start.30) | collective-permute-done | bytes 57376 | tf_op jit(solution)/shard_map/ppermute | solution.py:22
  157.8 1.8 %collective-permute-start.51 = (bf16[16,1536]{1,0:T(8,128)(2,1)S(1)}, bf16[16,1536]{1,0:T(8,128)(2,1)S(1)}, u32[]{:S(2)}, u32[]{:S(2)}) collective-permute-start(bf16[16,1536]{1,0:T(8,128)(2,1)S(1)} %slice.456), channel_id=1, source_target_pairs={{0,3},{1,2},{2,1},{3,0},{4,7},{5,6},{6,5},{7,4},{8,11},{9,10},{10,... | collective-permute-start | bytes 147464 | tf_op jit(solution)/shard_map/ppermute | solution.py:22
  (187 shorter events, 44.6 us)
Async XLA Ops:
  15.7 19.7 %collective-permute-start.1 = (bf16[1024,256]{1,0:T(8,128)(2,1)S(1)}, bf16[1024,256]{1,0:T(8,128)(2,1)S(1)}, u32[]{:S(2)}, u32[]{:S(2)}) collective-permute-start(bf16[1024,256]{1,0:T(8,128)(2,1)S(1)} %select_convert_fusion), channel_id=1, source_target_pairs={{0,32},{32,0},{64,96},{96,64},{1,33},{33,1},{65,97},{97,65},{2,34}... | collective-permute-start | bytes 1572872 | tf_op jit(solution)/shard_map/ppermute | solution.py:22
  16.2 9.9 %collective-permute-start.2 = (bf16[512,256]{1,0:T(8,128)(2,1)S(1)}, bf16[512,256]{1,0:T(8,128)(2,1)S(1)}, u32[]{:S(2)}, u32[]{:S(2)}) collective-permute-start(bf16[512,256]{1,0:T(8,128)(2,1)S(1)} %get-tuple-element.145.own_ref), channel_id=1, source_target_pairs={{0,64},{32,96},{64,0},{96,32},{1,65},{33,97},{65,1},{97,33},{2,66}... | collective-permute-start | bytes 786440 | tf_op jit(solution)/shard_map/ppermute | solution.py:22
  26.1 9.3 %collective-permute-start.3 = (bf16[512,256]{1,0:T(8,128)(2,1)S(1)}, bf16[512,256]{1,0:T(8,128)(2,1)S(1)}, u32[]{:S(2)}, u32[]{:S(2)}) collective-permute-start(bf16[512,256]{1,0:T(8,128)(2,1)S(1)} %collective-permute-done.2.far_ref), channel_id=1, source_target_pairs={{0,32},{32,0},{64,96},{96,64},{1,33},{33,1},{65,97},{97,65},{2,34}... | collective-permute-start | bytes 786440 | tf_op jit(solution)/shard_map/ppermute | solution.py:22
  32.1 10.3 %collective-permute-start.5 = (bf16[512,256]{1,0:T(8,128)(2,1)S(1)}, bf16[512,256]{1,0:T(8,128)(2,1)S(1)}, u32[]{:S(2)}, u32[]{:S(2)}) collective-permute-start(bf16[512,256]{1,0:T(8,128)(2,1)S(1)} %get-tuple-element.79.own_ref), channel_id=1, source_target_pairs={{0,64},{32,96},{64,0},{96,32},{1,65},{33,97},{65,1},{97,33},{2,66}... | collective-permute-start | bytes 786440 | tf_op jit(solution)/shard_map/ppermute | solution.py:22
  37.6 23.3 %collective-permute-start.15 = (bf16[256,1536]{1,0:T(8,128)(2,1)S(1)}, bf16[256,1536]{1,0:T(8,128)(2,1)S(1)}, u32[]{:S(2)}, u32[]{:S(2)}) collective-permute-start(bf16[256,1536]{1,0:T(8,128)(2,1)S(1)} %send3.3), channel_id=1, source_target_pairs={{0,24},{1,25},{2,26},{3,27},{4,28},{5,29},{6,30},{7,31},{8,16},{9,... | collective-permute-start | bytes 2359304 | tf_op jit(solution)/shard_map/ppermute | solution.py:22
  42.4 14.8 %collective-permute-start.6 = (bf16[512,256]{1,0:T(8,128)(2,1)S(1)}, bf16[512,256]{1,0:T(8,128)(2,1)S(1)}, u32[]{:S(2)}, u32[]{:S(2)}) collective-permute-start(bf16[512,256]{1,0:T(8,128)(2,1)S(1)} %collective-permute-done.5.far_ref), channel_id=1, source_target_pairs={{0,32},{32,0},{64,96},{96,64},{1,33},{33,1},{65,97},{97,65},{2,34}... | collective-permute-start | bytes 786440 | tf_op jit(solution)/shard_map/ppermute | solution.py:22
  44.3 21.0 %collective-permute-start.7 = (bf16[256,1536]{1,0:T(8,128)(2,1)S(1)}, bf16[256,1536]{1,0:T(8,128)(2,1)S(1)}, u32[]{:S(2)}, u32[]{:S(2)}) collective-permute-start(bf16[256,1536]{1,0:T(8,128)(2,1)S(1)} %send1.3), channel_id=1, source_target_pairs={{0,1},{1,0},{2,3},{3,2},{4,5},{5,4},{6,7},{7,6},{8,9},{9,8},{10,11... | collective-permute-start | bytes 2359304 | tf_op jit(solution)/shard_map/ppermute | solution.py:22
  48.6 28.8 %collective-permute-start.10 = (bf16[256,1792]{1,0:T(8,128)(2,1)S(1)}, bf16[256,1792]{1,0:T(8,128)(2,1)S(1)}, u32[]{:S(2)}, u32[]{:S(2)}) collective-permute-start(bf16[256,1792]{1,0:T(8,128)(2,1)S(1)} %send2.3), channel_id=1, source_target_pairs={{0,4},{1,5},{2,6},{3,7},{4,0},{5,1},{6,2},{7,3},{8,12},{9,13},{10,... | collective-permute-start | bytes 2752520 | tf_op jit(solution)/shard_map/ppermute | solution.py:22
  52.3 20.7 %collective-permute-start.22 = (bf16[256,1536]{1,0:T(8,128)(2,1)S(1)}, bf16[256,1536]{1,0:T(8,128)(2,1)S(1)}, u32[]{:S(2)}, u32[]{:S(2)}) collective-permute-start(bf16[256,1536]{1,0:T(8,128)(2,1)S(1)} %send4.3), channel_id=1, source_target_pairs={{0,3},{1,2},{2,1},{3,0},{4,7},{5,6},{6,5},{7,4},{8,11},{9,10},{10,... | collective-permute-start | bytes 2359304 | tf_op jit(solution)/shard_map/ppermute | solution.py:22
  57.1 22.9 %collective-permute-start.4 = (bf16[256,1792]{1,0:T(8,128)(2,1)S(1)}, bf16[256,1792]{1,0:T(8,128)(2,1)S(1)}, u32[]{:S(2)}, u32[]{:S(2)}) collective-permute-start(bf16[256,1792]{1,0:T(8,128)(2,1)S(1)} %send0.2), channel_id=1, source_target_pairs={{0,8},{1,9},{2,10},{3,11},{4,12},{5,13},{6,14},{7,15},{8,0},{9,1},... | collective-permute-start | bytes 2752520 | tf_op jit(solution)/shard_map/ppermute | solution.py:22
  60.8 23.1 %collective-permute-start.16 = (bf16[256,1536]{1,0:T(8,128)(2,1)S(1)}, bf16[256,1536]{1,0:T(8,128)(2,1)S(1)}, u32[]{:S(2)}, u32[]{:S(2)}) collective-permute-start(bf16[256,1536]{1,0:T(8,128)(2,1)S(1)} %send3.2), channel_id=1, source_target_pairs={{0,24},{1,25},{2,26},{3,27},{4,28},{5,29},{6,30},{7,31},{8,16},{9,... | collective-permute-start | bytes 2359304 | tf_op jit(solution)/shard_map/ppermute | solution.py:22
  65.3 31.0 %collective-permute-start.8 = (bf16[256,1792]{1,0:T(8,128)(2,1)S(1)}, bf16[256,1792]{1,0:T(8,128)(2,1)S(1)}, u32[]{:S(2)}, u32[]{:S(2)}) collective-permute-start(bf16[256,1792]{1,0:T(8,128)(2,1)S(1)} %send1.2), channel_id=1, source_target_pairs={{0,1},{1,0},{2,3},{3,2},{4,5},{5,4},{6,7},{7,6},{8,9},{9,8},{10,11... | collective-permute-start | bytes 2752520 | tf_op jit(solution)/shard_map/ppermute | solution.py:22
  73.0 25.1 %collective-permute-start.23 = (bf16[256,1792]{1,0:T(8,128)(2,1)S(1)}, bf16[256,1792]{1,0:T(8,128)(2,1)S(1)}, u32[]{:S(2)}, u32[]{:S(2)}) collective-permute-start(bf16[256,1792]{1,0:T(8,128)(2,1)S(1)} %send4.2), channel_id=1, source_target_pairs={{0,3},{1,2},{2,1},{3,0},{4,7},{5,6},{6,5},{7,4},{8,11},{9,10},{10,... | collective-permute-start | bytes 2752520 | tf_op jit(solution)/shard_map/ppermute | solution.py:22
  77.5 18.9 %collective-permute-start.11 = (bf16[256,1536]{1,0:T(8,128)(2,1)S(1)}, bf16[256,1536]{1,0:T(8,128)(2,1)S(1)}, u32[]{:S(2)}, u32[]{:S(2)}) collective-permute-start(bf16[256,1536]{1,0:T(8,128)(2,1)S(1)} %send2.2), channel_id=1, source_target_pairs={{0,4},{1,5},{2,6},{3,7},{4,0},{5,1},{6,2},{7,3},{8,12},{9,13},{10,... | collective-permute-start | bytes 2359304 | tf_op jit(solution)/shard_map/ppermute | solution.py:22
  80.1 18.7 %collective-permute-start.31 = (bf16[256,1536]{1,0:T(8,128)(2,1)S(1)}, bf16[256,1536]{1,0:T(8,128)(2,1)S(1)}, u32[]{:S(2)}, u32[]{:S(2)}) collective-permute-start(bf16[256,1536]{1,0:T(8,128)(2,1)S(1)} %send0.3), channel_id=1, source_target_pairs={{0,8},{1,9},{2,10},{3,11},{4,12},{5,13},{6,14},{7,15},{8,0},{9,1},... | collective-permute-start | bytes 2359304 | tf_op jit(solution)/shard_map/ppermute | solution.py:22
  84.0 24.2 %collective-permute-start.17 = (bf16[128,1792]{1,0:T(8,128)(2,1)S(1)}, bf16[128,1792]{1,0:T(8,128)(2,1)S(1)}, u32[]{:S(2)}, u32[]{:S(2)}) collective-permute-start(bf16[128,1792]{1,0:T(8,128)(2,1)S(1)} %get-tuple-element.93), channel_id=1, source_target_pairs={{0,24},{1,25},{2,26},{3,27},{4,28},{5,29},{6,30},{7,31},{8,16},{9,... | collective-permute-start | bytes 1376264 | tf_op jit(solution)/shard_map/ppermute | solution.py:22
  96.3 18.4 %collective-permute-start.9 = (bf16[128,1792]{1,0:T(8,128)(2,1)S(1)}, bf16[128,1792]{1,0:T(8,128)(2,1)S(1)}, u32[]{:S(2)}, u32[]{:S(2)}) collective-permute-start(bf16[128,1792]{1,0:T(8,128)(2,1)S(1)} %get-tuple-element.81), channel_id=1, source_target_pairs={{0,1},{1,0},{2,3},{3,2},{4,5},{5,4},{6,7},{7,6},{8,9},{9,8},{10,11... | collective-permute-start | bytes 1376264 | tf_op jit(solution)/shard_map/ppermute | solution.py:22
  96.4 14.0 %collective-permute-start.12 = (bf16[128,1536]{1,0:T(8,128)(2,1)S(1)}, bf16[128,1536]{1,0:T(8,128)(2,1)S(1)}, u32[]{:S(2)}, u32[]{:S(2)}) collective-permute-start(bf16[128,1536]{1,0:T(8,128)(2,1)S(1)} %get-tuple-element.85), channel_id=1, source_target_pairs={{0,4},{1,5},{2,6},{3,7},{4,0},{5,1},{6,2},{7,3},{8,12},{9,13},{10,... | collective-permute-start | bytes 1179656 | tf_op jit(solution)/shard_map/ppermute | solution.py:22
  98.0 14.2 %collective-permute-start.24 = (bf16[128,1536]{1,0:T(8,128)(2,1)S(1)}, bf16[128,1536]{1,0:T(8,128)(2,1)S(1)}, u32[]{:S(2)}, u32[]{:S(2)}) collective-permute-start(bf16[128,1536]{1,0:T(8,128)(2,1)S(1)} %get-tuple-element.103), channel_id=1, source_target_pairs={{0,3},{1,2},{2,1},{3,0},{4,7},{5,6},{6,5},{7,4},{8,11},{9,10},{10,... | collective-permute-start | bytes 1179656 | tf_op jit(solution)/shard_map/ppermute | solution.py:22
  98.8 15.1 %collective-permute-start.32 = (bf16[128,1536]{1,0:T(8,128)(2,1)S(1)}, bf16[128,1536]{1,0:T(8,128)(2,1)S(1)}, u32[]{:S(2)}, u32[]{:S(2)}) collective-permute-start(bf16[128,1536]{1,0:T(8,128)(2,1)S(1)} %get-tuple-element.115), channel_id=1, source_target_pairs={{0,8},{1,9},{2,10},{3,11},{4,12},{5,13},{6,14},{7,15},{8,0},{9,1},... | collective-permute-start | bytes 1179656 | tf_op jit(solution)/shard_map/ppermute | solution.py:22
  108.2 9.8 %collective-permute-start.18 = (bf16[128,1536]{1,0:T(8,128)(2,1)S(1)}, bf16[128,1536]{1,0:T(8,128)(2,1)S(1)}, u32[]{:S(2)}, u32[]{:S(2)}) collective-permute-start(bf16[128,1536]{1,0:T(8,128)(2,1)S(1)} %get-tuple-element.94), channel_id=1, source_target_pairs={{0,24},{1,25},{2,26},{3,27},{4,28},{5,29},{6,30},{7,31},{8,16},{9,... | collective-permute-start | bytes 1179656 | tf_op jit(solution)/shard_map/ppermute | solution.py:22
  110.4 13.1 %collective-permute-start.13 = (bf16[128,1792]{1,0:T(8,128)(2,1)S(1)}, bf16[128,1792]{1,0:T(8,128)(2,1)S(1)}, u32[]{:S(2)}, u32[]{:S(2)}) collective-permute-start(bf16[128,1792]{1,0:T(8,128)(2,1)S(1)} %get-tuple-element.86), channel_id=1, source_target_pairs={{0,4},{1,5},{2,6},{3,7},{4,0},{5,1},{6,2},{7,3},{8,12},{9,13},{10,... | collective-permute-start | bytes 1376264 | tf_op jit(solution)/shard_map/ppermute | solution.py:22
  112.2 9.3 %collective-permute-start.25 = (bf16[128,1536]{1,0:T(8,128)(2,1)S(1)}, bf16[128,1536]{1,0:T(8,128)(2,1)S(1)}, u32[]{:S(2)}, u32[]{:S(2)}) collective-permute-start(bf16[128,1536]{1,0:T(8,128)(2,1)S(1)} %get-tuple-element.104), channel_id=1, source_target_pairs={{0,3},{1,2},{2,1},{3,0},{4,7},{5,6},{6,5},{7,4},{8,11},{9,10},{10,... | collective-permute-start | bytes 1179656 | tf_op jit(solution)/shard_map/ppermute | solution.py:22
  113.9 10.2 %collective-permute-start.33 = (bf16[128,1792]{1,0:T(8,128)(2,1)S(1)}, bf16[128,1792]{1,0:T(8,128)(2,1)S(1)}, u32[]{:S(2)}, u32[]{:S(2)}) collective-permute-start(bf16[128,1792]{1,0:T(8,128)(2,1)S(1)} %get-tuple-element.116), channel_id=1, source_target_pairs={{0,8},{1,9},{2,10},{3,11},{4,12},{5,13},{6,14},{7,15},{8,0},{9,1},... | collective-permute-start | bytes 1376264 | tf_op jit(solution)/shard_map/ppermute | solution.py:22
  114.7 8.7 %collective-permute-start.39 = (bf16[128,1536]{1,0:T(8,128)(2,1)S(1)}, bf16[128,1536]{1,0:T(8,128)(2,1)S(1)}, u32[]{:S(2)}, u32[]{:S(2)}) collective-permute-start(bf16[128,1536]{1,0:T(8,128)(2,1)S(1)} %get-tuple-element.125), channel_id=1, source_target_pairs={{0,1},{1,0},{2,3},{3,2},{4,5},{5,4},{6,7},{7,6},{8,9},{9,8},{10,11... | collective-permute-start | bytes 1179656 | tf_op jit(solution)/shard_map/ppermute | solution.py:22
  118.0 8.0 %collective-permute-start.19 = (bf16[64,1536]{1,0:T(8,128)(2,1)S(1)}, bf16[64,1536]{1,0:T(8,128)(2,1)S(1)}, u32[]{:S(2)}, u32[]{:S(2)}) collective-permute-start(bf16[64,1536]{1,0:T(8,128)(2,1)S(1)} %slice.439), channel_id=1, source_target_pairs={{0,24},{1,25},{2,26},{3,27},{4,28},{5,29},{6,30},{7,31},{8,16},{9,... | collective-permute-start | bytes 589832 | tf_op jit(solution)/shard_map/ppermute | solution.py:22
  121.5 8.3 %collective-permute-start.26 = (bf16[64,1792]{1,0:T(8,128)(2,1)S(1)}, bf16[64,1792]{1,0:T(8,128)(2,1)S(1)}, u32[]{:S(2)}, u32[]{:S(2)}) collective-permute-start(bf16[64,1792]{1,0:T(8,128)(2,1)S(1)} %slice.431), channel_id=1, source_target_pairs={{0,3},{1,2},{2,1},{3,0},{4,7},{5,6},{6,5},{7,4},{8,11},{9,10},{10,... | collective-permute-start | bytes 688136 | tf_op jit(solution)/shard_map/ppermute | solution.py:22
  123.5 10.3 %collective-permute-start.14 = (bf16[64,1792]{1,0:T(8,128)(2,1)S(1)}, bf16[64,1792]{1,0:T(8,128)(2,1)S(1)}, u32[]{:S(2)}, u32[]{:S(2)}) collective-permute-start(bf16[64,1792]{1,0:T(8,128)(2,1)S(1)} %slice.433), channel_id=1, source_target_pairs={{0,4},{1,5},{2,6},{3,7},{4,0},{5,1},{6,2},{7,3},{8,12},{9,13},{10,... | collective-permute-start | bytes 688136 | tf_op jit(solution)/shard_map/ppermute | solution.py:22
  124.2 7.8 %collective-permute-start.34 = (bf16[64,1536]{1,0:T(8,128)(2,1)S(1)}, bf16[64,1536]{1,0:T(8,128)(2,1)S(1)}, u32[]{:S(2)}, u32[]{:S(2)}) collective-permute-start(bf16[64,1536]{1,0:T(8,128)(2,1)S(1)} %slice.436), channel_id=1, source_target_pairs={{0,8},{1,9},{2,10},{3,11},{4,12},{5,13},{6,14},{7,15},{8,0},{9,1},... | collective-permute-start | bytes 589832 | tf_op jit(solution)/shard_map/ppermute | solution.py:22
  125.2 8.5 %collective-permute-start.40 = (bf16[64,1536]{1,0:T(8,128)(2,1)S(1)}, bf16[64,1536]{1,0:T(8,128)(2,1)S(1)}, u32[]{:S(2)}, u32[]{:S(2)}) collective-permute-start(bf16[64,1536]{1,0:T(8,128)(2,1)S(1)} %slice.435), channel_id=1, source_target_pairs={{0,1},{1,0},{2,3},{3,2},{4,5},{5,4},{6,7},{7,6},{8,9},{9,8},{10,11... | collective-permute-start | bytes 589832 | tf_op jit(solution)/shard_map/ppermute | solution.py:22
  126.0 8.5 %collective-permute-start.20 = (bf16[64,1792]{1,0:T(8,128)(2,1)S(1)}, bf16[64,1792]{1,0:T(8,128)(2,1)S(1)}, u32[]{:S(2)}, u32[]{:S(2)}) collective-permute-start(bf16[64,1792]{1,0:T(8,128)(2,1)S(1)} %slice.432), channel_id=1, source_target_pairs={{0,24},{1,25},{2,26},{3,27},{4,28},{5,29},{6,30},{7,31},{8,16},{9,... | collective-permute-start | bytes 688136 | tf_op jit(solution)/shard_map/ppermute | solution.py:22
  129.8 7.9 %collective-permute-start.27 = (bf16[64,1536]{1,0:T(8,128)(2,1)S(1)}, bf16[64,1536]{1,0:T(8,128)(2,1)S(1)}, u32[]{:S(2)}, u32[]{:S(2)}) collective-permute-start(bf16[64,1536]{1,0:T(8,128)(2,1)S(1)} %slice.438), channel_id=1, source_target_pairs={{0,3},{1,2},{2,1},{3,0},{4,7},{5,6},{6,5},{7,4},{8,11},{9,10},{10,... | collective-permute-start | bytes 589832 | tf_op jit(solution)/shard_map/ppermute | solution.py:22
  132.0 7.8 %collective-permute-start.35 = (bf16[64,1536]{1,0:T(8,128)(2,1)S(1)}, bf16[64,1536]{1,0:T(8,128)(2,1)S(1)}, u32[]{:S(2)}, u32[]{:S(2)}) collective-permute-start(bf16[64,1536]{1,0:T(8,128)(2,1)S(1)} %slice.437), channel_id=1, source_target_pairs={{0,8},{1,9},{2,10},{3,11},{4,12},{5,13},{6,14},{7,15},{8,0},{9,1},... | collective-permute-start | bytes 589832 | tf_op jit(solution)/shard_map/ppermute | solution.py:22
  133.6 9.3 %collective-permute-start.41 = (bf16[64,1792]{1,0:T(8,128)(2,1)S(1)}, bf16[64,1792]{1,0:T(8,128)(2,1)S(1)}, u32[]{:S(2)}, u32[]{:S(2)}) collective-permute-start(bf16[64,1792]{1,0:T(8,128)(2,1)S(1)} %slice.430), channel_id=1, source_target_pairs={{0,1},{1,0},{2,3},{3,2},{4,5},{5,4},{6,7},{7,6},{8,9},{9,8},{10,11... | collective-permute-start | bytes 688136 | tf_op jit(solution)/shard_map/ppermute | solution.py:22
  133.8 7.0 %collective-permute-start.45 = (bf16[64,1536]{1,0:T(8,128)(2,1)S(1)}, bf16[64,1536]{1,0:T(8,128)(2,1)S(1)}, u32[]{:S(2)}, u32[]{:S(2)}) collective-permute-start(bf16[64,1536]{1,0:T(8,128)(2,1)S(1)} %slice.434), channel_id=1, source_target_pairs={{0,4},{1,5},{2,6},{3,7},{4,0},{5,1},{6,2},{7,3},{8,12},{9,13},{10,... | collective-permute-start | bytes 589832 | tf_op jit(solution)/shard_map/ppermute | solution.py:22
  134.4 6.3 %collective-permute-start.21 = (bf16[32,1792]{1,0:T(8,128)(2,1)S(1)}, bf16[32,1792]{1,0:T(8,128)(2,1)S(1)}, u32[]{:S(2)}, u32[]{:S(2)}) collective-permute-start(bf16[32,1792]{1,0:T(8,128)(2,1)S(1)} %slice.443), channel_id=1, source_target_pairs={{0,24},{1,25},{2,26},{3,27},{4,28},{5,29},{6,30},{7,31},{8,16},{9,... | collective-permute-start | bytes 344072 | tf_op jit(solution)/shard_map/ppermute | solution.py:22
  137.7 7.5 %collective-permute-start.28 = (bf16[32,1536]{1,0:T(8,128)(2,1)S(1)}, bf16[32,1536]{1,0:T(8,128)(2,1)S(1)}, u32[]{:S(2)}, u32[]{:S(2)}) collective-permute-start(bf16[32,1536]{1,0:T(8,128)(2,1)S(1)} %slice.449), channel_id=1, source_target_pairs={{0,3},{1,2},{2,1},{3,0},{4,7},{5,6},{6,5},{7,4},{8,11},{9,10},{10,... | collective-permute-start | bytes 294920 | tf_op jit(solution)/shard_map/ppermute | solution.py:22
  139.8 6.5 %collective-permute-start.36 = (bf16[32,1792]{1,0:T(8,128)(2,1)S(1)}, bf16[32,1792]{1,0:T(8,128)(2,1)S(1)}, u32[]{:S(2)}, u32[]{:S(2)}) collective-permute-start(bf16[32,1792]{1,0:T(8,128)(2,1)S(1)} %slice.441), channel_id=1, source_target_pairs={{0,8},{1,9},{2,10},{3,11},{4,12},{5,13},{6,14},{7,15},{8,0},{9,1},... | collective-permute-start | bytes 344072 | tf_op jit(solution)/shard_map/ppermute | solution.py:22
  140.8 5.9 %collective-permute-start.49 = (bf16[32,1536]{1,0:T(8,128)(2,1)S(1)}, bf16[32,1536]{1,0:T(8,128)(2,1)S(1)}, u32[]{:S(2)}, u32[]{:S(2)}) collective-permute-start(bf16[32,1536]{1,0:T(8,128)(2,1)S(1)} %slice.444), channel_id=1, source_target_pairs={{0,24},{1,25},{2,26},{3,27},{4,28},{5,29},{6,30},{7,31},{8,16},{9,... | collective-permute-start | bytes 294920 | tf_op jit(solution)/shard_map/ppermute | solution.py:22
  145.3 7.2 %collective-permute-start.29 = (bf16[32,1792]{1,0:T(8,128)(2,1)S(1)}, bf16[32,1792]{1,0:T(8,128)(2,1)S(1)}, u32[]{:S(2)}, u32[]{:S(2)}) collective-permute-start(bf16[32,1792]{1,0:T(8,128)(2,1)S(1)} %slice.442), channel_id=1, source_target_pairs={{0,3},{1,2},{2,1},{3,0},{4,7},{5,6},{6,5},{7,4},{8,11},{9,10},{10,... | collective-permute-start | bytes 344072 | tf_op jit(solution)/shard_map/ppermute | solution.py:22
  146.3 8.0 %collective-permute-start.37 = (bf16[32,1536]{1,0:T(8,128)(2,1)S(1)}, bf16[32,1536]{1,0:T(8,128)(2,1)S(1)}, u32[]{:S(2)}, u32[]{:S(2)}) collective-permute-start(bf16[32,1536]{1,0:T(8,128)(2,1)S(1)} %slice.448), channel_id=1, source_target_pairs={{0,8},{1,9},{2,10},{3,11},{4,12},{5,13},{6,14},{7,15},{8,0},{9,1},... | collective-permute-start | bytes 294920 | tf_op jit(solution)/shard_map/ppermute | solution.py:22
  148.1 6.3 %collective-permute-start.43 = (bf16[32,1536]{1,0:T(8,128)(2,1)S(1)}, bf16[32,1536]{1,0:T(8,128)(2,1)S(1)}, u32[]{:S(2)}, u32[]{:S(2)}) collective-permute-start(bf16[32,1536]{1,0:T(8,128)(2,1)S(1)} %slice.447), channel_id=1, source_target_pairs={{0,1},{1,0},{2,3},{3,2},{4,5},{5,4},{6,7},{7,6},{8,9},{9,8},{10,11... | collective-permute-start | bytes 294920 | tf_op jit(solution)/shard_map/ppermute | solution.py:22
  149.4 10.2 %collective-permute-start.47 = (bf16[32,1792]{1,0:T(8,128)(2,1)S(1)}, bf16[32,1792]{1,0:T(8,128)(2,1)S(1)}, u32[]{:S(2)}, u32[]{:S(2)}) collective-permute-start(bf16[32,1792]{1,0:T(8,128)(2,1)S(1)} %slice.440), channel_id=1, source_target_pairs={{0,4},{1,5},{2,6},{3,7},{4,0},{5,1},{6,2},{7,3},{8,12},{9,13},{10,... | collective-permute-start | bytes 344072 | tf_op jit(solution)/shard_map/ppermute | solution.py:22
  150.4 9.8 %collective-permute-start.50 = (bf16[16,1536]{1,0:T(8,128)(2,1)S(1)}, bf16[16,1536]{1,0:T(8,128)(2,1)S(1)}, u32[]{:S(2)}, u32[]{:S(2)}) collective-permute-start(bf16[16,1536]{1,0:T(8,128)(2,1)S(1)} %slice.457), channel_id=1, source_target_pairs={{0,24},{1,25},{2,26},{3,27},{4,28},{5,29},{6,30},{7,31},{8,16},{9,... | collective-permute-start | bytes 147464 | tf_op jit(solution)/shard_map/ppermute | solution.py:22
  152.4 5.4 %collective-permute-start.30 = (bf16[16,1792]{1,0:T(8,128)(2,1)S(1)}, bf16[16,1792]{1,0:T(8,128)(2,1)S(1)}, u32[]{:S(2)}, u32[]{:S(2)}) collective-permute-start(bf16[16,1792]{1,0:T(8,128)(2,1)S(1)} %slice.453), channel_id=1, source_target_pairs={{0,3},{1,2},{2,1},{3,0},{4,7},{5,6},{6,5},{7,4},{8,11},{9,10},{10,... | collective-permute-start | bytes 172040 | tf_op jit(solution)/shard_map/ppermute | solution.py:22
  154.3 7.3 %collective-permute-start.38 = (bf16[16,1536]{1,0:T(8,128)(2,1)S(1)}, bf16[16,1536]{1,0:T(8,128)(2,1)S(1)}, u32[]{:S(2)}, u32[]{:S(2)}) collective-permute-start(bf16[16,1536]{1,0:T(8,128)(2,1)S(1)} %slice.459), channel_id=1, source_target_pairs={{0,8},{1,9},{2,10},{3,11},{4,12},{5,13},{6,14},{7,15},{8,0},{9,1},... | collective-permute-start | bytes 147464 | tf_op jit(solution)/shard_map/ppermute | solution.py:22
  154.4 8.7 %collective-permute-start.44 = (bf16[16,1792]{1,0:T(8,128)(2,1)S(1)}, bf16[16,1792]{1,0:T(8,128)(2,1)S(1)}, u32[]{:S(2)}, u32[]{:S(2)}) collective-permute-start(bf16[16,1792]{1,0:T(8,128)(2,1)S(1)} %slice.452), channel_id=1, source_target_pairs={{0,1},{1,0},{2,3},{3,2},{4,5},{5,4},{6,7},{7,6},{8,9},{9,8},{10,11... | collective-permute-start | bytes 172040 | tf_op jit(solution)/shard_map/ppermute | solution.py:22
  160.2 7.7 %collective-permute-start.55 = (bf16[16,1792]{1,0:T(8,128)(2,1)S(1)}, bf16[16,1792]{1,0:T(8,128)(2,1)S(1)}, u32[]{:S(2)}, u32[]{:S(2)}) collective-permute-start(bf16[16,1792]{1,0:T(8,128)(2,1)S(1)} %slice.450), channel_id=1, source_target_pairs={{0,24},{1,25},{2,26},{3,27},{4,28},{5,29},{6,30},{7,31},{8,16},{9,... | collective-permute-start | bytes 172040 | tf_op jit(solution)/shard_map/ppermute | solution.py:22
  (15 other events, 168.0 us)

commit v3 on v2

--- a/solution.py
+++ b/solution.py
@@ -10,9 +10,9 @@
 BF16, F32 = jnp.bfloat16, jnp.float32
 LINKS = (8, 1, 4, 24, 3)
 STEPS = len(LINKS)
-TILE = 256
-PARTS = ((7, 6, 7, 6, 6), (6, 7, 6, 6, 7))
-WAVES = len(PARTS)
+LANES, TILE = 128, 256
+PARTS = (12, 13, 13, 13, 13)
+EARLY = (6, 6, 6, 6, 6)
 VMEM = pl.BlockSpec(memory_space=pltpu.VMEM)
 HBM = pl.BlockSpec(memory_space=pltpu.HBM)
 MIB = 1 << 20
@@ -45,44 +45,40 @@
     return out
 
 
-def encode_kernel(x_hbm, w_hbm, keep_ref, send_ref, xbuf, wbuf, xsem, wsem, *, masks, rows, chunks):
+def encode_kernel(
+    x_hbm, w_hbm, keep_ref, send_ref, xbuf, wbuf, xsem, wsem, *, masks, rows, chunks
+):
     me = lax.axis_index("lat")
     core = lax.axis_index("layer") % 2
     width = w_hbm.shape[2] // 2
-    depth = w_hbm.shape[1] // chunks
-    n = len(masks)
-    part = rows // WAVES
-    wcopies, xcopies = [], []
-    for k in range(chunks):
-        at = pl.ds(k * depth, depth)
-        wcopies.append(pltpu.make_async_copy(w_hbm.at[0, at], wbuf.at[at], wsem.at[k]))
-    for h in range(WAVES):
+    copies = []
+    for k, (at, depth) in enumerate(chunks):
+        ks = pl.ds(at, depth)
+        mine = [pltpu.make_async_copy(w_hbm.at[0, ks], wbuf.at[ks], wsem.at[k])]
         for j, mask in enumerate(masks):
-            src = jnp.bitwise_xor(me, mask) * rows + h * part
-            to = (h * n + j) * part
-            xcopies.append(
+            src = pl.multiple_of(jnp.bitwise_xor(me, mask) * rows, rows)
+            mine.append(
                 pltpu.make_async_copy(
-                    x_hbm.at[0, pl.ds(pl.multiple_of(src, part), part)],
-                    xbuf.at[pl.ds(to, part)],
-                    xsem.at[h * n + j],
+                    x_hbm.at[0, pl.ds(src, rows), ks],
+                    xbuf.at[pl.ds(j * rows, rows), ks],
+                    xsem.at[k * len(masks) + j],
                 )
             )
-    for c in wcopies[:1] + xcopies[:n] + wcopies[1:] + xcopies[n:]:
-        c.start()
-    mine = pl.ds(pl.multiple_of(core * width, width), width)
-    other = pl.ds(pl.multiple_of((1 - core) * width, width), width)
-    for h in range(WAVES):
-        for c in xcopies[h * n : (h + 1) * n]:
+        copies.append(mine)
+    for mine in copies:
+        for c in mine:
+            c.start()
+    half = (
+        pl.ds(pl.multiple_of((1 - core) * width, width), width),
+        pl.ds(pl.multiple_of(core * width, width), width),
+    )
+    for k, (at, depth) in enumerate(chunks):
+        for c in copies[k]:
             c.wait()
-        rs = pl.ds(h * n * part, n * part)
-        for k in range(chunks):
-            if h == 0:
-                wcopies[k].wait()
-            at = pl.ds(k * depth, depth)
-            x = xbuf[rs, at]
-            for ref, cols in ((send_ref, other), (keep_ref, mine)):
-                d = jnp.dot(x, wbuf[at, cols], preferred_element_type=F32)
-                ref[rs, :] = d if k == 0 else ref[rs, :] + d
+        ks = pl.ds(at, depth)
+        for ref, cols in zip((send_ref, keep_ref), half):
+            d = jnp.dot(xbuf[:, ks], wbuf[ks, cols], preferred_element_type=F32)
+            ref[...] = d if k == 0 else ref[...] + d
 
 
 def encode(x, w):
@@ -90,19 +86,21 @@
     width = w.shape[2] // 2
     masks = block_masks()
     rows = tokens // len(masks)
-    half = jax.ShapeDtypeStruct((tokens, width), F32)
-    return pl.pallas_call(
-        functools.partial(encode_kernel, masks=masks, rows=rows, chunks=4),
+    q = depth // 4
+    chunks = ((0, q), (q, q), (2 * q, 2 * q))
+    half = pltpu.VMEM((tokens, width), F32)
+    return pl.pallas_call(
+        functools.partial(encode_kernel, masks=masks, rows=rows, chunks=chunks),
         out_shape=(half, half),
-        in_specs=[HBM, HBM],
-        out_specs=[VMEM, VMEM],
+        in_specs=[HBM] * 2,
+        out_specs=[VMEM] * 2,
         scratch_shapes=[
             pltpu.VMEM((tokens, depth), BF16),
             pltpu.VMEM((depth, 2 * width), BF16),
-            pltpu.SemaphoreType.DMA((len(masks) * WAVES,)),
-            pltpu.SemaphoreType.DMA((4,)),
+            pltpu.SemaphoreType.DMA((len(masks) * len(chunks),)),
+            pltpu.SemaphoreType.DMA((len(chunks),)),
         ],
-        compiler_params=pltpu.CompilerParams(vmem_limit_bytes=56 * MIB),
+        compiler_params=pltpu.CompilerParams(vmem_limit_bytes=54 * MIB),
         cost_estimate=pl.CostEstimate(
             flops=4 * tokens * depth * width,
             bytes_accessed=2 * (tokens * depth + 2 * depth * width) + 8 * tokens * width,
@@ -174,30 +172,44 @@
         lhs[pl.ds(j * rows, rows), :] = codes_ref[pl.ds(b * rows, rows), :]
 
 
-def tile_product(lhs, w_ref, at, t):
-    w = w_ref[:, :, pl.ds(pl.multiple_of(at + t * TILE, TILE), TILE)]
-    return jnp.dot(lhs[...], w.reshape(lhs.shape[1], TILE), preferred_element_type=F32)
+def over_tiles(begin, end, body):
+    whole = (end - begin) // TILE
+
+    @pl.loop(0, whole)
+    def _(t):
+        body(pl.multiple_of(begin + t * TILE, LANES), TILE)
+
+    if begin + whole * TILE < end:
+        body(begin + whole * TILE, end - begin - whole * TILE)
+
+
+def product(lhs, w_ref, at, n):
+    w = w_ref[:, :, pl.ds(pl.multiple_of(at, LANES), n)]
+    return jnp.dot(lhs[...], w.reshape(lhs.shape[1], n), preferred_element_type=F32)
 
 
 def send_kernel(codes_ref, w_ref, send_ref, lhs, *, blocks, at):
     gather_rows(codes_ref, lhs, blocks)
 
-    @pl.loop(0, send_ref.shape[1] // TILE)
-    def _(t):
-        cols = pl.ds(pl.multiple_of(t * TILE, TILE), TILE)
-        send_ref[:, cols] = tile_product(lhs, w_ref, at, t).astype(BF16)
-
-
-def keep_kernel(codes_ref, w_ref, got_ref, keep_ref, send_ref, lhs, *, blocks, at):
+    def body(c, n):
+        send_ref[:, pl.ds(c, n)] = product(lhs, w_ref, at + c, n).astype(BF16)
+
+    over_tiles(0, send_ref.shape[1], body)
+
+
+def keep_kernel(codes_ref, w_ref, early_ref, late_ref, keep_ref, send_ref, lhs, *, blocks, at):
     gather_rows(codes_ref, lhs, blocks)
-    n2 = lhs.shape[0] // 2
-
-    @pl.loop(0, send_ref.shape[1] // TILE)
-    def _(t):
-        cols = pl.ds(pl.multiple_of(t * TILE, TILE), TILE)
-        total = tile_product(lhs, w_ref, at, t) + got_ref[:, cols].astype(F32)
-        keep_ref[:, cols] = total[:n2]
-        send_ref[:, cols] = total[n2:].astype(BF16)
+    m = lhs.shape[0] // 2
+    split = early_ref.shape[1]
+    for got_ref, begin, end in ((early_ref, 0, split), (late_ref, split, send_ref.shape[1])):
+
+        def body(c, n):
+            got = got_ref[:, pl.ds(pl.multiple_of(c - begin, LANES), n)]
+            total = product(lhs, w_ref, at + c, n) + got.astype(F32)
+            keep_ref[:, pl.ds(c, n)] = total[:m]
+            send_ref[:, pl.ds(c, n)] = total[m:].astype(BF16)
+
+        over_tiles(begin, end, body)
 
 
 def decode_send(codes, w, first, at, wide):
@@ -216,23 +228,25 @@
     )(codes, w)
 
 
-def decode_keep(codes, w, got, first, at, wide):
+def decode_keep(codes, w, early, late, first, at):
     tokens, depth = codes.shape
     blocks = part_blocks(first)
     n = tokens // 2
+    wide = early.shape[1] + late.shape[1]
     return pl.pallas_call(
         functools.partial(keep_kernel, blocks=blocks[: len(blocks) // 2], at=at),
         out_shape=(
             jax.ShapeDtypeStruct((n // 2, wide), F32),
             jax.ShapeDtypeStruct((n // 2, wide), BF16),
         ),
-        in_specs=[VMEM, VMEM, VMEM],
+        in_specs=[VMEM] * 4,
         out_specs=[VMEM, VMEM],
         scratch_shapes=[pltpu.VMEM((n, depth), BF16)],
         compiler_params=pltpu.CompilerParams(vmem_limit_bytes=8 * MIB),
         cost_estimate=pl.CostEstimate(flops=1000, bytes_accessed=1000, transcendentals=0),
         name=f"keep{first}",
-    )(codes, w, got)
+    )(codes, w, early, late)
+
 
 def shards(
     resid_halves,
@@ -258,12 +272,8 @@
     keep, send = encode(resid_halves, enc_weight)
     recv = xor_swap(send, "layer", 1)
 
-    part = rows // WAVES
-    within = jnp.arange(part, dtype=jnp.int32)
     row_token = (
-        (jnp.bitwise_xor(masks, me) * rows)[None, :, None]
-        + (jnp.arange(WAVES, dtype=jnp.int32) * part)[:, None, None]
-        + within[None, None, :]
+        jnp.bitwise_xor(masks, me)[:, None] * rows + jnp.arange(rows, dtype=jnp.int32)[None, :]
     ).reshape(tokens)
     my_rows = lax.dynamic_index_in_dim(clamp_rows, source, 0, keepdims=False)
     my_pick = lax.dynamic_index_in_dim(
@@ -285,42 +295,38 @@
     own = jnp.where(hit, value[:, None], pre * ramp).astype(BF16)
 
     own_sib = xor_swap(own, "layer", 1)
+
     weights = load(lax.optimization_barrier((dec_weight, own))[0])
-    n = tokens // WAVES
-    codes, far = [], None
-    for h in range(WAVES):
-        mine = own[h * n : (h + 1) * n]
-        sent = mine if far is None else lax.optimization_barrier((mine, far, weights))[0]
-        far = xor_swap(sent, "layer", 2)
-        codes.append(
-            assemble(mine, own_sib[h * n : (h + 1) * n], far, xor_swap(far, "layer", 1))
-        )
-
-    starts = [[sum(wave[:p]) * TILE for p in range(STEPS)] for wave in PARTS]
-    out, kept = {}, {}
-    for h in range(WAVES):
+    far, weights = lax.optimization_barrier((xor_swap(own, "layer", 2), weights))
+    codes = assemble(own, own_sib, far, xor_swap(far, "layer", 1))
+
+    starts = [sum(PARTS[:p]) * LANES for p in range(STEPS)]
+    last = [None] * STEPS
+
+    def exchange(data, link):
+        if last[link] is not None:
+            data = lax.optimization_barrier((data, last[link]))[0]
+        last[link] = xor_swap(data, "lat", LINKS[link])
+        return last[link]
+
+    got = [[] for _ in PARTS]
+    for late in (False, True):
         for p in range(STEPS):
-            out[h, p] = decode_send(codes[h], weights, p, starts[h][p], PARTS[h][p] * TILE)
-    last = [None] * STEPS
-    for i in range(STEPS):
-        for h in range(WAVES):
-            for p in range(STEPS):
-                link = (p + i) % STEPS
-                data = out[h, p]
-                if last[link] is not None:
-                    data = lax.optimization_barrier((data, last[link]))[0]
-                got = last[link] = xor_swap(data, "lat", LINKS[link])
-                if i == 0:
-                    kept[h, p], out[h, p] = decode_keep(
-                        codes[h], weights, got, p, starts[h][p], PARTS[h][p] * TILE
-                    )
-                else:
-                    total = kept[h, p] + got.astype(F32)
-                    m = total.shape[0] // 2
-                    kept[h, p] = total[:m] if i < STEPS - 1 else total
-                    out[h, p] = total[m:].astype(BF16)
-    summed = [jnp.concatenate([kept[h, p] for p in range(STEPS)], axis=1) for h in range(WAVES)]
-    return (jnp.concatenate(summed, axis=0) + dec_bias).astype(BF16)[None]
+            at, wide = starts[p], EARLY[p] * LANES
+            if late:
+                at, wide = at + wide, PARTS[p] * LANES - wide
+            got[p].append(exchange(decode_send(codes, weights, p, at, wide), p))
+    kept, out = {}, {}
+    for p in range(STEPS):
+        kept[p], out[p] = decode_keep(codes, weights, *got[p], p, starts[p])
+    for i in range(1, STEPS):
+        for p in range(STEPS):
+            total = kept[p] + exchange(out[p], (p + i) % STEPS).astype(F32)
+            m = total.shape[0] // 2
+            kept[p] = total[:m] if i < STEPS - 1 else total
+            out[p] = total[m:].astype(BF16)
+    summed = jnp.concatenate([kept[p] for p in range(STEPS)], axis=1)
+    return (summed + dec_bias).astype(BF16)[None]
 
 
 def solution(mesh):

time: 169 us -> 143 us (0.85)
  starting transfers between devices: 71.5 us -> 51.1 us
  Pallas kernels: 58.4 us -> 47.4 us
  waiting for transfers between devices: 30.1 us -> 37.7 us
    ppermute x56 -> x34, starting transfers between devices: 71.5 us -> 51.1 us  [xor_swap(): lax.ppermute(value, axis, [(i, i ^ mask) for i in range(lax.axis_size(axi...]
    ppermute x56 -> x34, waiting for transfers between devices: 30.1 us -> 37.7 us  [xor_swap(): lax.ppermute(value, axis, [(i, i ^ mask) for i in range(lax.axis_size(axi...]
    pallas_call x10 -> x5, Pallas kernels: 20.8 us -> 15.7 us  [decode_keep(): pl.pallas_call(functools.partial(keep_kernel, blocks=blocks[:len(blocks)...]
    pallas_call x10, Pallas kernels: 20.7 us -> 16 us  [decode_send(): pl.pallas_call(functools.partial(send_kernel, blocks=blocks[len(blocks) /...]
  transfers between devices with their start and end apart: 56 -> 34, of which waited for: 18 -> 18; matrix products, arithmetic and copies ran while one was open for 3% -> 4% of each run, Pallas kernels for 28% -> 25%
where the time goes in v3:
time: 143 us
  starting transfers between devices  51.1 us (36%)
  Pallas kernels  47.4 us (33%)
  waiting for transfers between devices  37.7 us (26%)
  other arithmetic  3.15 us (2%)
  local copies, waits for them, and re-layouts  2.06 us (1%)
    ppermute x34, starting transfers between devices, xor_swap(): lax.ppermute(value, axis, [(i, i ^ mask) for i in range(lax.axis_size(axi...  51.1 us
    ppermute x34, waiting for transfers between devices, xor_swap(): lax.ppermute(value, axis, [(i, i ^ mask) for i in range(lax.axis_size(axi...  37.7 us
    pallas_call x10, Pallas kernels, decode_send(): pl.pallas_call(functools.partial(send_kernel, blocks=blocks[len(blocks) /...  16 us
    pallas_call x5, Pallas kernels, decode_keep(): pl.pallas_call(functools.partial(keep_kernel, blocks=blocks[:len(blocks)...  15.7 us
    pallas_call x1, Pallas kernels, encode(): pl.pallas_call(functools.partial(encode_kernel, masks=masks, rows=rows, c...  9.49 us
    pallas_call x1, Pallas kernels, load(): pl.pallas_call(functools.partial(load_kernel, pieces=4), out_shape=pltpu....  5.92 us
  transfers between devices with their start and end apart: 34, of which 18 were waited for; matrix products, arithmetic and copies ran while one was open for 4% of the time, Pallas kernels for 25%

profile of v3, /device:TPU:0, one launch (start us, length us, event | category | flops | bytes accessed | tf_op | source)
XLA Modules:
  0.0 143.2 jit_solution(11348045120134800220)
XLA Ops:
  0.0 9.5 %encode.1 = (f32[1024,256]{1,0:T(8,128)S(1)}, f32[1024,256]{1,0:T(8,128)S(1)}) custom-call(bf16[1,1024,4096]{2,1,0:T(8,128)(2,1)} %x_hbm.1, bf16[1,4096,512]{2,1,0:T(8,128)(2,1)} %w_hbm.1), custom_call_target="tpu_custom_call" | custom-call | flops 4294967296 | bytes 14680064 | tf_op jit(solution)/shard_map/encode/pallas_call | solution.py:92
  13.2 3.4 %collective-permute-start.2 = (bf16[1024,256]{1,0:T(8,128)(2,1)S(1)}, bf16[1024,256]{1,0:T(8,128)(2,1)S(1)}, u32[]{:S(2)}, u32[]{:S(2)}) collective-permute-start(bf16[1024,256]{1,0:T(8,128)(2,1)S(1)} %select_convert_fusion.own_ref), channel_id=1, source_target_pairs={{0,64},{32,96},{64,0},{96,32},{1,65},{33,97},{65,1},{97,33},{2,66}... | collective-permute-start | bytes 1572872 | tf_op jit(solution)/shard_map/ppermute | solution.py:22
  16.7 5.9 %load.1.w_ref = bf16[2,512,8192]{2,1,0:T(8,128)(2,1)S(1)} custom-call(bf16[1,2,512,8192]{3,2,1,0:T(8,128)(2,1)} %w_hbm.2), custom_call_target="tpu_custom_call" | custom-call | bytes 33554432 | tf_op jit(solution)/shard_map/load/pallas_call | solution.py:130
  22.7 6.4 %collective-permute-done.2.far_ref = bf16[1024,256]{1,0:T(8,128)(2,1)S(1)} collective-permute-done((bf16[1024,256]{1,0:T(8,128)(2,1)S(1)}, bf16[1024,256]{1,0:T(8,128)(2,1)S(1)}, u32[]{:S(2)}, u32[]{:S(2)}) %collective-permute-start.2) | collective-permute-done | bytes 524320 | tf_op jit(solution)/shard_map/ppermute | solution.py:22
  29.1 1.9 %collective-permute-done.3.far_sib_ref = bf16[1024,256]{1,0:T(8,128)(2,1)S(1)} collective-permute-done((bf16[1024,256]{1,0:T(8,128)(2,1)S(1)}, bf16[1024,256]{1,0:T(8,128)(2,1)S(1)}, u32[]{:S(2)}, u32[]{:S(2)}) %collective-permute-start.3) | collective-permute-done | bytes 524320 | tf_op jit(solution)/shard_map/ppermute | solution.py:22
  31.3 1.4 send1.3
  32.8 2.1 %collective-permute-start.6 = (bf16[512,768]{1,0:T(8,128)(2,1)S(1)}, bf16[512,768]{1,0:T(8,128)(2,1)S(1)}, u32[]{:S(2)}, u32[]{:S(2)}) collective-permute-start(bf16[512,768]{1,0:T(8,128)(2,1)S(1)} %send1.3), channel_id=1, source_target_pairs={{0,1},{1,0},{2,3},{3,2},{4,5},{5,4},{6,7},{7,6},{8,9},{9,8},{10,11... | collective-permute-start | bytes 2359304 | tf_op jit(solution)/shard_map/ppermute | solution.py:22
  34.8 1.4 send0.2
  36.2 1.6 %collective-permute-start.4 = (bf16[512,768]{1,0:T(8,128)(2,1)S(1)}, bf16[512,768]{1,0:T(8,128)(2,1)S(1)}, u32[]{:S(2)}, u32[]{:S(2)}) collective-permute-start(bf16[512,768]{1,0:T(8,128)(2,1)S(1)} %send0.2), channel_id=1, source_target_pairs={{0,8},{1,9},{2,10},{3,11},{4,12},{5,13},{6,14},{7,15},{8,0},{9,1},... | collective-permute-start | bytes 2359304 | tf_op jit(solution)/shard_map/ppermute | solution.py:22
  37.8 1.4 send2.3
  39.3 1.7 %collective-permute-start.9 = (bf16[512,768]{1,0:T(8,128)(2,1)S(1)}, bf16[512,768]{1,0:T(8,128)(2,1)S(1)}, u32[]{:S(2)}, u32[]{:S(2)}) collective-permute-start(bf16[512,768]{1,0:T(8,128)(2,1)S(1)} %send2.3), channel_id=1, source_target_pairs={{0,4},{1,5},{2,6},{3,7},{4,0},{5,1},{6,2},{7,3},{8,12},{9,13},{10,... | collective-permute-start | bytes 2359304 | tf_op jit(solution)/shard_map/ppermute | solution.py:22
  40.9 1.4 send3.3
  42.3 2.2 %collective-permute-start.13 = (bf16[512,768]{1,0:T(8,128)(2,1)S(1)}, bf16[512,768]{1,0:T(8,128)(2,1)S(1)}, u32[]{:S(2)}, u32[]{:S(2)}) collective-permute-start(bf16[512,768]{1,0:T(8,128)(2,1)S(1)} %send3.3), channel_id=1, source_target_pairs={{0,24},{1,25},{2,26},{3,27},{4,28},{5,29},{6,30},{7,31},{8,16},{9,... | collective-permute-start | bytes 2359304 | tf_op jit(solution)/shard_map/ppermute | solution.py:22
  44.5 1.4 send4.3
  46.0 2.6 %collective-permute-start.18 = (bf16[512,768]{1,0:T(8,128)(2,1)S(1)}, bf16[512,768]{1,0:T(8,128)(2,1)S(1)}, u32[]{:S(2)}, u32[]{:S(2)}) collective-permute-start(bf16[512,768]{1,0:T(8,128)(2,1)S(1)} %send4.3), channel_id=1, source_target_pairs={{0,3},{1,2},{2,1},{3,0},{4,7},{5,6},{6,5},{7,4},{8,11},{9,10},{10,... | collective-permute-start | bytes 2359304 | tf_op jit(solution)/shard_map/ppermute | solution.py:22
  48.6 1.9 %send1.2 = bf16[512,896]{1,0:T(8,128)(2,1)S(1)} custom-call(bf16[1024,1024]{1,0:T(8,128)(2,1)S(1)} %assemble.1.codes_ref, bf16[2,512,8192]{2,1,0:T(8,128)(2,1)S(1)} %load.1.w_ref), custom_call_target="tpu_custom_call" | custom-call | flops 1000 | bytes 1000 | tf_op jit(solution)/shard_map/send1/pallas_call | solution.py:219
  50.4 2.2 %collective-permute-done.6.early_ref = bf16[512,768]{1,0:T(8,128)(2,1)S(1)} collective-permute-done((bf16[512,768]{1,0:T(8,128)(2,1)S(1)}, bf16[512,768]{1,0:T(8,128)(2,1)S(1)}, u32[]{:S(2)}, u32[]{:S(2)}) %collective-permute-start.6) | collective-permute-done | bytes 786464 | tf_op jit(solution)/shard_map/ppermute | solution.py:22
  52.7 1.7 %collective-permute-start.7 = (bf16[512,896]{1,0:T(8,128)(2,1)S(1)}, bf16[512,896]{1,0:T(8,128)(2,1)S(1)}, u32[]{:S(2)}, u32[]{:S(2)}) collective-permute-start(bf16[512,896]{1,0:T(8,128)(2,1)S(1)} %send1.2), channel_id=1, source_target_pairs={{0,1},{1,0},{2,3},{3,2},{4,5},{5,4},{6,7},{7,6},{8,9},{9,8},{10,11... | collective-permute-start | bytes 2752520 | tf_op jit(solution)/shard_map/ppermute | solution.py:22
  54.4 1.4 send0.3
  55.8 1.7 %collective-permute-start.5 = (bf16[512,768]{1,0:T(8,128)(2,1)S(1)}, bf16[512,768]{1,0:T(8,128)(2,1)S(1)}, u32[]{:S(2)}, u32[]{:S(2)}) collective-permute-start(bf16[512,768]{1,0:T(8,128)(2,1)S(1)} %send0.3), channel_id=1, source_target_pairs={{0,8},{1,9},{2,10},{3,11},{4,12},{5,13},{6,14},{7,15},{8,0},{9,1},... | collective-permute-start | bytes 2359304 | tf_op jit(solution)/shard_map/ppermute | solution.py:22
  57.6 1.9 %send2.2 = bf16[512,896]{1,0:T(8,128)(2,1)S(1)} custom-call(bf16[1024,1024]{1,0:T(8,128)(2,1)S(1)} %assemble.1.codes_ref, bf16[2,512,8192]{2,1,0:T(8,128)(2,1)S(1)} %load.1.w_ref), custom_call_target="tpu_custom_call" | custom-call | flops 1000 | bytes 1000 | tf_op jit(solution)/shard_map/send2/pallas_call | solution.py:219
  59.5 1.7 %collective-permute-start.10 = (bf16[512,896]{1,0:T(8,128)(2,1)S(1)}, bf16[512,896]{1,0:T(8,128)(2,1)S(1)}, u32[]{:S(2)}, u32[]{:S(2)}) collective-permute-start(bf16[512,896]{1,0:T(8,128)(2,1)S(1)} %send2.2), channel_id=1, source_target_pairs={{0,4},{1,5},{2,6},{3,7},{4,0},{5,1},{6,2},{7,3},{8,12},{9,13},{10,... | collective-permute-start | bytes 2752520 | tf_op jit(solution)/shard_map/ppermute | solution.py:22
  61.1 1.8 %send3.2 = bf16[512,896]{1,0:T(8,128)(2,1)S(1)} custom-call(bf16[1024,1024]{1,0:T(8,128)(2,1)S(1)} %assemble.1.codes_ref, bf16[2,512,8192]{2,1,0:T(8,128)(2,1)S(1)} %load.1.w_ref), custom_call_target="tpu_custom_call" | custom-call | flops 1000 | bytes 1000 | tf_op jit(solution)/shard_map/send3/pallas_call | solution.py:219
  63.0 2.2 %collective-permute-start.14 = (bf16[512,896]{1,0:T(8,128)(2,1)S(1)}, bf16[512,896]{1,0:T(8,128)(2,1)S(1)}, u32[]{:S(2)}, u32[]{:S(2)}) collective-permute-start(bf16[512,896]{1,0:T(8,128)(2,1)S(1)} %send3.2), channel_id=1, source_target_pairs={{0,24},{1,25},{2,26},{3,27},{4,28},{5,29},{6,30},{7,31},{8,16},{9,... | collective-permute-start | bytes 2752520 | tf_op jit(solution)/shard_map/ppermute | solution.py:22
  65.2 1.9 %send4.2 = bf16[512,896]{1,0:T(8,128)(2,1)S(1)} custom-call(bf16[1024,1024]{1,0:T(8,128)(2,1)S(1)} %assemble.1.codes_ref, bf16[2,512,8192]{2,1,0:T(8,128)(2,1)S(1)} %load.1.w_ref), custom_call_target="tpu_custom_call" | custom-call | flops 1000 | bytes 1000 | tf_op jit(solution)/shard_map/send4/pallas_call | solution.py:219
  67.0 2.6 %collective-permute-start.19 = (bf16[512,896]{1,0:T(8,128)(2,1)S(1)}, bf16[512,896]{1,0:T(8,128)(2,1)S(1)}, u32[]{:S(2)}, u32[]{:S(2)}) collective-permute-start(bf16[512,896]{1,0:T(8,128)(2,1)S(1)} %send4.2), channel_id=1, source_target_pairs={{0,3},{1,2},{2,1},{3,0},{4,7},{5,6},{6,5},{7,4},{8,11},{9,10},{10,... | collective-permute-start | bytes 2752520 | tf_op jit(solution)/shard_map/ppermute | solution.py:22
  69.6 5.0 %collective-permute-done.5.late_ref = bf16[512,768]{1,0:T(8,128)(2,1)S(1)} collective-permute-done((bf16[512,768]{1,0:T(8,128)(2,1)S(1)}, bf16[512,768]{1,0:T(8,128)(2,1)S(1)}, u32[]{:S(2)}, u32[]{:S(2)}) %collective-permute-start.5) | collective-permute-done | bytes 786464 | tf_op jit(solution)/shard_map/ppermute | solution.py:22
  74.6 2.8 %keep0.1 = (f32[256,1536]{1,0:T(8,128)S(1)}, bf16[256,1536]{1,0:T(8,128)(2,1)S(1)}) custom-call(bf16[1024,1024]{1,0:T(8,128)(2,1)S(1)} %assemble.1.codes_ref, bf16[2,512,8192]{2,1,0:T(8,128)(2,1)S(1)} %load.1.w_ref, bf16[512,768]{1,0:T(8,128)(2,1)S(1)} %collective-permute-done.4.early_ref, bf16[512,768]{1,0:T(8,128)(2,1)S(1)} %collective-permute-done.5.late_ref), custom_call_target="tpu_custom_call" | custom-call | flops 1000 | bytes 1000 | tf_op jit(solution)/shard_map/keep0/pallas_call | solution.py:236
  78.0 3.2 %keep1.1 = (f32[256,1664]{1,0:T(8,128)S(1)}, bf16[256,1664]{1,0:T(8,128)(2,1)S(1)}) custom-call(bf16[1024,1024]{1,0:T(8,128)(2,1)S(1)} %assemble.1.codes_ref, bf16[2,512,8192]{2,1,0:T(8,128)(2,1)S(1)} %load.1.w_ref, bf16[512,768]{1,0:T(8,128)(2,1)S(1)} %collective-permute-done.6.early_ref, bf16[512,896]{1,0:T(8,128)(2,1)S(1)} %collective-permute-done.7.late_ref), custom_call_target="tpu_custom_call" | custom-call | flops 1000 | bytes 1000 | tf_op jit(solution)/shard_map/keep1/pallas_call | solution.py:236
  81.3 1.6 %collective-permute-start.11 = (bf16[256,1664]{1,0:T(8,128)(2,1)S(1)}, bf16[256,1664]{1,0:T(8,128)(2,1)S(1)}, u32[]{:S(2)}, u32[]{:S(2)}) collective-permute-start(bf16[256,1664]{1,0:T(8,128)(2,1)S(1)} %get-tuple-element.57), channel_id=1, source_target_pairs={{0,4},{1,5},{2,6},{3,7},{4,0},{5,1},{6,2},{7,3},{8,12},{9,13},{10,... | collective-permute-start | bytes 2555912 | tf_op jit(solution)/shard_map/ppermute | solution.py:22
  82.8 3.2 %keep2.1 = (f32[256,1664]{1,0:T(8,128)S(1)}, bf16[256,1664]{1,0:T(8,128)(2,1)S(1)}) custom-call(bf16[1024,1024]{1,0:T(8,128)(2,1)S(1)} %assemble.1.codes_ref, bf16[2,512,8192]{2,1,0:T(8,128)(2,1)S(1)} %load.1.w_ref, bf16[512,768]{1,0:T(8,128)(2,1)S(1)} %collective-permute-done.9.early_ref, bf16[512,896]{1,0:T(8,128)(2,1)S(1)} %collective-permute-done.10.late_ref), custom_call_target="tpu_custom_call" | custom-call | flops 1000 | bytes 1000 | tf_op jit(solution)/shard_map/keep2/pallas_call | solution.py:236
  86.1 2.8 %collective-permute-start.15 = (bf16[256,1664]{1,0:T(8,128)(2,1)S(1)}, bf16[256,1664]{1,0:T(8,128)(2,1)S(1)}, u32[]{:S(2)}, u32[]{:S(2)}) collective-permute-start(bf16[256,1664]{1,0:T(8,128)(2,1)S(1)} %get-tuple-element.62), channel_id=1, source_target_pairs={{0,24},{1,25},{2,26},{3,27},{4,28},{5,29},{6,30},{7,31},{8,16},{9,... | collective-permute-start | bytes 2555912 | tf_op jit(solution)/shard_map/ppermute | solution.py:22
  88.9 3.2 %keep3.1 = (f32[256,1664]{1,0:T(8,128)S(1)}, bf16[256,1664]{1,0:T(8,128)(2,1)S(1)}) custom-call(bf16[1024,1024]{1,0:T(8,128)(2,1)S(1)} %assemble.1.codes_ref, bf16[2,512,8192]{2,1,0:T(8,128)(2,1)S(1)} %load.1.w_ref, bf16[512,768]{1,0:T(8,128)(2,1)S(1)} %collective-permute-done.13.early_ref, bf16[512,896]{1,0:T(8,128)(2,1)S(1)} %collective-permute-done.14.late_ref), custom_call_target="tpu_custom_call" | custom-call | flops 1000 | bytes 1000 | tf_op jit(solution)/shard_map/keep3/pallas_call | solution.py:236
  92.2 3.7 %collective-permute-start.20 = (bf16[256,1664]{1,0:T(8,128)(2,1)S(1)}, bf16[256,1664]{1,0:T(8,128)(2,1)S(1)}, u32[]{:S(2)}, u32[]{:S(2)}) collective-permute-start(bf16[256,1664]{1,0:T(8,128)(2,1)S(1)} %get-tuple-element.68), channel_id=1, source_target_pairs={{0,3},{1,2},{2,1},{3,0},{4,7},{5,6},{6,5},{7,4},{8,11},{9,10},{10,... | collective-permute-start | bytes 2555912 | tf_op jit(solution)/shard_map/ppermute | solution.py:22
  95.9 3.2 %keep4.1 = (f32[256,1664]{1,0:T(8,128)S(1)}, bf16[256,1664]{1,0:T(8,128)(2,1)S(1)}) custom-call(bf16[1024,1024]{1,0:T(8,128)(2,1)S(1)} %assemble.1.codes_ref, bf16[2,512,8192]{2,1,0:T(8,128)(2,1)S(1)} %load.1.w_ref, bf16[512,768]{1,0:T(8,128)(2,1)S(1)} %collective-permute-done.18.early_ref, bf16[512,896]{1,0:T(8,128)(2,1)S(1)} %collective-permute-done.19.late_ref), custom_call_target="tpu_custom_call" | custom-call | flops 1000 | bytes 1000 | tf_op jit(solution)/shard_map/keep4/pallas_call | solution.py:236
  100.4 1.5 %collective-permute-start.12 = (bf16[128,1536]{1,0:T(8,128)(2,1)S(1)}, bf16[128,1536]{1,0:T(8,128)(2,1)S(1)}, u32[]{:S(2)}, u32[]{:S(2)}) collective-permute-start(bf16[128,1536]{1,0:T(8,128)(2,1)S(1)} %slice.219), channel_id=1, source_target_pairs={{0,4},{1,5},{2,6},{3,7},{4,0},{5,1},{6,2},{7,3},{8,12},{9,13},{10,... | collective-permute-start | bytes 1179656 | tf_op jit(solution)/shard_map/ppermute | solution.py:22
  102.2 3.8 %collective-permute-done.15 = bf16[256,1664]{1,0:T(8,128)(2,1)S(1)} collective-permute-done((bf16[256,1664]{1,0:T(8,128)(2,1)S(1)}, bf16[256,1664]{1,0:T(8,128)(2,1)S(1)}, u32[]{:S(2)}, u32[]{:S(2)}) %collective-permute-start.15) | collective-permute-done | bytes 852000 | tf_op jit(solution)/shard_map/ppermute | solution.py:22
  106.0 2.8 %collective-permute-start.16 = (bf16[128,1664]{1,0:T(8,128)(2,1)S(1)}, bf16[128,1664]{1,0:T(8,128)(2,1)S(1)}, u32[]{:S(2)}, u32[]{:S(2)}) collective-permute-start(bf16[128,1664]{1,0:T(8,128)(2,1)S(1)} %slice.218), channel_id=1, source_target_pairs={{0,24},{1,25},{2,26},{3,27},{4,28},{5,29},{6,30},{7,31},{8,16},{9,... | collective-permute-start | bytes 1277960 | tf_op jit(solution)/shard_map/ppermute | solution.py:22
  109.0 3.3 %collective-permute-done.20 = bf16[256,1664]{1,0:T(8,128)(2,1)S(1)} collective-permute-done((bf16[256,1664]{1,0:T(8,128)(2,1)S(1)}, bf16[256,1664]{1,0:T(8,128)(2,1)S(1)}, u32[]{:S(2)}, u32[]{:S(2)}) %collective-permute-start.20) | collective-permute-done | bytes 852000 | tf_op jit(solution)/shard_map/ppermute | solution.py:22
  112.3 3.0 %collective-permute-start.21 = (bf16[128,1664]{1,0:T(8,128)(2,1)S(1)}, bf16[128,1664]{1,0:T(8,128)(2,1)S(1)}, u32[]{:S(2)}, u32[]{:S(2)}) collective-permute-start(bf16[128,1664]{1,0:T(8,128)(2,1)S(1)} %slice.217), channel_id=1, source_target_pairs={{0,3},{1,2},{2,1},{3,0},{4,7},{5,6},{6,5},{7,4},{8,11},{9,10},{10,... | collective-permute-start | bytes 1277960 | tf_op jit(solution)/shard_map/ppermute | solution.py:22
  115.5 2.8 %collective-permute-done.24 = bf16[256,1664]{1,0:T(8,128)(2,1)S(1)} collective-permute-done((bf16[256,1664]{1,0:T(8,128)(2,1)S(1)}, bf16[256,1664]{1,0:T(8,128)(2,1)S(1)}, u32[]{:S(2)}, u32[]{:S(2)}) %collective-permute-start.24) | collective-permute-done | bytes 852000 | tf_op jit(solution)/shard_map/ppermute | solution.py:22
  119.0 1.4 %collective-permute-start.17 = (bf16[64,1536]{1,0:T(8,128)(2,1)S(1)}, bf16[64,1536]{1,0:T(8,128)(2,1)S(1)}, u32[]{:S(2)}, u32[]{:S(2)}) collective-permute-start(bf16[64,1536]{1,0:T(8,128)(2,1)S(1)} %slice.224), channel_id=1, source_target_pairs={{0,24},{1,25},{2,26},{3,27},{4,28},{5,29},{6,30},{7,31},{8,16},{9,... | collective-permute-start | bytes 589832 | tf_op jit(solution)/shard_map/ppermute | solution.py:22
  120.6 1.7 %collective-permute-done.21 = bf16[128,1664]{1,0:T(8,128)(2,1)S(1)} collective-permute-done((bf16[128,1664]{1,0:T(8,128)(2,1)S(1)}, bf16[128,1664]{1,0:T(8,128)(2,1)S(1)}, u32[]{:S(2)}, u32[]{:S(2)}) %collective-permute-start.21) | collective-permute-done | bytes 426016 | tf_op jit(solution)/shard_map/ppermute | solution.py:22
  122.3 3.2 %collective-permute-start.22 = (bf16[64,1664]{1,0:T(8,128)(2,1)S(1)}, bf16[64,1664]{1,0:T(8,128)(2,1)S(1)}, u32[]{:S(2)}, u32[]{:S(2)}) collective-permute-start(bf16[64,1664]{1,0:T(8,128)(2,1)S(1)} %slice.223), channel_id=1, source_target_pairs={{0,3},{1,2},{2,1},{3,0},{4,7},{5,6},{6,5},{7,4},{8,11},{9,10},{10,... | collective-permute-start | bytes 638984 | tf_op jit(solution)/shard_map/ppermute | solution.py:22
  125.6 2.9 %collective-permute-done.25 = bf16[128,1664]{1,0:T(8,128)(2,1)S(1)} collective-permute-done((bf16[128,1664]{1,0:T(8,128)(2,1)S(1)}, bf16[128,1664]{1,0:T(8,128)(2,1)S(1)}, u32[]{:S(2)}, u32[]{:S(2)}) %collective-permute-start.25) | collective-permute-done | bytes 426016 | tf_op jit(solution)/shard_map/ppermute | solution.py:22
  130.4 3.2 %collective-permute-start.23 = (bf16[32,1536]{1,0:T(8,128)(2,1)S(1)}, bf16[32,1536]{1,0:T(8,128)(2,1)S(1)}, u32[]{:S(2)}, u32[]{:S(2)}) collective-permute-start(bf16[32,1536]{1,0:T(8,128)(2,1)S(1)} %slice.229), channel_id=1, source_target_pairs={{0,3},{1,2},{2,1},{3,0},{4,7},{5,6},{6,5},{7,4},{8,11},{9,10},{10,... | collective-permute-start | bytes 294920 | tf_op jit(solution)/shard_map/ppermute | solution.py:22
  137.5 2.1 %collective-permute-done.27 = bf16[32,1664]{1,0:T(8,128)(2,1)S(1)} collective-permute-done((bf16[32,1664]{1,0:T(8,128)(2,1)S(1)}, bf16[32,1664]{1,0:T(8,128)(2,1)S(1)}, u32[]{:S(2)}, u32[]{:S(2)}) %collective-permute-start.27) | collective-permute-done | bytes 106528 | tf_op jit(solution)/shard_map/ppermute | solution.py:22
  140.5 1.8 %collective-permute-done.33 = bf16[32,1664]{1,0:T(8,128)(2,1)S(1)} collective-permute-done((bf16[32,1664]{1,0:T(8,128)(2,1)S(1)}, bf16[32,1664]{1,0:T(8,128)(2,1)S(1)}, u32[]{:S(2)}, u32[]{:S(2)}) %collective-permute-start.33) | collective-permute-done | bytes 106528 | tf_op jit(solution)/shard_map/ppermute | solution.py:22
  (98 shorter events, 15.0 us)
Async XLA Ops:
  0.0 11.3 %copy-start = (s32[2,1024]{1,0:T(2,128)S(1)}, s32[2,1024]{1,0:T(2,128)}, u32[]{:S(2)}) copy-start(s32[2,1024]{1,0:T(2,128)} %param.17) | copy-start | bytes 24580
  0.0 11.2 %copy-start.6 = (s32[32]{0:T(128)S(1)}, s32[32]{0:T(128)}, u32[]{:S(2)}) copy-start(s32[32]{0:T(128)} %constant.82.clone) | copy-start | bytes 388
  0.0 11.3 %copy-start.4 = (s32[2,1024]{1,0:T(2,128)S(1)}, s32[2,1024]{1,0:T(2,128)}, u32[]{:S(2)}) copy-start(s32[2,1024]{1,0:T(2,128)} %param.19) | copy-start | bytes 24580
  0.0 11.3 %copy-start.5 = (s32[2,1024]{1,0:T(2,128)S(1)}, s32[2,1024]{1,0:T(2,128)}, u32[]{:S(2)}) copy-start(s32[2,1024]{1,0:T(2,128)} %param.18) | copy-start | bytes 24580
  0.0 12.7 %copy-start.3 = (f32[16]{0:T(128)S(1)}, f32[16]{0:T(128)}, u32[]{:S(2)}) copy-start(f32[16]{0:T(128)} %param.20) | copy-start | bytes 196
  9.5 3.3 %collective-permute-start = (f32[1024,256]{1,0:T(8,128)S(1)}, f32[1024,256]{1,0:T(8,128)S(1)}, u32[]{:S(2)}, u32[]{:S(2)}) collective-permute-start(f32[1024,256]{1,0:T(8,128)S(1)} %get-tuple-element.46), channel_id=1, source_target_pairs={{0,32},{32,0},{64,96},{96,64},{1,33},{33,1},{65,97},{97,65},{2,34}... | collective-permute-start | bytes 3145736 | tf_op jit(solution)/shard_map/ppermute | solution.py:22
  13.2 15.9 %collective-permute-start.2 = (bf16[1024,256]{1,0:T(8,128)(2,1)S(1)}, bf16[1024,256]{1,0:T(8,128)(2,1)S(1)}, u32[]{:S(2)}, u32[]{:S(2)}) collective-permute-start(bf16[1024,256]{1,0:T(8,128)(2,1)S(1)} %select_convert_fusion.own_ref), channel_id=1, source_target_pairs={{0,64},{32,96},{64,0},{96,32},{1,65},{33,97},{65,1},{97,33},{2,66}... | collective-permute-start | bytes 1572872 | tf_op jit(solution)/shard_map/ppermute | solution.py:22
  16.6 12.6 %collective-permute-start.1 = (bf16[1024,256]{1,0:T(8,128)(2,1)S(1)}, bf16[1024,256]{1,0:T(8,128)(2,1)S(1)}, u32[]{:S(2)}, u32[]{:S(2)}) collective-permute-start(bf16[1024,256]{1,0:T(8,128)(2,1)S(1)} %select_convert_fusion.own_ref), channel_id=1, source_target_pairs={{0,32},{32,0},{64,96},{96,64},{1,33},{33,1},{65,97},{97,65},{2,34}... | collective-permute-start | bytes 1572872 | tf_op jit(solution)/shard_map/ppermute | solution.py:22
  29.1 1.9 %collective-permute-start.3 = (bf16[1024,256]{1,0:T(8,128)(2,1)S(1)}, bf16[1024,256]{1,0:T(8,128)(2,1)S(1)}, u32[]{:S(2)}, u32[]{:S(2)}) collective-permute-start(bf16[1024,256]{1,0:T(8,128)(2,1)S(1)} %collective-permute-done.2.far_ref), channel_id=1, source_target_pairs={{0,32},{32,0},{64,96},{96,64},{1,33},{33,1},{65,97},{97,65},{2,34}... | collective-permute-start | bytes 1572872 | tf_op jit(solution)/shard_map/ppermute | solution.py:22
  32.8 19.9 %collective-permute-start.6 = (bf16[512,768]{1,0:T(8,128)(2,1)S(1)}, bf16[512,768]{1,0:T(8,128)(2,1)S(1)}, u32[]{:S(2)}, u32[]{:S(2)}) collective-permute-start(bf16[512,768]{1,0:T(8,128)(2,1)S(1)} %send1.3), channel_id=1, source_target_pairs={{0,1},{1,0},{2,3},{3,2},{4,5},{5,4},{6,7},{7,6},{8,9},{9,8},{10,11... | collective-permute-start | bytes 2359304 | tf_op jit(solution)/shard_map/ppermute | solution.py:22
  36.2 19.6 %collective-permute-start.4 = (bf16[512,768]{1,0:T(8,128)(2,1)S(1)}, bf16[512,768]{1,0:T(8,128)(2,1)S(1)}, u32[]{:S(2)}, u32[]{:S(2)}) collective-permute-start(bf16[512,768]{1,0:T(8,128)(2,1)S(1)} %send0.2), channel_id=1, source_target_pairs={{0,8},{1,9},{2,10},{3,11},{4,12},{5,13},{6,14},{7,15},{8,0},{9,1},... | collective-permute-start | bytes 2359304 | tf_op jit(solution)/shard_map/ppermute | solution.py:22
  39.3 20.2 %collective-permute-start.9 = (bf16[512,768]{1,0:T(8,128)(2,1)S(1)}, bf16[512,768]{1,0:T(8,128)(2,1)S(1)}, u32[]{:S(2)}, u32[]{:S(2)}) collective-permute-start(bf16[512,768]{1,0:T(8,128)(2,1)S(1)} %send2.3), channel_id=1, source_target_pairs={{0,4},{1,5},{2,6},{3,7},{4,0},{5,1},{6,2},{7,3},{8,12},{9,13},{10,... | collective-permute-start | bytes 2359304 | tf_op jit(solution)/shard_map/ppermute | solution.py:22
  42.3 20.6 %collective-permute-start.13 = (bf16[512,768]{1,0:T(8,128)(2,1)S(1)}, bf16[512,768]{1,0:T(8,128)(2,1)S(1)}, u32[]{:S(2)}, u32[]{:S(2)}) collective-permute-start(bf16[512,768]{1,0:T(8,128)(2,1)S(1)} %send3.3), channel_id=1, source_target_pairs={{0,24},{1,25},{2,26},{3,27},{4,28},{5,29},{6,30},{7,31},{8,16},{9,... | collective-permute-start | bytes 2359304 | tf_op jit(solution)/shard_map/ppermute | solution.py:22
  46.0 21.1 %collective-permute-start.18 = (bf16[512,768]{1,0:T(8,128)(2,1)S(1)}, bf16[512,768]{1,0:T(8,128)(2,1)S(1)}, u32[]{:S(2)}, u32[]{:S(2)}) collective-permute-start(bf16[512,768]{1,0:T(8,128)(2,1)S(1)} %send4.3), channel_id=1, source_target_pairs={{0,3},{1,2},{2,1},{3,0},{4,7},{5,6},{6,5},{7,4},{8,11},{9,10},{10,... | collective-permute-start | bytes 2359304 | tf_op jit(solution)/shard_map/ppermute | solution.py:22
  52.7 24.7 %collective-permute-start.7 = (bf16[512,896]{1,0:T(8,128)(2,1)S(1)}, bf16[512,896]{1,0:T(8,128)(2,1)S(1)}, u32[]{:S(2)}, u32[]{:S(2)}) collective-permute-start(bf16[512,896]{1,0:T(8,128)(2,1)S(1)} %send1.2), channel_id=1, source_target_pairs={{0,1},{1,0},{2,3},{3,2},{4,5},{5,4},{6,7},{7,6},{8,9},{9,8},{10,11... | collective-permute-start | bytes 2752520 | tf_op jit(solution)/shard_map/ppermute | solution.py:22
  55.8 18.7 %collective-permute-start.5 = (bf16[512,768]{1,0:T(8,128)(2,1)S(1)}, bf16[512,768]{1,0:T(8,128)(2,1)S(1)}, u32[]{:S(2)}, u32[]{:S(2)}) collective-permute-start(bf16[512,768]{1,0:T(8,128)(2,1)S(1)} %send0.3), channel_id=1, source_target_pairs={{0,8},{1,9},{2,10},{3,11},{4,12},{5,13},{6,14},{7,15},{8,0},{9,1},... | collective-permute-start | bytes 2359304 | tf_op jit(solution)/shard_map/ppermute | solution.py:22
  59.5 21.8 %collective-permute-start.10 = (bf16[512,896]{1,0:T(8,128)(2,1)S(1)}, bf16[512,896]{1,0:T(8,128)(2,1)S(1)}, u32[]{:S(2)}, u32[]{:S(2)}) collective-permute-start(bf16[512,896]{1,0:T(8,128)(2,1)S(1)} %send2.2), channel_id=1, source_target_pairs={{0,4},{1,5},{2,6},{3,7},{4,0},{5,1},{6,2},{7,3},{8,12},{9,13},{10,... | collective-permute-start | bytes 2752520 | tf_op jit(solution)/shard_map/ppermute | solution.py:22
  63.0 23.1 %collective-permute-start.14 = (bf16[512,896]{1,0:T(8,128)(2,1)S(1)}, bf16[512,896]{1,0:T(8,128)(2,1)S(1)}, u32[]{:S(2)}, u32[]{:S(2)}) collective-permute-start(bf16[512,896]{1,0:T(8,128)(2,1)S(1)} %send3.2), channel_id=1, source_target_pairs={{0,24},{1,25},{2,26},{3,27},{4,28},{5,29},{6,30},{7,31},{8,16},{9,... | collective-permute-start | bytes 2752520 | tf_op jit(solution)/shard_map/ppermute | solution.py:22
  67.0 25.1 %collective-permute-start.19 = (bf16[512,896]{1,0:T(8,128)(2,1)S(1)}, bf16[512,896]{1,0:T(8,128)(2,1)S(1)}, u32[]{:S(2)}, u32[]{:S(2)}) collective-permute-start(bf16[512,896]{1,0:T(8,128)(2,1)S(1)} %send4.2), channel_id=1, source_target_pairs={{0,3},{1,2},{2,1},{3,0},{4,7},{5,6},{6,5},{7,4},{8,11},{9,10},{10,... | collective-permute-start | bytes 2752520 | tf_op jit(solution)/shard_map/ppermute | solution.py:22
  77.4 22.1 %collective-permute-start.8 = (bf16[256,1536]{1,0:T(8,128)(2,1)S(1)}, bf16[256,1536]{1,0:T(8,128)(2,1)S(1)}, u32[]{:S(2)}, u32[]{:S(2)}) collective-permute-start(bf16[256,1536]{1,0:T(8,128)(2,1)S(1)} %get-tuple-element.54), channel_id=1, source_target_pairs={{0,1},{1,0},{2,3},{3,2},{4,5},{5,4},{6,7},{7,6},{8,9},{9,8},{10,11... | collective-permute-start | bytes 2359304 | tf_op jit(solution)/shard_map/ppermute | solution.py:22
  81.3 19.2 %collective-permute-start.11 = (bf16[256,1664]{1,0:T(8,128)(2,1)S(1)}, bf16[256,1664]{1,0:T(8,128)(2,1)S(1)}, u32[]{:S(2)}, u32[]{:S(2)}) collective-permute-start(bf16[256,1664]{1,0:T(8,128)(2,1)S(1)} %get-tuple-element.57), channel_id=1, source_target_pairs={{0,4},{1,5},{2,6},{3,7},{4,0},{5,1},{6,2},{7,3},{8,12},{9,13},{10,... | collective-permute-start | bytes 2555912 | tf_op jit(solution)/shard_map/ppermute | solution.py:22
  86.1 19.9 %collective-permute-start.15 = (bf16[256,1664]{1,0:T(8,128)(2,1)S(1)}, bf16[256,1664]{1,0:T(8,128)(2,1)S(1)}, u32[]{:S(2)}, u32[]{:S(2)}) collective-permute-start(bf16[256,1664]{1,0:T(8,128)(2,1)S(1)} %get-tuple-element.62), channel_id=1, source_target_pairs={{0,24},{1,25},{2,26},{3,27},{4,28},{5,29},{6,30},{7,31},{8,16},{9,... | collective-permute-start | bytes 2555912 | tf_op jit(solution)/shard_map/ppermute | solution.py:22
  92.2 20.1 %collective-permute-start.20 = (bf16[256,1664]{1,0:T(8,128)(2,1)S(1)}, bf16[256,1664]{1,0:T(8,128)(2,1)S(1)}, u32[]{:S(2)}, u32[]{:S(2)}) collective-permute-start(bf16[256,1664]{1,0:T(8,128)(2,1)S(1)} %get-tuple-element.68), channel_id=1, source_target_pairs={{0,3},{1,2},{2,1},{3,0},{4,7},{5,6},{6,5},{7,4},{8,11},{9,10},{10,... | collective-permute-start | bytes 2555912 | tf_op jit(solution)/shard_map/ppermute | solution.py:22
  99.1 19.2 %collective-permute-start.24 = (bf16[256,1664]{1,0:T(8,128)(2,1)S(1)}, bf16[256,1664]{1,0:T(8,128)(2,1)S(1)}, u32[]{:S(2)}, u32[]{:S(2)}) collective-permute-start(bf16[256,1664]{1,0:T(8,128)(2,1)S(1)} %get-tuple-element.74), channel_id=1, source_target_pairs={{0,8},{1,9},{2,10},{3,11},{4,12},{5,13},{6,14},{7,15},{8,0},{9,1},... | collective-permute-start | bytes 2555912 | tf_op jit(solution)/shard_map/ppermute | solution.py:22
  100.4 18.4 %collective-permute-start.12 = (bf16[128,1536]{1,0:T(8,128)(2,1)S(1)}, bf16[128,1536]{1,0:T(8,128)(2,1)S(1)}, u32[]{:S(2)}, u32[]{:S(2)}) collective-permute-start(bf16[128,1536]{1,0:T(8,128)(2,1)S(1)} %slice.219), channel_id=1, source_target_pairs={{0,4},{1,5},{2,6},{3,7},{4,0},{5,1},{6,2},{7,3},{8,12},{9,13},{10,... | collective-permute-start | bytes 1179656 | tf_op jit(solution)/shard_map/ppermute | solution.py:22
  106.0 13.1 %collective-permute-start.16 = (bf16[128,1664]{1,0:T(8,128)(2,1)S(1)}, bf16[128,1664]{1,0:T(8,128)(2,1)S(1)}, u32[]{:S(2)}, u32[]{:S(2)}) collective-permute-start(bf16[128,1664]{1,0:T(8,128)(2,1)S(1)} %slice.218), channel_id=1, source_target_pairs={{0,24},{1,25},{2,26},{3,27},{4,28},{5,29},{6,30},{7,31},{8,16},{9,... | collective-permute-start | bytes 1277960 | tf_op jit(solution)/shard_map/ppermute | solution.py:22
  112.3 10.0 %collective-permute-start.21 = (bf16[128,1664]{1,0:T(8,128)(2,1)S(1)}, bf16[128,1664]{1,0:T(8,128)(2,1)S(1)}, u32[]{:S(2)}, u32[]{:S(2)}) collective-permute-start(bf16[128,1664]{1,0:T(8,128)(2,1)S(1)} %slice.217), channel_id=1, source_target_pairs={{0,3},{1,2},{2,1},{3,0},{4,7},{5,6},{6,5},{7,4},{8,11},{9,10},{10,... | collective-permute-start | bytes 1277960 | tf_op jit(solution)/shard_map/ppermute | solution.py:22
  118.3 10.2 %collective-permute-start.25 = (bf16[128,1664]{1,0:T(8,128)(2,1)S(1)}, bf16[128,1664]{1,0:T(8,128)(2,1)S(1)}, u32[]{:S(2)}, u32[]{:S(2)}) collective-permute-start(bf16[128,1664]{1,0:T(8,128)(2,1)S(1)} %slice.216), channel_id=1, source_target_pairs={{0,8},{1,9},{2,10},{3,11},{4,12},{5,13},{6,14},{7,15},{8,0},{9,1},... | collective-permute-start | bytes 1277960 | tf_op jit(solution)/shard_map/ppermute | solution.py:22
  118.8 10.5 %collective-permute-start.28 = (bf16[128,1664]{1,0:T(8,128)(2,1)S(1)}, bf16[128,1664]{1,0:T(8,128)(2,1)S(1)}, u32[]{:S(2)}, u32[]{:S(2)}) collective-permute-start(bf16[128,1664]{1,0:T(8,128)(2,1)S(1)} %slice.215), channel_id=1, source_target_pairs={{0,1},{1,0},{2,3},{3,2},{4,5},{5,4},{6,7},{7,6},{8,9},{9,8},{10,11... | collective-permute-start | bytes 1277960 | tf_op jit(solution)/shard_map/ppermute | solution.py:22
  119.0 10.9 %collective-permute-start.17 = (bf16[64,1536]{1,0:T(8,128)(2,1)S(1)}, bf16[64,1536]{1,0:T(8,128)(2,1)S(1)}, u32[]{:S(2)}, u32[]{:S(2)}) collective-permute-start(bf16[64,1536]{1,0:T(8,128)(2,1)S(1)} %slice.224), channel_id=1, source_target_pairs={{0,24},{1,25},{2,26},{3,27},{4,28},{5,29},{6,30},{7,31},{8,16},{9,... | collective-permute-start | bytes 589832 | tf_op jit(solution)/shard_map/ppermute | solution.py:22
  122.3 8.1 %collective-permute-start.22 = (bf16[64,1664]{1,0:T(8,128)(2,1)S(1)}, bf16[64,1664]{1,0:T(8,128)(2,1)S(1)}, u32[]{:S(2)}, u32[]{:S(2)}) collective-permute-start(bf16[64,1664]{1,0:T(8,128)(2,1)S(1)} %slice.223), channel_id=1, source_target_pairs={{0,3},{1,2},{2,1},{3,0},{4,7},{5,6},{6,5},{7,4},{8,11},{9,10},{10,... | collective-permute-start | bytes 638984 | tf_op jit(solution)/shard_map/ppermute | solution.py:22
  128.5 6.3 %collective-permute-start.26 = (bf16[64,1664]{1,0:T(8,128)(2,1)S(1)}, bf16[64,1664]{1,0:T(8,128)(2,1)S(1)}, u32[]{:S(2)}, u32[]{:S(2)}) collective-permute-start(bf16[64,1664]{1,0:T(8,128)(2,1)S(1)} %slice.222), channel_id=1, source_target_pairs={{0,8},{1,9},{2,10},{3,11},{4,12},{5,13},{6,14},{7,15},{8,0},{9,1},... | collective-permute-start | bytes 638984 | tf_op jit(solution)/shard_map/ppermute | solution.py:22
  129.3 6.0 %collective-permute-start.29 = (bf16[64,1664]{1,0:T(8,128)(2,1)S(1)}, bf16[64,1664]{1,0:T(8,128)(2,1)S(1)}, u32[]{:S(2)}, u32[]{:S(2)}) collective-permute-start(bf16[64,1664]{1,0:T(8,128)(2,1)S(1)} %slice.221), channel_id=1, source_target_pairs={{0,1},{1,0},{2,3},{3,2},{4,5},{5,4},{6,7},{7,6},{8,9},{9,8},{10,11... | collective-permute-start | bytes 638984 | tf_op jit(solution)/shard_map/ppermute | solution.py:22
  129.4 6.3 %collective-permute-start.31 = (bf16[64,1664]{1,0:T(8,128)(2,1)S(1)}, bf16[64,1664]{1,0:T(8,128)(2,1)S(1)}, u32[]{:S(2)}, u32[]{:S(2)}) collective-permute-start(bf16[64,1664]{1,0:T(8,128)(2,1)S(1)} %slice.220), channel_id=1, source_target_pairs={{0,4},{1,5},{2,6},{3,7},{4,0},{5,1},{6,2},{7,3},{8,12},{9,13},{10,... | collective-permute-start | bytes 638984 | tf_op jit(solution)/shard_map/ppermute | solution.py:22
  130.4 7.1 %collective-permute-start.23 = (bf16[32,1536]{1,0:T(8,128)(2,1)S(1)}, bf16[32,1536]{1,0:T(8,128)(2,1)S(1)}, u32[]{:S(2)}, u32[]{:S(2)}) collective-permute-start(bf16[32,1536]{1,0:T(8,128)(2,1)S(1)} %slice.229), channel_id=1, source_target_pairs={{0,3},{1,2},{2,1},{3,0},{4,7},{5,6},{6,5},{7,4},{8,11},{9,10},{10,... | collective-permute-start | bytes 294920 | tf_op jit(solution)/shard_map/ppermute | solution.py:22
  134.9 4.7 %collective-permute-start.27 = (bf16[32,1664]{1,0:T(8,128)(2,1)S(1)}, bf16[32,1664]{1,0:T(8,128)(2,1)S(1)}, u32[]{:S(2)}, u32[]{:S(2)}) collective-permute-start(bf16[32,1664]{1,0:T(8,128)(2,1)S(1)} %slice.228), channel_id=1, source_target_pairs={{0,8},{1,9},{2,10},{3,11},{4,12},{5,13},{6,14},{7,15},{8,0},{9,1},... | collective-permute-start | bytes 319496 | tf_op jit(solution)/shard_map/ppermute | solution.py:22
  135.3 4.7 %collective-permute-start.30 = (bf16[32,1664]{1,0:T(8,128)(2,1)S(1)}, bf16[32,1664]{1,0:T(8,128)(2,1)S(1)}, u32[]{:S(2)}, u32[]{:S(2)}) collective-permute-start(bf16[32,1664]{1,0:T(8,128)(2,1)S(1)} %slice.227), channel_id=1, source_target_pairs={{0,1},{1,0},{2,3},{3,2},{4,5},{5,4},{6,7},{7,6},{8,9},{9,8},{10,11... | collective-permute-start | bytes 319496 | tf_op jit(solution)/shard_map/ppermute | solution.py:22
  135.7 6.7 %copy-start.2 = (f32[1,8192]{1,0:T(1,128)S(1)}, f32[1,8192]{1,0:T(1,128)}, u32[]{:S(2)}) copy-start(f32[1,8192]{1,0:T(1,128)} %param.16) | copy-start | bytes 98308
  135.7 4.8 %collective-permute-start.32 = (bf16[32,1664]{1,0:T(8,128)(2,1)S(1)}, bf16[32,1664]{1,0:T(8,128)(2,1)S(1)}, u32[]{:S(2)}, u32[]{:S(2)}) collective-permute-start(bf16[32,1664]{1,0:T(8,128)(2,1)S(1)} %slice.226), channel_id=1, source_target_pairs={{0,4},{1,5},{2,6},{3,7},{4,0},{5,1},{6,2},{7,3},{8,12},{9,13},{10,... | collective-permute-start | bytes 319496 | tf_op jit(solution)/shard_map/ppermute | solution.py:22
  136.3 6.0 %collective-permute-start.33 = (bf16[32,1664]{1,0:T(8,128)(2,1)S(1)}, bf16[32,1664]{1,0:T(8,128)(2,1)S(1)}, u32[]{:S(2)}, u32[]{:S(2)}) collective-permute-start(bf16[32,1664]{1,0:T(8,128)(2,1)S(1)} %slice.225), channel_id=1, source_target_pairs={{0,24},{1,25},{2,26},{3,27},{4,28},{5,29},{6,30},{7,31},{8,16},{9,... | collective-permute-start | bytes 319496 | tf_op jit(solution)/shard_map/ppermute | solution.py:22
  139.6 3.6 %copy-start.1 = (s32[2,1024]{1,0:T(2,128)S(1)}, s32[2,1024]{1,0:T(2,128)}, u32[]{:S(2)}) copy-start(s32[2,1024]{1,0:T(2,128)} %param.17) | copy-start | bytes 24580

commit v4 on v3

--- a/solution.py
+++ b/solution.py
@@ -16,6 +16,7 @@
 VMEM = pl.BlockSpec(memory_space=pltpu.VMEM)
 HBM = pl.BlockSpec(memory_space=pltpu.HBM)
 MIB = 1 << 20
+COPIES = 4
 
 
 def xor_swap(value, axis, mask):
@@ -110,60 +111,34 @@
     )(x, w)
 
 
-def load_kernel(w_hbm, out, sem, *, pieces):
-    step = w_hbm.shape[2] // pieces
-    copies = [
-        pltpu.make_async_copy(
-            w_hbm.at[0, s, pl.ds(q * step, step)], out.at[s, pl.ds(q * step, step)], sem.at[s * pieces + q]
-        )
-        for s in range(2)
-        for q in range(pieces)
-    ]
-    for c in copies:
-        c.start()
-    for c in copies:
-        c.wait()
-
-
-def load(w):
-    _, sources, depth, wide = w.shape
+def copy_weights(dec_hbm, source, out_ref, sem, start):
+    step = out_ref.shape[0] // COPIES
+    for q in range(COPIES):
+        at = pl.ds(q * step, step)
+        c = pltpu.make_async_copy(dec_hbm.at[0, source, at], out_ref.at[at], sem.at[q])
+        if start:
+            c.start()
+        else:
+            c.wait()
+
+
+def join_kernel(mine_ref, sib_ref, out_ref):
+    core = lax.axis_index("layer") % 2
+    hw = mine_ref.shape[1]
+    out_ref[:, pl.ds(pl.multiple_of(core * hw, hw), hw)] = mine_ref[...]
+    out_ref[:, pl.ds(pl.multiple_of((1 - core) * hw, hw), hw)] = sib_ref[...]
+
+
+def join(mine, sib):
+    n, hw = mine.shape
     return pl.pallas_call(
-        functools.partial(load_kernel, pieces=4),
-        out_shape=pltpu.VMEM((sources, depth, wide), BF16),
-        in_specs=[HBM],
-        out_specs=VMEM,
-        scratch_shapes=[pltpu.SemaphoreType.DMA((8,))],
-        compiler_params=pltpu.CompilerParams(vmem_limit_bytes=40 * MIB),
-        cost_estimate=pl.CostEstimate(
-            flops=0, bytes_accessed=4 * sources * depth * wide, transcendentals=0
-        ),
-        name="load",
-    )(w)
-
-
-def assemble_kernel(own_ref, own_sib_ref, far_ref, far_sib_ref, out_ref):
-    group = lax.axis_index("layer")
-    source, core = group // 2, group % 2
-    hw = own_ref.shape[1]
-    for ref, s, c in (
-        (own_ref, source, core),
-        (own_sib_ref, source, 1 - core),
-        (far_ref, 1 - source, core),
-        (far_sib_ref, 1 - source, 1 - core),
-    ):
-        out_ref[:, pl.ds(pl.multiple_of((s * 2 + c) * hw, hw), hw)] = ref[...]
-
-
-def assemble(*pieces):
-    n, hw = pieces[0].shape
-    return pl.pallas_call(
-        assemble_kernel,
-        out_shape=pltpu.VMEM((n, 4 * hw), BF16),
-        in_specs=[VMEM] * 4,
+        join_kernel,
+        out_shape=pltpu.VMEM((n, 2 * hw), BF16),
+        in_specs=[VMEM] * 2,
         out_specs=VMEM,
         compiler_params=pltpu.CompilerParams(vmem_limit_bytes=8 * MIB),
-        name="assemble",
-    )(*pieces)
+        name="join",
+    )(mine, sib)
 
 
 def gather_rows(codes_ref, lhs, blocks):
@@ -184,68 +159,135 @@
 
 
 def product(lhs, w_ref, at, n):
-    w = w_ref[:, :, pl.ds(pl.multiple_of(at, LANES), n)]
-    return jnp.dot(lhs[...], w.reshape(lhs.shape[1], n), preferred_element_type=F32)
-
-
-def send_kernel(codes_ref, w_ref, send_ref, lhs, *, blocks, at):
+    w = w_ref[:, pl.ds(pl.multiple_of(at, LANES), n)]
+    return jnp.dot(lhs[...], w, preferred_element_type=F32)
+
+
+def own_kernel(mine_ref, sib_ref, dec_hbm, *refs, spans):
+    codes_ref, w_ref, far_ref, *accs = refs[: 3 + len(spans)]
+    lhs, w_sem, far_sem = refs[3 + len(spans) :]
+    source = lax.axis_index("layer") // 2
+    copy_weights(dec_hbm, source, w_ref, w_sem, True)
+    copy_weights(dec_hbm, 1 - source, far_ref, far_sem, True)
+    join_kernel(mine_ref, sib_ref, codes_ref)
+    copy_weights(dec_hbm, source, w_ref, w_sem, False)
+    done = None
+    for (part, at, wide), acc in zip(spans, accs):
+        if part != done:
+            gather_rows(codes_ref, lhs, send_blocks(part))
+            done = part
+
+        def body(c, n):
+            acc[:, pl.ds(c, n)] = product(lhs, w_ref, at + c, n)
+
+        over_tiles(0, wide, body)
+    copy_weights(dec_hbm, 1 - source, far_ref, far_sem, False)
+
+
+def own_part(mine, sib, dec, spans):
+    tokens, hw = mine.shape
+    _, _, depth, wide = dec.shape
+    n = tokens // 2
+    codes, w_own, w_far, *accs = pl.pallas_call(
+        functools.partial(own_kernel, spans=spans),
+        out_shape=[pltpu.VMEM((tokens, 2 * hw), BF16)]
+        + [pltpu.VMEM((depth, wide), BF16)] * 2
+        + [pltpu.VMEM((n, span[2]), F32) for span in spans],
+        in_specs=[VMEM, VMEM, HBM],
+        out_specs=[VMEM] * (3 + len(spans)),
+        scratch_shapes=[pltpu.VMEM((n, depth), BF16)] + [pltpu.SemaphoreType.DMA((COPIES,))] * 2,
+        compiler_params=pltpu.CompilerParams(vmem_limit_bytes=14 * MIB),
+        cost_estimate=pl.CostEstimate(
+            flops=2 * n * depth * wide, bytes_accessed=4 * depth * wide, transcendentals=0
+        ),
+        name="own",
+    )(mine, sib, dec)
+    return codes, w_own, w_far, accs
+
+
+def send_blocks(part):
+    blocks = part_blocks(part)
+    return blocks[len(blocks) // 2 :]
+
+
+def keep_blocks(part):
+    blocks = part_blocks(part)
+    return blocks[: len(blocks) // 2]
+
+
+def send_kernel(codes_ref, w_ref, acc_ref, send_ref, lhs, *, blocks, at):
     gather_rows(codes_ref, lhs, blocks)
 
     def body(c, n):
-        send_ref[:, pl.ds(c, n)] = product(lhs, w_ref, at + c, n).astype(BF16)
+        cols = pl.ds(c, n)
+        send_ref[:, cols] = (acc_ref[:, cols] + product(lhs, w_ref, at + c, n)).astype(BF16)
 
     over_tiles(0, send_ref.shape[1], body)
 
 
-def keep_kernel(codes_ref, w_ref, early_ref, late_ref, keep_ref, send_ref, lhs, *, blocks, at):
-    gather_rows(codes_ref, lhs, blocks)
-    m = lhs.shape[0] // 2
-    split = early_ref.shape[1]
-    for got_ref, begin, end in ((early_ref, 0, split), (late_ref, split, send_ref.shape[1])):
-
-        def body(c, n):
-            got = got_ref[:, pl.ds(pl.multiple_of(c - begin, LANES), n)]
-            total = product(lhs, w_ref, at + c, n) + got.astype(F32)
-            keep_ref[:, pl.ds(c, n)] = total[:m]
-            send_ref[:, pl.ds(c, n)] = total[m:].astype(BF16)
-
-        over_tiles(begin, end, body)
-
-
-def decode_send(codes, w, first, at, wide):
-    tokens, depth = codes.shape
-    blocks = part_blocks(first)
+def decode_send(codes, w, acc, part, at):
+    n, wide = acc.shape
+    return pl.pallas_call(
+        functools.partial(send_kernel, blocks=send_blocks(part), at=at),
+        out_shape=jax.ShapeDtypeStruct((n, wide), BF16),
+        in_specs=[VMEM] * 3,
+        out_specs=VMEM,
+        scratch_shapes=[pltpu.VMEM((n, codes.shape[1]), BF16)],
+        compiler_params=pltpu.CompilerParams(vmem_limit_bytes=6 * MIB),
+        cost_estimate=pl.CostEstimate(flops=1000, bytes_accessed=1000, transcendentals=0),
+        name=f"send{part}",
+    )(codes, w, acc)
+
+
+def keep_kernel(own_ref, far_ref, w_own_ref, w_far_ref, keep_ref, own_lhs, far_lhs, *, blocks, at):
+    gather_rows(own_ref, own_lhs, blocks)
+    gather_rows(far_ref, far_lhs, blocks)
+
+    def body(c, n):
+        keep_ref[:, pl.ds(c, n)] = product(own_lhs, w_own_ref, at + c, n) + product(
+            far_lhs, w_far_ref, at + c, n
+        )
+
+    over_tiles(0, keep_ref.shape[1], body)
+
+
+def decode_keep(own, far, w_own, w_far, part, at, wide):
+    tokens, depth = own.shape
     n = tokens // 2
     return pl.pallas_call(
-        functools.partial(send_kernel, blocks=blocks[len(blocks) // 2 :], at=at),
-        out_shape=jax.ShapeDtypeStruct((n, wide), BF16),
-        in_specs=[VMEM, VMEM],
+        functools.partial(keep_kernel, blocks=keep_blocks(part), at=at),
+        out_shape=jax.ShapeDtypeStruct((n, wide), F32),
+        in_specs=[VMEM] * 4,
         out_specs=VMEM,
-        scratch_shapes=[pltpu.VMEM((n, depth), BF16)],
+        scratch_shapes=[pltpu.VMEM((n, depth), BF16)] * 2,
         compiler_params=pltpu.CompilerParams(vmem_limit_bytes=8 * MIB),
         cost_estimate=pl.CostEstimate(flops=1000, bytes_accessed=1000, transcendentals=0),
-        name=f"send{first}",
-    )(codes, w)
-
-
-def decode_keep(codes, w, early, late, first, at):
-    tokens, depth = codes.shape
-    blocks = part_blocks(first)
-    n = tokens // 2
-    wide = early.shape[1] + late.shape[1]
+        name=f"keep{part}",
+    )(own, far, w_own, w_far)
+
+
+def merge_kernel(keep_ref, early_ref, late_ref, new_ref, send_ref):
+    m = new_ref.shape[0]
+    split = early_ref.shape[1]
+    for got, cols in ((early_ref, pl.ds(0, split)), (late_ref, pl.ds(split, late_ref.shape[1]))):
+        new_ref[:, cols] = keep_ref[:m, cols] + got[:m, :].astype(F32)
+        send_ref[:, cols] = (keep_ref[m:, cols] + got[m:, :].astype(F32)).astype(BF16)
+
+
+def merge(keep, early, late):
+    n, wide = keep.shape
     return pl.pallas_call(
-        functools.partial(keep_kernel, blocks=blocks[: len(blocks) // 2], at=at),
+        merge_kernel,
         out_shape=(
             jax.ShapeDtypeStruct((n // 2, wide), F32),
             jax.ShapeDtypeStruct((n // 2, wide), BF16),
         ),
-        in_specs=[VMEM] * 4,
-        out_specs=[VMEM, VMEM],
-        scratch_shapes=[pltpu.VMEM((n, depth), BF16)],
+        in_specs=[VMEM] * 3,
+        out_specs=[VMEM] * 2,
         compiler_params=pltpu.CompilerParams(vmem_limit_bytes=8 * MIB),
         cost_estimate=pl.CostEstimate(flops=1000, bytes_accessed=1000, transcendentals=0),
-        name=f"keep{first}",
-    )(codes, w, early, late)
+        name="merge",
+    )(keep, early, late)
 
 
 def shards(
@@ -296,11 +338,16 @@
 
     own_sib = xor_swap(own, "layer", 1)
 
-    weights = load(lax.optimization_barrier((dec_weight, own))[0])
-    far, weights = lax.optimization_barrier((xor_swap(own, "layer", 2), weights))
-    codes = assemble(own, own_sib, far, xor_swap(far, "layer", 1))
-
     starts = [sum(PARTS[:p]) * LANES for p in range(STEPS)]
+    spans = []
+    for late in (False, True):
+        for p in range(STEPS):
+            wide = (PARTS[p] - EARLY[p] if late else EARLY[p]) * LANES
+            spans.append((p, starts[p] + (EARLY[p] * LANES if late else 0), wide))
+    own_codes, w_own, w_far, accs = own_part(own, own_sib, dec_weight, spans)
+    far, w_far = lax.optimization_barrier((xor_swap(own, "layer", 2), w_far))
+    far_codes = join(far, xor_swap(far, "layer", 1))
+
     last = [None] * STEPS
 
     def exchange(data, link):
@@ -309,16 +356,19 @@
         last[link] = xor_swap(data, "lat", LINKS[link])
         return last[link]
 
-    got = [[] for _ in PARTS]
-    for late in (False, True):
-        for p in range(STEPS):
-            at, wide = starts[p], EARLY[p] * LANES
-            if late:
-                at, wide = at + wide, PARTS[p] * LANES - wide
-            got[p].append(exchange(decode_send(codes, weights, p, at, wide), p))
+    got = [
+        exchange(decode_send(far_codes, w_far, acc, p, at), p)
+        for (p, at, _), acc in zip(spans, accs)
+    ]
+    keeps = [
+        decode_keep(own_codes, far_codes, w_own, w_far, p, starts[p], PARTS[p] * LANES)
+        for p in range(STEPS)
+    ]
+    first, *keeps = lax.optimization_barrier((got[STEPS], *keeps))
+    got[STEPS] = first
     kept, out = {}, {}
     for p in range(STEPS):
-        kept[p], out[p] = decode_keep(codes, weights, *got[p], p, starts[p])
+        kept[p], out[p] = merge(keeps[p], got[p], got[STEPS + p])
     for i in range(1, STEPS):
         for p in range(STEPS):
             total = kept[p] + exchange(out[p], (p + i) % STEPS).astype(F32)

time: 143 us -> 142 us (level)
  starting transfers between devices: 51.1 us -> 41 us
  Pallas kernels: 47.4 us -> 53.3 us
  local copies, waits for them, and re-layouts: 2.06 us -> 5.36 us
    ppermute x34, starting transfers between devices: 51.1 us -> 41 us  [xor_swap(): lax.ppermute(value, axis, [(i, i ^ mask) for i in range(lax.axis_size(axi...]
    pallas_call x17 -> x22, Pallas kernels: 37.9 us -> 43.8 us  [the longest x1 15.9 us: own_part(): pl.pallas_call(functools.partial(own_kernel, spans=spans), out_shape=[plt...]
    unnamed x14 -> x20, local copies, waits for them, and re-layouts: 0.03 us -> 3.33 us
  transfers between devices with their start and end apart: 34 -> 34, of which waited for: 18 -> 12; matrix products, arithmetic and copies ran while one was open for 4% -> 4% of each run, Pallas kernels for 25% -> 30%
where the time goes in v4:
time: 142 us
  Pallas kernels  53.3 us (38%)
  starting transfers between devices  41 us (29%)
  waiting for transfers between devices  37.6 us (26%)
  local copies, waits for them, and re-layouts  5.36 us (4%)
  other arithmetic  2.9 us (2%)
    ppermute x34, starting transfers between devices, xor_swap(): lax.ppermute(value, axis, [(i, i ^ mask) for i in range(lax.axis_size(axi...  41 us
    ppermute x34, waiting for transfers between devices, xor_swap(): lax.ppermute(value, axis, [(i, i ^ mask) for i in range(lax.axis_size(axi...  37.6 us
    pallas_call x1, Pallas kernels, own_part(): pl.pallas_call(functools.partial(own_kernel, spans=spans), out_shape=[plt...  15.9 us
    pallas_call x5, Pallas kernels, decode_keep(): pl.pallas_call(functools.partial(keep_kernel, blocks=keep_blocks(part), a...  15.6 us
    pallas_call x10, Pallas kernels, decode_send(): pl.pallas_call(functools.partial(send_kernel, blocks=send_blocks(part), a...  10.7 us
    pallas_call x1, Pallas kernels, encode(): pl.pallas_call(functools.partial(encode_kernel, masks=masks, rows=rows, c...  9.49 us
    unnamed x20, local copies, waits for them, and re-layouts  3.33 us
  transfers between devices with their start and end apart: 34, of which 12 were waited for; matrix products, arithmetic and copies ran while one was open for 4% of the time, Pallas kernels for 30%

profile of v4, /device:TPU:0, one launch (start us, length us, event | category | flops | bytes accessed | tf_op | source)
XLA Modules:
  0.0 142.1 jit_solution(3467849578182811995)
XLA Ops:
  0.0 9.5 %encode.1 = (f32[1024,256]{1,0:T(8,128)S(1)}, f32[1024,256]{1,0:T(8,128)S(1)}) custom-call(bf16[1,1024,4096]{2,1,0:T(8,128)(2,1)} %x_hbm.1, bf16[1,4096,512]{2,1,0:T(8,128)(2,1)} %w_hbm.1), custom_call_target="tpu_custom_call" | custom-call | flops 4294967296 | bytes 14680064 | tf_op jit(solution)/shard_map/encode/pallas_call | solution.py:93
  11.4 1.3 fusion
  13.7 3.3 %collective-permute-start.1 = (bf16[1024,256]{1,0:T(8,128)(2,1)S(1)}, bf16[1024,256]{1,0:T(8,128)(2,1)S(1)}, u32[]{:S(2)}, u32[]{:S(2)}) collective-permute-start(bf16[1024,256]{1,0:T(8,128)(2,1)S(1)} %select_convert_fusion.mine_ref), channel_id=1, source_target_pairs={{0,64},{32,96},{64,0},{96,32},{1,65},{33,97},{65,1},{97,33},{2,66}... | collective-permute-start | bytes 1572872 | tf_op jit(solution)/shard_map/ppermute | solution.py:23
  17.0 15.9 %own.1 = (bf16[1024,512]{1,0:T(8,128)(2,1)S(1)}, bf16[512,8192]{1,0:T(8,128)(2,1)S(1)}, bf16[512,8192]{1,0:T(8,128)(2,1)S(1)}, f32[512,768]{1,0:T(8,128)S(1)}, f...) custom-call(bf16[1024,256]{1,0:T(8,128)(2,1)S(1)} %select_convert_fu, ...), custom_call_target="tpu_custom_call" | custom-call | flops 4294967296 | bytes 16777216 | tf_op jit(solution)/shard_map/own/pallas_call | solution.py:191
  33.0 3.3 %copy-done.2 = bf16[512,8192]{1,0:T(8,128)(2,1)} copy-done((bf16[512,8192]{1,0:T(8,128)(2,1)}, bf16[512,8192]{1,0:T(8,128)(2,1)S(1)}, u32[]{:S(2)}) %copy-start.2) | copy-done | bytes 8388632
  36.3 1.9 %collective-permute-done.3.sib_ref = bf16[1024,256]{1,0:T(8,128)(2,1)S(1)} collective-permute-done((bf16[1024,256]{1,0:T(8,128)(2,1)S(1)}, bf16[1024,256]{1,0:T(8,128)(2,1)S(1)}, u32[]{:S(2)}, u32[]{:S(2)}) %collective-permute-start.3) | collective-permute-done | bytes 524320 | tf_op jit(solution)/shard_map/ppermute | solution.py:23
  38.3 1.0 send1.3
  39.3 2.0 %collective-permute-start.6 = (bf16[512,768]{1,0:T(8,128)(2,1)S(1)}, bf16[512,768]{1,0:T(8,128)(2,1)S(1)}, u32[]{:S(2)}, u32[]{:S(2)}) collective-permute-start(bf16[512,768]{1,0:T(8,128)(2,1)S(1)} %send1.3), channel_id=1, source_target_pairs={{0,1},{1,0},{2,3},{3,2},{4,5},{5,4},{6,7},{7,6},{8,9},{9,8},{10,11... | collective-permute-start | bytes 2359304 | tf_op jit(solution)/shard_map/ppermute | solution.py:23
  42.2 1.6 %collective-permute-start.4 = (bf16[512,768]{1,0:T(8,128)(2,1)S(1)}, bf16[512,768]{1,0:T(8,128)(2,1)S(1)}, u32[]{:S(2)}, u32[]{:S(2)}) collective-permute-start(bf16[512,768]{1,0:T(8,128)(2,1)S(1)} %send0.3), channel_id=1, source_target_pairs={{0,8},{1,9},{2,10},{3,11},{4,12},{5,13},{6,14},{7,15},{8,0},{9,1},... | collective-permute-start | bytes 2359304 | tf_op jit(solution)/shard_map/ppermute | solution.py:23
  43.8 1.0 send2.3
  45.7 1.0 send3.3
  46.7 2.2 %collective-permute-start.13 = (bf16[512,768]{1,0:T(8,128)(2,1)S(1)}, bf16[512,768]{1,0:T(8,128)(2,1)S(1)}, u32[]{:S(2)}, u32[]{:S(2)}) collective-permute-start(bf16[512,768]{1,0:T(8,128)(2,1)S(1)} %send3.3), channel_id=1, source_target_pairs={{0,24},{1,25},{2,26},{3,27},{4,28},{5,29},{6,30},{7,31},{8,16},{9,... | collective-permute-start | bytes 2359304 | tf_op jit(solution)/shard_map/ppermute | solution.py:23
  48.9 1.0 send4.3
  49.8 2.6 %collective-permute-start.18 = (bf16[512,768]{1,0:T(8,128)(2,1)S(1)}, bf16[512,768]{1,0:T(8,128)(2,1)S(1)}, u32[]{:S(2)}, u32[]{:S(2)}) collective-permute-start(bf16[512,768]{1,0:T(8,128)(2,1)S(1)} %send4.3), channel_id=1, source_target_pairs={{0,3},{1,2},{2,1},{3,0},{4,7},{5,6},{6,5},{7,4},{8,11},{9,10},{10,... | collective-permute-start | bytes 2359304 | tf_op jit(solution)/shard_map/ppermute | solution.py:23
  52.5 1.2 send1.2
  53.7 5.4 %collective-permute-done.6.early_ref = bf16[512,768]{1,0:T(8,128)(2,1)S(1)} collective-permute-done((bf16[512,768]{1,0:T(8,128)(2,1)S(1)}, bf16[512,768]{1,0:T(8,128)(2,1)S(1)}, u32[]{:S(2)}, u32[]{:S(2)}) %collective-permute-start.6) | collective-permute-done | bytes 786464 | tf_op jit(solution)/shard_map/ppermute | solution.py:23
  59.1 1.7 %collective-permute-start.7 = (bf16[512,896]{1,0:T(8,128)(2,1)S(1)}, bf16[512,896]{1,0:T(8,128)(2,1)S(1)}, u32[]{:S(2)}, u32[]{:S(2)}) collective-permute-start(bf16[512,896]{1,0:T(8,128)(2,1)S(1)} %send1.2), channel_id=1, source_target_pairs={{0,1},{1,0},{2,3},{3,2},{4,5},{5,4},{6,7},{7,6},{8,9},{9,8},{10,11... | collective-permute-start | bytes 2752520 | tf_op jit(solution)/shard_map/ppermute | solution.py:23
  60.9 1.0 send0.2
  61.9 1.6 %collective-permute-start.5 = (bf16[512,768]{1,0:T(8,128)(2,1)S(1)}, bf16[512,768]{1,0:T(8,128)(2,1)S(1)}, u32[]{:S(2)}, u32[]{:S(2)}) collective-permute-start(bf16[512,768]{1,0:T(8,128)(2,1)S(1)} %send0.2), channel_id=1, source_target_pairs={{0,8},{1,9},{2,10},{3,11},{4,12},{5,13},{6,14},{7,15},{8,0},{9,1},... | collective-permute-start | bytes 2359304 | tf_op jit(solution)/shard_map/ppermute | solution.py:23
  63.4 1.2 send2.2
  65.5 1.2 send3.2
  66.7 2.1 %collective-permute-start.14 = (bf16[512,896]{1,0:T(8,128)(2,1)S(1)}, bf16[512,896]{1,0:T(8,128)(2,1)S(1)}, u32[]{:S(2)}, u32[]{:S(2)}) collective-permute-start(bf16[512,896]{1,0:T(8,128)(2,1)S(1)} %send3.2), channel_id=1, source_target_pairs={{0,24},{1,25},{2,26},{3,27},{4,28},{5,29},{6,30},{7,31},{8,16},{9,... | collective-permute-start | bytes 2752520 | tf_op jit(solution)/shard_map/ppermute | solution.py:23
  68.9 1.2 send4.2
  70.1 2.6 %collective-permute-start.19 = (bf16[512,896]{1,0:T(8,128)(2,1)S(1)}, bf16[512,896]{1,0:T(8,128)(2,1)S(1)}, u32[]{:S(2)}, u32[]{:S(2)}) collective-permute-start(bf16[512,896]{1,0:T(8,128)(2,1)S(1)} %send4.2), channel_id=1, source_target_pairs={{0,3},{1,2},{2,1},{3,0},{4,7},{5,6},{6,5},{7,4},{8,11},{9,10},{10,... | collective-permute-start | bytes 2752520 | tf_op jit(solution)/shard_map/ppermute | solution.py:23
  72.8 2.8 %keep0.1.keep_ref = f32[512,1536]{1,0:T(8,128)S(1)} custom-call(bf16[1024,512]{1,0:T(8,128)(2,1)S(1)} %get-tuple-element.71.own_ref, bf16[1024,512]{1,0:T(8,128)(2,1)S(1)} %join.1.codes_ref.far_ref, bf16[512,8192]{1,0:T(8,128)(2,1)S(1)} %bitcast.30, bf16[512,8192]{1,0:T(8,128)(2,1)S(1)} %get-tuple-element.67.w_ref.w_far_ref), custom_call_target="tpu_custom_call" | custom-call | flops 1000 | bytes 1000 | tf_op jit(solution)/shard_map/keep0/pallas_call | solution.py:257
  75.5 3.2 %keep4.1.keep_ref = f32[512,1664]{1,0:T(8,128)S(1)} custom-call(bf16[1024,512]{1,0:T(8,128)(2,1)S(1)} %get-tuple-element.71.own_ref, bf16[1024,512]{1,0:T(8,128)(2,1)S(1)} %join.1.codes_ref.far_ref, bf16[512,8192]{1,0:T(8,128)(2,1)S(1)} %bitcast.30, bf16[512,8192]{1,0:T(8,128)(2,1)S(1)} %get-tuple-element.67.w_ref.w_far_ref), custom_call_target="tpu_custom_call" | custom-call | flops 1000 | bytes 1000 | tf_op jit(solution)/shard_map/keep4/pallas_call | solution.py:257
  78.8 3.2 %keep3.1.keep_ref = f32[512,1664]{1,0:T(8,128)S(1)} custom-call(bf16[1024,512]{1,0:T(8,128)(2,1)S(1)} %get-tuple-element.71.own_ref, bf16[1024,512]{1,0:T(8,128)(2,1)S(1)} %join.1.codes_ref.far_ref, bf16[512,8192]{1,0:T(8,128)(2,1)S(1)} %bitcast.30, bf16[512,8192]{1,0:T(8,128)(2,1)S(1)} %get-tuple-element.67.w_ref.w_far_ref), custom_call_target="tpu_custom_call" | custom-call | flops 1000 | bytes 1000 | tf_op jit(solution)/shard_map/keep3/pallas_call | solution.py:257
  82.0 3.2 %keep2.1.keep_ref = f32[512,1664]{1,0:T(8,128)S(1)} custom-call(bf16[1024,512]{1,0:T(8,128)(2,1)S(1)} %get-tuple-element.71.own_ref, bf16[1024,512]{1,0:T(8,128)(2,1)S(1)} %join.1.codes_ref.far_ref, bf16[512,8192]{1,0:T(8,128)(2,1)S(1)} %bitcast.30, bf16[512,8192]{1,0:T(8,128)(2,1)S(1)} %get-tuple-element.67.w_ref.w_far_ref), custom_call_target="tpu_custom_call" | custom-call | flops 1000 | bytes 1000 | tf_op jit(solution)/shard_map/keep2/pallas_call | solution.py:257
  85.2 3.2 %keep1.1.keep_ref = f32[512,1664]{1,0:T(8,128)S(1)} custom-call(bf16[1024,512]{1,0:T(8,128)(2,1)S(1)} %get-tuple-element.71.own_ref, bf16[1024,512]{1,0:T(8,128)(2,1)S(1)} %join.1.codes_ref.far_ref, bf16[512,8192]{1,0:T(8,128)(2,1)S(1)} %bitcast.30, bf16[512,8192]{1,0:T(8,128)(2,1)S(1)} %get-tuple-element.67.w_ref.w_far_ref), custom_call_target="tpu_custom_call" | custom-call | flops 1000 | bytes 1000 | tf_op jit(solution)/shard_map/keep1/pallas_call | solution.py:257
  88.7 1.1 collective-permute-start.8
  90.1 1.4 %collective-permute-start.11 = (bf16[256,1664]{1,0:T(8,128)(2,1)S(1)}, bf16[256,1664]{1,0:T(8,128)(2,1)S(1)}, u32[]{:S(2)}, u32[]{:S(2)}) collective-permute-start(bf16[256,1664]{1,0:T(8,128)(2,1)S(1)} %get-tuple-element.86), channel_id=1, source_target_pairs={{0,4},{1,5},{2,6},{3,7},{4,0},{5,1},{6,2},{7,3},{8,12},{9,13},{10,... | collective-permute-start | bytes 2555912 | tf_op jit(solution)/shard_map/ppermute | solution.py:23
  91.8 1.2 collective-permute-start.15
  93.3 1.5 %collective-permute-start.20 = (bf16[256,1664]{1,0:T(8,128)(2,1)S(1)}, bf16[256,1664]{1,0:T(8,128)(2,1)S(1)}, u32[]{:S(2)}, u32[]{:S(2)}) collective-permute-start(bf16[256,1664]{1,0:T(8,128)(2,1)S(1)} %get-tuple-element.103), channel_id=1, source_target_pairs={{0,3},{1,2},{2,1},{3,0},{4,7},{5,6},{6,5},{7,4},{8,11},{9,10},{10,... | collective-permute-start | bytes 2555912 | tf_op jit(solution)/shard_map/ppermute | solution.py:23
  95.4 10.8 %collective-permute-done.8 = bf16[256,1536]{1,0:T(8,128)(2,1)S(1)} collective-permute-done((bf16[256,1536]{1,0:T(8,128)(2,1)S(1)}, bf16[256,1536]{1,0:T(8,128)(2,1)S(1)}, u32[]{:S(2)}, u32[]{:S(2)}) %collective-permute-start.8) | collective-permute-done | bytes 786464 | tf_op jit(solution)/shard_map/ppermute | solution.py:23
  106.4 2.9 %collective-permute-done.11 = bf16[256,1664]{1,0:T(8,128)(2,1)S(1)} collective-permute-done((bf16[256,1664]{1,0:T(8,128)(2,1)S(1)}, bf16[256,1664]{1,0:T(8,128)(2,1)S(1)}, u32[]{:S(2)}, u32[]{:S(2)}) %collective-permute-start.11) | collective-permute-done | bytes 852000 | tf_op jit(solution)/shard_map/ppermute | solution.py:23
  109.3 1.4 collective-permute-start.12
  111.6 1.5 %collective-permute-start.16 = (bf16[128,1664]{1,0:T(8,128)(2,1)S(1)}, bf16[128,1664]{1,0:T(8,128)(2,1)S(1)}, u32[]{:S(2)}, u32[]{:S(2)}) collective-permute-start(bf16[128,1664]{1,0:T(8,128)(2,1)S(1)} %slice.218), channel_id=1, source_target_pairs={{0,24},{1,25},{2,26},{3,27},{4,28},{5,29},{6,30},{7,31},{8,16},{9,... | collective-permute-start | bytes 1277960 | tf_op jit(solution)/shard_map/ppermute | solution.py:23
  113.2 1.8 %collective-permute-start.21 = (bf16[128,1664]{1,0:T(8,128)(2,1)S(1)}, bf16[128,1664]{1,0:T(8,128)(2,1)S(1)}, u32[]{:S(2)}, u32[]{:S(2)}) collective-permute-start(bf16[128,1664]{1,0:T(8,128)(2,1)S(1)} %slice.217), channel_id=1, source_target_pairs={{0,3},{1,2},{2,1},{3,0},{4,7},{5,6},{6,5},{7,4},{8,11},{9,10},{10,... | collective-permute-start | bytes 1277960 | tf_op jit(solution)/shard_map/ppermute | solution.py:23
  115.4 1.7 %collective-permute-done.12 = bf16[128,1536]{1,0:T(8,128)(2,1)S(1)} collective-permute-done((bf16[128,1536]{1,0:T(8,128)(2,1)S(1)}, bf16[128,1536]{1,0:T(8,128)(2,1)S(1)}, u32[]{:S(2)}, u32[]{:S(2)}) %collective-permute-start.12) | collective-permute-done | bytes 393248 | tf_op jit(solution)/shard_map/ppermute | solution.py:23
  117.2 4.9 %collective-permute-done.16 = bf16[128,1664]{1,0:T(8,128)(2,1)S(1)} collective-permute-done((bf16[128,1664]{1,0:T(8,128)(2,1)S(1)}, bf16[128,1664]{1,0:T(8,128)(2,1)S(1)}, u32[]{:S(2)}, u32[]{:S(2)}) %collective-permute-start.16) | collective-permute-done | bytes 426016 | tf_op jit(solution)/shard_map/ppermute | solution.py:23
  122.1 1.2 collective-permute-start.17
  123.5 1.5 %collective-permute-start.22 = (bf16[64,1664]{1,0:T(8,128)(2,1)S(1)}, bf16[64,1664]{1,0:T(8,128)(2,1)S(1)}, u32[]{:S(2)}, u32[]{:S(2)}) collective-permute-start(bf16[64,1664]{1,0:T(8,128)(2,1)S(1)} %slice.223), channel_id=1, source_target_pairs={{0,3},{1,2},{2,1},{3,0},{4,7},{5,6},{6,5},{7,4},{8,11},{9,10},{10,... | collective-permute-start | bytes 638984 | tf_op jit(solution)/shard_map/ppermute | solution.py:23
  126.9 2.1 %collective-permute-done.17 = bf16[64,1536]{1,0:T(8,128)(2,1)S(1)} collective-permute-done((bf16[64,1536]{1,0:T(8,128)(2,1)S(1)}, bf16[64,1536]{1,0:T(8,128)(2,1)S(1)}, u32[]{:S(2)}, u32[]{:S(2)}) %collective-permute-start.17) | collective-permute-done | bytes 196640 | tf_op jit(solution)/shard_map/ppermute | solution.py:23
  129.0 2.6 %collective-permute-done.22 = bf16[64,1664]{1,0:T(8,128)(2,1)S(1)} collective-permute-done((bf16[64,1664]{1,0:T(8,128)(2,1)S(1)}, bf16[64,1664]{1,0:T(8,128)(2,1)S(1)}, u32[]{:S(2)}, u32[]{:S(2)}) %collective-permute-start.22) | collective-permute-done | bytes 213024 | tf_op jit(solution)/shard_map/ppermute | solution.py:23
  131.6 1.5 %collective-permute-start.23 = (bf16[32,1536]{1,0:T(8,128)(2,1)S(1)}, bf16[32,1536]{1,0:T(8,128)(2,1)S(1)}, u32[]{:S(2)}, u32[]{:S(2)}) collective-permute-start(bf16[32,1536]{1,0:T(8,128)(2,1)S(1)} %slice.229), channel_id=1, source_target_pairs={{0,3},{1,2},{2,1},{3,0},{4,7},{5,6},{6,5},{7,4},{8,11},{9,10},{10,... | collective-permute-start | bytes 294920 | tf_op jit(solution)/shard_map/ppermute | solution.py:23
  133.1 2.2 %collective-permute-start.33 = (bf16[32,1664]{1,0:T(8,128)(2,1)S(1)}, bf16[32,1664]{1,0:T(8,128)(2,1)S(1)}, u32[]{:S(2)}, u32[]{:S(2)}) collective-permute-start(bf16[32,1664]{1,0:T(8,128)(2,1)S(1)} %slice.225), channel_id=1, source_target_pairs={{0,24},{1,25},{2,26},{3,27},{4,28},{5,29},{6,30},{7,31},{8,16},{9,... | collective-permute-start | bytes 319496 | tf_op jit(solution)/shard_map/ppermute | solution.py:23
  136.4 1.0 collective-permute-done.23
  137.4 3.7 %collective-permute-done.27 = bf16[32,1664]{1,0:T(8,128)(2,1)S(1)} collective-permute-done((bf16[32,1664]{1,0:T(8,128)(2,1)S(1)}, bf16[32,1664]{1,0:T(8,128)(2,1)S(1)}, u32[]{:S(2)}, u32[]{:S(2)}) %collective-permute-start.27) | collective-permute-done | bytes 106528 | tf_op jit(solution)/shard_map/ppermute | solution.py:23
  (110 shorter events, 13.3 us)
Async XLA Ops:
  0.0 11.3 %copy-start = (s32[2,1024]{1,0:T(2,128)S(1)}, s32[2,1024]{1,0:T(2,128)}, u32[]{:S(2)}) copy-start(s32[2,1024]{1,0:T(2,128)} %param.17) | copy-start | bytes 24580
  0.0 11.2 %copy-start.7 = (s32[32]{0:T(128)S(1)}, s32[32]{0:T(128)}, u32[]{:S(2)}) copy-start(s32[32]{0:T(128)} %constant.82.clone) | copy-start | bytes 388
  0.0 11.3 %copy-start.5 = (s32[2,1024]{1,0:T(2,128)S(1)}, s32[2,1024]{1,0:T(2,128)}, u32[]{:S(2)}) copy-start(s32[2,1024]{1,0:T(2,128)} %param.19) | copy-start | bytes 24580
  0.0 11.3 %copy-start.6 = (s32[2,1024]{1,0:T(2,128)S(1)}, s32[2,1024]{1,0:T(2,128)}, u32[]{:S(2)}) copy-start(s32[2,1024]{1,0:T(2,128)} %param.18) | copy-start | bytes 24580
  0.0 12.7 %copy-start.4 = (f32[16]{0:T(128)S(1)}, f32[16]{0:T(128)}, u32[]{:S(2)}) copy-start(f32[16]{0:T(128)} %param.20) | copy-start | bytes 196
  9.5 3.3 %collective-permute-start = (f32[1024,256]{1,0:T(8,128)S(1)}, f32[1024,256]{1,0:T(8,128)S(1)}, u32[]{:S(2)}, u32[]{:S(2)}) collective-permute-start(f32[1024,256]{1,0:T(8,128)S(1)} %get-tuple-element.64), channel_id=1, source_target_pairs={{0,32},{32,0},{64,96},{96,64},{1,33},{33,1},{65,97},{97,65},{2,34}... | collective-permute-start | bytes 3145736 | tf_op jit(solution)/shard_map/ppermute | solution.py:23
  13.2 3.8 %collective-permute-start.2 = (bf16[1024,256]{1,0:T(8,128)(2,1)S(1)}, bf16[1024,256]{1,0:T(8,128)(2,1)S(1)}, u32[]{:S(2)}, u32[]{:S(2)}) collective-permute-start(bf16[1024,256]{1,0:T(8,128)(2,1)S(1)} %select_convert_fusion.mine_ref), channel_id=1, source_target_pairs={{0,32},{32,0},{64,96},{96,64},{1,33},{33,1},{65,97},{97,65},{2,34}... | collective-permute-start | bytes 1572872 | tf_op jit(solution)/shard_map/ppermute | solution.py:23
  13.7 22.5 %collective-permute-start.1 = (bf16[1024,256]{1,0:T(8,128)(2,1)S(1)}, bf16[1024,256]{1,0:T(8,128)(2,1)S(1)}, u32[]{:S(2)}, u32[]{:S(2)}) collective-permute-start(bf16[1024,256]{1,0:T(8,128)(2,1)S(1)} %select_convert_fusion.mine_ref), channel_id=1, source_target_pairs={{0,64},{32,96},{64,0},{96,32},{1,65},{33,97},{65,1},{97,33},{2,66}... | collective-permute-start | bytes 1572872 | tf_op jit(solution)/shard_map/ppermute | solution.py:23
  33.0 3.3 %copy-start.2 = (bf16[512,8192]{1,0:T(8,128)(2,1)}, bf16[512,8192]{1,0:T(8,128)(2,1)S(1)}, u32[]{:S(2)}) copy-start(bf16[512,8192]{1,0:T(8,128)(2,1)S(1)} %get-tuple-element.72.w_own_ref) | copy-start | bytes 25165828
  36.3 1.9 %collective-permute-start.3 = (bf16[1024,256]{1,0:T(8,128)(2,1)S(1)}, bf16[1024,256]{1,0:T(8,128)(2,1)S(1)}, u32[]{:S(2)}, u32[]{:S(2)}) collective-permute-start(bf16[1024,256]{1,0:T(8,128)(2,1)S(1)} %collective-permute-done.1.mine_ref), channel_id=1, source_target_pairs={{0,32},{32,0},{64,96},{96,64},{1,33},{33,1},{65,97},{97,65},{2,34}... | collective-permute-start | bytes 1572872 | tf_op jit(solution)/shard_map/ppermute | solution.py:23
  39.3 19.8 %collective-permute-start.6 = (bf16[512,768]{1,0:T(8,128)(2,1)S(1)}, bf16[512,768]{1,0:T(8,128)(2,1)S(1)}, u32[]{:S(2)}, u32[]{:S(2)}) collective-permute-start(bf16[512,768]{1,0:T(8,128)(2,1)S(1)} %send1.3), channel_id=1, source_target_pairs={{0,1},{1,0},{2,3},{3,2},{4,5},{5,4},{6,7},{7,6},{8,9},{9,8},{10,11... | collective-permute-start | bytes 2359304 | tf_op jit(solution)/shard_map/ppermute | solution.py:23
  42.2 19.6 %collective-permute-start.4 = (bf16[512,768]{1,0:T(8,128)(2,1)S(1)}, bf16[512,768]{1,0:T(8,128)(2,1)S(1)}, u32[]{:S(2)}, u32[]{:S(2)}) collective-permute-start(bf16[512,768]{1,0:T(8,128)(2,1)S(1)} %send0.3), channel_id=1, source_target_pairs={{0,8},{1,9},{2,10},{3,11},{4,12},{5,13},{6,14},{7,15},{8,0},{9,1},... | collective-permute-start | bytes 2359304 | tf_op jit(solution)/shard_map/ppermute | solution.py:23
  44.8 19.9 %collective-permute-start.9 = (bf16[512,768]{1,0:T(8,128)(2,1)S(1)}, bf16[512,768]{1,0:T(8,128)(2,1)S(1)}, u32[]{:S(2)}, u32[]{:S(2)}) collective-permute-start(bf16[512,768]{1,0:T(8,128)(2,1)S(1)} %send2.3), channel_id=1, source_target_pairs={{0,4},{1,5},{2,6},{3,7},{4,0},{5,1},{6,2},{7,3},{8,12},{9,13},{10,... | collective-permute-start | bytes 2359304 | tf_op jit(solution)/shard_map/ppermute | solution.py:23
  46.7 20.0 %collective-permute-start.13 = (bf16[512,768]{1,0:T(8,128)(2,1)S(1)}, bf16[512,768]{1,0:T(8,128)(2,1)S(1)}, u32[]{:S(2)}, u32[]{:S(2)}) collective-permute-start(bf16[512,768]{1,0:T(8,128)(2,1)S(1)} %send3.3), channel_id=1, source_target_pairs={{0,24},{1,25},{2,26},{3,27},{4,28},{5,29},{6,30},{7,31},{8,16},{9,... | collective-permute-start | bytes 2359304 | tf_op jit(solution)/shard_map/ppermute | solution.py:23
  49.8 20.3 %collective-permute-start.18 = (bf16[512,768]{1,0:T(8,128)(2,1)S(1)}, bf16[512,768]{1,0:T(8,128)(2,1)S(1)}, u32[]{:S(2)}, u32[]{:S(2)}) collective-permute-start(bf16[512,768]{1,0:T(8,128)(2,1)S(1)} %send4.3), channel_id=1, source_target_pairs={{0,3},{1,2},{2,1},{3,0},{4,7},{5,6},{6,5},{7,4},{8,11},{9,10},{10,... | collective-permute-start | bytes 2359304 | tf_op jit(solution)/shard_map/ppermute | solution.py:23
  59.1 29.6 %collective-permute-start.7 = (bf16[512,896]{1,0:T(8,128)(2,1)S(1)}, bf16[512,896]{1,0:T(8,128)(2,1)S(1)}, u32[]{:S(2)}, u32[]{:S(2)}) collective-permute-start(bf16[512,896]{1,0:T(8,128)(2,1)S(1)} %send1.2), channel_id=1, source_target_pairs={{0,1},{1,0},{2,3},{3,2},{4,5},{5,4},{6,7},{7,6},{8,9},{9,8},{10,11... | collective-permute-start | bytes 2752520 | tf_op jit(solution)/shard_map/ppermute | solution.py:23
  61.9 26.6 %collective-permute-start.5 = (bf16[512,768]{1,0:T(8,128)(2,1)S(1)}, bf16[512,768]{1,0:T(8,128)(2,1)S(1)}, u32[]{:S(2)}, u32[]{:S(2)}) collective-permute-start(bf16[512,768]{1,0:T(8,128)(2,1)S(1)} %send0.2), channel_id=1, source_target_pairs={{0,8},{1,9},{2,10},{3,11},{4,12},{5,13},{6,14},{7,15},{8,0},{9,1},... | collective-permute-start | bytes 2359304 | tf_op jit(solution)/shard_map/ppermute | solution.py:23
  64.7 25.4 %collective-permute-start.10 = (bf16[512,896]{1,0:T(8,128)(2,1)S(1)}, bf16[512,896]{1,0:T(8,128)(2,1)S(1)}, u32[]{:S(2)}, u32[]{:S(2)}) collective-permute-start(bf16[512,896]{1,0:T(8,128)(2,1)S(1)} %send2.2), channel_id=1, source_target_pairs={{0,4},{1,5},{2,6},{3,7},{4,0},{5,1},{6,2},{7,3},{8,12},{9,13},{10,... | collective-permute-start | bytes 2752520 | tf_op jit(solution)/shard_map/ppermute | solution.py:23
  65.4 7.3 %slice-start = ((s8[8388608]{0:T(1024)(128)(4,1)}), s8[4194304]{0:T(1024)(128)(4,1)S(1)}, s32[]{:S(2)}) async-start(s8[8388608]{0:T(1024)(128)(4,1)} %bitcast.29), calls=%async_computation | async-start | bytes 8388608
  66.7 25.1 %collective-permute-start.14 = (bf16[512,896]{1,0:T(8,128)(2,1)S(1)}, bf16[512,896]{1,0:T(8,128)(2,1)S(1)}, u32[]{:S(2)}, u32[]{:S(2)}) collective-permute-start(bf16[512,896]{1,0:T(8,128)(2,1)S(1)} %send3.2), channel_id=1, source_target_pairs={{0,24},{1,25},{2,26},{3,27},{4,28},{5,29},{6,30},{7,31},{8,16},{9,... | collective-permute-start | bytes 2752520 | tf_op jit(solution)/shard_map/ppermute | solution.py:23
  68.9 3.9 %slice-start.1 = ((s8[8388608]{0:T(1024)(128)(4,1)}), s8[4194304]{0:T(1024)(128)(4,1)S(1)}, s32[]{:S(2)}) async-start(s8[8388608]{0:T(1024)(128)(4,1)} %bitcast.29), calls=%async_computation.1 | async-start | bytes 8388608
  70.1 23.2 %collective-permute-start.19 = (bf16[512,896]{1,0:T(8,128)(2,1)S(1)}, bf16[512,896]{1,0:T(8,128)(2,1)S(1)}, u32[]{:S(2)}, u32[]{:S(2)}) collective-permute-start(bf16[512,896]{1,0:T(8,128)(2,1)S(1)} %send4.2), channel_id=1, source_target_pairs={{0,3},{1,2},{2,1},{3,0},{4,7},{5,6},{6,5},{7,4},{8,11},{9,10},{10,... | collective-permute-start | bytes 2752520 | tf_op jit(solution)/shard_map/ppermute | solution.py:23
  88.7 17.4 %collective-permute-start.8 = (bf16[256,1536]{1,0:T(8,128)(2,1)S(1)}, bf16[256,1536]{1,0:T(8,128)(2,1)S(1)}, u32[]{:S(2)}, u32[]{:S(2)}) collective-permute-start(bf16[256,1536]{1,0:T(8,128)(2,1)S(1)} %get-tuple-element.80), channel_id=1, source_target_pairs={{0,1},{1,0},{2,3},{3,2},{4,5},{5,4},{6,7},{7,6},{8,9},{9,8},{10,11... | collective-permute-start | bytes 2359304 | tf_op jit(solution)/shard_map/ppermute | solution.py:23
  90.1 19.2 %collective-permute-start.11 = (bf16[256,1664]{1,0:T(8,128)(2,1)S(1)}, bf16[256,1664]{1,0:T(8,128)(2,1)S(1)}, u32[]{:S(2)}, u32[]{:S(2)}) collective-permute-start(bf16[256,1664]{1,0:T(8,128)(2,1)S(1)} %get-tuple-element.86), channel_id=1, source_target_pairs={{0,4},{1,5},{2,6},{3,7},{4,0},{5,1},{6,2},{7,3},{8,12},{9,13},{10,... | collective-permute-start | bytes 2555912 | tf_op jit(solution)/shard_map/ppermute | solution.py:23
  91.8 19.5 %collective-permute-start.15 = (bf16[256,1664]{1,0:T(8,128)(2,1)S(1)}, bf16[256,1664]{1,0:T(8,128)(2,1)S(1)}, u32[]{:S(2)}, u32[]{:S(2)}) collective-permute-start(bf16[256,1664]{1,0:T(8,128)(2,1)S(1)} %get-tuple-element.94), channel_id=1, source_target_pairs={{0,24},{1,25},{2,26},{3,27},{4,28},{5,29},{6,30},{7,31},{8,16},{9,... | collective-permute-start | bytes 2555912 | tf_op jit(solution)/shard_map/ppermute | solution.py:23
  93.3 19.7 %collective-permute-start.20 = (bf16[256,1664]{1,0:T(8,128)(2,1)S(1)}, bf16[256,1664]{1,0:T(8,128)(2,1)S(1)}, u32[]{:S(2)}, u32[]{:S(2)}) collective-permute-start(bf16[256,1664]{1,0:T(8,128)(2,1)S(1)} %get-tuple-element.103), channel_id=1, source_target_pairs={{0,3},{1,2},{2,1},{3,0},{4,7},{5,6},{6,5},{7,4},{8,11},{9,10},{10,... | collective-permute-start | bytes 2555912 | tf_op jit(solution)/shard_map/ppermute | solution.py:23
  95.2 19.9 %collective-permute-start.24 = (bf16[256,1664]{1,0:T(8,128)(2,1)S(1)}, bf16[256,1664]{1,0:T(8,128)(2,1)S(1)}, u32[]{:S(2)}, u32[]{:S(2)}) collective-permute-start(bf16[256,1664]{1,0:T(8,128)(2,1)S(1)} %get-tuple-element.110), channel_id=1, source_target_pairs={{0,8},{1,9},{2,10},{3,11},{4,12},{5,13},{6,14},{7,15},{8,0},{9,1},... | collective-permute-start | bytes 2555912 | tf_op jit(solution)/shard_map/ppermute | solution.py:23
  109.3 7.8 %collective-permute-start.12 = (bf16[128,1536]{1,0:T(8,128)(2,1)S(1)}, bf16[128,1536]{1,0:T(8,128)(2,1)S(1)}, u32[]{:S(2)}, u32[]{:S(2)}) collective-permute-start(bf16[128,1536]{1,0:T(8,128)(2,1)S(1)} %slice.219), channel_id=1, source_target_pairs={{0,4},{1,5},{2,6},{3,7},{4,0},{5,1},{6,2},{7,3},{8,12},{9,13},{10,... | collective-permute-start | bytes 1179656 | tf_op jit(solution)/shard_map/ppermute | solution.py:23
  111.6 10.5 %collective-permute-start.16 = (bf16[128,1664]{1,0:T(8,128)(2,1)S(1)}, bf16[128,1664]{1,0:T(8,128)(2,1)S(1)}, u32[]{:S(2)}, u32[]{:S(2)}) collective-permute-start(bf16[128,1664]{1,0:T(8,128)(2,1)S(1)} %slice.218), channel_id=1, source_target_pairs={{0,24},{1,25},{2,26},{3,27},{4,28},{5,29},{6,30},{7,31},{8,16},{9,... | collective-permute-start | bytes 1277960 | tf_op jit(solution)/shard_map/ppermute | solution.py:23
  113.2 10.3 %collective-permute-start.21 = (bf16[128,1664]{1,0:T(8,128)(2,1)S(1)}, bf16[128,1664]{1,0:T(8,128)(2,1)S(1)}, u32[]{:S(2)}, u32[]{:S(2)}) collective-permute-start(bf16[128,1664]{1,0:T(8,128)(2,1)S(1)} %slice.217), channel_id=1, source_target_pairs={{0,3},{1,2},{2,1},{3,0},{4,7},{5,6},{6,5},{7,4},{8,11},{9,10},{10,... | collective-permute-start | bytes 1277960 | tf_op jit(solution)/shard_map/ppermute | solution.py:23
  115.2 9.7 %collective-permute-start.28 = (bf16[128,1664]{1,0:T(8,128)(2,1)S(1)}, bf16[128,1664]{1,0:T(8,128)(2,1)S(1)}, u32[]{:S(2)}, u32[]{:S(2)}) collective-permute-start(bf16[128,1664]{1,0:T(8,128)(2,1)S(1)} %slice.215), channel_id=1, source_target_pairs={{0,1},{1,0},{2,3},{3,2},{4,5},{5,4},{6,7},{7,6},{8,9},{9,8},{10,11... | collective-permute-start | bytes 1277960 | tf_op jit(solution)/shard_map/ppermute | solution.py:23
  115.3 10.6 %collective-permute-start.25 = (bf16[128,1664]{1,0:T(8,128)(2,1)S(1)}, bf16[128,1664]{1,0:T(8,128)(2,1)S(1)}, u32[]{:S(2)}, u32[]{:S(2)}) collective-permute-start(bf16[128,1664]{1,0:T(8,128)(2,1)S(1)} %slice.216), channel_id=1, source_target_pairs={{0,8},{1,9},{2,10},{3,11},{4,12},{5,13},{6,14},{7,15},{8,0},{9,1},... | collective-permute-start | bytes 1277960 | tf_op jit(solution)/shard_map/ppermute | solution.py:23
  122.1 6.9 %collective-permute-start.17 = (bf16[64,1536]{1,0:T(8,128)(2,1)S(1)}, bf16[64,1536]{1,0:T(8,128)(2,1)S(1)}, u32[]{:S(2)}, u32[]{:S(2)}) collective-permute-start(bf16[64,1536]{1,0:T(8,128)(2,1)S(1)} %slice.224), channel_id=1, source_target_pairs={{0,24},{1,25},{2,26},{3,27},{4,28},{5,29},{6,30},{7,31},{8,16},{9,... | collective-permute-start | bytes 589832 | tf_op jit(solution)/shard_map/ppermute | solution.py:23
  123.5 8.1 %collective-permute-start.22 = (bf16[64,1664]{1,0:T(8,128)(2,1)S(1)}, bf16[64,1664]{1,0:T(8,128)(2,1)S(1)}, u32[]{:S(2)}, u32[]{:S(2)}) collective-permute-start(bf16[64,1664]{1,0:T(8,128)(2,1)S(1)} %slice.223), channel_id=1, source_target_pairs={{0,3},{1,2},{2,1},{3,0},{4,7},{5,6},{6,5},{7,4},{8,11},{9,10},{10,... | collective-permute-start | bytes 638984 | tf_op jit(solution)/shard_map/ppermute | solution.py:23
  125.0 8.0 %collective-permute-start.31 = (bf16[64,1664]{1,0:T(8,128)(2,1)S(1)}, bf16[64,1664]{1,0:T(8,128)(2,1)S(1)}, u32[]{:S(2)}, u32[]{:S(2)}) collective-permute-start(bf16[64,1664]{1,0:T(8,128)(2,1)S(1)} %slice.220), channel_id=1, source_target_pairs={{0,4},{1,5},{2,6},{3,7},{4,0},{5,1},{6,2},{7,3},{8,12},{9,13},{10,... | collective-permute-start | bytes 638984 | tf_op jit(solution)/shard_map/ppermute | solution.py:23
  126.1 9.2 %collective-permute-start.29 = (bf16[64,1664]{1,0:T(8,128)(2,1)S(1)}, bf16[64,1664]{1,0:T(8,128)(2,1)S(1)}, u32[]{:S(2)}, u32[]{:S(2)}) collective-permute-start(bf16[64,1664]{1,0:T(8,128)(2,1)S(1)} %slice.221), channel_id=1, source_target_pairs={{0,1},{1,0},{2,3},{3,2},{4,5},{5,4},{6,7},{7,6},{8,9},{9,8},{10,11... | collective-permute-start | bytes 638984 | tf_op jit(solution)/shard_map/ppermute | solution.py:23
  126.6 9.5 %collective-permute-start.26 = (bf16[64,1664]{1,0:T(8,128)(2,1)S(1)}, bf16[64,1664]{1,0:T(8,128)(2,1)S(1)}, u32[]{:S(2)}, u32[]{:S(2)}) collective-permute-start(bf16[64,1664]{1,0:T(8,128)(2,1)S(1)} %slice.222), channel_id=1, source_target_pairs={{0,8},{1,9},{2,10},{3,11},{4,12},{5,13},{6,14},{7,15},{8,0},{9,1},... | collective-permute-start | bytes 638984 | tf_op jit(solution)/shard_map/ppermute | solution.py:23
  131.6 5.8 %collective-permute-start.23 = (bf16[32,1536]{1,0:T(8,128)(2,1)S(1)}, bf16[32,1536]{1,0:T(8,128)(2,1)S(1)}, u32[]{:S(2)}, u32[]{:S(2)}) collective-permute-start(bf16[32,1536]{1,0:T(8,128)(2,1)S(1)} %slice.229), channel_id=1, source_target_pairs={{0,3},{1,2},{2,1},{3,0},{4,7},{5,6},{6,5},{7,4},{8,11},{9,10},{10,... | collective-permute-start | bytes 294920 | tf_op jit(solution)/shard_map/ppermute | solution.py:23
  133.1 8.1 %collective-permute-start.33 = (bf16[32,1664]{1,0:T(8,128)(2,1)S(1)}, bf16[32,1664]{1,0:T(8,128)(2,1)S(1)}, u32[]{:S(2)}, u32[]{:S(2)}) collective-permute-start(bf16[32,1664]{1,0:T(8,128)(2,1)S(1)} %slice.225), channel_id=1, source_target_pairs={{0,24},{1,25},{2,26},{3,27},{4,28},{5,29},{6,30},{7,31},{8,16},{9,... | collective-permute-start | bytes 319496 | tf_op jit(solution)/shard_map/ppermute | solution.py:23
  135.3 5.8 %collective-permute-start.32 = (bf16[32,1664]{1,0:T(8,128)(2,1)S(1)}, bf16[32,1664]{1,0:T(8,128)(2,1)S(1)}, u32[]{:S(2)}, u32[]{:S(2)}) collective-permute-start(bf16[32,1664]{1,0:T(8,128)(2,1)S(1)} %slice.226), channel_id=1, source_target_pairs={{0,4},{1,5},{2,6},{3,7},{4,0},{5,1},{6,2},{7,3},{8,12},{9,13},{10,... | collective-permute-start | bytes 319496 | tf_op jit(solution)/shard_map/ppermute | solution.py:23
  136.2 5.1 %copy-start.3 = (f32[1,8192]{1,0:T(1,128)S(1)}, f32[1,8192]{1,0:T(1,128)}, u32[]{:S(2)}) copy-start(f32[1,8192]{1,0:T(1,128)} %param.16) | copy-start | bytes 98308
  136.2 4.9 %collective-permute-start.30 = (bf16[32,1664]{1,0:T(8,128)(2,1)S(1)}, bf16[32,1664]{1,0:T(8,128)(2,1)S(1)}, u32[]{:S(2)}, u32[]{:S(2)}) collective-permute-start(bf16[32,1664]{1,0:T(8,128)(2,1)S(1)} %slice.227), channel_id=1, source_target_pairs={{0,1},{1,0},{2,3},{3,2},{4,5},{5,4},{6,7},{7,6},{8,9},{9,8},{10,11... | collective-permute-start | bytes 319496 | tf_op jit(solution)/shard_map/ppermute | solution.py:23
  136.3 4.8 %collective-permute-start.27 = (bf16[32,1664]{1,0:T(8,128)(2,1)S(1)}, bf16[32,1664]{1,0:T(8,128)(2,1)S(1)}, u32[]{:S(2)}, u32[]{:S(2)}) collective-permute-start(bf16[32,1664]{1,0:T(8,128)(2,1)S(1)} %slice.228), channel_id=1, source_target_pairs={{0,8},{1,9},{2,10},{3,11},{4,12},{5,13},{6,14},{7,15},{8,0},{9,1},... | collective-permute-start | bytes 319496 | tf_op jit(solution)/shard_map/ppermute | solution.py:23
  141.1 1.0 copy-start.1

commit v5 on v4

--- a/solution.py
+++ b/solution.py
@@ -13,6 +13,7 @@
 LANES, TILE = 128, 256
 PARTS = (12, 13, 13, 13, 13)
 EARLY = (6, 6, 6, 6, 6)
+READY = 4
 VMEM = pl.BlockSpec(memory_space=pltpu.VMEM)
 HBM = pl.BlockSpec(memory_space=pltpu.HBM)
 MIB = 1 << 20
@@ -88,7 +89,7 @@
     masks = block_masks()
     rows = tokens // len(masks)
     q = depth // 4
-    chunks = ((0, q), (q, q), (2 * q, 2 * q))
+    chunks = ((0, q), (q, 3 * q))
     half = pltpu.VMEM((tokens, width), F32)
     return pl.pallas_call(
         functools.partial(encode_kernel, masks=masks, rows=rows, chunks=chunks),
@@ -129,22 +130,35 @@
     out_ref[:, pl.ds(pl.multiple_of((1 - core) * hw, hw), hw)] = sib_ref[...]
 
 
-def join(mine, sib):
-    n, hw = mine.shape
+def assemble_kernel(own_ref, own_sib_ref, far_ref, far_sib_ref, out_ref):
+    group = lax.axis_index("layer")
+    source, core = group // 2, group % 2
+    hw = own_ref.shape[1]
+    for ref, s, c in (
+        (own_ref, source, core),
+        (own_sib_ref, source, 1 - core),
+        (far_ref, 1 - source, core),
+        (far_sib_ref, 1 - source, 1 - core),
+    ):
+        out_ref[:, pl.ds(pl.multiple_of((s * 2 + c) * hw, hw), hw)] = ref[...]
+
+
+def assemble(*pieces):
+    n, hw = pieces[0].shape
     return pl.pallas_call(
-        join_kernel,
-        out_shape=pltpu.VMEM((n, 2 * hw), BF16),
-        in_specs=[VMEM] * 2,
+        assemble_kernel,
+        out_shape=pltpu.VMEM((n, 4 * hw), BF16),
+        in_specs=[VMEM] * 4,
         out_specs=VMEM,
         compiler_params=pltpu.CompilerParams(vmem_limit_bytes=8 * MIB),
-        name="join",
-    )(mine, sib)
-
-
-def gather_rows(codes_ref, lhs, blocks):
+        name="assemble",
+    )(*pieces)
+
+
+def gather_rows(codes_ref, lhs, blocks, cols=slice(None)):
     rows = lhs.shape[0] // len(blocks)
     for j, b in enumerate(blocks):
-        lhs[pl.ds(j * rows, rows), :] = codes_ref[pl.ds(b * rows, rows), :]
+        lhs[pl.ds(j * rows, rows), :] = codes_ref[pl.ds(b * rows, rows), cols]
 
 
 def over_tiles(begin, end, body):
@@ -159,50 +173,49 @@
 
 
 def product(lhs, w_ref, at, n):
-    w = w_ref[:, pl.ds(pl.multiple_of(at, LANES), n)]
+    cols = pl.ds(pl.multiple_of(at, LANES), n)
+    w = w_ref[:, cols] if len(w_ref.shape) == 2 else w_ref[:, :, cols].reshape(lhs.shape[1], n)
     return jnp.dot(lhs[...], w, preferred_element_type=F32)
 
 
 def own_kernel(mine_ref, sib_ref, dec_hbm, *refs, spans):
-    codes_ref, w_ref, far_ref, *accs = refs[: 3 + len(spans)]
-    lhs, w_sem, far_sem = refs[3 + len(spans) :]
+    w_ref, *accs = refs[: 1 + len(spans)]
+    codes, lhs, own_sem, far_sem = refs[1 + len(spans) :]
     source = lax.axis_index("layer") // 2
-    copy_weights(dec_hbm, source, w_ref, w_sem, True)
-    copy_weights(dec_hbm, 1 - source, far_ref, far_sem, True)
-    join_kernel(mine_ref, sib_ref, codes_ref)
-    copy_weights(dec_hbm, source, w_ref, w_sem, False)
-    done = None
+    own, far = w_ref.at[source], w_ref.at[1 - source]
+    copy_weights(dec_hbm, source, own, own_sem, True)
+    copy_weights(dec_hbm, 1 - source, far, far_sem, True)
+    join_kernel(mine_ref, sib_ref, codes)
+    copy_weights(dec_hbm, source, own, own_sem, False)
     for (part, at, wide), acc in zip(spans, accs):
-        if part != done:
-            gather_rows(codes_ref, lhs, send_blocks(part))
-            done = part
+        gather_rows(codes, lhs, send_blocks(part))
 
         def body(c, n):
-            acc[:, pl.ds(c, n)] = product(lhs, w_ref, at + c, n)
+            acc[:, pl.ds(c, n)] = product(lhs, own, at + c, n)
 
         over_tiles(0, wide, body)
-    copy_weights(dec_hbm, 1 - source, far_ref, far_sem, False)
+    copy_weights(dec_hbm, 1 - source, far, far_sem, False)
 
 
 def own_part(mine, sib, dec, spans):
     tokens, hw = mine.shape
-    _, _, depth, wide = dec.shape
+    _, sources, depth, wide = dec.shape
     n = tokens // 2
-    codes, w_own, w_far, *accs = pl.pallas_call(
+    weights, *accs = pl.pallas_call(
         functools.partial(own_kernel, spans=spans),
-        out_shape=[pltpu.VMEM((tokens, 2 * hw), BF16)]
-        + [pltpu.VMEM((depth, wide), BF16)] * 2
+        out_shape=[pltpu.VMEM((sources, depth, wide), BF16)]
         + [pltpu.VMEM((n, span[2]), F32) for span in spans],
         in_specs=[VMEM, VMEM, HBM],
-        out_specs=[VMEM] * (3 + len(spans)),
-        scratch_shapes=[pltpu.VMEM((n, depth), BF16)] + [pltpu.SemaphoreType.DMA((COPIES,))] * 2,
+        out_specs=[VMEM] * (1 + len(spans)),
+        scratch_shapes=[pltpu.VMEM((tokens, depth), BF16), pltpu.VMEM((n, depth), BF16)]
+        + [pltpu.SemaphoreType.DMA((COPIES,))] * 2,
         compiler_params=pltpu.CompilerParams(vmem_limit_bytes=14 * MIB),
         cost_estimate=pl.CostEstimate(
-            flops=2 * n * depth * wide, bytes_accessed=4 * depth * wide, transcendentals=0
+            flops=n * depth * wide, bytes_accessed=8 * depth * wide, transcendentals=0
         ),
         name="own",
     )(mine, sib, dec)
-    return codes, w_own, w_far, accs
+    return weights, accs
 
 
 def send_blocks(part):
@@ -215,55 +228,66 @@
     return blocks[: len(blocks) // 2]
 
 
-def send_kernel(codes_ref, w_ref, acc_ref, send_ref, lhs, *, blocks, at):
-    gather_rows(codes_ref, lhs, blocks)
+def call_tiny(kernel, out_shape, scratch, name, *args):
+    many = isinstance(out_shape, tuple)
+    return pl.pallas_call(
+        kernel,
+        out_shape=out_shape,
+        in_specs=[VMEM] * len(args),
+        out_specs=[VMEM] * len(out_shape) if many else VMEM,
+        scratch_shapes=scratch,
+        compiler_params=pltpu.CompilerParams(vmem_limit_bytes=8 * MIB),
+        cost_estimate=pl.CostEstimate(flops=1000, bytes_accessed=1000, transcendentals=0),
+        name=name,
+    )(*args)
+
+
+def send_early_kernel(codes_ref, w_ref, acc_ref, send_ref, lhs, *, blocks, at):
+    other = 1 - lax.axis_index("layer") // 2
+    depth = lhs.shape[1]
+    gather_rows(codes_ref, lhs, blocks, pl.ds(pl.multiple_of(other * depth, depth), depth))
 
     def body(c, n):
         cols = pl.ds(c, n)
-        send_ref[:, cols] = (acc_ref[:, cols] + product(lhs, w_ref, at + c, n)).astype(BF16)
+        total = acc_ref[:, cols] + product(lhs, w_ref.at[other], at + c, n)
+        send_ref[:, cols] = total.astype(BF16)
 
     over_tiles(0, send_ref.shape[1], body)
 
 
-def decode_send(codes, w, acc, part, at):
+def send_early(codes, w, acc, part, at):
     n, wide = acc.shape
-    return pl.pallas_call(
-        functools.partial(send_kernel, blocks=send_blocks(part), at=at),
-        out_shape=jax.ShapeDtypeStruct((n, wide), BF16),
-        in_specs=[VMEM] * 3,
-        out_specs=VMEM,
-        scratch_shapes=[pltpu.VMEM((n, codes.shape[1]), BF16)],
-        compiler_params=pltpu.CompilerParams(vmem_limit_bytes=6 * MIB),
-        cost_estimate=pl.CostEstimate(flops=1000, bytes_accessed=1000, transcendentals=0),
-        name=f"send{part}",
-    )(codes, w, acc)
-
-
-def keep_kernel(own_ref, far_ref, w_own_ref, w_far_ref, keep_ref, own_lhs, far_lhs, *, blocks, at):
-    gather_rows(own_ref, own_lhs, blocks)
-    gather_rows(far_ref, far_lhs, blocks)
+    return call_tiny(
+        functools.partial(send_early_kernel, blocks=send_blocks(part), at=at),
+        jax.ShapeDtypeStruct((n, wide), BF16),
+        [pltpu.VMEM((n, codes.shape[1] // 2), BF16)],
+        f"early{part}",
+        codes,
+        w,
+        acc,
+    )
+
+
+def rows_kernel(codes_ref, w_ref, out_ref, lhs, *, blocks, at):
+    gather_rows(codes_ref, lhs, blocks)
 
     def body(c, n):
-        keep_ref[:, pl.ds(c, n)] = product(own_lhs, w_own_ref, at + c, n) + product(
-            far_lhs, w_far_ref, at + c, n
-        )
-
-    over_tiles(0, keep_ref.shape[1], body)
-
-
-def decode_keep(own, far, w_own, w_far, part, at, wide):
-    tokens, depth = own.shape
+        out_ref[:, pl.ds(c, n)] = product(lhs, w_ref, at + c, n).astype(out_ref.dtype)
+
+    over_tiles(0, out_ref.shape[1], body)
+
+
+def decode_rows(codes, w, blocks, at, wide, dtype, name):
+    tokens, depth = codes.shape
     n = tokens // 2
-    return pl.pallas_call(
-        functools.partial(keep_kernel, blocks=keep_blocks(part), at=at),
-        out_shape=jax.ShapeDtypeStruct((n, wide), F32),
-        in_specs=[VMEM] * 4,
-        out_specs=VMEM,
-        scratch_shapes=[pltpu.VMEM((n, depth), BF16)] * 2,
-        compiler_params=pltpu.CompilerParams(vmem_limit_bytes=8 * MIB),
-        cost_estimate=pl.CostEstimate(flops=1000, bytes_accessed=1000, transcendentals=0),
-        name=f"keep{part}",
-    )(own, far, w_own, w_far)
+    return call_tiny(
+        functools.partial(rows_kernel, blocks=blocks, at=at),
+        jax.ShapeDtypeStruct((n, wide), dtype),
+        [pltpu.VMEM((n, depth), BF16)],
+        name,
+        codes,
+        w,
+    )
 
 
 def merge_kernel(keep_ref, early_ref, late_ref, new_ref, send_ref):
@@ -339,14 +363,10 @@
     own_sib = xor_swap(own, "layer", 1)
 
     starts = [sum(PARTS[:p]) * LANES for p in range(STEPS)]
-    spans = []
-    for late in (False, True):
-        for p in range(STEPS):
-            wide = (PARTS[p] - EARLY[p] if late else EARLY[p]) * LANES
-            spans.append((p, starts[p] + (EARLY[p] * LANES if late else 0), wide))
-    own_codes, w_own, w_far, accs = own_part(own, own_sib, dec_weight, spans)
-    far, w_far = lax.optimization_barrier((xor_swap(own, "layer", 2), w_far))
-    far_codes = join(far, xor_swap(far, "layer", 1))
+    spans = [(p, starts[p], EARLY[p] * LANES) for p in range(STEPS)]
+    weights, accs = own_part(own, own_sib, dec_weight, spans)
+    far, weights = lax.optimization_barrier((xor_swap(own, "layer", 2), weights))
+    codes = assemble(own, own_sib, far, xor_swap(far, "layer", 1))
 
     last = [None] * STEPS
 
@@ -356,19 +376,23 @@
         last[link] = xor_swap(data, "lat", LINKS[link])
         return last[link]
 
-    got = [
-        exchange(decode_send(far_codes, w_far, acc, p, at), p)
-        for (p, at, _), acc in zip(spans, accs)
+    early = [
+        exchange(send_early(codes, weights, acc, p, at), p) for (p, at, _), acc in zip(spans, accs)
     ]
+    sends = [
+        decode_rows(codes, weights, send_blocks(p), at + wide, PARTS[p] * LANES - wide, BF16, f"late{p}")
+        for p, at, wide in spans
+    ]
+    sends[:READY] = lax.optimization_barrier(tuple(sends[:READY]))
+    late = [exchange(sends[p], p) for p in range(STEPS)]
     keeps = [
-        decode_keep(own_codes, far_codes, w_own, w_far, p, starts[p], PARTS[p] * LANES)
+        decode_rows(codes, weights, keep_blocks(p), starts[p], PARTS[p] * LANES, F32, f"keep{p}")
         for p in range(STEPS)
     ]
-    first, *keeps = lax.optimization_barrier((got[STEPS], *keeps))
-    got[STEPS] = first
+    late[0], *keeps[:READY] = lax.optimization_barrier((late[0], *keeps[:READY]))
     kept, out = {}, {}
     for p in range(STEPS):
-        kept[p], out[p] = merge(keeps[p], got[p], got[STEPS + p])
+        kept[p], out[p] = merge(keeps[p], early[p], late[p])
     for i in range(1, STEPS):
         for p in range(STEPS):
             total = kept[p] + exchange(out[p], (p + i) % STEPS).astype(F32)

time: 142 us -> 135 us (0.951)
  Pallas kernels: 53.3 us -> 48.3 us
  local copies, waits for them, and re-layouts: 5.36 us -> 2.06 us
  starting transfers between devices: 41 us -> 44.1 us
  waiting for transfers between devices: 37.6 us -> 35.2 us
    pallas_call x1, Pallas kernels: 15.9 us -> 8.27 us  [own_part(): pl.pallas_call(functools.partial(own_kernel, spans=spans), out_shape=[plt...]
    unnamed x20 -> x14, local copies, waits for them, and re-layouts: 3.33 us -> 0.03 us
    ppermute x34, starting transfers between devices: 41 us -> 44.1 us  [xor_swap(): lax.ppermute(value, axis, [(i, i ^ mask) for i in range(lax.axis_size(axi...]
    pallas_call x16, Pallas kernels: 26.5 us -> 29.6 us  [the longest x15 29.3 us: call_tiny(): pl.pallas_call(kernel, out_shape=out_shape, in_specs=[VMEM] * len(args),...]
    ppermute x34, waiting for transfers between devices: 37.6 us -> 35.2 us  [xor_swap(): lax.ppermute(value, axis, [(i, i ^ mask) for i in range(lax.axis_size(axi...]
  transfers between devices with their start and end apart: 34 -> 34, of which waited for: 12 -> 14; matrix products, arithmetic and copies ran while one was open for 4% -> 4% of each run, Pallas kernels for 30% -> 28%
where the time goes in v5:
time: 135 us; the launch traced here: 134 us
  Pallas kernels  48.3 us (36%)
  starting transfers between devices  44.1 us (33%)
  waiting for transfers between devices  35.2 us (26%)
  other arithmetic  2.93 us (2%)
  local copies, waits for them, and re-layouts  2.06 us (2%)
    ppermute x34, starting transfers between devices, xor_swap(): lax.ppermute(value, axis, [(i, i ^ mask) for i in range(lax.axis_size(axi...  44.1 us
    ppermute x34, waiting for transfers between devices, xor_swap(): lax.ppermute(value, axis, [(i, i ^ mask) for i in range(lax.axis_size(axi...  35.2 us
    pallas_call x15, Pallas kernels, call_tiny(): pl.pallas_call(kernel, out_shape=out_shape, in_specs=[VMEM] * len(args),...  29.3 us
    pallas_call x1, Pallas kernels, encode(): pl.pallas_call(functools.partial(encode_kernel, masks=masks, rows=rows, c...  9.09 us
    pallas_call x1, Pallas kernels, own_part(): pl.pallas_call(functools.partial(own_kernel, spans=spans), out_shape=[plt...  8.27 us
  transfers between devices with their start and end apart: 34, of which 14 were waited for; matrix products, arithmetic and copies ran while one was open for 4% of the time, Pallas kernels for 28%

profile of v5, /device:TPU:0, one launch (start us, length us, event | category | flops | bytes accessed | tf_op | source)
XLA Modules:
  0.0 134.5 jit_solution(16226577341572320413)
XLA Ops:
  0.0 9.1 %encode.1 = (f32[1024,256]{1,0:T(8,128)S(1)}, f32[1024,256]{1,0:T(8,128)S(1)}) custom-call(bf16[1,1024,4096]{2,1,0:T(8,128)(2,1)} %x_hbm.1, bf16[1,4096,512]{2,1,0:T(8,128)(2,1)} %w_hbm.1), custom_call_target="tpu_custom_call" | custom-call | flops 4294967296 | bytes 14680064 | tf_op jit(solution)/shard_map/encode/pallas_call | solution.py:94
  11.0 1.3 %fusion = f32[1,1024]{1,0:T(1,128)S(1)} fusion(s32[1024]{0:T(1024)S(1)} %add.145, s32[1024]{0:T(1024)S(1)} %bitcast.33, s32[2,1024]{1,0:T(2,128)S(1)} %copy-done.4, s32[]{:T(128)S(6)} %select_n.42, s32[2,1024]{1,0:T(2,128)S(1)} %copy-done.5), kind=kOutput, calls=%fused_computation | convolution fusion | flops 13634560 | bytes 20484 | tf_op jit(solution)/shard_map/dot_general | solution.py:349
  13.3 3.3 %collective-permute-start.2 = (bf16[1024,256]{1,0:T(8,128)(2,1)S(1)}, bf16[1024,256]{1,0:T(8,128)(2,1)S(1)}, u32[]{:S(2)}, u32[]{:S(2)}) collective-permute-start(bf16[1024,256]{1,0:T(8,128)(2,1)S(1)} %select_convert_fusion.mine_ref.own_ref), channel_id=1, source_target_pairs={{0,64},{32,96},{64,0},{96,32},{1,65},{33,97},{65,1},{97,33},{2,66}... | collective-permute-start | bytes 1572872 | tf_op jit(solution)/shard_map/ppermute | solution.py:24
  16.6 8.3 %own.1 = (bf16[2,512,8192]{2,1,0:T(8,128)(2,1)S(1)}, f32[512,768]{1,0:T(8,128)S(1)}, f32[512,768]{1,0:T(8,128)S(1)}, f32[512,768]{1,0:T(8,128)S(1)}, f32[512,768]{1,0:T(8,128)S(1)}, /*index=5*/f32[512,768]{1,0:T(8,128)S(1)}) custom-call(bf16[1024,256]{1,0:T(8,128)(2,1)S(1)} %select_convert_fusion.mine_ref.own_ref, ...), custom_call_target="tpu_custom_call" | custom-call | flops 2147483648 | bytes 33554432 | tf_op jit(solution)/shard_map/own/pallas_call | solution.py:204
  24.9 3.9 %collective-permute-done.2.far_ref = bf16[1024,256]{1,0:T(8,128)(2,1)S(1)} collective-permute-done((bf16[1024,256]{1,0:T(8,128)(2,1)S(1)}, bf16[1024,256]{1,0:T(8,128)(2,1)S(1)}, u32[]{:S(2)}, u32[]{:S(2)}) %collective-permute-start.2) | collective-permute-done | bytes 524320 | tf_op jit(solution)/shard_map/ppermute | solution.py:24
  28.8 1.9 %collective-permute-done.3.far_sib_ref = bf16[1024,256]{1,0:T(8,128)(2,1)S(1)} collective-permute-done((bf16[1024,256]{1,0:T(8,128)(2,1)S(1)}, bf16[1024,256]{1,0:T(8,128)(2,1)S(1)}, u32[]{:S(2)}, u32[]{:S(2)}) %collective-permute-start.3) | collective-permute-done | bytes 524320 | tf_op jit(solution)/shard_map/ppermute | solution.py:24
  31.0 1.0 early1.1
  32.0 2.0 %collective-permute-start.6 = (bf16[512,768]{1,0:T(8,128)(2,1)S(1)}, bf16[512,768]{1,0:T(8,128)(2,1)S(1)}, u32[]{:S(2)}, u32[]{:S(2)}) collective-permute-start(bf16[512,768]{1,0:T(8,128)(2,1)S(1)} %early1.1), channel_id=1, source_target_pairs={{0,1},{1,0},{2,3},{3,2},{4,5},{5,4},{6,7},{7,6},{8,9},{9,8},{10,11... | collective-permute-start | bytes 2359304 | tf_op jit(solution)/shard_map/ppermute | solution.py:24
  35.0 1.6 %collective-permute-start.4 = (bf16[512,768]{1,0:T(8,128)(2,1)S(1)}, bf16[512,768]{1,0:T(8,128)(2,1)S(1)}, u32[]{:S(2)}, u32[]{:S(2)}) collective-permute-start(bf16[512,768]{1,0:T(8,128)(2,1)S(1)} %early0.1), channel_id=1, source_target_pairs={{0,8},{1,9},{2,10},{3,11},{4,12},{5,13},{6,14},{7,15},{8,0},{9,1},... | collective-permute-start | bytes 2359304 | tf_op jit(solution)/shard_map/ppermute | solution.py:24
  36.6 1.0 early4.1
  37.6 2.6 %collective-permute-start.18 = (bf16[512,768]{1,0:T(8,128)(2,1)S(1)}, bf16[512,768]{1,0:T(8,128)(2,1)S(1)}, u32[]{:S(2)}, u32[]{:S(2)}) collective-permute-start(bf16[512,768]{1,0:T(8,128)(2,1)S(1)} %early4.1), channel_id=1, source_target_pairs={{0,3},{1,2},{2,1},{3,0},{4,7},{5,6},{6,5},{7,4},{8,11},{9,10},{10,... | collective-permute-start | bytes 2359304 | tf_op jit(solution)/shard_map/ppermute | solution.py:24
  40.2 1.0 early2.1
  41.1 1.7 %collective-permute-start.9 = (bf16[512,768]{1,0:T(8,128)(2,1)S(1)}, bf16[512,768]{1,0:T(8,128)(2,1)S(1)}, u32[]{:S(2)}, u32[]{:S(2)}) collective-permute-start(bf16[512,768]{1,0:T(8,128)(2,1)S(1)} %early2.1), channel_id=1, source_target_pairs={{0,4},{1,5},{2,6},{3,7},{4,0},{5,1},{6,2},{7,3},{8,12},{9,13},{10,... | collective-permute-start | bytes 2359304 | tf_op jit(solution)/shard_map/ppermute | solution.py:24
  42.8 1.0 early3.1
  43.8 2.3 %collective-permute-start.13 = (bf16[512,768]{1,0:T(8,128)(2,1)S(1)}, bf16[512,768]{1,0:T(8,128)(2,1)S(1)}, u32[]{:S(2)}, u32[]{:S(2)}) collective-permute-start(bf16[512,768]{1,0:T(8,128)(2,1)S(1)} %early3.1), channel_id=1, source_target_pairs={{0,24},{1,25},{2,26},{3,27},{4,28},{5,29},{6,30},{7,31},{8,16},{9,... | collective-permute-start | bytes 2359304 | tf_op jit(solution)/shard_map/ppermute | solution.py:24
  46.1 1.4 %late0.1 = bf16[512,768]{1,0:T(8,128)(2,1)S(1)} custom-call(bf16[1024,1024]{1,0:T(8,128)(2,1)S(1)} %assemble.1.codes_ref, bf16[2,512,8192]{2,1,0:T(8,128)(2,1)S(1)} %get-tuple-element.63.w_ref), custom_call_target="tpu_custom_call" | custom-call | flops 1000 | bytes 1000 | tf_op jit(solution)/shard_map/late0/pallas_call | solution.py:233
  47.5 1.8 %late3.1 = bf16[512,896]{1,0:T(8,128)(2,1)S(1)} custom-call(bf16[1024,1024]{1,0:T(8,128)(2,1)S(1)} %assemble.1.codes_ref, bf16[2,512,8192]{2,1,0:T(8,128)(2,1)S(1)} %get-tuple-element.63.w_ref), custom_call_target="tpu_custom_call" | custom-call | flops 1000 | bytes 1000 | tf_op jit(solution)/shard_map/late3/pallas_call | solution.py:233
  49.4 1.9 %late2.1 = bf16[512,896]{1,0:T(8,128)(2,1)S(1)} custom-call(bf16[1024,1024]{1,0:T(8,128)(2,1)S(1)} %assemble.1.codes_ref, bf16[2,512,8192]{2,1,0:T(8,128)(2,1)S(1)} %get-tuple-element.63.w_ref), custom_call_target="tpu_custom_call" | custom-call | flops 1000 | bytes 1000 | tf_op jit(solution)/shard_map/late2/pallas_call | solution.py:233
  51.3 1.9 %late1.1 = bf16[512,896]{1,0:T(8,128)(2,1)S(1)} custom-call(bf16[1024,1024]{1,0:T(8,128)(2,1)S(1)} %assemble.1.codes_ref, bf16[2,512,8192]{2,1,0:T(8,128)(2,1)S(1)} %get-tuple-element.63.w_ref), custom_call_target="tpu_custom_call" | custom-call | flops 1000 | bytes 1000 | tf_op jit(solution)/shard_map/late1/pallas_call | solution.py:233
  53.1 1.1 collective-permute-start.7
  54.4 1.5 %collective-permute-start.5 = (bf16[512,768]{1,0:T(8,128)(2,1)S(1)}, bf16[512,768]{1,0:T(8,128)(2,1)S(1)}, u32[]{:S(2)}, u32[]{:S(2)}) collective-permute-start(bf16[512,768]{1,0:T(8,128)(2,1)S(1)} %late0.1), channel_id=1, source_target_pairs={{0,8},{1,9},{2,10},{3,11},{4,12},{5,13},{6,14},{7,15},{8,0},{9,1},... | collective-permute-start | bytes 2359304 | tf_op jit(solution)/shard_map/ppermute | solution.py:24
  55.9 1.8 %late4.1 = bf16[512,896]{1,0:T(8,128)(2,1)S(1)} custom-call(bf16[1024,1024]{1,0:T(8,128)(2,1)S(1)} %assemble.1.codes_ref, bf16[2,512,8192]{2,1,0:T(8,128)(2,1)S(1)} %get-tuple-element.63.w_ref), custom_call_target="tpu_custom_call" | custom-call | flops 1000 | bytes 1000 | tf_op jit(solution)/shard_map/late4/pallas_call | solution.py:233
  57.9 2.5 %collective-permute-start.19 = (bf16[512,896]{1,0:T(8,128)(2,1)S(1)}, bf16[512,896]{1,0:T(8,128)(2,1)S(1)}, u32[]{:S(2)}, u32[]{:S(2)}) collective-permute-start(bf16[512,896]{1,0:T(8,128)(2,1)S(1)} %late4.1), channel_id=1, source_target_pairs={{0,3},{1,2},{2,1},{3,0},{4,7},{5,6},{6,5},{7,4},{8,11},{9,10},{10,... | collective-permute-start | bytes 2752520 | tf_op jit(solution)/shard_map/ppermute | solution.py:24
  60.4 1.6 %collective-permute-start.10 = (bf16[512,896]{1,0:T(8,128)(2,1)S(1)}, bf16[512,896]{1,0:T(8,128)(2,1)S(1)}, u32[]{:S(2)}, u32[]{:S(2)}) collective-permute-start(bf16[512,896]{1,0:T(8,128)(2,1)S(1)} %late2.1), channel_id=1, source_target_pairs={{0,4},{1,5},{2,6},{3,7},{4,0},{5,1},{6,2},{7,3},{8,12},{9,13},{10,... | collective-permute-start | bytes 2752520 | tf_op jit(solution)/shard_map/ppermute | solution.py:24
  62.0 1.7 %collective-permute-done.13.early_ref = bf16[512,768]{1,0:T(8,128)(2,1)S(1)} collective-permute-done((bf16[512,768]{1,0:T(8,128)(2,1)S(1)}, bf16[512,768]{1,0:T(8,128)(2,1)S(1)}, u32[]{:S(2)}, u32[]{:S(2)}) %collective-permute-start.13) | collective-permute-done | bytes 786464 | tf_op jit(solution)/shard_map/ppermute | solution.py:24
  63.7 2.1 %collective-permute-start.14 = (bf16[512,896]{1,0:T(8,128)(2,1)S(1)}, bf16[512,896]{1,0:T(8,128)(2,1)S(1)}, u32[]{:S(2)}, u32[]{:S(2)}) collective-permute-start(bf16[512,896]{1,0:T(8,128)(2,1)S(1)} %late3.1), channel_id=1, source_target_pairs={{0,24},{1,25},{2,26},{3,27},{4,28},{5,29},{6,30},{7,31},{8,16},{9,... | collective-permute-start | bytes 2752520 | tf_op jit(solution)/shard_map/ppermute | solution.py:24
  65.8 2.8 %keep0.1.keep_ref = f32[512,1536]{1,0:T(8,128)S(1)} custom-call(bf16[1024,1024]{1,0:T(8,128)(2,1)S(1)} %assemble.1.codes_ref, bf16[2,512,8192]{2,1,0:T(8,128)(2,1)S(1)} %get-tuple-element.63.w_ref), custom_call_target="tpu_custom_call" | custom-call | flops 1000 | bytes 1000 | tf_op jit(solution)/shard_map/keep0/pallas_call | solution.py:233
  68.6 3.2 %keep3.1.keep_ref = f32[512,1664]{1,0:T(8,128)S(1)} custom-call(bf16[1024,1024]{1,0:T(8,128)(2,1)S(1)} %assemble.1.codes_ref, bf16[2,512,8192]{2,1,0:T(8,128)(2,1)S(1)} %get-tuple-element.63.w_ref), custom_call_target="tpu_custom_call" | custom-call | flops 1000 | bytes 1000 | tf_op jit(solution)/shard_map/keep3/pallas_call | solution.py:233
  71.8 3.2 %keep2.1.keep_ref = f32[512,1664]{1,0:T(8,128)S(1)} custom-call(bf16[1024,1024]{1,0:T(8,128)(2,1)S(1)} %assemble.1.codes_ref, bf16[2,512,8192]{2,1,0:T(8,128)(2,1)S(1)} %get-tuple-element.63.w_ref), custom_call_target="tpu_custom_call" | custom-call | flops 1000 | bytes 1000 | tf_op jit(solution)/shard_map/keep2/pallas_call | solution.py:233
  75.0 3.2 %keep1.1.keep_ref = f32[512,1664]{1,0:T(8,128)S(1)} custom-call(bf16[1024,1024]{1,0:T(8,128)(2,1)S(1)} %assemble.1.codes_ref, bf16[2,512,8192]{2,1,0:T(8,128)(2,1)S(1)} %get-tuple-element.63.w_ref), custom_call_target="tpu_custom_call" | custom-call | flops 1000 | bytes 1000 | tf_op jit(solution)/shard_map/keep1/pallas_call | solution.py:233
  78.5 1.1 collective-permute-start.8
  79.6 3.2 %keep4.1.keep_ref = f32[512,1664]{1,0:T(8,128)S(1)} custom-call(bf16[1024,1024]{1,0:T(8,128)(2,1)S(1)} %assemble.1.codes_ref, bf16[2,512,8192]{2,1,0:T(8,128)(2,1)S(1)} %get-tuple-element.63.w_ref), custom_call_target="tpu_custom_call" | custom-call | flops 1000 | bytes 1000 | tf_op jit(solution)/shard_map/keep4/pallas_call | solution.py:233
  85.2 2.1 %collective-permute-start.15 = (bf16[256,1664]{1,0:T(8,128)(2,1)S(1)}, bf16[256,1664]{1,0:T(8,128)(2,1)S(1)}, u32[]{:S(2)}, u32[]{:S(2)}) collective-permute-start(bf16[256,1664]{1,0:T(8,128)(2,1)S(1)} %get-tuple-element.88), channel_id=1, source_target_pairs={{0,24},{1,25},{2,26},{3,27},{4,28},{5,29},{6,30},{7,31},{8,16},{9,... | collective-permute-start | bytes 2555912 | tf_op jit(solution)/shard_map/ppermute | solution.py:24
  87.6 1.2 collective-permute-start.20
  88.9 7.0 %collective-permute-done.8 = bf16[256,1536]{1,0:T(8,128)(2,1)S(1)} collective-permute-done((bf16[256,1536]{1,0:T(8,128)(2,1)S(1)}, bf16[256,1536]{1,0:T(8,128)(2,1)S(1)}, u32[]{:S(2)}, u32[]{:S(2)}) %collective-permute-start.8) | collective-permute-done | bytes 786464 | tf_op jit(solution)/shard_map/ppermute | solution.py:24
  96.1 5.5 %collective-permute-done.24 = bf16[256,1664]{1,0:T(8,128)(2,1)S(1)} collective-permute-done((bf16[256,1664]{1,0:T(8,128)(2,1)S(1)}, bf16[256,1664]{1,0:T(8,128)(2,1)S(1)}, u32[]{:S(2)}, u32[]{:S(2)}) %collective-permute-start.24) | collective-permute-done | bytes 852000 | tf_op jit(solution)/shard_map/ppermute | solution.py:24
  101.8 1.1 collective-permute-start.28
  104.7 2.4 %collective-permute-start.16 = (bf16[128,1664]{1,0:T(8,128)(2,1)S(1)}, bf16[128,1664]{1,0:T(8,128)(2,1)S(1)}, u32[]{:S(2)}, u32[]{:S(2)}) collective-permute-start(bf16[128,1664]{1,0:T(8,128)(2,1)S(1)} %slice.218), channel_id=1, source_target_pairs={{0,24},{1,25},{2,26},{3,27},{4,28},{5,29},{6,30},{7,31},{8,16},{9,... | collective-permute-start | bytes 1277960 | tf_op jit(solution)/shard_map/ppermute | solution.py:24
  107.4 1.2 collective-permute-start.21
  108.6 3.4 %collective-permute-done.12 = bf16[128,1536]{1,0:T(8,128)(2,1)S(1)} collective-permute-done((bf16[128,1536]{1,0:T(8,128)(2,1)S(1)}, bf16[128,1536]{1,0:T(8,128)(2,1)S(1)}, u32[]{:S(2)}, u32[]{:S(2)}) %collective-permute-start.12) | collective-permute-done | bytes 393248 | tf_op jit(solution)/shard_map/ppermute | solution.py:24
  112.8 2.5 %collective-permute-done.16 = bf16[128,1664]{1,0:T(8,128)(2,1)S(1)} collective-permute-done((bf16[128,1664]{1,0:T(8,128)(2,1)S(1)}, bf16[128,1664]{1,0:T(8,128)(2,1)S(1)}, u32[]{:S(2)}, u32[]{:S(2)}) %collective-permute-start.16) | collective-permute-done | bytes 426016 | tf_op jit(solution)/shard_map/ppermute | solution.py:24
  115.3 2.1 %collective-permute-start.17 = (bf16[64,1536]{1,0:T(8,128)(2,1)S(1)}, bf16[64,1536]{1,0:T(8,128)(2,1)S(1)}, u32[]{:S(2)}, u32[]{:S(2)}) collective-permute-start(bf16[64,1536]{1,0:T(8,128)(2,1)S(1)} %slice.224), channel_id=1, source_target_pairs={{0,24},{1,25},{2,26},{3,27},{4,28},{5,29},{6,30},{7,31},{8,16},{9,... | collective-permute-start | bytes 589832 | tf_op jit(solution)/shard_map/ppermute | solution.py:24
  117.6 1.1 collective-permute-start.29
  120.2 3.2 %collective-permute-done.17 = bf16[64,1536]{1,0:T(8,128)(2,1)S(1)} collective-permute-done((bf16[64,1536]{1,0:T(8,128)(2,1)S(1)}, bf16[64,1536]{1,0:T(8,128)(2,1)S(1)}, u32[]{:S(2)}, u32[]{:S(2)}) %collective-permute-start.17) | collective-permute-done | bytes 196640 | tf_op jit(solution)/shard_map/ppermute | solution.py:24
  123.5 2.2 %collective-permute-start.33 = (bf16[32,1664]{1,0:T(8,128)(2,1)S(1)}, bf16[32,1664]{1,0:T(8,128)(2,1)S(1)}, u32[]{:S(2)}, u32[]{:S(2)}) collective-permute-start(bf16[32,1664]{1,0:T(8,128)(2,1)S(1)} %slice.225), channel_id=1, source_target_pairs={{0,24},{1,25},{2,26},{3,27},{4,28},{5,29},{6,30},{7,31},{8,16},{9,... | collective-permute-start | bytes 319496 | tf_op jit(solution)/shard_map/ppermute | solution.py:24
  126.4 1.1 collective-permute-start.30
  127.5 1.1 collective-permute-start.23
  129.6 3.7 %collective-permute-done.23 = bf16[32,1536]{1,0:T(8,128)(2,1)S(1)} collective-permute-done((bf16[32,1536]{1,0:T(8,128)(2,1)S(1)}, bf16[32,1536]{1,0:T(8,128)(2,1)S(1)}, u32[]{:S(2)}, u32[]{:S(2)}) %collective-permute-start.23) | collective-permute-done | bytes 98336 | tf_op jit(solution)/shard_map/ppermute | solution.py:24
  (103 shorter events, 15.0 us)
Async XLA Ops:
  0.0 10.9 %copy-start = (s32[2,1024]{1,0:T(2,128)S(1)}, s32[2,1024]{1,0:T(2,128)}, u32[]{:S(2)}) copy-start(s32[2,1024]{1,0:T(2,128)} %param.17) | copy-start | bytes 24580
  0.0 10.8 %copy-start.6 = (s32[32]{0:T(128)S(1)}, s32[32]{0:T(128)}, u32[]{:S(2)}) copy-start(s32[32]{0:T(128)} %constant.82.clone) | copy-start | bytes 388
  0.0 10.9 %copy-start.4 = (s32[2,1024]{1,0:T(2,128)S(1)}, s32[2,1024]{1,0:T(2,128)}, u32[]{:S(2)}) copy-start(s32[2,1024]{1,0:T(2,128)} %param.19) | copy-start | bytes 24580
  0.0 10.9 %copy-start.5 = (s32[2,1024]{1,0:T(2,128)S(1)}, s32[2,1024]{1,0:T(2,128)}, u32[]{:S(2)}) copy-start(s32[2,1024]{1,0:T(2,128)} %param.18) | copy-start | bytes 24580
  0.0 12.3 %copy-start.3 = (f32[16]{0:T(128)S(1)}, f32[16]{0:T(128)}, u32[]{:S(2)}) copy-start(f32[16]{0:T(128)} %param.20) | copy-start | bytes 196
  9.1 3.3 %collective-permute-start = (f32[1024,256]{1,0:T(8,128)S(1)}, f32[1024,256]{1,0:T(8,128)S(1)}, u32[]{:S(2)}, u32[]{:S(2)}) collective-permute-start(f32[1024,256]{1,0:T(8,128)S(1)} %get-tuple-element.60), channel_id=1, source_target_pairs={{0,32},{32,0},{64,96},{96,64},{1,33},{33,1},{65,97},{97,65},{2,34}... | collective-permute-start | bytes 3145736 | tf_op jit(solution)/shard_map/ppermute | solution.py:24
  12.8 3.8 %collective-permute-start.1 = (bf16[1024,256]{1,0:T(8,128)(2,1)S(1)}, bf16[1024,256]{1,0:T(8,128)(2,1)S(1)}, u32[]{:S(2)}, u32[]{:S(2)}) collective-permute-start(bf16[1024,256]{1,0:T(8,128)(2,1)S(1)} %select_convert_fusion.mine_ref.own_ref), channel_id=1, source_target_pairs={{0,32},{32,0},{64,96},{96,64},{1,33},{33,1},{65,97},{97,65},{2,34}... | collective-permute-start | bytes 1572872 | tf_op jit(solution)/shard_map/ppermute | solution.py:24
  13.3 15.5 %collective-permute-start.2 = (bf16[1024,256]{1,0:T(8,128)(2,1)S(1)}, bf16[1024,256]{1,0:T(8,128)(2,1)S(1)}, u32[]{:S(2)}, u32[]{:S(2)}) collective-permute-start(bf16[1024,256]{1,0:T(8,128)(2,1)S(1)} %select_convert_fusion.mine_ref.own_ref), channel_id=1, source_target_pairs={{0,64},{32,96},{64,0},{96,32},{1,65},{33,97},{65,1},{97,33},{2,66}... | collective-permute-start | bytes 1572872 | tf_op jit(solution)/shard_map/ppermute | solution.py:24
  28.8 1.9 %collective-permute-start.3 = (bf16[1024,256]{1,0:T(8,128)(2,1)S(1)}, bf16[1024,256]{1,0:T(8,128)(2,1)S(1)}, u32[]{:S(2)}, u32[]{:S(2)}) collective-permute-start(bf16[1024,256]{1,0:T(8,128)(2,1)S(1)} %collective-permute-done.2.far_ref), channel_id=1, source_target_pairs={{0,32},{32,0},{64,96},{96,64},{1,33},{33,1},{65,97},{97,65},{2,34}... | collective-permute-start | bytes 1572872 | tf_op jit(solution)/shard_map/ppermute | solution.py:24
  32.0 21.1 %collective-permute-start.6 = (bf16[512,768]{1,0:T(8,128)(2,1)S(1)}, bf16[512,768]{1,0:T(8,128)(2,1)S(1)}, u32[]{:S(2)}, u32[]{:S(2)}) collective-permute-start(bf16[512,768]{1,0:T(8,128)(2,1)S(1)} %early1.1), channel_id=1, source_target_pairs={{0,1},{1,0},{2,3},{3,2},{4,5},{5,4},{6,7},{7,6},{8,9},{9,8},{10,11... | collective-permute-start | bytes 2359304 | tf_op jit(solution)/shard_map/ppermute | solution.py:24
  35.0 19.4 %collective-permute-start.4 = (bf16[512,768]{1,0:T(8,128)(2,1)S(1)}, bf16[512,768]{1,0:T(8,128)(2,1)S(1)}, u32[]{:S(2)}, u32[]{:S(2)}) collective-permute-start(bf16[512,768]{1,0:T(8,128)(2,1)S(1)} %early0.1), channel_id=1, source_target_pairs={{0,8},{1,9},{2,10},{3,11},{4,12},{5,13},{6,14},{7,15},{8,0},{9,1},... | collective-permute-start | bytes 2359304 | tf_op jit(solution)/shard_map/ppermute | solution.py:24
  37.6 20.3 %collective-permute-start.18 = (bf16[512,768]{1,0:T(8,128)(2,1)S(1)}, bf16[512,768]{1,0:T(8,128)(2,1)S(1)}, u32[]{:S(2)}, u32[]{:S(2)}) collective-permute-start(bf16[512,768]{1,0:T(8,128)(2,1)S(1)} %early4.1), channel_id=1, source_target_pairs={{0,3},{1,2},{2,1},{3,0},{4,7},{5,6},{6,5},{7,4},{8,11},{9,10},{10,... | collective-permute-start | bytes 2359304 | tf_op jit(solution)/shard_map/ppermute | solution.py:24
  41.1 19.3 %collective-permute-start.9 = (bf16[512,768]{1,0:T(8,128)(2,1)S(1)}, bf16[512,768]{1,0:T(8,128)(2,1)S(1)}, u32[]{:S(2)}, u32[]{:S(2)}) collective-permute-start(bf16[512,768]{1,0:T(8,128)(2,1)S(1)} %early2.1), channel_id=1, source_target_pairs={{0,4},{1,5},{2,6},{3,7},{4,0},{5,1},{6,2},{7,3},{8,12},{9,13},{10,... | collective-permute-start | bytes 2359304 | tf_op jit(solution)/shard_map/ppermute | solution.py:24
  43.8 19.9 %collective-permute-start.13 = (bf16[512,768]{1,0:T(8,128)(2,1)S(1)}, bf16[512,768]{1,0:T(8,128)(2,1)S(1)}, u32[]{:S(2)}, u32[]{:S(2)}) collective-permute-start(bf16[512,768]{1,0:T(8,128)(2,1)S(1)} %early3.1), channel_id=1, source_target_pairs={{0,24},{1,25},{2,26},{3,27},{4,28},{5,29},{6,30},{7,31},{8,16},{9,... | collective-permute-start | bytes 2359304 | tf_op jit(solution)/shard_map/ppermute | solution.py:24
  53.1 25.4 %collective-permute-start.7 = (bf16[512,896]{1,0:T(8,128)(2,1)S(1)}, bf16[512,896]{1,0:T(8,128)(2,1)S(1)}, u32[]{:S(2)}, u32[]{:S(2)}) collective-permute-start(bf16[512,896]{1,0:T(8,128)(2,1)S(1)} %late1.1), channel_id=1, source_target_pairs={{0,1},{1,0},{2,3},{3,2},{4,5},{5,4},{6,7},{7,6},{8,9},{9,8},{10,11... | collective-permute-start | bytes 2752520 | tf_op jit(solution)/shard_map/ppermute | solution.py:24
  54.4 23.8 %collective-permute-start.5 = (bf16[512,768]{1,0:T(8,128)(2,1)S(1)}, bf16[512,768]{1,0:T(8,128)(2,1)S(1)}, u32[]{:S(2)}, u32[]{:S(2)}) collective-permute-start(bf16[512,768]{1,0:T(8,128)(2,1)S(1)} %late0.1), channel_id=1, source_target_pairs={{0,8},{1,9},{2,10},{3,11},{4,12},{5,13},{6,14},{7,15},{8,0},{9,1},... | collective-permute-start | bytes 2359304 | tf_op jit(solution)/shard_map/ppermute | solution.py:24
  57.9 24.9 %collective-permute-start.19 = (bf16[512,896]{1,0:T(8,128)(2,1)S(1)}, bf16[512,896]{1,0:T(8,128)(2,1)S(1)}, u32[]{:S(2)}, u32[]{:S(2)}) collective-permute-start(bf16[512,896]{1,0:T(8,128)(2,1)S(1)} %late4.1), channel_id=1, source_target_pairs={{0,3},{1,2},{2,1},{3,0},{4,7},{5,6},{6,5},{7,4},{8,11},{9,10},{10,... | collective-permute-start | bytes 2752520 | tf_op jit(solution)/shard_map/ppermute | solution.py:24
  60.4 23.1 %collective-permute-start.10 = (bf16[512,896]{1,0:T(8,128)(2,1)S(1)}, bf16[512,896]{1,0:T(8,128)(2,1)S(1)}, u32[]{:S(2)}, u32[]{:S(2)}) collective-permute-start(bf16[512,896]{1,0:T(8,128)(2,1)S(1)} %late2.1), channel_id=1, source_target_pairs={{0,4},{1,5},{2,6},{3,7},{4,0},{5,1},{6,2},{7,3},{8,12},{9,13},{10,... | collective-permute-start | bytes 2752520 | tf_op jit(solution)/shard_map/ppermute | solution.py:24
  63.7 21.6 %collective-permute-start.14 = (bf16[512,896]{1,0:T(8,128)(2,1)S(1)}, bf16[512,896]{1,0:T(8,128)(2,1)S(1)}, u32[]{:S(2)}, u32[]{:S(2)}) collective-permute-start(bf16[512,896]{1,0:T(8,128)(2,1)S(1)} %late3.1), channel_id=1, source_target_pairs={{0,24},{1,25},{2,26},{3,27},{4,28},{5,29},{6,30},{7,31},{8,16},{9,... | collective-permute-start | bytes 2752520 | tf_op jit(solution)/shard_map/ppermute | solution.py:24
  78.5 17.4 %collective-permute-start.8 = (bf16[256,1536]{1,0:T(8,128)(2,1)S(1)}, bf16[256,1536]{1,0:T(8,128)(2,1)S(1)}, u32[]{:S(2)}, u32[]{:S(2)}) collective-permute-start(bf16[256,1536]{1,0:T(8,128)(2,1)S(1)} %get-tuple-element.74), channel_id=1, source_target_pairs={{0,1},{1,0},{2,3},{3,2},{4,5},{5,4},{6,7},{7,6},{8,9},{9,8},{10,11... | collective-permute-start | bytes 2359304 | tf_op jit(solution)/shard_map/ppermute | solution.py:24
  83.1 18.5 %collective-permute-start.24 = (bf16[256,1664]{1,0:T(8,128)(2,1)S(1)}, bf16[256,1664]{1,0:T(8,128)(2,1)S(1)}, u32[]{:S(2)}, u32[]{:S(2)}) collective-permute-start(bf16[256,1664]{1,0:T(8,128)(2,1)S(1)} %get-tuple-element.102), channel_id=1, source_target_pairs={{0,8},{1,9},{2,10},{3,11},{4,12},{5,13},{6,14},{7,15},{8,0},{9,1},... | collective-permute-start | bytes 2555912 | tf_op jit(solution)/shard_map/ppermute | solution.py:24
  83.5 19.4 %collective-permute-start.11 = (bf16[256,1664]{1,0:T(8,128)(2,1)S(1)}, bf16[256,1664]{1,0:T(8,128)(2,1)S(1)}, u32[]{:S(2)}, u32[]{:S(2)}) collective-permute-start(bf16[256,1664]{1,0:T(8,128)(2,1)S(1)} %get-tuple-element.80), channel_id=1, source_target_pairs={{0,4},{1,5},{2,6},{3,7},{4,0},{5,1},{6,2},{7,3},{8,12},{9,13},{10,... | collective-permute-start | bytes 2555912 | tf_op jit(solution)/shard_map/ppermute | solution.py:24
  85.2 19.2 %collective-permute-start.15 = (bf16[256,1664]{1,0:T(8,128)(2,1)S(1)}, bf16[256,1664]{1,0:T(8,128)(2,1)S(1)}, u32[]{:S(2)}, u32[]{:S(2)}) collective-permute-start(bf16[256,1664]{1,0:T(8,128)(2,1)S(1)} %get-tuple-element.88), channel_id=1, source_target_pairs={{0,24},{1,25},{2,26},{3,27},{4,28},{5,29},{6,30},{7,31},{8,16},{9,... | collective-permute-start | bytes 2555912 | tf_op jit(solution)/shard_map/ppermute | solution.py:24
  87.6 19.5 %collective-permute-start.20 = (bf16[256,1664]{1,0:T(8,128)(2,1)S(1)}, bf16[256,1664]{1,0:T(8,128)(2,1)S(1)}, u32[]{:S(2)}, u32[]{:S(2)}) collective-permute-start(bf16[256,1664]{1,0:T(8,128)(2,1)S(1)} %get-tuple-element.96), channel_id=1, source_target_pairs={{0,3},{1,2},{2,1},{3,0},{4,7},{5,6},{6,5},{7,4},{8,11},{9,10},{10,... | collective-permute-start | bytes 2555912 | tf_op jit(solution)/shard_map/ppermute | solution.py:24
  101.8 10.4 %collective-permute-start.28 = (bf16[128,1664]{1,0:T(8,128)(2,1)S(1)}, bf16[128,1664]{1,0:T(8,128)(2,1)S(1)}, u32[]{:S(2)}, u32[]{:S(2)}) collective-permute-start(bf16[128,1664]{1,0:T(8,128)(2,1)S(1)} %slice.215), channel_id=1, source_target_pairs={{0,1},{1,0},{2,3},{3,2},{4,5},{5,4},{6,7},{7,6},{8,9},{9,8},{10,11... | collective-permute-start | bytes 1277960 | tf_op jit(solution)/shard_map/ppermute | solution.py:24
  102.9 9.2 %collective-permute-start.12 = (bf16[128,1536]{1,0:T(8,128)(2,1)S(1)}, bf16[128,1536]{1,0:T(8,128)(2,1)S(1)}, u32[]{:S(2)}, u32[]{:S(2)}) collective-permute-start(bf16[128,1536]{1,0:T(8,128)(2,1)S(1)} %slice.219), channel_id=1, source_target_pairs={{0,4},{1,5},{2,6},{3,7},{4,0},{5,1},{6,2},{7,3},{8,12},{9,13},{10,... | collective-permute-start | bytes 1179656 | tf_op jit(solution)/shard_map/ppermute | solution.py:24
  104.7 10.7 %collective-permute-start.16 = (bf16[128,1664]{1,0:T(8,128)(2,1)S(1)}, bf16[128,1664]{1,0:T(8,128)(2,1)S(1)}, u32[]{:S(2)}, u32[]{:S(2)}) collective-permute-start(bf16[128,1664]{1,0:T(8,128)(2,1)S(1)} %slice.218), channel_id=1, source_target_pairs={{0,24},{1,25},{2,26},{3,27},{4,28},{5,29},{6,30},{7,31},{8,16},{9,... | collective-permute-start | bytes 1277960 | tf_op jit(solution)/shard_map/ppermute | solution.py:24
  107.3 10.2 %collective-permute-start.25 = (bf16[128,1664]{1,0:T(8,128)(2,1)S(1)}, bf16[128,1664]{1,0:T(8,128)(2,1)S(1)}, u32[]{:S(2)}, u32[]{:S(2)}) collective-permute-start(bf16[128,1664]{1,0:T(8,128)(2,1)S(1)} %slice.216), channel_id=1, source_target_pairs={{0,8},{1,9},{2,10},{3,11},{4,12},{5,13},{6,14},{7,15},{8,0},{9,1},... | collective-permute-start | bytes 1277960 | tf_op jit(solution)/shard_map/ppermute | solution.py:24
  107.4 11.4 %collective-permute-start.21 = (bf16[128,1664]{1,0:T(8,128)(2,1)S(1)}, bf16[128,1664]{1,0:T(8,128)(2,1)S(1)}, u32[]{:S(2)}, u32[]{:S(2)}) collective-permute-start(bf16[128,1664]{1,0:T(8,128)(2,1)S(1)} %slice.217), channel_id=1, source_target_pairs={{0,3},{1,2},{2,1},{3,0},{4,7},{5,6},{6,5},{7,4},{8,11},{9,10},{10,... | collective-permute-start | bytes 1277960 | tf_op jit(solution)/shard_map/ppermute | solution.py:24
  112.3 11.1 %collective-permute-start.31 = (bf16[64,1664]{1,0:T(8,128)(2,1)S(1)}, bf16[64,1664]{1,0:T(8,128)(2,1)S(1)}, u32[]{:S(2)}, u32[]{:S(2)}) collective-permute-start(bf16[64,1664]{1,0:T(8,128)(2,1)S(1)} %slice.220), channel_id=1, source_target_pairs={{0,4},{1,5},{2,6},{3,7},{4,0},{5,1},{6,2},{7,3},{8,12},{9,13},{10,... | collective-permute-start | bytes 638984 | tf_op jit(solution)/shard_map/ppermute | solution.py:24
  115.3 8.0 %collective-permute-start.17 = (bf16[64,1536]{1,0:T(8,128)(2,1)S(1)}, bf16[64,1536]{1,0:T(8,128)(2,1)S(1)}, u32[]{:S(2)}, u32[]{:S(2)}) collective-permute-start(bf16[64,1536]{1,0:T(8,128)(2,1)S(1)} %slice.224), channel_id=1, source_target_pairs={{0,24},{1,25},{2,26},{3,27},{4,28},{5,29},{6,30},{7,31},{8,16},{9,... | collective-permute-start | bytes 589832 | tf_op jit(solution)/shard_map/ppermute | solution.py:24
  117.6 8.1 %collective-permute-start.29 = (bf16[64,1664]{1,0:T(8,128)(2,1)S(1)}, bf16[64,1664]{1,0:T(8,128)(2,1)S(1)}, u32[]{:S(2)}, u32[]{:S(2)}) collective-permute-start(bf16[64,1664]{1,0:T(8,128)(2,1)S(1)} %slice.221), channel_id=1, source_target_pairs={{0,1},{1,0},{2,3},{3,2},{4,5},{5,4},{6,7},{7,6},{8,9},{9,8},{10,11... | collective-permute-start | bytes 638984 | tf_op jit(solution)/shard_map/ppermute | solution.py:24
  118.9 7.4 %collective-permute-start.26 = (bf16[64,1664]{1,0:T(8,128)(2,1)S(1)}, bf16[64,1664]{1,0:T(8,128)(2,1)S(1)}, u32[]{:S(2)}, u32[]{:S(2)}) collective-permute-start(bf16[64,1664]{1,0:T(8,128)(2,1)S(1)} %slice.222), channel_id=1, source_target_pairs={{0,8},{1,9},{2,10},{3,11},{4,12},{5,13},{6,14},{7,15},{8,0},{9,1},... | collective-permute-start | bytes 638984 | tf_op jit(solution)/shard_map/ppermute | solution.py:24
  119.6 7.9 %collective-permute-start.22 = (bf16[64,1664]{1,0:T(8,128)(2,1)S(1)}, bf16[64,1664]{1,0:T(8,128)(2,1)S(1)}, u32[]{:S(2)}, u32[]{:S(2)}) collective-permute-start(bf16[64,1664]{1,0:T(8,128)(2,1)S(1)} %slice.223), channel_id=1, source_target_pairs={{0,3},{1,2},{2,1},{3,0},{4,7},{5,6},{6,5},{7,4},{8,11},{9,10},{10,... | collective-permute-start | bytes 638984 | tf_op jit(solution)/shard_map/ppermute | solution.py:24
  123.5 10.0 %collective-permute-start.33 = (bf16[32,1664]{1,0:T(8,128)(2,1)S(1)}, bf16[32,1664]{1,0:T(8,128)(2,1)S(1)}, u32[]{:S(2)}, u32[]{:S(2)}) collective-permute-start(bf16[32,1664]{1,0:T(8,128)(2,1)S(1)} %slice.225), channel_id=1, source_target_pairs={{0,24},{1,25},{2,26},{3,27},{4,28},{5,29},{6,30},{7,31},{8,16},{9,... | collective-permute-start | bytes 319496 | tf_op jit(solution)/shard_map/ppermute | solution.py:24
  125.8 7.7 %collective-permute-start.32 = (bf16[32,1664]{1,0:T(8,128)(2,1)S(1)}, bf16[32,1664]{1,0:T(8,128)(2,1)S(1)}, u32[]{:S(2)}, u32[]{:S(2)}) collective-permute-start(bf16[32,1664]{1,0:T(8,128)(2,1)S(1)} %slice.226), channel_id=1, source_target_pairs={{0,4},{1,5},{2,6},{3,7},{4,0},{5,1},{6,2},{7,3},{8,12},{9,13},{10,... | collective-permute-start | bytes 319496 | tf_op jit(solution)/shard_map/ppermute | solution.py:24
  126.4 7.2 %copy-start.2 = (f32[1,8192]{1,0:T(1,128)S(1)}, f32[1,8192]{1,0:T(1,128)}, u32[]{:S(2)}) copy-start(f32[1,8192]{1,0:T(1,128)} %param.16) | copy-start | bytes 98308
  126.4 7.1 %collective-permute-start.30 = (bf16[32,1664]{1,0:T(8,128)(2,1)S(1)}, bf16[32,1664]{1,0:T(8,128)(2,1)S(1)}, u32[]{:S(2)}, u32[]{:S(2)}) collective-permute-start(bf16[32,1664]{1,0:T(8,128)(2,1)S(1)} %slice.227), channel_id=1, source_target_pairs={{0,1},{1,0},{2,3},{3,2},{4,5},{5,4},{6,7},{7,6},{8,9},{9,8},{10,11... | collective-permute-start | bytes 319496 | tf_op jit(solution)/shard_map/ppermute | solution.py:24
  127.5 5.8 %collective-permute-start.23 = (bf16[32,1536]{1,0:T(8,128)(2,1)S(1)}, bf16[32,1536]{1,0:T(8,128)(2,1)S(1)}, u32[]{:S(2)}, u32[]{:S(2)}) collective-permute-start(bf16[32,1536]{1,0:T(8,128)(2,1)S(1)} %slice.229), channel_id=1, source_target_pairs={{0,3},{1,2},{2,1},{3,0},{4,7},{5,6},{6,5},{7,4},{8,11},{9,10},{10,... | collective-permute-start | bytes 294920 | tf_op jit(solution)/shard_map/ppermute | solution.py:24
  128.6 4.8 %collective-permute-start.27 = (bf16[32,1664]{1,0:T(8,128)(2,1)S(1)}, bf16[32,1664]{1,0:T(8,128)(2,1)S(1)}, u32[]{:S(2)}, u32[]{:S(2)}) collective-permute-start(bf16[32,1664]{1,0:T(8,128)(2,1)S(1)} %slice.228), channel_id=1, source_target_pairs={{0,8},{1,9},{2,10},{3,11},{4,12},{5,13},{6,14},{7,15},{8,0},{9,1},... | collective-permute-start | bytes 319496 | tf_op jit(solution)/shard_map/ppermute | solution.py:24
  133.4 1.0 copy-start.1

commit v6 on v5

--- a/solution.py
+++ b/solution.py
@@ -12,8 +12,8 @@
 STEPS = len(LINKS)
 LANES, TILE = 128, 256
 PARTS = (12, 13, 13, 13, 13)
-EARLY = (6, 6, 6, 6, 6)
-READY = 4
+AHEAD = 4
+READY = 5
 VMEM = pl.BlockSpec(memory_space=pltpu.VMEM)
 HBM = pl.BlockSpec(memory_space=pltpu.HBM)
 MIB = 1 << 20
@@ -197,6 +197,31 @@
     copy_weights(dec_hbm, 1 - source, far, far_sem, False)
 
 
+def own_rest_kernel(mine_ref, sib_ref, w_ref, acc, codes, lhs, *, part, at):
+    source = lax.axis_index("layer") // 2
+    join_kernel(mine_ref, sib_ref, codes)
+    gather_rows(codes, lhs, send_blocks(part))
+
+    def body(c, n):
+        acc[:, pl.ds(c, n)] = product(lhs, w_ref.at[source], at + c, n)
+
+    over_tiles(0, acc.shape[1], body)
+
+
+def own_rest(mine, sib, w, part, at, wide):
+    tokens, hw = mine.shape
+    n = tokens // 2
+    return call_tiny(
+        functools.partial(own_rest_kernel, part=part, at=at),
+        jax.ShapeDtypeStruct((n, wide), F32),
+        [pltpu.VMEM((tokens, 2 * hw), BF16), pltpu.VMEM((n, 2 * hw), BF16)],
+        "rest",
+        mine,
+        sib,
+        w,
+    )
+
+
 def own_part(mine, sib, dec, spans):
     tokens, hw = mine.shape
     _, sources, depth, wide = dec.shape
@@ -242,7 +267,7 @@
     )(*args)
 
 
-def send_early_kernel(codes_ref, w_ref, acc_ref, send_ref, lhs, *, blocks, at):
+def decode_send_kernel(codes_ref, w_ref, acc_ref, send_ref, lhs, *, blocks, at):
     other = 1 - lax.axis_index("layer") // 2
     depth = lhs.shape[1]
     gather_rows(codes_ref, lhs, blocks, pl.ds(pl.multiple_of(other * depth, depth), depth))
@@ -255,13 +280,13 @@
     over_tiles(0, send_ref.shape[1], body)
 
 
-def send_early(codes, w, acc, part, at):
+def decode_send(codes, w, acc, part, at):
     n, wide = acc.shape
     return call_tiny(
-        functools.partial(send_early_kernel, blocks=send_blocks(part), at=at),
+        functools.partial(decode_send_kernel, blocks=send_blocks(part), at=at),
         jax.ShapeDtypeStruct((n, wide), BF16),
         [pltpu.VMEM((n, codes.shape[1] // 2), BF16)],
-        f"early{part}",
+        f"send{part}",
         codes,
         w,
         acc,
@@ -290,28 +315,16 @@
     )
 
 
-def merge_kernel(keep_ref, early_ref, late_ref, new_ref, send_ref):
+def merge_kernel(keep_ref, got_ref, new_ref, send_ref):
     m = new_ref.shape[0]
-    split = early_ref.shape[1]
-    for got, cols in ((early_ref, pl.ds(0, split)), (late_ref, pl.ds(split, late_ref.shape[1]))):
-        new_ref[:, cols] = keep_ref[:m, cols] + got[:m, :].astype(F32)
-        send_ref[:, cols] = (keep_ref[m:, cols] + got[m:, :].astype(F32)).astype(BF16)
-
-
-def merge(keep, early, late):
+    new_ref[...] = keep_ref[:m, :] + got_ref[:m, :].astype(F32)
+    send_ref[...] = (keep_ref[m:, :] + got_ref[m:, :].astype(F32)).astype(BF16)
+
+
+def merge(keep, got):
     n, wide = keep.shape
-    return pl.pallas_call(
-        merge_kernel,
-        out_shape=(
-            jax.ShapeDtypeStruct((n // 2, wide), F32),
-            jax.ShapeDtypeStruct((n // 2, wide), BF16),
-        ),
-        in_specs=[VMEM] * 3,
-        out_specs=[VMEM] * 2,
-        compiler_params=pltpu.CompilerParams(vmem_limit_bytes=8 * MIB),
-        cost_estimate=pl.CostEstimate(flops=1000, bytes_accessed=1000, transcendentals=0),
-        name="merge",
-    )(keep, early, late)
+    out = tuple(jax.ShapeDtypeStruct((n // 2, wide), dtype) for dtype in (F32, BF16))
+    return call_tiny(merge_kernel, out, [], "merge", keep, got)
 
 
 def shards(
@@ -363,10 +376,13 @@
     own_sib = xor_swap(own, "layer", 1)
 
     starts = [sum(PARTS[:p]) * LANES for p in range(STEPS)]
-    spans = [(p, starts[p], EARLY[p] * LANES) for p in range(STEPS)]
-    weights, accs = own_part(own, own_sib, dec_weight, spans)
+    spans = [(p, starts[p], PARTS[p] * LANES) for p in range(STEPS)]
+    weights, accs = own_part(own, own_sib, dec_weight, spans[:AHEAD])
     far, weights = lax.optimization_barrier((xor_swap(own, "layer", 2), weights))
-    codes = assemble(own, own_sib, far, xor_swap(far, "layer", 1))
+    far_sib = xor_swap(far, "layer", 1)
+    accs += [own_rest(own, own_sib, weights, *span) for span in spans[AHEAD:]]
+    far_sib, *accs = lax.optimization_barrier((far_sib, *accs))
+    codes = assemble(own, own_sib, far, far_sib)
 
     last = [None] * STEPS
 
@@ -376,23 +392,16 @@
         last[link] = xor_swap(data, "lat", LINKS[link])
         return last[link]
 
-    early = [
-        exchange(send_early(codes, weights, acc, p, at), p) for (p, at, _), acc in zip(spans, accs)
+    got = [
+        exchange(decode_send(codes, weights, acc, p, at), p) for (p, at, _), acc in zip(spans, accs)
     ]
-    sends = [
-        decode_rows(codes, weights, send_blocks(p), at + wide, PARTS[p] * LANES - wide, BF16, f"late{p}")
-        for p, at, wide in spans
+    keeps = [
+        decode_rows(codes, weights, keep_blocks(p), at, wide, F32, f"keep{p}") for p, at, wide in spans
     ]
-    sends[:READY] = lax.optimization_barrier(tuple(sends[:READY]))
-    late = [exchange(sends[p], p) for p in range(STEPS)]
-    keeps = [
-        decode_rows(codes, weights, keep_blocks(p), starts[p], PARTS[p] * LANES, F32, f"keep{p}")
-        for p in range(STEPS)
-    ]
-    late[0], *keeps[:READY] = lax.optimization_barrier((late[0], *keeps[:READY]))
+    got[0], *keeps[:READY] = lax.optimization_barrier((got[0], *keeps[:READY]))
     kept, out = {}, {}
     for p in range(STEPS):
-        kept[p], out[p] = merge(keeps[p], early[p], late[p])
+        kept[p], out[p] = merge(keeps[p], got[p])
     for i in range(1, STEPS):
         for p in range(STEPS):
             total = kept[p] + exchange(out[p], (p + i) % STEPS).astype(F32)

time: 135 us -> 139 us (1.030)
  Pallas kernels: 48.3 us -> 54.1 us
  starting transfers between devices: 44.1 us -> 39.8 us
  waiting for transfers between devices: 35.2 us -> 38 us
    ppermute x34 -> x29, starting transfers between devices: 44.1 us -> 39.8 us  [xor_swap(): lax.ppermute(value, axis, [(i, i ^ mask) for i in range(lax.axis_size(axi...]
    pallas_call x1, Pallas kernels: 8.27 us -> 11.9 us  [own_part(): pl.pallas_call(functools.partial(own_kernel, spans=spans), out_shape=[plt...]
    pallas_call x15 -> x16, Pallas kernels: 29.3 us -> 32.8 us  [call_tiny(): pl.pallas_call(kernel, out_shape=out_shape, in_specs=[VMEM] * len(args),...]
    ppermute x34 -> x29, waiting for transfers between devices: 35.2 us -> 38 us  [xor_swap(): lax.ppermute(value, axis, [(i, i ^ mask) for i in range(lax.axis_size(axi...]
  transfers between devices with their start and end apart: 34 -> 29, of which waited for: 14 -> 14; matrix products, arithmetic and copies ran while one was open for 4% -> 4% of each run, Pallas kernels for 28% -> 31%
where the time goes in v6:
time: 139 us
  Pallas kernels  54.1 us (39%)
  starting transfers between devices  39.8 us (29%)
  waiting for transfers between devices  38 us (27%)
  other arithmetic  2.82 us (2%)
  local copies, waits for them, and re-layouts  2.06 us (1%)
    ppermute x29, starting transfers between devices, xor_swap(): lax.ppermute(value, axis, [(i, i ^ mask) for i in range(lax.axis_size(axi...  39.8 us
    ppermute x29, waiting for transfers between devices, xor_swap(): lax.ppermute(value, axis, [(i, i ^ mask) for i in range(lax.axis_size(axi...  38 us
    pallas_call x16, Pallas kernels, call_tiny(): pl.pallas_call(kernel, out_shape=out_shape, in_specs=[VMEM] * len(args),...  32.8 us
    pallas_call x1, Pallas kernels, own_part(): pl.pallas_call(functools.partial(own_kernel, spans=spans), out_shape=[plt...  11.9 us
    pallas_call x1, Pallas kernels, encode(): pl.pallas_call(functools.partial(encode_kernel, masks=masks, rows=rows, c...  9.09 us
  transfers between devices with their start and end apart: 29, of which 14 were waited for; matrix products, arithmetic and copies ran while one was open for 4% of the time, Pallas kernels for 31%

profile of v6, /device:TPU:0, one launch (start us, length us, event | category | flops | bytes accessed | tf_op | source)
XLA Modules:
  0.0 138.7 jit_solution(11976213853691106284)
XLA Ops:
  0.0 9.1 %encode.1 = (f32[1024,256]{1,0:T(8,128)S(1)}, f32[1024,256]{1,0:T(8,128)S(1)}) custom-call(bf16[1,1024,4096]{2,1,0:T(8,128)(2,1)} %x_hbm.1, bf16[1,4096,512]{2,1,0:T(8,128)(2,1)} %w_hbm.1), custom_call_target="tpu_custom_call" | custom-call | flops 4294967296 | bytes 14680064 | tf_op jit(solution)/shard_map/encode/pallas_call | solution.py:94
  9.2 0.8 dynamic_slice.15
  10.0 0.8 dynamic_slice.16
  11.0 1.3 fusion
  13.3 3.3 %collective-permute-start.2 = (bf16[1024,256]{1,0:T(8,128)(2,1)S(1)}, bf16[1024,256]{1,0:T(8,128)(2,1)S(1)}, u32[]{:S(2)}, u32[]{:S(2)}) collective-permute-start(bf16[1024,256]{1,0:T(8,128)(2,1)S(1)} %select_convert_fusion.mine_ref.own_ref), channel_id=1, source_target_pairs={{0,64},{32,96},{64,0},{96,32},{1,65},{33,97},{65,1},{97,33},{2,66}... | collective-permute-start | bytes 1572872 | tf_op jit(solution)/shard_map/ppermute | solution.py:24
  16.6 11.9 %own.1 = (bf16[2,512,8192]{2,1,0:T(8,128)(2,1)S(1)}, f32[512,1536]{1,0:T(8,128)S(1)}, f32[512,1664]{1,0:T(8,128)S(1)}, f32[512,1664]{1,0:T(8,128)S(1)}, f32[512,1664]{1,0:T(8,128)S(1)}) custom-call(bf16[1024,256]{1,0:T(8,128)(2,1)S(1)} %select_convert_fusion.mine_ref.own_ref, bf16[1024,256]{1,0:T(8,128)(2,1)S(1)} %collective-permute-done.1.sib_ref.own_sib_ref, ...), custom_call_target="tpu_custom_call" | custom-call | flops 2147483648 | bytes 33554432 | tf_op jit(solution)/shard_map/own/pallas_call | solution.py:229
  28.8 2.3 %rest.1.acc_ref = f32[512,1664]{1,0:T(8,128)S(1)} custom-call(bf16[1024,256]{1,0:T(8,128)(2,1)S(1)} %select_convert_fusion.mine_ref.own_ref, bf16[1024,256]{1,0:T(8,128)(2,1)S(1)} %collective-permute-done.1.sib_ref.own_sib_ref, bf16[2,512,8192]{2,1,0:T(8,128)(2,1)S(1)} %get-tuple-element.64.w_ref), custom_call_target="tpu_custom_call" | custom-call | flops 1000 | bytes 1000 | tf_op jit(solution)/shard_map/rest/pallas_call | solution.py:258
  31.4 2.2 %send1.1 = bf16[512,1664]{1,0:T(8,128)(2,1)S(1)} custom-call(bf16[1024,1024]{1,0:T(8,128)(2,1)S(1)} %assemble.1.codes_ref, bf16[2,512,8192]{2,1,0:T(8,128)(2,1)S(1)} %get-tuple-element.64.w_ref, f32[512,1664]{1,0:T(8,128)S(1)} %get-tuple-element.71.acc_ref), custom_call_target="tpu_custom_call" | custom-call | flops 1000 | bytes 1000 | tf_op jit(solution)/shard_map/send1/pallas_call | solution.py:258
  33.7 2.0 %collective-permute-start.5 = (bf16[512,1664]{1,0:T(8,128)(2,1)S(1)}, bf16[512,1664]{1,0:T(8,128)(2,1)}, u32[]{:S(2)}, u32[]{:S(2)}) collective-permute-start(bf16[512,1664]{1,0:T(8,128)(2,1)S(1)} %send1.1), channel_id=1, source_target_pairs={{0,1},{1,0},{2,3},{3,2},{4,5},{5,4},{6,7},{7,6},{8,9},{9,8},{10,11... | collective-permute-start | bytes 5111816 | tf_op jit(solution)/shard_map/ppermute | solution.py:24
  35.7 1.9 %send0.1 = bf16[512,1536]{1,0:T(8,128)(2,1)S(1)} custom-call(bf16[1024,1024]{1,0:T(8,128)(2,1)S(1)} %assemble.1.codes_ref, bf16[2,512,8192]{2,1,0:T(8,128)(2,1)S(1)} %get-tuple-element.64.w_ref, f32[512,1536]{1,0:T(8,128)S(1)} %get-tuple-element.66.acc_ref), custom_call_target="tpu_custom_call" | custom-call | flops 1000 | bytes 1000 | tf_op jit(solution)/shard_map/send0/pallas_call | solution.py:258
  37.6 1.6 %collective-permute-start.4 = (bf16[512,1536]{1,0:T(8,128)(2,1)S(1)}, bf16[512,1536]{1,0:T(8,128)(2,1)S(1)}, u32[]{:S(2)}, u32[]{:S(2)}) collective-permute-start(bf16[512,1536]{1,0:T(8,128)(2,1)S(1)} %send0.1), channel_id=1, source_target_pairs={{0,8},{1,9},{2,10},{3,11},{4,12},{5,13},{6,14},{7,15},{8,0},{9,1},... | collective-permute-start | bytes 4718600 | tf_op jit(solution)/shard_map/ppermute | solution.py:24
  39.2 2.2 %send2.1 = bf16[512,1664]{1,0:T(8,128)(2,1)S(1)} custom-call(bf16[1024,1024]{1,0:T(8,128)(2,1)S(1)} %assemble.1.codes_ref, bf16[2,512,8192]{2,1,0:T(8,128)(2,1)S(1)} %get-tuple-element.64.w_ref, f32[512,1664]{1,0:T(8,128)S(1)} %get-tuple-element.75.acc_ref), custom_call_target="tpu_custom_call" | custom-call | flops 1000 | bytes 1000 | tf_op jit(solution)/shard_map/send2/pallas_call | solution.py:258
  41.4 1.7 %collective-permute-start.7 = (bf16[512,1664]{1,0:T(8,128)(2,1)S(1)}, bf16[512,1664]{1,0:T(8,128)(2,1)}, u32[]{:S(2)}, u32[]{:S(2)}) collective-permute-start(bf16[512,1664]{1,0:T(8,128)(2,1)S(1)} %send2.1), channel_id=1, source_target_pairs={{0,4},{1,5},{2,6},{3,7},{4,0},{5,1},{6,2},{7,3},{8,12},{9,13},{10,... | collective-permute-start | bytes 5111816 | tf_op jit(solution)/shard_map/ppermute | solution.py:24
  43.0 2.2 %send3.1 = bf16[512,1664]{1,0:T(8,128)(2,1)S(1)} custom-call(bf16[1024,1024]{1,0:T(8,128)(2,1)S(1)} %assemble.1.codes_ref, bf16[2,512,8192]{2,1,0:T(8,128)(2,1)S(1)} %get-tuple-element.64.w_ref, f32[512,1664]{1,0:T(8,128)S(1)} %get-tuple-element.81.acc_ref), custom_call_target="tpu_custom_call" | custom-call | flops 1000 | bytes 1000 | tf_op jit(solution)/shard_map/send3/pallas_call | solution.py:258
  45.2 2.4 %collective-permute-start.10 = (bf16[512,1664]{1,0:T(8,128)(2,1)S(1)}, bf16[512,1664]{1,0:T(8,128)(2,1)S(1)}, u32[]{:S(2)}, u32[]{:S(2)}) collective-permute-start(bf16[512,1664]{1,0:T(8,128)(2,1)S(1)} %send3.1), channel_id=1, source_target_pairs={{0,24},{1,25},{2,26},{3,27},{4,28},{5,29},{6,30},{7,31},{8,16},{9,... | collective-permute-start | bytes 5111816 | tf_op jit(solution)/shard_map/ppermute | solution.py:24
  47.5 2.2 %send4.1 = bf16[512,1664]{1,0:T(8,128)(2,1)S(1)} custom-call(bf16[1024,1024]{1,0:T(8,128)(2,1)S(1)} %assemble.1.codes_ref, bf16[2,512,8192]{2,1,0:T(8,128)(2,1)S(1)} %get-tuple-element.64.w_ref, f32[512,1664]{1,0:T(8,128)S(1)} %rest.1.acc_ref), custom_call_target="tpu_custom_call" | custom-call | flops 1000 | bytes 1000 | tf_op jit(solution)/shard_map/send4/pallas_call | solution.py:258
  49.7 2.6 %collective-permute-start.14 = (bf16[512,1664]{1,0:T(8,128)(2,1)S(1)}, bf16[512,1664]{1,0:T(8,128)(2,1)S(1)}, u32[]{:S(2)}, u32[]{:S(2)}) collective-permute-start(bf16[512,1664]{1,0:T(8,128)(2,1)S(1)} %send4.1), channel_id=1, source_target_pairs={{0,3},{1,2},{2,1},{3,0},{4,7},{5,6},{6,5},{7,4},{8,11},{9,10},{10,... | collective-permute-start | bytes 5111816 | tf_op jit(solution)/shard_map/ppermute | solution.py:24
  52.3 2.8 %keep0.1.keep_ref = f32[512,1536]{1,0:T(8,128)S(1)} custom-call(bf16[1024,1024]{1,0:T(8,128)(2,1)S(1)} %assemble.1.codes_ref, bf16[2,512,8192]{2,1,0:T(8,128)(2,1)S(1)} %get-tuple-element.64.w_ref), custom_call_target="tpu_custom_call" | custom-call | flops 1000 | bytes 1000 | tf_op jit(solution)/shard_map/keep0/pallas_call | solution.py:258
  55.1 3.2 %keep4.1.keep_ref = f32[512,1664]{1,0:T(8,128)S(1)} custom-call(bf16[1024,1024]{1,0:T(8,128)(2,1)S(1)} %assemble.1.codes_ref, bf16[2,512,8192]{2,1,0:T(8,128)(2,1)S(1)} %get-tuple-element.64.w_ref), custom_call_target="tpu_custom_call" | custom-call | flops 1000 | bytes 1000 | tf_op jit(solution)/shard_map/keep4/pallas_call | solution.py:258
  58.3 3.2 %keep3.1.keep_ref = f32[512,1664]{1,0:T(8,128)S(1)} custom-call(bf16[1024,1024]{1,0:T(8,128)(2,1)S(1)} %assemble.1.codes_ref, bf16[2,512,8192]{2,1,0:T(8,128)(2,1)S(1)} %get-tuple-element.64.w_ref), custom_call_target="tpu_custom_call" | custom-call | flops 1000 | bytes 1000 | tf_op jit(solution)/shard_map/keep3/pallas_call | solution.py:258
  61.6 3.2 %keep2.1.keep_ref = f32[512,1664]{1,0:T(8,128)S(1)} custom-call(bf16[1024,1024]{1,0:T(8,128)(2,1)S(1)} %assemble.1.codes_ref, bf16[2,512,8192]{2,1,0:T(8,128)(2,1)S(1)} %get-tuple-element.64.w_ref), custom_call_target="tpu_custom_call" | custom-call | flops 1000 | bytes 1000 | tf_op jit(solution)/shard_map/keep2/pallas_call | solution.py:258
  64.8 3.2 %keep1.1.keep_ref = f32[512,1664]{1,0:T(8,128)S(1)} custom-call(bf16[1024,1024]{1,0:T(8,128)(2,1)S(1)} %assemble.1.codes_ref, bf16[2,512,8192]{2,1,0:T(8,128)(2,1)S(1)} %get-tuple-element.64.w_ref), custom_call_target="tpu_custom_call" | custom-call | flops 1000 | bytes 1000 | tf_op jit(solution)/shard_map/keep1/pallas_call | solution.py:258
  68.0 6.2 %collective-permute-done.4.got_ref = bf16[512,1536]{1,0:T(8,128)(2,1)S(1)} collective-permute-done((bf16[512,1536]{1,0:T(8,128)(2,1)S(1)}, bf16[512,1536]{1,0:T(8,128)(2,1)S(1)}, u32[]{:S(2)}, u32[]{:S(2)}) %collective-permute-start.4) | collective-permute-done | bytes 1572896 | tf_op jit(solution)/shard_map/ppermute | solution.py:24
  74.5 1.0 collective-permute-start.6
  75.4 1.7 %merge.6 = (f32[256,1664]{1,0:T(8,128)S(1)}, bf16[256,1664]{1,0:T(8,128)(2,1)S(1)}) custom-call(f32[512,1664]{1,0:T(8,128)S(1)} %keep1.1.keep_ref, bf16[512,1664]{1,0:T(8,128)(2,1)} %collective-permute-done.5.got_ref), custom_call_target="tpu_custom_call" | custom-call | flops 1000 | bytes 1000 | tf_op jit(solution)/shard_map/merge/pallas_call | solution.py:258
  77.2 3.4 %collective-permute-done.7.got_ref = bf16[512,1664]{1,0:T(8,128)(2,1)} collective-permute-done((bf16[512,1664]{1,0:T(8,128)(2,1)S(1)}, bf16[512,1664]{1,0:T(8,128)(2,1)}, u32[]{:S(2)}, u32[]{:S(2)}) %collective-permute-start.7) | collective-permute-done | bytes 1703968 | tf_op jit(solution)/shard_map/ppermute | solution.py:24
  80.6 1.6 %collective-permute-start.8 = (bf16[256,1664]{1,0:T(8,128)(2,1)S(1)}, bf16[256,1664]{1,0:T(8,128)(2,1)S(1)}, u32[]{:S(2)}, u32[]{:S(2)}) collective-permute-start(bf16[256,1664]{1,0:T(8,128)(2,1)S(1)} %get-tuple-element.76), channel_id=1, source_target_pairs={{0,4},{1,5},{2,6},{3,7},{4,0},{5,1},{6,2},{7,3},{8,12},{9,13},{10,... | collective-permute-start | bytes 2555912 | tf_op jit(solution)/shard_map/ppermute | solution.py:24
  82.2 1.7 %merge.7 = (f32[256,1664]{1,0:T(8,128)S(1)}, bf16[256,1664]{1,0:T(8,128)(2,1)S(1)}) custom-call(f32[512,1664]{1,0:T(8,128)S(1)} %keep2.1.keep_ref, bf16[512,1664]{1,0:T(8,128)(2,1)} %collective-permute-done.7.got_ref), custom_call_target="tpu_custom_call" | custom-call | flops 1000 | bytes 1000 | tf_op jit(solution)/shard_map/merge/pallas_call | solution.py:258
  83.9 1.5 %collective-permute-done.10.got_ref = bf16[512,1664]{1,0:T(8,128)(2,1)S(1)} collective-permute-done((bf16[512,1664]{1,0:T(8,128)(2,1)S(1)}, bf16[512,1664]{1,0:T(8,128)(2,1)S(1)}, u32[]{:S(2)}, u32[]{:S(2)}) %collective-permute-start.10) | collective-permute-done | bytes 1703968 | tf_op jit(solution)/shard_map/ppermute | solution.py:24
  85.4 2.1 %collective-permute-start.11 = (bf16[256,1664]{1,0:T(8,128)(2,1)S(1)}, bf16[256,1664]{1,0:T(8,128)(2,1)S(1)}, u32[]{:S(2)}, u32[]{:S(2)}) collective-permute-start(bf16[256,1664]{1,0:T(8,128)(2,1)S(1)} %get-tuple-element.82), channel_id=1, source_target_pairs={{0,24},{1,25},{2,26},{3,27},{4,28},{5,29},{6,30},{7,31},{8,16},{9,... | collective-permute-start | bytes 2555912 | tf_op jit(solution)/shard_map/ppermute | solution.py:24
  87.8 1.7 %collective-permute-done.14.got_ref = bf16[512,1664]{1,0:T(8,128)(2,1)S(1)} collective-permute-done((bf16[512,1664]{1,0:T(8,128)(2,1)S(1)}, bf16[512,1664]{1,0:T(8,128)(2,1)S(1)}, u32[]{:S(2)}, u32[]{:S(2)}) %collective-permute-start.14) | collective-permute-done | bytes 1703968 | tf_op jit(solution)/shard_map/ppermute | solution.py:24
  89.5 2.5 %collective-permute-start.15 = (bf16[256,1664]{1,0:T(8,128)(2,1)S(1)}, bf16[256,1664]{1,0:T(8,128)(2,1)S(1)}, u32[]{:S(2)}, u32[]{:S(2)}) collective-permute-start(bf16[256,1664]{1,0:T(8,128)(2,1)S(1)} %get-tuple-element.89), channel_id=1, source_target_pairs={{0,3},{1,2},{2,1},{3,0},{4,7},{5,6},{6,5},{7,4},{8,11},{9,10},{10,... | collective-permute-start | bytes 2555912 | tf_op jit(solution)/shard_map/ppermute | solution.py:24
  92.3 0.7 collective-permute-start.19
  93.8 6.8 %collective-permute-done.8 = bf16[256,1664]{1,0:T(8,128)(2,1)S(1)} collective-permute-done((bf16[256,1664]{1,0:T(8,128)(2,1)S(1)}, bf16[256,1664]{1,0:T(8,128)(2,1)S(1)}, u32[]{:S(2)}, u32[]{:S(2)}) %collective-permute-start.8) | collective-permute-done | bytes 852000 | tf_op jit(solution)/shard_map/ppermute | solution.py:24
  100.5 1.6 %collective-permute-start.9 = (bf16[128,1536]{1,0:T(8,128)(2,1)S(1)}, bf16[128,1536]{1,0:T(8,128)(2,1)S(1)}, u32[]{:S(2)}, u32[]{:S(2)}) collective-permute-start(bf16[128,1536]{1,0:T(8,128)(2,1)S(1)} %slice.219), channel_id=1, source_target_pairs={{0,4},{1,5},{2,6},{3,7},{4,0},{5,1},{6,2},{7,3},{8,12},{9,13},{10,... | collective-permute-start | bytes 1179656 | tf_op jit(solution)/shard_map/ppermute | solution.py:24
  102.3 4.0 %collective-permute-done.11 = bf16[256,1664]{1,0:T(8,128)(2,1)S(1)} collective-permute-done((bf16[256,1664]{1,0:T(8,128)(2,1)S(1)}, bf16[256,1664]{1,0:T(8,128)(2,1)S(1)}, u32[]{:S(2)}, u32[]{:S(2)}) %collective-permute-start.11) | collective-permute-done | bytes 852000 | tf_op jit(solution)/shard_map/ppermute | solution.py:24
  106.5 2.2 %collective-permute-start.12 = (bf16[128,1664]{1,0:T(8,128)(2,1)S(1)}, bf16[128,1664]{1,0:T(8,128)(2,1)S(1)}, u32[]{:S(2)}, u32[]{:S(2)}) collective-permute-start(bf16[128,1664]{1,0:T(8,128)(2,1)S(1)} %slice.218), channel_id=1, source_target_pairs={{0,24},{1,25},{2,26},{3,27},{4,28},{5,29},{6,30},{7,31},{8,16},{9,... | collective-permute-start | bytes 1277960 | tf_op jit(solution)/shard_map/ppermute | solution.py:24
  108.7 1.3 collective-permute-done.15
  110.2 2.6 %collective-permute-start.16 = (bf16[128,1664]{1,0:T(8,128)(2,1)S(1)}, bf16[128,1664]{1,0:T(8,128)(2,1)S(1)}, u32[]{:S(2)}, u32[]{:S(2)}) collective-permute-start(bf16[128,1664]{1,0:T(8,128)(2,1)S(1)} %slice.217), channel_id=1, source_target_pairs={{0,3},{1,2},{2,1},{3,0},{4,7},{5,6},{6,5},{7,4},{8,11},{9,10},{10,... | collective-permute-start | bytes 1277960 | tf_op jit(solution)/shard_map/ppermute | solution.py:24
  113.9 3.5 %collective-permute-done.12 = bf16[128,1664]{1,0:T(8,128)(2,1)S(1)} collective-permute-done((bf16[128,1664]{1,0:T(8,128)(2,1)S(1)}, bf16[128,1664]{1,0:T(8,128)(2,1)S(1)}, u32[]{:S(2)}, u32[]{:S(2)}) %collective-permute-start.12) | collective-permute-done | bytes 426016 | tf_op jit(solution)/shard_map/ppermute | solution.py:24
  117.4 2.1 %collective-permute-start.13 = (bf16[64,1536]{1,0:T(8,128)(2,1)S(1)}, bf16[64,1536]{1,0:T(8,128)(2,1)S(1)}, u32[]{:S(2)}, u32[]{:S(2)}) collective-permute-start(bf16[64,1536]{1,0:T(8,128)(2,1)S(1)} %slice.224), channel_id=1, source_target_pairs={{0,24},{1,25},{2,26},{3,27},{4,28},{5,29},{6,30},{7,31},{8,16},{9,... | collective-permute-start | bytes 589832 | tf_op jit(solution)/shard_map/ppermute | solution.py:24
  119.6 1.2 collective-permute-done.16
  120.8 2.5 %collective-permute-start.17 = (bf16[64,1664]{1,0:T(8,128)(2,1)S(1)}, bf16[64,1664]{1,0:T(8,128)(2,1)S(1)}, u32[]{:S(2)}, u32[]{:S(2)}) collective-permute-start(bf16[64,1664]{1,0:T(8,128)(2,1)S(1)} %slice.223), channel_id=1, source_target_pairs={{0,3},{1,2},{2,1},{3,0},{4,7},{5,6},{6,5},{7,4},{8,11},{9,10},{10,... | collective-permute-start | bytes 638984 | tf_op jit(solution)/shard_map/ppermute | solution.py:24
  125.0 3.2 %collective-permute-done.17 = bf16[64,1664]{1,0:T(8,128)(2,1)S(1)} collective-permute-done((bf16[64,1664]{1,0:T(8,128)(2,1)S(1)}, bf16[64,1664]{1,0:T(8,128)(2,1)S(1)}, u32[]{:S(2)}, u32[]{:S(2)}) %collective-permute-start.17) | collective-permute-done | bytes 213024 | tf_op jit(solution)/shard_map/ppermute | solution.py:24
  128.2 2.5 %collective-permute-start.18 = (bf16[32,1536]{1,0:T(8,128)(2,1)S(1)}, bf16[32,1536]{1,0:T(8,128)(2,1)S(1)}, u32[]{:S(2)}, u32[]{:S(2)}) collective-permute-start(bf16[32,1536]{1,0:T(8,128)(2,1)S(1)} %slice.229), channel_id=1, source_target_pairs={{0,3},{1,2},{2,1},{3,0},{4,7},{5,6},{6,5},{7,4},{8,11},{9,10},{10,... | collective-permute-start | bytes 294920 | tf_op jit(solution)/shard_map/ppermute | solution.py:24
  130.8 1.2 collective-permute-start.28
  134.1 3.6 %collective-permute-done.22 = bf16[32,1664]{1,0:T(8,128)(2,1)S(1)} collective-permute-done((bf16[32,1664]{1,0:T(8,128)(2,1)S(1)}, bf16[32,1664]{1,0:T(8,128)(2,1)S(1)}, u32[]{:S(2)}, u32[]{:S(2)}) %collective-permute-start.22) | collective-permute-done | bytes 106528 | tf_op jit(solution)/shard_map/ppermute | solution.py:24
  137.8 0.9 add_convert_fusion
  (89 shorter events, 8.9 us)
Async XLA Ops:
  0.0 10.9 %copy-start = (s32[2,1024]{1,0:T(2,128)S(1)}, s32[2,1024]{1,0:T(2,128)}, u32[]{:S(2)}) copy-start(s32[2,1024]{1,0:T(2,128)} %param.17) | copy-start | bytes 24580
  0.0 10.8 %copy-start.6 = (s32[32]{0:T(128)S(1)}, s32[32]{0:T(128)}, u32[]{:S(2)}) copy-start(s32[32]{0:T(128)} %constant.82.clone) | copy-start | bytes 388
  0.0 10.9 %copy-start.4 = (s32[2,1024]{1,0:T(2,128)S(1)}, s32[2,1024]{1,0:T(2,128)}, u32[]{:S(2)}) copy-start(s32[2,1024]{1,0:T(2,128)} %param.19) | copy-start | bytes 24580
  0.0 10.9 %copy-start.5 = (s32[2,1024]{1,0:T(2,128)S(1)}, s32[2,1024]{1,0:T(2,128)}, u32[]{:S(2)}) copy-start(s32[2,1024]{1,0:T(2,128)} %param.18) | copy-start | bytes 24580
  0.0 12.3 %copy-start.3 = (f32[16]{0:T(128)S(1)}, f32[16]{0:T(128)}, u32[]{:S(2)}) copy-start(f32[16]{0:T(128)} %param.20) | copy-start | bytes 196
  9.1 3.3 %collective-permute-start = (f32[1024,256]{1,0:T(8,128)S(1)}, f32[1024,256]{1,0:T(8,128)S(1)}, u32[]{:S(2)}, u32[]{:S(2)}) collective-permute-start(f32[1024,256]{1,0:T(8,128)S(1)} %get-tuple-element.57), channel_id=1, source_target_pairs={{0,32},{32,0},{64,96},{96,64},{1,33},{33,1},{65,97},{97,65},{2,34}... | collective-permute-start | bytes 3145736 | tf_op jit(solution)/shard_map/ppermute | solution.py:24
  12.8 3.8 %collective-permute-start.1 = (bf16[1024,256]{1,0:T(8,128)(2,1)S(1)}, bf16[1024,256]{1,0:T(8,128)(2,1)S(1)}, u32[]{:S(2)}, u32[]{:S(2)}) collective-permute-start(bf16[1024,256]{1,0:T(8,128)(2,1)S(1)} %select_convert_fusion.mine_ref.own_ref), channel_id=1, source_target_pairs={{0,32},{32,0},{64,96},{96,64},{1,33},{33,1},{65,97},{97,65},{2,34}... | collective-permute-start | bytes 1572872 | tf_op jit(solution)/shard_map/ppermute | solution.py:24
  13.3 15.5 %collective-permute-start.2 = (bf16[1024,256]{1,0:T(8,128)(2,1)S(1)}, bf16[1024,256]{1,0:T(8,128)(2,1)S(1)}, u32[]{:S(2)}, u32[]{:S(2)}) collective-permute-start(bf16[1024,256]{1,0:T(8,128)(2,1)S(1)} %select_convert_fusion.mine_ref.own_ref), channel_id=1, source_target_pairs={{0,64},{32,96},{64,0},{96,32},{1,65},{33,97},{65,1},{97,33},{2,66}... | collective-permute-start | bytes 1572872 | tf_op jit(solution)/shard_map/ppermute | solution.py:24
  28.8 2.3 %collective-permute-start.3 = (bf16[1024,256]{1,0:T(8,128)(2,1)S(1)}, bf16[1024,256]{1,0:T(8,128)(2,1)S(1)}, u32[]{:S(2)}, u32[]{:S(2)}) collective-permute-start(bf16[1024,256]{1,0:T(8,128)(2,1)S(1)} %collective-permute-done.2.far_ref), channel_id=1, source_target_pairs={{0,32},{32,0},{64,96},{96,64},{1,33},{33,1},{65,97},{97,65},{2,34}... | collective-permute-start | bytes 1572872 | tf_op jit(solution)/shard_map/ppermute | solution.py:24
  33.7 40.8 %collective-permute-start.5 = (bf16[512,1664]{1,0:T(8,128)(2,1)S(1)}, bf16[512,1664]{1,0:T(8,128)(2,1)}, u32[]{:S(2)}, u32[]{:S(2)}) collective-permute-start(bf16[512,1664]{1,0:T(8,128)(2,1)S(1)} %send1.1), channel_id=1, source_target_pairs={{0,1},{1,0},{2,3},{3,2},{4,5},{5,4},{6,7},{7,6},{8,9},{9,8},{10,11... | collective-permute-start | bytes 5111816 | tf_op jit(solution)/shard_map/ppermute | solution.py:24
  37.6 36.6 %collective-permute-start.4 = (bf16[512,1536]{1,0:T(8,128)(2,1)S(1)}, bf16[512,1536]{1,0:T(8,128)(2,1)S(1)}, u32[]{:S(2)}, u32[]{:S(2)}) collective-permute-start(bf16[512,1536]{1,0:T(8,128)(2,1)S(1)} %send0.1), channel_id=1, source_target_pairs={{0,8},{1,9},{2,10},{3,11},{4,12},{5,13},{6,14},{7,15},{8,0},{9,1},... | collective-permute-start | bytes 4718600 | tf_op jit(solution)/shard_map/ppermute | solution.py:24
  41.4 39.2 %collective-permute-start.7 = (bf16[512,1664]{1,0:T(8,128)(2,1)S(1)}, bf16[512,1664]{1,0:T(8,128)(2,1)}, u32[]{:S(2)}, u32[]{:S(2)}) collective-permute-start(bf16[512,1664]{1,0:T(8,128)(2,1)S(1)} %send2.1), channel_id=1, source_target_pairs={{0,4},{1,5},{2,6},{3,7},{4,0},{5,1},{6,2},{7,3},{8,12},{9,13},{10,... | collective-permute-start | bytes 5111816 | tf_op jit(solution)/shard_map/ppermute | solution.py:24
  45.2 40.2 %collective-permute-start.10 = (bf16[512,1664]{1,0:T(8,128)(2,1)S(1)}, bf16[512,1664]{1,0:T(8,128)(2,1)S(1)}, u32[]{:S(2)}, u32[]{:S(2)}) collective-permute-start(bf16[512,1664]{1,0:T(8,128)(2,1)S(1)} %send3.1), channel_id=1, source_target_pairs={{0,24},{1,25},{2,26},{3,27},{4,28},{5,29},{6,30},{7,31},{8,16},{9,... | collective-permute-start | bytes 5111816 | tf_op jit(solution)/shard_map/ppermute | solution.py:24
  49.7 39.8 %collective-permute-start.14 = (bf16[512,1664]{1,0:T(8,128)(2,1)S(1)}, bf16[512,1664]{1,0:T(8,128)(2,1)S(1)}, u32[]{:S(2)}, u32[]{:S(2)}) collective-permute-start(bf16[512,1664]{1,0:T(8,128)(2,1)S(1)} %send4.1), channel_id=1, source_target_pairs={{0,3},{1,2},{2,1},{3,0},{4,7},{5,6},{6,5},{7,4},{8,11},{9,10},{10,... | collective-permute-start | bytes 5111816 | tf_op jit(solution)/shard_map/ppermute | solution.py:24
  74.5 19.0 %collective-permute-start.6 = (bf16[256,1536]{1,0:T(8,128)(2,1)S(1)}, bf16[256,1536]{1,0:T(8,128)(2,1)S(1)}, u32[]{:S(2)}, u32[]{:S(2)}) collective-permute-start(bf16[256,1536]{1,0:T(8,128)(2,1)S(1)} %get-tuple-element.72), channel_id=1, source_target_pairs={{0,1},{1,0},{2,3},{3,2},{4,5},{5,4},{6,7},{7,6},{8,9},{9,8},{10,11... | collective-permute-start | bytes 2359304 | tf_op jit(solution)/shard_map/ppermute | solution.py:24
  80.6 19.9 %collective-permute-start.8 = (bf16[256,1664]{1,0:T(8,128)(2,1)S(1)}, bf16[256,1664]{1,0:T(8,128)(2,1)S(1)}, u32[]{:S(2)}, u32[]{:S(2)}) collective-permute-start(bf16[256,1664]{1,0:T(8,128)(2,1)S(1)} %get-tuple-element.76), channel_id=1, source_target_pairs={{0,4},{1,5},{2,6},{3,7},{4,0},{5,1},{6,2},{7,3},{8,12},{9,13},{10,... | collective-permute-start | bytes 2555912 | tf_op jit(solution)/shard_map/ppermute | solution.py:24
  85.4 20.8 %collective-permute-start.11 = (bf16[256,1664]{1,0:T(8,128)(2,1)S(1)}, bf16[256,1664]{1,0:T(8,128)(2,1)S(1)}, u32[]{:S(2)}, u32[]{:S(2)}) collective-permute-start(bf16[256,1664]{1,0:T(8,128)(2,1)S(1)} %get-tuple-element.82), channel_id=1, source_target_pairs={{0,24},{1,25},{2,26},{3,27},{4,28},{5,29},{6,30},{7,31},{8,16},{9,... | collective-permute-start | bytes 2555912 | tf_op jit(solution)/shard_map/ppermute | solution.py:24
  89.5 20.5 %collective-permute-start.15 = (bf16[256,1664]{1,0:T(8,128)(2,1)S(1)}, bf16[256,1664]{1,0:T(8,128)(2,1)S(1)}, u32[]{:S(2)}, u32[]{:S(2)}) collective-permute-start(bf16[256,1664]{1,0:T(8,128)(2,1)S(1)} %get-tuple-element.89), channel_id=1, source_target_pairs={{0,3},{1,2},{2,1},{3,0},{4,7},{5,6},{6,5},{7,4},{8,11},{9,10},{10,... | collective-permute-start | bytes 2555912 | tf_op jit(solution)/shard_map/ppermute | solution.py:24
  92.3 20.5 %collective-permute-start.19 = (bf16[256,1664]{1,0:T(8,128)(2,1)S(1)}, bf16[256,1664]{1,0:T(8,128)(2,1)S(1)}, u32[]{:S(2)}, u32[]{:S(2)}) collective-permute-start(bf16[256,1664]{1,0:T(8,128)(2,1)S(1)} %get-tuple-element.96), channel_id=1, source_target_pairs={{0,8},{1,9},{2,10},{3,11},{4,12},{5,13},{6,14},{7,15},{8,0},{9,1},... | collective-permute-start | bytes 2555912 | tf_op jit(solution)/shard_map/ppermute | solution.py:24
  100.5 13.3 %collective-permute-start.9 = (bf16[128,1536]{1,0:T(8,128)(2,1)S(1)}, bf16[128,1536]{1,0:T(8,128)(2,1)S(1)}, u32[]{:S(2)}, u32[]{:S(2)}) collective-permute-start(bf16[128,1536]{1,0:T(8,128)(2,1)S(1)} %slice.219), channel_id=1, source_target_pairs={{0,4},{1,5},{2,6},{3,7},{4,0},{5,1},{6,2},{7,3},{8,12},{9,13},{10,... | collective-permute-start | bytes 1179656 | tf_op jit(solution)/shard_map/ppermute | solution.py:24
  106.5 10.9 %collective-permute-start.12 = (bf16[128,1664]{1,0:T(8,128)(2,1)S(1)}, bf16[128,1664]{1,0:T(8,128)(2,1)S(1)}, u32[]{:S(2)}, u32[]{:S(2)}) collective-permute-start(bf16[128,1664]{1,0:T(8,128)(2,1)S(1)} %slice.218), channel_id=1, source_target_pairs={{0,24},{1,25},{2,26},{3,27},{4,28},{5,29},{6,30},{7,31},{8,16},{9,... | collective-permute-start | bytes 1277960 | tf_op jit(solution)/shard_map/ppermute | solution.py:24
  110.2 10.5 %collective-permute-start.16 = (bf16[128,1664]{1,0:T(8,128)(2,1)S(1)}, bf16[128,1664]{1,0:T(8,128)(2,1)S(1)}, u32[]{:S(2)}, u32[]{:S(2)}) collective-permute-start(bf16[128,1664]{1,0:T(8,128)(2,1)S(1)} %slice.217), channel_id=1, source_target_pairs={{0,3},{1,2},{2,1},{3,0},{4,7},{5,6},{6,5},{7,4},{8,11},{9,10},{10,... | collective-permute-start | bytes 1277960 | tf_op jit(solution)/shard_map/ppermute | solution.py:24
  113.0 10.3 %collective-permute-start.23 = (bf16[128,1664]{1,0:T(8,128)(2,1)S(1)}, bf16[128,1664]{1,0:T(8,128)(2,1)S(1)}, u32[]{:S(2)}, u32[]{:S(2)}) collective-permute-start(bf16[128,1664]{1,0:T(8,128)(2,1)S(1)} %slice.215), channel_id=1, source_target_pairs={{0,1},{1,0},{2,3},{3,2},{4,5},{5,4},{6,7},{7,6},{8,9},{9,8},{10,11... | collective-permute-start | bytes 1277960 | tf_op jit(solution)/shard_map/ppermute | solution.py:24
  113.1 10.9 %collective-permute-start.20 = (bf16[128,1664]{1,0:T(8,128)(2,1)S(1)}, bf16[128,1664]{1,0:T(8,128)(2,1)S(1)}, u32[]{:S(2)}, u32[]{:S(2)}) collective-permute-start(bf16[128,1664]{1,0:T(8,128)(2,1)S(1)} %slice.216), channel_id=1, source_target_pairs={{0,8},{1,9},{2,10},{3,11},{4,12},{5,13},{6,14},{7,15},{8,0},{9,1},... | collective-permute-start | bytes 1277960 | tf_op jit(solution)/shard_map/ppermute | solution.py:24
  117.4 7.5 %collective-permute-start.13 = (bf16[64,1536]{1,0:T(8,128)(2,1)S(1)}, bf16[64,1536]{1,0:T(8,128)(2,1)S(1)}, u32[]{:S(2)}, u32[]{:S(2)}) collective-permute-start(bf16[64,1536]{1,0:T(8,128)(2,1)S(1)} %slice.224), channel_id=1, source_target_pairs={{0,24},{1,25},{2,26},{3,27},{4,28},{5,29},{6,30},{7,31},{8,16},{9,... | collective-permute-start | bytes 589832 | tf_op jit(solution)/shard_map/ppermute | solution.py:24
  120.8 7.4 %collective-permute-start.17 = (bf16[64,1664]{1,0:T(8,128)(2,1)S(1)}, bf16[64,1664]{1,0:T(8,128)(2,1)S(1)}, u32[]{:S(2)}, u32[]{:S(2)}) collective-permute-start(bf16[64,1664]{1,0:T(8,128)(2,1)S(1)} %slice.223), channel_id=1, source_target_pairs={{0,3},{1,2},{2,1},{3,0},{4,7},{5,6},{6,5},{7,4},{8,11},{9,10},{10,... | collective-permute-start | bytes 638984 | tf_op jit(solution)/shard_map/ppermute | solution.py:24
  123.4 7.3 %collective-permute-start.26 = (bf16[64,1664]{1,0:T(8,128)(2,1)S(1)}, bf16[64,1664]{1,0:T(8,128)(2,1)S(1)}, u32[]{:S(2)}, u32[]{:S(2)}) collective-permute-start(bf16[64,1664]{1,0:T(8,128)(2,1)S(1)} %slice.220), channel_id=1, source_target_pairs={{0,4},{1,5},{2,6},{3,7},{4,0},{5,1},{6,2},{7,3},{8,12},{9,13},{10,... | collective-permute-start | bytes 638984 | tf_op jit(solution)/shard_map/ppermute | solution.py:24
  124.2 7.8 %collective-permute-start.24 = (bf16[64,1664]{1,0:T(8,128)(2,1)S(1)}, bf16[64,1664]{1,0:T(8,128)(2,1)S(1)}, u32[]{:S(2)}, u32[]{:S(2)}) collective-permute-start(bf16[64,1664]{1,0:T(8,128)(2,1)S(1)} %slice.221), channel_id=1, source_target_pairs={{0,1},{1,0},{2,3},{3,2},{4,5},{5,4},{6,7},{7,6},{8,9},{9,8},{10,11... | collective-permute-start | bytes 638984 | tf_op jit(solution)/shard_map/ppermute | solution.py:24
  124.3 8.4 %collective-permute-start.21 = (bf16[64,1664]{1,0:T(8,128)(2,1)S(1)}, bf16[64,1664]{1,0:T(8,128)(2,1)S(1)}, u32[]{:S(2)}, u32[]{:S(2)}) collective-permute-start(bf16[64,1664]{1,0:T(8,128)(2,1)S(1)} %slice.222), channel_id=1, source_target_pairs={{0,8},{1,9},{2,10},{3,11},{4,12},{5,13},{6,14},{7,15},{8,0},{9,1},... | collective-permute-start | bytes 638984 | tf_op jit(solution)/shard_map/ppermute | solution.py:24
  128.2 5.8 %collective-permute-start.18 = (bf16[32,1536]{1,0:T(8,128)(2,1)S(1)}, bf16[32,1536]{1,0:T(8,128)(2,1)S(1)}, u32[]{:S(2)}, u32[]{:S(2)}) collective-permute-start(bf16[32,1536]{1,0:T(8,128)(2,1)S(1)} %slice.229), channel_id=1, source_target_pairs={{0,3},{1,2},{2,1},{3,0},{4,7},{5,6},{6,5},{7,4},{8,11},{9,10},{10,... | collective-permute-start | bytes 294920 | tf_op jit(solution)/shard_map/ppermute | solution.py:24
  130.8 7.0 %collective-permute-start.28 = (bf16[32,1664]{1,0:T(8,128)(2,1)S(1)}, bf16[32,1664]{1,0:T(8,128)(2,1)S(1)}, u32[]{:S(2)}, u32[]{:S(2)}) collective-permute-start(bf16[32,1664]{1,0:T(8,128)(2,1)S(1)} %slice.225), channel_id=1, source_target_pairs={{0,24},{1,25},{2,26},{3,27},{4,28},{5,29},{6,30},{7,31},{8,16},{9,... | collective-permute-start | bytes 319496 | tf_op jit(solution)/shard_map/ppermute | solution.py:24
  132.1 5.6 %collective-permute-start.27 = (bf16[32,1664]{1,0:T(8,128)(2,1)S(1)}, bf16[32,1664]{1,0:T(8,128)(2,1)S(1)}, u32[]{:S(2)}, u32[]{:S(2)}) collective-permute-start(bf16[32,1664]{1,0:T(8,128)(2,1)S(1)} %slice.226), channel_id=1, source_target_pairs={{0,4},{1,5},{2,6},{3,7},{4,0},{5,1},{6,2},{7,3},{8,12},{9,13},{10,... | collective-permute-start | bytes 319496 | tf_op jit(solution)/shard_map/ppermute | solution.py:24
  132.7 5.1 %copy-start.2 = (f32[1,8192]{1,0:T(1,128)S(1)}, f32[1,8192]{1,0:T(1,128)}, u32[]{:S(2)}) copy-start(f32[1,8192]{1,0:T(1,128)} %param.16) | copy-start | bytes 98308
  132.8 4.9 %collective-permute-start.25 = (bf16[32,1664]{1,0:T(8,128)(2,1)S(1)}, bf16[32,1664]{1,0:T(8,128)(2,1)S(1)}, u32[]{:S(2)}, u32[]{:S(2)}) collective-permute-start(bf16[32,1664]{1,0:T(8,128)(2,1)S(1)} %slice.227), channel_id=1, source_target_pairs={{0,1},{1,0},{2,3},{3,2},{4,5},{5,4},{6,7},{7,6},{8,9},{9,8},{10,11... | collective-permute-start | bytes 319496 | tf_op jit(solution)/shard_map/ppermute | solution.py:24
  132.9 4.8 %collective-permute-start.22 = (bf16[32,1664]{1,0:T(8,128)(2,1)S(1)}, bf16[32,1664]{1,0:T(8,128)(2,1)S(1)}, u32[]{:S(2)}, u32[]{:S(2)}) collective-permute-start(bf16[32,1664]{1,0:T(8,128)(2,1)S(1)} %slice.228), channel_id=1, source_target_pairs={{0,8},{1,9},{2,10},{3,11},{4,12},{5,13},{6,14},{7,15},{8,0},{9,1},... | collective-permute-start | bytes 319496 | tf_op jit(solution)/shard_map/ppermute | solution.py:24
  137.7 1.0 copy-start.1

commit v7 on v5

--- a/solution.py
+++ b/solution.py
@@ -13,7 +13,9 @@
 LANES, TILE = 128, 256
 PARTS = (12, 13, 13, 13, 13)
 EARLY = (6, 6, 6, 6, 6)
-READY = 4
+READY = 3
+KEPT = 3
+FIRST = 0
 VMEM = pl.BlockSpec(memory_space=pltpu.VMEM)
 HBM = pl.BlockSpec(memory_space=pltpu.HBM)
 MIB = 1 << 20
@@ -389,13 +391,13 @@
         decode_rows(codes, weights, keep_blocks(p), starts[p], PARTS[p] * LANES, F32, f"keep{p}")
         for p in range(STEPS)
     ]
-    late[0], *keeps[:READY] = lax.optimization_barrier((late[0], *keeps[:READY]))
+    late[FIRST], *keeps[:KEPT] = lax.optimization_barrier((late[FIRST], *keeps[:KEPT]))
     kept, out = {}, {}
     for p in range(STEPS):
         kept[p], out[p] = merge(keeps[p], early[p], late[p])
     for i in range(1, STEPS):
         for p in range(STEPS):
-            total = kept[p] + exchange(out[p], (p + i) % STEPS).astype(F32)
+            total = kept[p] + xor_swap(out[p], "lat", LINKS[(p + i) % STEPS]).astype(F32)
             m = total.shape[0] // 2
             kept[p] = total[:m] if i < STEPS - 1 else total
             out[p] = total[m:].astype(BF16)

time: 135 us -> 144 us (1.067)
  waiting for transfers between devices: 35.2 us -> 41.7 us
  starting transfers between devices: 44.1 us -> 46.9 us
    ppermute x34, waiting for transfers between devices: 35.2 us -> 41.7 us  [xor_swap(): lax.ppermute(value, axis, [(i, i ^ mask) for i in range(lax.axis_size(axi...]
    ppermute x34, starting transfers between devices: 44.1 us -> 46.9 us  [xor_swap(): lax.ppermute(value, axis, [(i, i ^ mask) for i in range(lax.axis_size(axi...]
  transfers between devices with their start and end apart: 34 -> 34, of which waited for: 14 -> 16; matrix products, arithmetic and copies ran while one was open for 4% -> 4% of each run, Pallas kernels for 28% -> 26%
where the time goes in v7:
time: 144 us
  Pallas kernels  48.5 us (34%)
  starting transfers between devices  46.9 us (33%)
  waiting for transfers between devices  41.7 us (29%)
  other arithmetic  3.06 us (2%)
  local copies, waits for them, and re-layouts  2.06 us (1%)
    ppermute x34, starting transfers between devices, xor_swap(): lax.ppermute(value, axis, [(i, i ^ mask) for i in range(lax.axis_size(axi...  46.9 us
    ppermute x34, waiting for transfers between devices, xor_swap(): lax.ppermute(value, axis, [(i, i ^ mask) for i in range(lax.axis_size(axi...  41.7 us
    pallas_call x15, Pallas kernels, call_tiny(): pl.pallas_call(kernel, out_shape=out_shape, in_specs=[VMEM] * len(args),...  29.2 us
    pallas_call x1, Pallas kernels, encode(): pl.pallas_call(functools.partial(encode_kernel, masks=masks, rows=rows, c...  9.09 us
    pallas_call x1, Pallas kernels, own_part(): pl.pallas_call(functools.partial(own_kernel, spans=spans), out_shape=[plt...  8.27 us
  transfers between devices with their start and end apart: 34, of which 16 were waited for; matrix products, arithmetic and copies ran while one was open for 4% of the time, Pallas kernels for 26%

profile of v7, /device:TPU:0, one launch (start us, length us, event | category | flops | bytes accessed | tf_op | source)
XLA Modules:
  0.0 144.0 jit_solution(11668857168532137508)
XLA Ops:
  0.0 9.1 %encode.1 = (f32[1024,256]{1,0:T(8,128)S(1)}, f32[1024,256]{1,0:T(8,128)S(1)}) custom-call(bf16[1,1024,4096]{2,1,0:T(8,128)(2,1)} %x_hbm.1, bf16[1,4096,512]{2,1,0:T(8,128)(2,1)} %w_hbm.1), custom_call_target="tpu_custom_call" | custom-call | flops 4294967296 | bytes 14680064 | tf_op jit(solution)/shard_map/encode/pallas_call | solution.py:96
  11.0 1.3 fusion
  13.3 3.3 %collective-permute-start.2 = (bf16[1024,256]{1,0:T(8,128)(2,1)S(1)}, bf16[1024,256]{1,0:T(8,128)(2,1)S(1)}, u32[]{:S(2)}, u32[]{:S(2)}) collective-permute-start(bf16[1024,256]{1,0:T(8,128)(2,1)S(1)} %select_convert_fusion.mine_ref.own_ref), channel_id=1, source_target_pairs={{0,64},{32,96},{64,0},{96,32},{1,65},{33,97},{65,1},{97,33},{2,66}... | collective-permute-start | bytes 1572872 | tf_op jit(solution)/shard_map/ppermute | solution.py:26
  16.6 8.3 %own.1 = (bf16[2,512,8192]{2,1,0:T(8,128)(2,1)S(1)}, f32[512,768]{1,0:T(8,128)S(1)}, f32[512,768]{1,0:T(8,128)S(1)}, f32[512,768]{1,0:T(8,128)S(1)}, f32[512,768]{1,0:T(8,128)S(1)}, /*index=5*/f32[512,768]{1,0:T(8,128)S(1)}) custom-call(bf16[1024,256]{1,0:T(8,128)(2,1)S(1)} %select_convert_fusion.mine_ref.own_ref, ...), custom_call_target="tpu_custom_call" | custom-call | flops 2147483648 | bytes 33554432 | tf_op jit(solution)/shard_map/own/pallas_call | solution.py:206
  24.9 3.9 %collective-permute-done.2.far_ref = bf16[1024,256]{1,0:T(8,128)(2,1)S(1)} collective-permute-done((bf16[1024,256]{1,0:T(8,128)(2,1)S(1)}, bf16[1024,256]{1,0:T(8,128)(2,1)S(1)}, u32[]{:S(2)}, u32[]{:S(2)}) %collective-permute-start.2) | collective-permute-done | bytes 524320 | tf_op jit(solution)/shard_map/ppermute | solution.py:26
  28.8 1.9 %collective-permute-done.3.far_sib_ref = bf16[1024,256]{1,0:T(8,128)(2,1)S(1)} collective-permute-done((bf16[1024,256]{1,0:T(8,128)(2,1)S(1)}, bf16[1024,256]{1,0:T(8,128)(2,1)S(1)}, u32[]{:S(2)}, u32[]{:S(2)}) %collective-permute-start.3) | collective-permute-done | bytes 524320 | tf_op jit(solution)/shard_map/ppermute | solution.py:26
  31.0 1.0 early0.1
  32.0 1.6 %collective-permute-start.4 = (bf16[512,768]{1,0:T(8,128)(2,1)S(1)}, bf16[512,768]{1,0:T(8,128)(2,1)S(1)}, u32[]{:S(2)}, u32[]{:S(2)}) collective-permute-start(bf16[512,768]{1,0:T(8,128)(2,1)S(1)} %early0.1), channel_id=1, source_target_pairs={{0,8},{1,9},{2,10},{3,11},{4,12},{5,13},{6,14},{7,15},{8,0},{9,1},... | collective-permute-start | bytes 2359304 | tf_op jit(solution)/shard_map/ppermute | solution.py:26
  33.6 1.0 early4.1
  34.6 4.1 %collective-permute-start.28 = (bf16[512,768]{1,0:T(8,128)(2,1)S(1)}, bf16[512,768]{1,0:T(8,128)(2,1)S(1)}, u32[]{:S(2)}, u32[]{:S(2)}) collective-permute-start(bf16[512,768]{1,0:T(8,128)(2,1)S(1)} %early4.1), channel_id=1, source_target_pairs={{0,3},{1,2},{2,1},{3,0},{4,7},{5,6},{6,5},{7,4},{8,11},{9,10},{10,... | collective-permute-start | bytes 2359304 | tf_op jit(solution)/shard_map/ppermute | solution.py:26
  39.7 2.2 %collective-permute-start.22 = (bf16[512,768]{1,0:T(8,128)(2,1)S(1)}, bf16[512,768]{1,0:T(8,128)(2,1)S(1)}, u32[]{:S(2)}, u32[]{:S(2)}) collective-permute-start(bf16[512,768]{1,0:T(8,128)(2,1)S(1)} %early3.1), channel_id=1, source_target_pairs={{0,24},{1,25},{2,26},{3,27},{4,28},{5,29},{6,30},{7,31},{8,16},{9,... | collective-permute-start | bytes 2359304 | tf_op jit(solution)/shard_map/ppermute | solution.py:26
  42.8 1.7 %collective-permute-start.16 = (bf16[512,768]{1,0:T(8,128)(2,1)S(1)}, bf16[512,768]{1,0:T(8,128)(2,1)S(1)}, u32[]{:S(2)}, u32[]{:S(2)}) collective-permute-start(bf16[512,768]{1,0:T(8,128)(2,1)S(1)} %early2.1), channel_id=1, source_target_pairs={{0,4},{1,5},{2,6},{3,7},{4,0},{5,1},{6,2},{7,3},{8,12},{9,13},{10,... | collective-permute-start | bytes 2359304 | tf_op jit(solution)/shard_map/ppermute | solution.py:26
  45.7 1.4 late0.1
  47.2 1.9 %late2.1 = bf16[512,896]{1,0:T(8,128)(2,1)S(1)} custom-call(bf16[1024,1024]{1,0:T(8,128)(2,1)S(1)} %assemble.1.codes_ref, bf16[2,512,8192]{2,1,0:T(8,128)(2,1)S(1)} %get-tuple-element.41.w_ref), custom_call_target="tpu_custom_call" | custom-call | flops 1000 | bytes 1000 | tf_op jit(solution)/shard_map/late2/pallas_call | solution.py:235
  49.0 1.9 %late1.1 = bf16[512,896]{1,0:T(8,128)(2,1)S(1)} custom-call(bf16[1024,1024]{1,0:T(8,128)(2,1)S(1)} %assemble.1.codes_ref, bf16[2,512,8192]{2,1,0:T(8,128)(2,1)S(1)} %get-tuple-element.41.w_ref), custom_call_target="tpu_custom_call" | custom-call | flops 1000 | bytes 1000 | tf_op jit(solution)/shard_map/late1/pallas_call | solution.py:235
  51.7 1.5 %collective-permute-start.5 = (bf16[512,768]{1,0:T(8,128)(2,1)S(1)}, bf16[512,768]{1,0:T(8,128)(2,1)S(1)}, u32[]{:S(2)}, u32[]{:S(2)}) collective-permute-start(bf16[512,768]{1,0:T(8,128)(2,1)S(1)} %late0.1), channel_id=1, source_target_pairs={{0,8},{1,9},{2,10},{3,11},{4,12},{5,13},{6,14},{7,15},{8,0},{9,1},... | collective-permute-start | bytes 2359304 | tf_op jit(solution)/shard_map/ppermute | solution.py:26
  53.2 1.8 %late4.1 = bf16[512,896]{1,0:T(8,128)(2,1)S(1)} custom-call(bf16[1024,1024]{1,0:T(8,128)(2,1)S(1)} %assemble.1.codes_ref, bf16[2,512,8192]{2,1,0:T(8,128)(2,1)S(1)} %get-tuple-element.41.w_ref), custom_call_target="tpu_custom_call" | custom-call | flops 1000 | bytes 1000 | tf_op jit(solution)/shard_map/late4/pallas_call | solution.py:235
  55.1 1.2 collective-permute-done.28.early_ref
  56.3 3.0 %collective-permute-start.29 = (bf16[512,896]{1,0:T(8,128)(2,1)S(1)}, bf16[512,896]{1,0:T(8,128)(2,1)S(1)}, u32[]{:S(2)}, u32[]{:S(2)}) collective-permute-start(bf16[512,896]{1,0:T(8,128)(2,1)S(1)} %late4.1), channel_id=1, source_target_pairs={{0,3},{1,2},{2,1},{3,0},{4,7},{5,6},{6,5},{7,4},{8,11},{9,10},{10,... | collective-permute-start | bytes 2752520 | tf_op jit(solution)/shard_map/ppermute | solution.py:26
  59.2 1.8 %late3.1 = bf16[512,896]{1,0:T(8,128)(2,1)S(1)} custom-call(bf16[1024,1024]{1,0:T(8,128)(2,1)S(1)} %assemble.1.codes_ref, bf16[2,512,8192]{2,1,0:T(8,128)(2,1)S(1)} %get-tuple-element.41.w_ref), custom_call_target="tpu_custom_call" | custom-call | flops 1000 | bytes 1000 | tf_op jit(solution)/shard_map/late3/pallas_call | solution.py:235
  61.1 2.2 %collective-permute-start.23 = (bf16[512,896]{1,0:T(8,128)(2,1)S(1)}, bf16[512,896]{1,0:T(8,128)(2,1)S(1)}, u32[]{:S(2)}, u32[]{:S(2)}) collective-permute-start(bf16[512,896]{1,0:T(8,128)(2,1)S(1)} %late3.1), channel_id=1, source_target_pairs={{0,24},{1,25},{2,26},{3,27},{4,28},{5,29},{6,30},{7,31},{8,16},{9,... | collective-permute-start | bytes 2752520 | tf_op jit(solution)/shard_map/ppermute | solution.py:26
  63.3 1.6 %collective-permute-start.17 = (bf16[512,896]{1,0:T(8,128)(2,1)S(1)}, bf16[512,896]{1,0:T(8,128)(2,1)S(1)}, u32[]{:S(2)}, u32[]{:S(2)}) collective-permute-start(bf16[512,896]{1,0:T(8,128)(2,1)S(1)} %late2.1), channel_id=1, source_target_pairs={{0,4},{1,5},{2,6},{3,7},{4,0},{5,1},{6,2},{7,3},{8,12},{9,13},{10,... | collective-permute-start | bytes 2752520 | tf_op jit(solution)/shard_map/ppermute | solution.py:26
  64.8 2.8 %keep0.1.keep_ref = f32[512,1536]{1,0:T(8,128)S(1)} custom-call(bf16[1024,1024]{1,0:T(8,128)(2,1)S(1)} %assemble.1.codes_ref, bf16[2,512,8192]{2,1,0:T(8,128)(2,1)S(1)} %get-tuple-element.41.w_ref), custom_call_target="tpu_custom_call" | custom-call | flops 1000 | bytes 1000 | tf_op jit(solution)/shard_map/keep0/pallas_call | solution.py:235
  67.6 3.2 %keep2.1.keep_ref = f32[512,1664]{1,0:T(8,128)S(1)} custom-call(bf16[1024,1024]{1,0:T(8,128)(2,1)S(1)} %assemble.1.codes_ref, bf16[2,512,8192]{2,1,0:T(8,128)(2,1)S(1)} %get-tuple-element.41.w_ref), custom_call_target="tpu_custom_call" | custom-call | flops 1000 | bytes 1000 | tf_op jit(solution)/shard_map/keep2/pallas_call | solution.py:235
  70.9 3.2 %keep1.1.keep_ref = f32[512,1664]{1,0:T(8,128)S(1)} custom-call(bf16[1024,1024]{1,0:T(8,128)(2,1)S(1)} %assemble.1.codes_ref, bf16[2,512,8192]{2,1,0:T(8,128)(2,1)S(1)} %get-tuple-element.41.w_ref), custom_call_target="tpu_custom_call" | custom-call | flops 1000 | bytes 1000 | tf_op jit(solution)/shard_map/keep1/pallas_call | solution.py:235
  74.4 2.1 %collective-permute-start.6 = (bf16[256,1536]{1,0:T(8,128)(2,1)S(1)}, bf16[256,1536]{1,0:T(8,128)(2,1)S(1)}, u32[]{:S(2)}, u32[]{:S(2)}) collective-permute-start(bf16[256,1536]{1,0:T(8,128)(2,1)S(1)} %get-tuple-element.48), channel_id=1, source_target_pairs={{0,1},{1,0},{2,3},{3,2},{4,5},{5,4},{6,7},{7,6},{8,9},{9,8},{10,11... | collective-permute-start | bytes 2359304 | tf_op jit(solution)/shard_map/ppermute | solution.py:26
  76.5 3.2 %keep4.1.keep_ref = f32[512,1664]{1,0:T(8,128)S(1)} custom-call(bf16[1024,1024]{1,0:T(8,128)(2,1)S(1)} %assemble.1.codes_ref, bf16[2,512,8192]{2,1,0:T(8,128)(2,1)S(1)} %get-tuple-element.41.w_ref), custom_call_target="tpu_custom_call" | custom-call | flops 1000 | bytes 1000 | tf_op jit(solution)/shard_map/keep4/pallas_call | solution.py:235
  80.7 3.2 %keep3.1.keep_ref = f32[512,1664]{1,0:T(8,128)S(1)} custom-call(bf16[1024,1024]{1,0:T(8,128)(2,1)S(1)} %assemble.1.codes_ref, bf16[2,512,8192]{2,1,0:T(8,128)(2,1)S(1)} %get-tuple-element.41.w_ref), custom_call_target="tpu_custom_call" | custom-call | flops 1000 | bytes 1000 | tf_op jit(solution)/shard_map/keep3/pallas_call | solution.py:235
  84.3 2.0 %collective-permute-start.24 = (bf16[256,1664]{1,0:T(8,128)(2,1)S(1)}, bf16[256,1664]{1,0:T(8,128)(2,1)S(1)}, u32[]{:S(2)}, u32[]{:S(2)}) collective-permute-start(bf16[256,1664]{1,0:T(8,128)(2,1)S(1)} %get-tuple-element.64), channel_id=1, source_target_pairs={{0,3},{1,2},{2,1},{3,0},{4,7},{5,6},{6,5},{7,4},{8,11},{9,10},{10,... | collective-permute-start | bytes 2555912 | tf_op jit(solution)/shard_map/ppermute | solution.py:26
  86.6 2.8 %collective-permute-start.18 = (bf16[256,1664]{1,0:T(8,128)(2,1)S(1)}, bf16[256,1664]{1,0:T(8,128)(2,1)S(1)}, u32[]{:S(2)}, u32[]{:S(2)}) collective-permute-start(bf16[256,1664]{1,0:T(8,128)(2,1)S(1)} %get-tuple-element.60), channel_id=1, source_target_pairs={{0,24},{1,25},{2,26},{3,27},{4,28},{5,29},{6,30},{7,31},{8,16},{9,... | collective-permute-start | bytes 2555912 | tf_op jit(solution)/shard_map/ppermute | solution.py:26
  89.7 1.7 %collective-permute-start.12 = (bf16[256,1664]{1,0:T(8,128)(2,1)S(1)}, bf16[256,1664]{1,0:T(8,128)(2,1)S(1)}, u32[]{:S(2)}, u32[]{:S(2)}) collective-permute-start(bf16[256,1664]{1,0:T(8,128)(2,1)S(1)} %get-tuple-element.54), channel_id=1, source_target_pairs={{0,4},{1,5},{2,6},{3,7},{4,0},{5,1},{6,2},{7,3},{8,12},{9,13},{10,... | collective-permute-start | bytes 2555912 | tf_op jit(solution)/shard_map/ppermute | solution.py:26
  91.3 10.8 %collective-permute-done.6 = bf16[256,1536]{1,0:T(8,128)(2,1)S(1)} collective-permute-done((bf16[256,1536]{1,0:T(8,128)(2,1)S(1)}, bf16[256,1536]{1,0:T(8,128)(2,1)S(1)}, u32[]{:S(2)}, u32[]{:S(2)}) %collective-permute-start.6) | collective-permute-done | bytes 786464 | tf_op jit(solution)/shard_map/ppermute | solution.py:26
  104.1 1.8 %collective-permute-start.25 = (bf16[128,1664]{1,0:T(8,128)(2,1)S(1)}, bf16[128,1664]{1,0:T(8,128)(2,1)S(1)}, u32[]{:S(2)}, u32[]{:S(2)}) collective-permute-start(bf16[128,1664]{1,0:T(8,128)(2,1)S(1)} %slice.216), channel_id=1, source_target_pairs={{0,8},{1,9},{2,10},{3,11},{4,12},{5,13},{6,14},{7,15},{8,0},{9,1},... | collective-permute-start | bytes 1277960 | tf_op jit(solution)/shard_map/ppermute | solution.py:26
  106.5 2.1 %collective-permute-start.19 = (bf16[128,1664]{1,0:T(8,128)(2,1)S(1)}, bf16[128,1664]{1,0:T(8,128)(2,1)S(1)}, u32[]{:S(2)}, u32[]{:S(2)}) collective-permute-start(bf16[128,1664]{1,0:T(8,128)(2,1)S(1)} %slice.217), channel_id=1, source_target_pairs={{0,3},{1,2},{2,1},{3,0},{4,7},{5,6},{6,5},{7,4},{8,11},{9,10},{10,... | collective-permute-start | bytes 1277960 | tf_op jit(solution)/shard_map/ppermute | solution.py:26
  108.5 7.7 %collective-permute-done.7 = bf16[128,1536]{1,0:T(8,128)(2,1)S(1)} collective-permute-done((bf16[128,1536]{1,0:T(8,128)(2,1)S(1)}, bf16[128,1536]{1,0:T(8,128)(2,1)S(1)}, u32[]{:S(2)}, u32[]{:S(2)}) %collective-permute-start.7) | collective-permute-done | bytes 393248 | tf_op jit(solution)/shard_map/ppermute | solution.py:26
  117.1 2.8 %collective-permute-start.13 = (bf16[128,1664]{1,0:T(8,128)(2,1)S(1)}, bf16[128,1664]{1,0:T(8,128)(2,1)S(1)}, u32[]{:S(2)}, u32[]{:S(2)}) collective-permute-start(bf16[128,1664]{1,0:T(8,128)(2,1)S(1)} %slice.218), channel_id=1, source_target_pairs={{0,24},{1,25},{2,26},{3,27},{4,28},{5,29},{6,30},{7,31},{8,16},{9,... | collective-permute-start | bytes 1277960 | tf_op jit(solution)/shard_map/ppermute | solution.py:26
  120.0 5.4 %collective-permute-done.8 = bf16[64,1536]{1,0:T(8,128)(2,1)S(1)} collective-permute-done((bf16[64,1536]{1,0:T(8,128)(2,1)S(1)}, bf16[64,1536]{1,0:T(8,128)(2,1)S(1)}, u32[]{:S(2)}, u32[]{:S(2)}) %collective-permute-start.8) | collective-permute-done | bytes 196640 | tf_op jit(solution)/shard_map/ppermute | solution.py:26
  125.4 1.2 collective-permute-start.9
  126.7 1.7 %collective-permute-start.32 = (bf16[64,1664]{1,0:T(8,128)(2,1)S(1)}, bf16[64,1664]{1,0:T(8,128)(2,1)S(1)}, u32[]{:S(2)}, u32[]{:S(2)}) collective-permute-start(bf16[64,1664]{1,0:T(8,128)(2,1)S(1)} %slice.220), channel_id=1, source_target_pairs={{0,4},{1,5},{2,6},{3,7},{4,0},{5,1},{6,2},{7,3},{8,12},{9,13},{10,... | collective-permute-start | bytes 638984 | tf_op jit(solution)/shard_map/ppermute | solution.py:26
  128.8 1.1 collective-permute-done.13
  130.0 1.3 collective-permute-start.14
  131.3 1.0 collective-permute-done.9
  132.4 1.4 collective-permute-done.32
  134.5 1.2 collective-permute-start.27
  135.7 1.5 %collective-permute-done.14 = bf16[64,1664]{1,0:T(8,128)(2,1)S(1)} collective-permute-done((bf16[64,1664]{1,0:T(8,128)(2,1)S(1)}, bf16[64,1664]{1,0:T(8,128)(2,1)S(1)}, u32[]{:S(2)}, u32[]{:S(2)}) %collective-permute-start.14) | collective-permute-done | bytes 213024 | tf_op jit(solution)/shard_map/ppermute | solution.py:26
  137.2 1.0 collective-permute-start.15
  139.1 2.9 %collective-permute-done.15 = bf16[32,1664]{1,0:T(8,128)(2,1)S(1)} collective-permute-done((bf16[32,1664]{1,0:T(8,128)(2,1)S(1)}, bf16[32,1664]{1,0:T(8,128)(2,1)S(1)}, u32[]{:S(2)}, u32[]{:S(2)}) %collective-permute-start.15) | collective-permute-done | bytes 106528 | tf_op jit(solution)/shard_map/ppermute | solution.py:26
  142.0 1.0 collective-permute-done.21
  (103 shorter events, 16.0 us)
Async XLA Ops:
  0.0 10.9 %copy-start = (s32[2,1024]{1,0:T(2,128)S(1)}, s32[2,1024]{1,0:T(2,128)}, u32[]{:S(2)}) copy-start(s32[2,1024]{1,0:T(2,128)} %param.17) | copy-start | bytes 24580
  0.0 10.8 %copy-start.6 = (s32[32]{0:T(128)S(1)}, s32[32]{0:T(128)}, u32[]{:S(2)}) copy-start(s32[32]{0:T(128)} %constant.82.clone) | copy-start | bytes 388
  0.0 10.9 %copy-start.4 = (s32[2,1024]{1,0:T(2,128)S(1)}, s32[2,1024]{1,0:T(2,128)}, u32[]{:S(2)}) copy-start(s32[2,1024]{1,0:T(2,128)} %param.19) | copy-start | bytes 24580
  0.0 10.9 %copy-start.5 = (s32[2,1024]{1,0:T(2,128)S(1)}, s32[2,1024]{1,0:T(2,128)}, u32[]{:S(2)}) copy-start(s32[2,1024]{1,0:T(2,128)} %param.18) | copy-start | bytes 24580
  0.0 12.3 %copy-start.3 = (f32[16]{0:T(128)S(1)}, f32[16]{0:T(128)}, u32[]{:S(2)}) copy-start(f32[16]{0:T(128)} %param.20) | copy-start | bytes 196
  9.1 3.3 %collective-permute-start = (f32[1024,256]{1,0:T(8,128)S(1)}, f32[1024,256]{1,0:T(8,128)S(1)}, u32[]{:S(2)}, u32[]{:S(2)}) collective-permute-start(f32[1024,256]{1,0:T(8,128)S(1)} %get-tuple-element.38), channel_id=1, source_target_pairs={{0,32},{32,0},{64,96},{96,64},{1,33},{33,1},{65,97},{97,65},{2,34}... | collective-permute-start | bytes 3145736 | tf_op jit(solution)/shard_map/ppermute | solution.py:26
  12.8 3.8 %collective-permute-start.1 = (bf16[1024,256]{1,0:T(8,128)(2,1)S(1)}, bf16[1024,256]{1,0:T(8,128)(2,1)S(1)}, u32[]{:S(2)}, u32[]{:S(2)}) collective-permute-start(bf16[1024,256]{1,0:T(8,128)(2,1)S(1)} %select_convert_fusion.mine_ref.own_ref), channel_id=1, source_target_pairs={{0,32},{32,0},{64,96},{96,64},{1,33},{33,1},{65,97},{97,65},{2,34}... | collective-permute-start | bytes 1572872 | tf_op jit(solution)/shard_map/ppermute | solution.py:26
  13.3 15.5 %collective-permute-start.2 = (bf16[1024,256]{1,0:T(8,128)(2,1)S(1)}, bf16[1024,256]{1,0:T(8,128)(2,1)S(1)}, u32[]{:S(2)}, u32[]{:S(2)}) collective-permute-start(bf16[1024,256]{1,0:T(8,128)(2,1)S(1)} %select_convert_fusion.mine_ref.own_ref), channel_id=1, source_target_pairs={{0,64},{32,96},{64,0},{96,32},{1,65},{33,97},{65,1},{97,33},{2,66}... | collective-permute-start | bytes 1572872 | tf_op jit(solution)/shard_map/ppermute | solution.py:26
  28.8 1.9 %collective-permute-start.3 = (bf16[1024,256]{1,0:T(8,128)(2,1)S(1)}, bf16[1024,256]{1,0:T(8,128)(2,1)S(1)}, u32[]{:S(2)}, u32[]{:S(2)}) collective-permute-start(bf16[1024,256]{1,0:T(8,128)(2,1)S(1)} %collective-permute-done.2.far_ref), channel_id=1, source_target_pairs={{0,32},{32,0},{64,96},{96,64},{1,33},{33,1},{65,97},{97,65},{2,34}... | collective-permute-start | bytes 1572872 | tf_op jit(solution)/shard_map/ppermute | solution.py:26
  32.0 19.7 %collective-permute-start.4 = (bf16[512,768]{1,0:T(8,128)(2,1)S(1)}, bf16[512,768]{1,0:T(8,128)(2,1)S(1)}, u32[]{:S(2)}, u32[]{:S(2)}) collective-permute-start(bf16[512,768]{1,0:T(8,128)(2,1)S(1)} %early0.1), channel_id=1, source_target_pairs={{0,8},{1,9},{2,10},{3,11},{4,12},{5,13},{6,14},{7,15},{8,0},{9,1},... | collective-permute-start | bytes 2359304 | tf_op jit(solution)/shard_map/ppermute | solution.py:26
  34.6 21.7 %collective-permute-start.28 = (bf16[512,768]{1,0:T(8,128)(2,1)S(1)}, bf16[512,768]{1,0:T(8,128)(2,1)S(1)}, u32[]{:S(2)}, u32[]{:S(2)}) collective-permute-start(bf16[512,768]{1,0:T(8,128)(2,1)S(1)} %early4.1), channel_id=1, source_target_pairs={{0,3},{1,2},{2,1},{3,0},{4,7},{5,6},{6,5},{7,4},{8,11},{9,10},{10,... | collective-permute-start | bytes 2359304 | tf_op jit(solution)/shard_map/ppermute | solution.py:26
  39.7 21.4 %collective-permute-start.22 = (bf16[512,768]{1,0:T(8,128)(2,1)S(1)}, bf16[512,768]{1,0:T(8,128)(2,1)S(1)}, u32[]{:S(2)}, u32[]{:S(2)}) collective-permute-start(bf16[512,768]{1,0:T(8,128)(2,1)S(1)} %early3.1), channel_id=1, source_target_pairs={{0,24},{1,25},{2,26},{3,27},{4,28},{5,29},{6,30},{7,31},{8,16},{9,... | collective-permute-start | bytes 2359304 | tf_op jit(solution)/shard_map/ppermute | solution.py:26
  42.8 20.4 %collective-permute-start.16 = (bf16[512,768]{1,0:T(8,128)(2,1)S(1)}, bf16[512,768]{1,0:T(8,128)(2,1)S(1)}, u32[]{:S(2)}, u32[]{:S(2)}) collective-permute-start(bf16[512,768]{1,0:T(8,128)(2,1)S(1)} %early2.1), channel_id=1, source_target_pairs={{0,4},{1,5},{2,6},{3,7},{4,0},{5,1},{6,2},{7,3},{8,12},{9,13},{10,... | collective-permute-start | bytes 2359304 | tf_op jit(solution)/shard_map/ppermute | solution.py:26
  45.5 19.4 %collective-permute-start.10 = (bf16[512,768]{1,0:T(8,128)(2,1)S(1)}, bf16[512,768]{1,0:T(8,128)(2,1)S(1)}, u32[]{:S(2)}, u32[]{:S(2)}) collective-permute-start(bf16[512,768]{1,0:T(8,128)(2,1)S(1)} %early1.1), channel_id=1, source_target_pairs={{0,1},{1,0},{2,3},{3,2},{4,5},{5,4},{6,7},{7,6},{8,9},{9,8},{10,11... | collective-permute-start | bytes 2359304 | tf_op jit(solution)/shard_map/ppermute | solution.py:26
  51.7 22.4 %collective-permute-start.5 = (bf16[512,768]{1,0:T(8,128)(2,1)S(1)}, bf16[512,768]{1,0:T(8,128)(2,1)S(1)}, u32[]{:S(2)}, u32[]{:S(2)}) collective-permute-start(bf16[512,768]{1,0:T(8,128)(2,1)S(1)} %late0.1), channel_id=1, source_target_pairs={{0,8},{1,9},{2,10},{3,11},{4,12},{5,13},{6,14},{7,15},{8,0},{9,1},... | collective-permute-start | bytes 2359304 | tf_op jit(solution)/shard_map/ppermute | solution.py:26
  56.3 23.4 %collective-permute-start.29 = (bf16[512,896]{1,0:T(8,128)(2,1)S(1)}, bf16[512,896]{1,0:T(8,128)(2,1)S(1)}, u32[]{:S(2)}, u32[]{:S(2)}) collective-permute-start(bf16[512,896]{1,0:T(8,128)(2,1)S(1)} %late4.1), channel_id=1, source_target_pairs={{0,3},{1,2},{2,1},{3,0},{4,7},{5,6},{6,5},{7,4},{8,11},{9,10},{10,... | collective-permute-start | bytes 2752520 | tf_op jit(solution)/shard_map/ppermute | solution.py:26
  61.1 22.8 %collective-permute-start.23 = (bf16[512,896]{1,0:T(8,128)(2,1)S(1)}, bf16[512,896]{1,0:T(8,128)(2,1)S(1)}, u32[]{:S(2)}, u32[]{:S(2)}) collective-permute-start(bf16[512,896]{1,0:T(8,128)(2,1)S(1)} %late3.1), channel_id=1, source_target_pairs={{0,24},{1,25},{2,26},{3,27},{4,28},{5,29},{6,30},{7,31},{8,16},{9,... | collective-permute-start | bytes 2752520 | tf_op jit(solution)/shard_map/ppermute | solution.py:26
  63.3 23.0 %collective-permute-start.17 = (bf16[512,896]{1,0:T(8,128)(2,1)S(1)}, bf16[512,896]{1,0:T(8,128)(2,1)S(1)}, u32[]{:S(2)}, u32[]{:S(2)}) collective-permute-start(bf16[512,896]{1,0:T(8,128)(2,1)S(1)} %late2.1), channel_id=1, source_target_pairs={{0,4},{1,5},{2,6},{3,7},{4,0},{5,1},{6,2},{7,3},{8,12},{9,13},{10,... | collective-permute-start | bytes 2752520 | tf_op jit(solution)/shard_map/ppermute | solution.py:26
  64.8 24.6 %collective-permute-start.11 = (bf16[512,896]{1,0:T(8,128)(2,1)S(1)}, bf16[512,896]{1,0:T(8,128)(2,1)S(1)}, u32[]{:S(2)}, u32[]{:S(2)}) collective-permute-start(bf16[512,896]{1,0:T(8,128)(2,1)S(1)} %late1.1), channel_id=1, source_target_pairs={{0,1},{1,0},{2,3},{3,2},{4,5},{5,4},{6,7},{7,6},{8,9},{9,8},{10,11... | collective-permute-start | bytes 2752520 | tf_op jit(solution)/shard_map/ppermute | solution.py:26
  74.4 27.7 %collective-permute-start.6 = (bf16[256,1536]{1,0:T(8,128)(2,1)S(1)}, bf16[256,1536]{1,0:T(8,128)(2,1)S(1)}, u32[]{:S(2)}, u32[]{:S(2)}) collective-permute-start(bf16[256,1536]{1,0:T(8,128)(2,1)S(1)} %get-tuple-element.48), channel_id=1, source_target_pairs={{0,1},{1,0},{2,3},{3,2},{4,5},{5,4},{6,7},{7,6},{8,9},{9,8},{10,11... | collective-permute-start | bytes 2359304 | tf_op jit(solution)/shard_map/ppermute | solution.py:26
  80.0 22.9 %collective-permute-start.30 = (bf16[256,1664]{1,0:T(8,128)(2,1)S(1)}, bf16[256,1664]{1,0:T(8,128)(2,1)S(1)}, u32[]{:S(2)}, u32[]{:S(2)}) collective-permute-start(bf16[256,1664]{1,0:T(8,128)(2,1)S(1)} %get-tuple-element.68), channel_id=1, source_target_pairs={{0,8},{1,9},{2,10},{3,11},{4,12},{5,13},{6,14},{7,15},{8,0},{9,1},... | collective-permute-start | bytes 2555912 | tf_op jit(solution)/shard_map/ppermute | solution.py:26
  84.3 19.5 %collective-permute-start.24 = (bf16[256,1664]{1,0:T(8,128)(2,1)S(1)}, bf16[256,1664]{1,0:T(8,128)(2,1)S(1)}, u32[]{:S(2)}, u32[]{:S(2)}) collective-permute-start(bf16[256,1664]{1,0:T(8,128)(2,1)S(1)} %get-tuple-element.64), channel_id=1, source_target_pairs={{0,3},{1,2},{2,1},{3,0},{4,7},{5,6},{6,5},{7,4},{8,11},{9,10},{10,... | collective-permute-start | bytes 2555912 | tf_op jit(solution)/shard_map/ppermute | solution.py:26
  86.6 19.6 %collective-permute-start.18 = (bf16[256,1664]{1,0:T(8,128)(2,1)S(1)}, bf16[256,1664]{1,0:T(8,128)(2,1)S(1)}, u32[]{:S(2)}, u32[]{:S(2)}) collective-permute-start(bf16[256,1664]{1,0:T(8,128)(2,1)S(1)} %get-tuple-element.60), channel_id=1, source_target_pairs={{0,24},{1,25},{2,26},{3,27},{4,28},{5,29},{6,30},{7,31},{8,16},{9,... | collective-permute-start | bytes 2555912 | tf_op jit(solution)/shard_map/ppermute | solution.py:26
  89.7 27.3 %collective-permute-start.12 = (bf16[256,1664]{1,0:T(8,128)(2,1)S(1)}, bf16[256,1664]{1,0:T(8,128)(2,1)S(1)}, u32[]{:S(2)}, u32[]{:S(2)}) collective-permute-start(bf16[256,1664]{1,0:T(8,128)(2,1)S(1)} %get-tuple-element.54), channel_id=1, source_target_pairs={{0,4},{1,5},{2,6},{3,7},{4,0},{5,1},{6,2},{7,3},{8,12},{9,13},{10,... | collective-permute-start | bytes 2555912 | tf_op jit(solution)/shard_map/ppermute | solution.py:26
  102.4 13.9 %collective-permute-start.7 = (bf16[128,1536]{1,0:T(8,128)(2,1)S(1)}, bf16[128,1536]{1,0:T(8,128)(2,1)S(1)}, u32[]{:S(2)}, u32[]{:S(2)}) collective-permute-start(bf16[128,1536]{1,0:T(8,128)(2,1)S(1)} %slice.219), channel_id=1, source_target_pairs={{0,4},{1,5},{2,6},{3,7},{4,0},{5,1},{6,2},{7,3},{8,12},{9,13},{10,... | collective-permute-start | bytes 1179656 | tf_op jit(solution)/shard_map/ppermute | solution.py:26
  103.2 23.4 %collective-permute-start.31 = (bf16[128,1664]{1,0:T(8,128)(2,1)S(1)}, bf16[128,1664]{1,0:T(8,128)(2,1)S(1)}, u32[]{:S(2)}, u32[]{:S(2)}) collective-permute-start(bf16[128,1664]{1,0:T(8,128)(2,1)S(1)} %slice.215), channel_id=1, source_target_pairs={{0,1},{1,0},{2,3},{3,2},{4,5},{5,4},{6,7},{7,6},{8,9},{9,8},{10,11... | collective-permute-start | bytes 1277960 | tf_op jit(solution)/shard_map/ppermute | solution.py:26
  104.1 24.3 %collective-permute-start.25 = (bf16[128,1664]{1,0:T(8,128)(2,1)S(1)}, bf16[128,1664]{1,0:T(8,128)(2,1)S(1)}, u32[]{:S(2)}, u32[]{:S(2)}) collective-permute-start(bf16[128,1664]{1,0:T(8,128)(2,1)S(1)} %slice.216), channel_id=1, source_target_pairs={{0,8},{1,9},{2,10},{3,11},{4,12},{5,13},{6,14},{7,15},{8,0},{9,1},... | collective-permute-start | bytes 1277960 | tf_op jit(solution)/shard_map/ppermute | solution.py:26
  106.5 22.1 %collective-permute-start.19 = (bf16[128,1664]{1,0:T(8,128)(2,1)S(1)}, bf16[128,1664]{1,0:T(8,128)(2,1)S(1)}, u32[]{:S(2)}, u32[]{:S(2)}) collective-permute-start(bf16[128,1664]{1,0:T(8,128)(2,1)S(1)} %slice.217), channel_id=1, source_target_pairs={{0,3},{1,2},{2,1},{3,0},{4,7},{5,6},{6,5},{7,4},{8,11},{9,10},{10,... | collective-permute-start | bytes 1277960 | tf_op jit(solution)/shard_map/ppermute | solution.py:26
  116.4 9.0 %collective-permute-start.8 = (bf16[64,1536]{1,0:T(8,128)(2,1)S(1)}, bf16[64,1536]{1,0:T(8,128)(2,1)S(1)}, u32[]{:S(2)}, u32[]{:S(2)}) collective-permute-start(bf16[64,1536]{1,0:T(8,128)(2,1)S(1)} %slice.224), channel_id=1, source_target_pairs={{0,24},{1,25},{2,26},{3,27},{4,28},{5,29},{6,30},{7,31},{8,16},{9,... | collective-permute-start | bytes 589832 | tf_op jit(solution)/shard_map/ppermute | solution.py:26
  117.1 12.7 %collective-permute-start.13 = (bf16[128,1664]{1,0:T(8,128)(2,1)S(1)}, bf16[128,1664]{1,0:T(8,128)(2,1)S(1)}, u32[]{:S(2)}, u32[]{:S(2)}) collective-permute-start(bf16[128,1664]{1,0:T(8,128)(2,1)S(1)} %slice.218), channel_id=1, source_target_pairs={{0,24},{1,25},{2,26},{3,27},{4,28},{5,29},{6,30},{7,31},{8,16},{9,... | collective-permute-start | bytes 1277960 | tf_op jit(solution)/shard_map/ppermute | solution.py:26
  125.4 7.0 %collective-permute-start.9 = (bf16[32,1536]{1,0:T(8,128)(2,1)S(1)}, bf16[32,1536]{1,0:T(8,128)(2,1)S(1)}, u32[]{:S(2)}, u32[]{:S(2)}) collective-permute-start(bf16[32,1536]{1,0:T(8,128)(2,1)S(1)} %slice.229), channel_id=1, source_target_pairs={{0,3},{1,2},{2,1},{3,0},{4,7},{5,6},{6,5},{7,4},{8,11},{9,10},{10,... | collective-permute-start | bytes 294920 | tf_op jit(solution)/shard_map/ppermute | solution.py:26
  126.7 7.1 %collective-permute-start.32 = (bf16[64,1664]{1,0:T(8,128)(2,1)S(1)}, bf16[64,1664]{1,0:T(8,128)(2,1)S(1)}, u32[]{:S(2)}, u32[]{:S(2)}) collective-permute-start(bf16[64,1664]{1,0:T(8,128)(2,1)S(1)} %slice.220), channel_id=1, source_target_pairs={{0,4},{1,5},{2,6},{3,7},{4,0},{5,1},{6,2},{7,3},{8,12},{9,13},{10,... | collective-permute-start | bytes 638984 | tf_op jit(solution)/shard_map/ppermute | solution.py:26
  128.5 5.9 %collective-permute-start.26 = (bf16[64,1664]{1,0:T(8,128)(2,1)S(1)}, bf16[64,1664]{1,0:T(8,128)(2,1)S(1)}, u32[]{:S(2)}, u32[]{:S(2)}) collective-permute-start(bf16[64,1664]{1,0:T(8,128)(2,1)S(1)} %slice.221), channel_id=1, source_target_pairs={{0,1},{1,0},{2,3},{3,2},{4,5},{5,4},{6,7},{7,6},{8,9},{9,8},{10,11... | collective-permute-start | bytes 638984 | tf_op jit(solution)/shard_map/ppermute | solution.py:26
  128.7 9.5 %collective-permute-start.20 = (bf16[64,1664]{1,0:T(8,128)(2,1)S(1)}, bf16[64,1664]{1,0:T(8,128)(2,1)S(1)}, u32[]{:S(2)}, u32[]{:S(2)}) collective-permute-start(bf16[64,1664]{1,0:T(8,128)(2,1)S(1)} %slice.222), channel_id=1, source_target_pairs={{0,8},{1,9},{2,10},{3,11},{4,12},{5,13},{6,14},{7,15},{8,0},{9,1},... | collective-permute-start | bytes 638984 | tf_op jit(solution)/shard_map/ppermute | solution.py:26
  130.0 7.1 %collective-permute-start.14 = (bf16[64,1664]{1,0:T(8,128)(2,1)S(1)}, bf16[64,1664]{1,0:T(8,128)(2,1)S(1)}, u32[]{:S(2)}, u32[]{:S(2)}) collective-permute-start(bf16[64,1664]{1,0:T(8,128)(2,1)S(1)} %slice.223), channel_id=1, source_target_pairs={{0,3},{1,2},{2,1},{3,0},{4,7},{5,6},{6,5},{7,4},{8,11},{9,10},{10,... | collective-permute-start | bytes 638984 | tf_op jit(solution)/shard_map/ppermute | solution.py:26
  133.8 9.3 %collective-permute-start.33 = (bf16[32,1664]{1,0:T(8,128)(2,1)S(1)}, bf16[32,1664]{1,0:T(8,128)(2,1)S(1)}, u32[]{:S(2)}, u32[]{:S(2)}) collective-permute-start(bf16[32,1664]{1,0:T(8,128)(2,1)S(1)} %slice.225), channel_id=1, source_target_pairs={{0,24},{1,25},{2,26},{3,27},{4,28},{5,29},{6,30},{7,31},{8,16},{9,... | collective-permute-start | bytes 319496 | tf_op jit(solution)/shard_map/ppermute | solution.py:26
  134.5 8.6 %collective-permute-start.27 = (bf16[32,1664]{1,0:T(8,128)(2,1)S(1)}, bf16[32,1664]{1,0:T(8,128)(2,1)S(1)}, u32[]{:S(2)}, u32[]{:S(2)}) collective-permute-start(bf16[32,1664]{1,0:T(8,128)(2,1)S(1)} %slice.226), channel_id=1, source_target_pairs={{0,4},{1,5},{2,6},{3,7},{4,0},{5,1},{6,2},{7,3},{8,12},{9,13},{10,... | collective-permute-start | bytes 319496 | tf_op jit(solution)/shard_map/ppermute | solution.py:26
  137.2 6.0 %copy-start.2 = (f32[1,8192]{1,0:T(1,128)S(1)}, f32[1,8192]{1,0:T(1,128)}, u32[]{:S(2)}) copy-start(f32[1,8192]{1,0:T(1,128)} %param.16) | copy-start | bytes 98308
  137.2 4.8 %collective-permute-start.15 = (bf16[32,1664]{1,0:T(8,128)(2,1)S(1)}, bf16[32,1664]{1,0:T(8,128)(2,1)S(1)}, u32[]{:S(2)}, u32[]{:S(2)}) collective-permute-start(bf16[32,1664]{1,0:T(8,128)(2,1)S(1)} %slice.228), channel_id=1, source_target_pairs={{0,8},{1,9},{2,10},{3,11},{4,12},{5,13},{6,14},{7,15},{8,0},{9,1},... | collective-permute-start | bytes 319496 | tf_op jit(solution)/shard_map/ppermute | solution.py:26
  138.3 4.8 %collective-permute-start.21 = (bf16[32,1664]{1,0:T(8,128)(2,1)S(1)}, bf16[32,1664]{1,0:T(8,128)(2,1)S(1)}, u32[]{:S(2)}, u32[]{:S(2)}) collective-permute-start(bf16[32,1664]{1,0:T(8,128)(2,1)S(1)} %slice.227), channel_id=1, source_target_pairs={{0,1},{1,0},{2,3},{3,2},{4,5},{5,4},{6,7},{7,6},{8,9},{9,8},{10,11... | collective-permute-start | bytes 319496 | tf_op jit(solution)/shard_map/ppermute | solution.py:26
  142.0 2.0 %copy-start.1 = (s32[2,1024]{1,0:T(2,128)S(1)}, s32[2,1024]{1,0:T(2,128)}, u32[]{:S(2)}) copy-start(s32[2,1024]{1,0:T(2,128)} %param.17) | copy-start | bytes 24580

commit v8 on v7

--- a/solution.py
+++ b/solution.py
@@ -397,7 +397,7 @@
         kept[p], out[p] = merge(keeps[p], early[p], late[p])
     for i in range(1, STEPS):
         for p in range(STEPS):
-            total = kept[p] + xor_swap(out[p], "lat", LINKS[(p + i) % STEPS]).astype(F32)
+            total = kept[p] + exchange(out[p], (p + i) % STEPS).astype(F32)
             m = total.shape[0] // 2
             kept[p] = total[:m] if i < STEPS - 1 else total
             out[p] = total[m:].astype(BF16)

time: 144 us -> 141 us (0.979)
  waiting for transfers between devices: 41.7 us -> 32.1 us
  starting transfers between devices: 46.9 us -> 53.3 us
    ppermute x34, waiting for transfers between devices: 41.7 us -> 32.1 us  [xor_swap(): lax.ppermute(value, axis, [(i, i ^ mask) for i in range(lax.axis_size(axi...]
    ppermute x34, starting transfers between devices: 46.9 us -> 53.3 us  [xor_swap(): lax.ppermute(value, axis, [(i, i ^ mask) for i in range(lax.axis_size(axi...]
  transfers between devices with their start and end apart: 34 -> 34, of which waited for: 16 -> 16; matrix products, arithmetic and copies ran while one was open for 4% -> 4% of each run, Pallas kernels for 26% -> 27%
where the time goes in v8:
time: 141 us
  starting transfers between devices  53.3 us (38%)
  Pallas kernels  48.5 us (34%)
  waiting for transfers between devices  32.1 us (23%)
  other arithmetic  3.12 us (2%)
  local copies, waits for them, and re-layouts  2.06 us (1%)
    ppermute x34, starting transfers between devices, xor_swap(): lax.ppermute(value, axis, [(i, i ^ mask) for i in range(lax.axis_size(axi...  53.3 us
    ppermute x34, waiting for transfers between devices, xor_swap(): lax.ppermute(value, axis, [(i, i ^ mask) for i in range(lax.axis_size(axi...  32.1 us
    pallas_call x15, Pallas kernels, call_tiny(): pl.pallas_call(kernel, out_shape=out_shape, in_specs=[VMEM] * len(args),...  29.3 us
    pallas_call x1, Pallas kernels, encode(): pl.pallas_call(functools.partial(encode_kernel, masks=masks, rows=rows, c...  9.09 us
    pallas_call x1, Pallas kernels, own_part(): pl.pallas_call(functools.partial(own_kernel, spans=spans), out_shape=[plt...  8.27 us
  transfers between devices with their start and end apart: 34, of which 16 were waited for; matrix products, arithmetic and copies ran while one was open for 4% of the time, Pallas kernels for 27%

profile of v8, /device:TPU:0, one launch (start us, length us, event | category | flops | bytes accessed | tf_op | source)
XLA Modules:
  0.0 141.0 jit_solution(2409337835222432123)
XLA Ops:
  0.0 9.1 %encode.1 = (f32[1024,256]{1,0:T(8,128)S(1)}, f32[1024,256]{1,0:T(8,128)S(1)}) custom-call(bf16[1,1024,4096]{2,1,0:T(8,128)(2,1)} %x_hbm.1, bf16[1,4096,512]{2,1,0:T(8,128)(2,1)} %w_hbm.1), custom_call_target="tpu_custom_call" | custom-call | flops 4294967296 | bytes 14680064 | tf_op jit(solution)/shard_map/encode/pallas_call | solution.py:96
  11.0 1.3 fusion
  13.3 3.3 %collective-permute-start.2 = (bf16[1024,256]{1,0:T(8,128)(2,1)S(1)}, bf16[1024,256]{1,0:T(8,128)(2,1)S(1)}, u32[]{:S(2)}, u32[]{:S(2)}) collective-permute-start(bf16[1024,256]{1,0:T(8,128)(2,1)S(1)} %select_convert_fusion.mine_ref.own_ref), channel_id=1, source_target_pairs={{0,64},{32,96},{64,0},{96,32},{1,65},{33,97},{65,1},{97,33},{2,66}... | collective-permute-start | bytes 1572872 | tf_op jit(solution)/shard_map/ppermute | solution.py:26
  16.6 8.3 %own.1 = (bf16[2,512,8192]{2,1,0:T(8,128)(2,1)S(1)}, f32[512,768]{1,0:T(8,128)S(1)}, f32[512,768]{1,0:T(8,128)S(1)}, f32[512,768]{1,0:T(8,128)S(1)}, f32[512,768]{1,0:T(8,128)S(1)}, /*index=5*/f32[512,768]{1,0:T(8,128)S(1)}) custom-call(bf16[1024,256]{1,0:T(8,128)(2,1)S(1)} %select_convert_fusion.mine_ref.own_ref, ...), custom_call_target="tpu_custom_call" | custom-call | flops 2147483648 | bytes 33554432 | tf_op jit(solution)/shard_map/own/pallas_call | solution.py:206
  24.9 3.9 %collective-permute-done.2.far_ref = bf16[1024,256]{1,0:T(8,128)(2,1)S(1)} collective-permute-done((bf16[1024,256]{1,0:T(8,128)(2,1)S(1)}, bf16[1024,256]{1,0:T(8,128)(2,1)S(1)}, u32[]{:S(2)}, u32[]{:S(2)}) %collective-permute-start.2) | collective-permute-done | bytes 524320 | tf_op jit(solution)/shard_map/ppermute | solution.py:26
  28.8 1.9 %collective-permute-done.3.far_sib_ref = bf16[1024,256]{1,0:T(8,128)(2,1)S(1)} collective-permute-done((bf16[1024,256]{1,0:T(8,128)(2,1)S(1)}, bf16[1024,256]{1,0:T(8,128)(2,1)S(1)}, u32[]{:S(2)}, u32[]{:S(2)}) %collective-permute-start.3) | collective-permute-done | bytes 524320 | tf_op jit(solution)/shard_map/ppermute | solution.py:26
  31.0 1.0 early1.1
  32.0 2.0 %collective-permute-start.6 = (bf16[512,768]{1,0:T(8,128)(2,1)S(1)}, bf16[512,768]{1,0:T(8,128)(2,1)S(1)}, u32[]{:S(2)}, u32[]{:S(2)}) collective-permute-start(bf16[512,768]{1,0:T(8,128)(2,1)S(1)} %early1.1), channel_id=1, source_target_pairs={{0,1},{1,0},{2,3},{3,2},{4,5},{5,4},{6,7},{7,6},{8,9},{9,8},{10,11... | collective-permute-start | bytes 2359304 | tf_op jit(solution)/shard_map/ppermute | solution.py:26
  35.0 1.6 %collective-permute-start.4 = (bf16[512,768]{1,0:T(8,128)(2,1)S(1)}, bf16[512,768]{1,0:T(8,128)(2,1)S(1)}, u32[]{:S(2)}, u32[]{:S(2)}) collective-permute-start(bf16[512,768]{1,0:T(8,128)(2,1)S(1)} %early0.1), channel_id=1, source_target_pairs={{0,8},{1,9},{2,10},{3,11},{4,12},{5,13},{6,14},{7,15},{8,0},{9,1},... | collective-permute-start | bytes 2359304 | tf_op jit(solution)/shard_map/ppermute | solution.py:26
  36.6 1.0 early4.1
  37.6 2.6 %collective-permute-start.18 = (bf16[512,768]{1,0:T(8,128)(2,1)S(1)}, bf16[512,768]{1,0:T(8,128)(2,1)S(1)}, u32[]{:S(2)}, u32[]{:S(2)}) collective-permute-start(bf16[512,768]{1,0:T(8,128)(2,1)S(1)} %early4.1), channel_id=1, source_target_pairs={{0,3},{1,2},{2,1},{3,0},{4,7},{5,6},{6,5},{7,4},{8,11},{9,10},{10,... | collective-permute-start | bytes 2359304 | tf_op jit(solution)/shard_map/ppermute | solution.py:26
  41.1 2.2 %collective-permute-start.13 = (bf16[512,768]{1,0:T(8,128)(2,1)S(1)}, bf16[512,768]{1,0:T(8,128)(2,1)S(1)}, u32[]{:S(2)}, u32[]{:S(2)}) collective-permute-start(bf16[512,768]{1,0:T(8,128)(2,1)S(1)} %early3.1), channel_id=1, source_target_pairs={{0,24},{1,25},{2,26},{3,27},{4,28},{5,29},{6,30},{7,31},{8,16},{9,... | collective-permute-start | bytes 2359304 | tf_op jit(solution)/shard_map/ppermute | solution.py:26
  44.3 1.8 %collective-permute-start.9 = (bf16[512,768]{1,0:T(8,128)(2,1)S(1)}, bf16[512,768]{1,0:T(8,128)(2,1)S(1)}, u32[]{:S(2)}, u32[]{:S(2)}) collective-permute-start(bf16[512,768]{1,0:T(8,128)(2,1)S(1)} %early2.1), channel_id=1, source_target_pairs={{0,4},{1,5},{2,6},{3,7},{4,0},{5,1},{6,2},{7,3},{8,12},{9,13},{10,... | collective-permute-start | bytes 2359304 | tf_op jit(solution)/shard_map/ppermute | solution.py:26
  46.1 1.4 %late0.1 = bf16[512,768]{1,0:T(8,128)(2,1)S(1)} custom-call(bf16[1024,1024]{1,0:T(8,128)(2,1)S(1)} %assemble.1.codes_ref, bf16[2,512,8192]{2,1,0:T(8,128)(2,1)S(1)} %get-tuple-element.61.w_ref), custom_call_target="tpu_custom_call" | custom-call | flops 1000 | bytes 1000 | tf_op jit(solution)/shard_map/late0/pallas_call | solution.py:235
  47.5 1.9 %late2.1 = bf16[512,896]{1,0:T(8,128)(2,1)S(1)} custom-call(bf16[1024,1024]{1,0:T(8,128)(2,1)S(1)} %assemble.1.codes_ref, bf16[2,512,8192]{2,1,0:T(8,128)(2,1)S(1)} %get-tuple-element.61.w_ref), custom_call_target="tpu_custom_call" | custom-call | flops 1000 | bytes 1000 | tf_op jit(solution)/shard_map/late2/pallas_call | solution.py:235
  49.4 1.9 %late1.1 = bf16[512,896]{1,0:T(8,128)(2,1)S(1)} custom-call(bf16[1024,1024]{1,0:T(8,128)(2,1)S(1)} %assemble.1.codes_ref, bf16[2,512,8192]{2,1,0:T(8,128)(2,1)S(1)} %get-tuple-element.61.w_ref), custom_call_target="tpu_custom_call" | custom-call | flops 1000 | bytes 1000 | tf_op jit(solution)/shard_map/late1/pallas_call | solution.py:235
  51.9 1.7 %collective-permute-start.7 = (bf16[512,896]{1,0:T(8,128)(2,1)S(1)}, bf16[512,896]{1,0:T(8,128)(2,1)S(1)}, u32[]{:S(2)}, u32[]{:S(2)}) collective-permute-start(bf16[512,896]{1,0:T(8,128)(2,1)S(1)} %late1.1), channel_id=1, source_target_pairs={{0,1},{1,0},{2,3},{3,2},{4,5},{5,4},{6,7},{7,6},{8,9},{9,8},{10,11... | collective-permute-start | bytes 2752520 | tf_op jit(solution)/shard_map/ppermute | solution.py:26
  54.4 1.5 %collective-permute-start.5 = (bf16[512,768]{1,0:T(8,128)(2,1)S(1)}, bf16[512,768]{1,0:T(8,128)(2,1)S(1)}, u32[]{:S(2)}, u32[]{:S(2)}) collective-permute-start(bf16[512,768]{1,0:T(8,128)(2,1)S(1)} %late0.1), channel_id=1, source_target_pairs={{0,8},{1,9},{2,10},{3,11},{4,12},{5,13},{6,14},{7,15},{8,0},{9,1},... | collective-permute-start | bytes 2359304 | tf_op jit(solution)/shard_map/ppermute | solution.py:26
  55.9 1.8 %late4.1 = bf16[512,896]{1,0:T(8,128)(2,1)S(1)} custom-call(bf16[1024,1024]{1,0:T(8,128)(2,1)S(1)} %assemble.1.codes_ref, bf16[2,512,8192]{2,1,0:T(8,128)(2,1)S(1)} %get-tuple-element.61.w_ref), custom_call_target="tpu_custom_call" | custom-call | flops 1000 | bytes 1000 | tf_op jit(solution)/shard_map/late4/pallas_call | solution.py:235
  57.9 2.5 %collective-permute-start.19 = (bf16[512,896]{1,0:T(8,128)(2,1)S(1)}, bf16[512,896]{1,0:T(8,128)(2,1)S(1)}, u32[]{:S(2)}, u32[]{:S(2)}) collective-permute-start(bf16[512,896]{1,0:T(8,128)(2,1)S(1)} %late4.1), channel_id=1, source_target_pairs={{0,3},{1,2},{2,1},{3,0},{4,7},{5,6},{6,5},{7,4},{8,11},{9,10},{10,... | collective-permute-start | bytes 2752520 | tf_op jit(solution)/shard_map/ppermute | solution.py:26
  60.4 1.9 %late3.1 = bf16[512,896]{1,0:T(8,128)(2,1)S(1)} custom-call(bf16[1024,1024]{1,0:T(8,128)(2,1)S(1)} %assemble.1.codes_ref, bf16[2,512,8192]{2,1,0:T(8,128)(2,1)S(1)} %get-tuple-element.61.w_ref), custom_call_target="tpu_custom_call" | custom-call | flops 1000 | bytes 1000 | tf_op jit(solution)/shard_map/late3/pallas_call | solution.py:235
  62.3 2.2 %collective-permute-start.14 = (bf16[512,896]{1,0:T(8,128)(2,1)S(1)}, bf16[512,896]{1,0:T(8,128)(2,1)S(1)}, u32[]{:S(2)}, u32[]{:S(2)}) collective-permute-start(bf16[512,896]{1,0:T(8,128)(2,1)S(1)} %late3.1), channel_id=1, source_target_pairs={{0,24},{1,25},{2,26},{3,27},{4,28},{5,29},{6,30},{7,31},{8,16},{9,... | collective-permute-start | bytes 2752520 | tf_op jit(solution)/shard_map/ppermute | solution.py:26
  64.4 1.6 %collective-permute-start.10 = (bf16[512,896]{1,0:T(8,128)(2,1)S(1)}, bf16[512,896]{1,0:T(8,128)(2,1)S(1)}, u32[]{:S(2)}, u32[]{:S(2)}) collective-permute-start(bf16[512,896]{1,0:T(8,128)(2,1)S(1)} %late2.1), channel_id=1, source_target_pairs={{0,4},{1,5},{2,6},{3,7},{4,0},{5,1},{6,2},{7,3},{8,12},{9,13},{10,... | collective-permute-start | bytes 2752520 | tf_op jit(solution)/shard_map/ppermute | solution.py:26
  66.0 2.8 %keep0.1.keep_ref = f32[512,1536]{1,0:T(8,128)S(1)} custom-call(bf16[1024,1024]{1,0:T(8,128)(2,1)S(1)} %assemble.1.codes_ref, bf16[2,512,8192]{2,1,0:T(8,128)(2,1)S(1)} %get-tuple-element.61.w_ref), custom_call_target="tpu_custom_call" | custom-call | flops 1000 | bytes 1000 | tf_op jit(solution)/shard_map/keep0/pallas_call | solution.py:235
  68.8 3.2 %keep2.1.keep_ref = f32[512,1664]{1,0:T(8,128)S(1)} custom-call(bf16[1024,1024]{1,0:T(8,128)(2,1)S(1)} %assemble.1.codes_ref, bf16[2,512,8192]{2,1,0:T(8,128)(2,1)S(1)} %get-tuple-element.61.w_ref), custom_call_target="tpu_custom_call" | custom-call | flops 1000 | bytes 1000 | tf_op jit(solution)/shard_map/keep2/pallas_call | solution.py:235
  72.0 3.2 %keep1.1.keep_ref = f32[512,1664]{1,0:T(8,128)S(1)} custom-call(bf16[1024,1024]{1,0:T(8,128)(2,1)S(1)} %assemble.1.codes_ref, bf16[2,512,8192]{2,1,0:T(8,128)(2,1)S(1)} %get-tuple-element.61.w_ref), custom_call_target="tpu_custom_call" | custom-call | flops 1000 | bytes 1000 | tf_op jit(solution)/shard_map/keep1/pallas_call | solution.py:235
  75.6 1.0 collective-permute-start.8
  76.6 3.2 %keep4.1.keep_ref = f32[512,1664]{1,0:T(8,128)S(1)} custom-call(bf16[1024,1024]{1,0:T(8,128)(2,1)S(1)} %assemble.1.codes_ref, bf16[2,512,8192]{2,1,0:T(8,128)(2,1)S(1)} %get-tuple-element.61.w_ref), custom_call_target="tpu_custom_call" | custom-call | flops 1000 | bytes 1000 | tf_op jit(solution)/shard_map/keep4/pallas_call | solution.py:235
  80.9 3.2 %keep3.1.keep_ref = f32[512,1664]{1,0:T(8,128)S(1)} custom-call(bf16[1024,1024]{1,0:T(8,128)(2,1)S(1)} %assemble.1.codes_ref, bf16[2,512,8192]{2,1,0:T(8,128)(2,1)S(1)} %get-tuple-element.61.w_ref), custom_call_target="tpu_custom_call" | custom-call | flops 1000 | bytes 1000 | tf_op jit(solution)/shard_map/keep3/pallas_call | solution.py:235
  84.5 2.6 %collective-permute-start.20 = (bf16[256,1664]{1,0:T(8,128)(2,1)S(1)}, bf16[256,1664]{1,0:T(8,128)(2,1)S(1)}, u32[]{:S(2)}, u32[]{:S(2)}) collective-permute-start(bf16[256,1664]{1,0:T(8,128)(2,1)S(1)} %get-tuple-element.92), channel_id=1, source_target_pairs={{0,3},{1,2},{2,1},{3,0},{4,7},{5,6},{6,5},{7,4},{8,11},{9,10},{10,... | collective-permute-start | bytes 2555912 | tf_op jit(solution)/shard_map/ppermute | solution.py:26
  87.4 1.7 %collective-permute-start.11 = (bf16[256,1664]{1,0:T(8,128)(2,1)S(1)}, bf16[256,1664]{1,0:T(8,128)(2,1)S(1)}, u32[]{:S(2)}, u32[]{:S(2)}) collective-permute-start(bf16[256,1664]{1,0:T(8,128)(2,1)S(1)} %get-tuple-element.78), channel_id=1, source_target_pairs={{0,4},{1,5},{2,6},{3,7},{4,0},{5,1},{6,2},{7,3},{8,12},{9,13},{10,... | collective-permute-start | bytes 2555912 | tf_op jit(solution)/shard_map/ppermute | solution.py:26
  89.4 2.8 %collective-permute-start.15 = (bf16[256,1664]{1,0:T(8,128)(2,1)S(1)}, bf16[256,1664]{1,0:T(8,128)(2,1)S(1)}, u32[]{:S(2)}, u32[]{:S(2)}) collective-permute-start(bf16[256,1664]{1,0:T(8,128)(2,1)S(1)} %get-tuple-element.85), channel_id=1, source_target_pairs={{0,24},{1,25},{2,26},{3,27},{4,28},{5,29},{6,30},{7,31},{8,16},{9,... | collective-permute-start | bytes 2555912 | tf_op jit(solution)/shard_map/ppermute | solution.py:26
  93.2 5.8 %collective-permute-done.24 = bf16[256,1664]{1,0:T(8,128)(2,1)S(1)} collective-permute-done((bf16[256,1664]{1,0:T(8,128)(2,1)S(1)}, bf16[256,1664]{1,0:T(8,128)(2,1)S(1)}, u32[]{:S(2)}, u32[]{:S(2)}) %collective-permute-start.24) | collective-permute-done | bytes 852000 | tf_op jit(solution)/shard_map/ppermute | solution.py:26
  99.2 5.0 %collective-permute-done.20 = bf16[256,1664]{1,0:T(8,128)(2,1)S(1)} collective-permute-done((bf16[256,1664]{1,0:T(8,128)(2,1)S(1)}, bf16[256,1664]{1,0:T(8,128)(2,1)S(1)}, u32[]{:S(2)}, u32[]{:S(2)}) %collective-permute-start.20) | collective-permute-done | bytes 852000 | tf_op jit(solution)/shard_map/ppermute | solution.py:26
  104.4 1.5 %collective-permute-start.25 = (bf16[128,1664]{1,0:T(8,128)(2,1)S(1)}, bf16[128,1664]{1,0:T(8,128)(2,1)S(1)}, u32[]{:S(2)}, u32[]{:S(2)}) collective-permute-start(bf16[128,1664]{1,0:T(8,128)(2,1)S(1)} %slice.216), channel_id=1, source_target_pairs={{0,8},{1,9},{2,10},{3,11},{4,12},{5,13},{6,14},{7,15},{8,0},{9,1},... | collective-permute-start | bytes 1277960 | tf_op jit(solution)/shard_map/ppermute | solution.py:26
  106.1 1.6 %collective-permute-start.12 = (bf16[128,1536]{1,0:T(8,128)(2,1)S(1)}, bf16[128,1536]{1,0:T(8,128)(2,1)S(1)}, u32[]{:S(2)}, u32[]{:S(2)}) collective-permute-start(bf16[128,1536]{1,0:T(8,128)(2,1)S(1)} %slice.219), channel_id=1, source_target_pairs={{0,4},{1,5},{2,6},{3,7},{4,0},{5,1},{6,2},{7,3},{8,12},{9,13},{10,... | collective-permute-start | bytes 1179656 | tf_op jit(solution)/shard_map/ppermute | solution.py:26
  108.7 2.0 %collective-permute-start.21 = (bf16[128,1664]{1,0:T(8,128)(2,1)S(1)}, bf16[128,1664]{1,0:T(8,128)(2,1)S(1)}, u32[]{:S(2)}, u32[]{:S(2)}) collective-permute-start(bf16[128,1664]{1,0:T(8,128)(2,1)S(1)} %slice.217), channel_id=1, source_target_pairs={{0,3},{1,2},{2,1},{3,0},{4,7},{5,6},{6,5},{7,4},{8,11},{9,10},{10,... | collective-permute-start | bytes 1277960 | tf_op jit(solution)/shard_map/ppermute | solution.py:26
  110.7 2.1 %collective-permute-start.16 = (bf16[128,1664]{1,0:T(8,128)(2,1)S(1)}, bf16[128,1664]{1,0:T(8,128)(2,1)S(1)}, u32[]{:S(2)}, u32[]{:S(2)}) collective-permute-start(bf16[128,1664]{1,0:T(8,128)(2,1)S(1)} %slice.218), channel_id=1, source_target_pairs={{0,24},{1,25},{2,26},{3,27},{4,28},{5,29},{6,30},{7,31},{8,16},{9,... | collective-permute-start | bytes 1277960 | tf_op jit(solution)/shard_map/ppermute | solution.py:26
  112.8 1.3 collective-permute-done.12
  115.4 1.9 %collective-permute-start.29 = (bf16[64,1664]{1,0:T(8,128)(2,1)S(1)}, bf16[64,1664]{1,0:T(8,128)(2,1)S(1)}, u32[]{:S(2)}, u32[]{:S(2)}) collective-permute-start(bf16[64,1664]{1,0:T(8,128)(2,1)S(1)} %slice.221), channel_id=1, source_target_pairs={{0,1},{1,0},{2,3},{3,2},{4,5},{5,4},{6,7},{7,6},{8,9},{9,8},{10,11... | collective-permute-start | bytes 638984 | tf_op jit(solution)/shard_map/ppermute | solution.py:26
  117.4 1.6 %collective-permute-start.31 = (bf16[64,1664]{1,0:T(8,128)(2,1)S(1)}, bf16[64,1664]{1,0:T(8,128)(2,1)S(1)}, u32[]{:S(2)}, u32[]{:S(2)}) collective-permute-start(bf16[64,1664]{1,0:T(8,128)(2,1)S(1)} %slice.220), channel_id=1, source_target_pairs={{0,4},{1,5},{2,6},{3,7},{4,0},{5,1},{6,2},{7,3},{8,12},{9,13},{10,... | collective-permute-start | bytes 638984 | tf_op jit(solution)/shard_map/ppermute | solution.py:26
  119.7 1.6 %collective-permute-done.16 = bf16[128,1664]{1,0:T(8,128)(2,1)S(1)} collective-permute-done((bf16[128,1664]{1,0:T(8,128)(2,1)S(1)}, bf16[128,1664]{1,0:T(8,128)(2,1)S(1)}, u32[]{:S(2)}, u32[]{:S(2)}) %collective-permute-start.16) | collective-permute-done | bytes 426016 | tf_op jit(solution)/shard_map/ppermute | solution.py:26
  121.3 2.1 %collective-permute-start.17 = (bf16[64,1536]{1,0:T(8,128)(2,1)S(1)}, bf16[64,1536]{1,0:T(8,128)(2,1)S(1)}, u32[]{:S(2)}, u32[]{:S(2)}) collective-permute-start(bf16[64,1536]{1,0:T(8,128)(2,1)S(1)} %slice.224), channel_id=1, source_target_pairs={{0,24},{1,25},{2,26},{3,27},{4,28},{5,29},{6,30},{7,31},{8,16},{9,... | collective-permute-start | bytes 589832 | tf_op jit(solution)/shard_map/ppermute | solution.py:26
  123.5 2.2 %collective-permute-start.22 = (bf16[64,1664]{1,0:T(8,128)(2,1)S(1)}, bf16[64,1664]{1,0:T(8,128)(2,1)S(1)}, u32[]{:S(2)}, u32[]{:S(2)}) collective-permute-start(bf16[64,1664]{1,0:T(8,128)(2,1)S(1)} %slice.223), channel_id=1, source_target_pairs={{0,3},{1,2},{2,1},{3,0},{4,7},{5,6},{6,5},{7,4},{8,11},{9,10},{10,... | collective-permute-start | bytes 638984 | tf_op jit(solution)/shard_map/ppermute | solution.py:26
  125.7 3.0 %collective-permute-done.17 = bf16[64,1536]{1,0:T(8,128)(2,1)S(1)} collective-permute-done((bf16[64,1536]{1,0:T(8,128)(2,1)S(1)}, bf16[64,1536]{1,0:T(8,128)(2,1)S(1)}, u32[]{:S(2)}, u32[]{:S(2)}) %collective-permute-start.17) | collective-permute-done | bytes 196640 | tf_op jit(solution)/shard_map/ppermute | solution.py:26
  129.1 2.9 %collective-permute-start.30 = (bf16[32,1664]{1,0:T(8,128)(2,1)S(1)}, bf16[32,1664]{1,0:T(8,128)(2,1)S(1)}, u32[]{:S(2)}, u32[]{:S(2)}) collective-permute-start(bf16[32,1664]{1,0:T(8,128)(2,1)S(1)} %slice.227), channel_id=1, source_target_pairs={{0,1},{1,0},{2,3},{3,2},{4,5},{5,4},{6,7},{7,6},{8,9},{9,8},{10,11... | collective-permute-start | bytes 319496 | tf_op jit(solution)/shard_map/ppermute | solution.py:26
  132.0 2.1 %collective-permute-start.33 = (bf16[32,1664]{1,0:T(8,128)(2,1)S(1)}, bf16[32,1664]{1,0:T(8,128)(2,1)S(1)}, u32[]{:S(2)}, u32[]{:S(2)}) collective-permute-start(bf16[32,1664]{1,0:T(8,128)(2,1)S(1)} %slice.225), channel_id=1, source_target_pairs={{0,24},{1,25},{2,26},{3,27},{4,28},{5,29},{6,30},{7,31},{8,16},{9,... | collective-permute-start | bytes 319496 | tf_op jit(solution)/shard_map/ppermute | solution.py:26
  134.3 5.6 %collective-permute-done.23 = bf16[32,1536]{1,0:T(8,128)(2,1)S(1)} collective-permute-done((bf16[32,1536]{1,0:T(8,128)(2,1)S(1)}, bf16[32,1536]{1,0:T(8,128)(2,1)S(1)}, u32[]{:S(2)}, u32[]{:S(2)}) %collective-permute-start.23) | collective-permute-done | bytes 98336 | tf_op jit(solution)/shard_map/ppermute | solution.py:26
  (103 shorter events, 16.1 us)
Async XLA Ops:
  0.0 10.9 %copy-start = (s32[2,1024]{1,0:T(2,128)S(1)}, s32[2,1024]{1,0:T(2,128)}, u32[]{:S(2)}) copy-start(s32[2,1024]{1,0:T(2,128)} %param.17) | copy-start | bytes 24580
  0.0 10.8 %copy-start.6 = (s32[32]{0:T(128)S(1)}, s32[32]{0:T(128)}, u32[]{:S(2)}) copy-start(s32[32]{0:T(128)} %constant.82.clone) | copy-start | bytes 388
  0.0 10.9 %copy-start.4 = (s32[2,1024]{1,0:T(2,128)S(1)}, s32[2,1024]{1,0:T(2,128)}, u32[]{:S(2)}) copy-start(s32[2,1024]{1,0:T(2,128)} %param.19) | copy-start | bytes 24580
  0.0 10.9 %copy-start.5 = (s32[2,1024]{1,0:T(2,128)S(1)}, s32[2,1024]{1,0:T(2,128)}, u32[]{:S(2)}) copy-start(s32[2,1024]{1,0:T(2,128)} %param.18) | copy-start | bytes 24580
  0.0 12.3 %copy-start.3 = (f32[16]{0:T(128)S(1)}, f32[16]{0:T(128)}, u32[]{:S(2)}) copy-start(f32[16]{0:T(128)} %param.20) | copy-start | bytes 196
  9.1 3.3 %collective-permute-start = (f32[1024,256]{1,0:T(8,128)S(1)}, f32[1024,256]{1,0:T(8,128)S(1)}, u32[]{:S(2)}, u32[]{:S(2)}) collective-permute-start(f32[1024,256]{1,0:T(8,128)S(1)} %get-tuple-element.58), channel_id=1, source_target_pairs={{0,32},{32,0},{64,96},{96,64},{1,33},{33,1},{65,97},{97,65},{2,34}... | collective-permute-start | bytes 3145736 | tf_op jit(solution)/shard_map/ppermute | solution.py:26
  12.8 3.8 %collective-permute-start.1 = (bf16[1024,256]{1,0:T(8,128)(2,1)S(1)}, bf16[1024,256]{1,0:T(8,128)(2,1)S(1)}, u32[]{:S(2)}, u32[]{:S(2)}) collective-permute-start(bf16[1024,256]{1,0:T(8,128)(2,1)S(1)} %select_convert_fusion.mine_ref.own_ref), channel_id=1, source_target_pairs={{0,32},{32,0},{64,96},{96,64},{1,33},{33,1},{65,97},{97,65},{2,34}... | collective-permute-start | bytes 1572872 | tf_op jit(solution)/shard_map/ppermute | solution.py:26
  13.3 15.5 %collective-permute-start.2 = (bf16[1024,256]{1,0:T(8,128)(2,1)S(1)}, bf16[1024,256]{1,0:T(8,128)(2,1)S(1)}, u32[]{:S(2)}, u32[]{:S(2)}) collective-permute-start(bf16[1024,256]{1,0:T(8,128)(2,1)S(1)} %select_convert_fusion.mine_ref.own_ref), channel_id=1, source_target_pairs={{0,64},{32,96},{64,0},{96,32},{1,65},{33,97},{65,1},{97,33},{2,66}... | collective-permute-start | bytes 1572872 | tf_op jit(solution)/shard_map/ppermute | solution.py:26
  28.8 1.9 %collective-permute-start.3 = (bf16[1024,256]{1,0:T(8,128)(2,1)S(1)}, bf16[1024,256]{1,0:T(8,128)(2,1)S(1)}, u32[]{:S(2)}, u32[]{:S(2)}) collective-permute-start(bf16[1024,256]{1,0:T(8,128)(2,1)S(1)} %collective-permute-done.2.far_ref), channel_id=1, source_target_pairs={{0,32},{32,0},{64,96},{96,64},{1,33},{33,1},{65,97},{97,65},{2,34}... | collective-permute-start | bytes 1572872 | tf_op jit(solution)/shard_map/ppermute | solution.py:26
  32.0 19.9 %collective-permute-start.6 = (bf16[512,768]{1,0:T(8,128)(2,1)S(1)}, bf16[512,768]{1,0:T(8,128)(2,1)S(1)}, u32[]{:S(2)}, u32[]{:S(2)}) collective-permute-start(bf16[512,768]{1,0:T(8,128)(2,1)S(1)} %early1.1), channel_id=1, source_target_pairs={{0,1},{1,0},{2,3},{3,2},{4,5},{5,4},{6,7},{7,6},{8,9},{9,8},{10,11... | collective-permute-start | bytes 2359304 | tf_op jit(solution)/shard_map/ppermute | solution.py:26
  35.0 19.4 %collective-permute-start.4 = (bf16[512,768]{1,0:T(8,128)(2,1)S(1)}, bf16[512,768]{1,0:T(8,128)(2,1)S(1)}, u32[]{:S(2)}, u32[]{:S(2)}) collective-permute-start(bf16[512,768]{1,0:T(8,128)(2,1)S(1)} %early0.1), channel_id=1, source_target_pairs={{0,8},{1,9},{2,10},{3,11},{4,12},{5,13},{6,14},{7,15},{8,0},{9,1},... | collective-permute-start | bytes 2359304 | tf_op jit(solution)/shard_map/ppermute | solution.py:26
  37.6 20.3 %collective-permute-start.18 = (bf16[512,768]{1,0:T(8,128)(2,1)S(1)}, bf16[512,768]{1,0:T(8,128)(2,1)S(1)}, u32[]{:S(2)}, u32[]{:S(2)}) collective-permute-start(bf16[512,768]{1,0:T(8,128)(2,1)S(1)} %early4.1), channel_id=1, source_target_pairs={{0,3},{1,2},{2,1},{3,0},{4,7},{5,6},{6,5},{7,4},{8,11},{9,10},{10,... | collective-permute-start | bytes 2359304 | tf_op jit(solution)/shard_map/ppermute | solution.py:26
  41.1 21.1 %collective-permute-start.13 = (bf16[512,768]{1,0:T(8,128)(2,1)S(1)}, bf16[512,768]{1,0:T(8,128)(2,1)S(1)}, u32[]{:S(2)}, u32[]{:S(2)}) collective-permute-start(bf16[512,768]{1,0:T(8,128)(2,1)S(1)} %early3.1), channel_id=1, source_target_pairs={{0,24},{1,25},{2,26},{3,27},{4,28},{5,29},{6,30},{7,31},{8,16},{9,... | collective-permute-start | bytes 2359304 | tf_op jit(solution)/shard_map/ppermute | solution.py:26
  44.3 20.2 %collective-permute-start.9 = (bf16[512,768]{1,0:T(8,128)(2,1)S(1)}, bf16[512,768]{1,0:T(8,128)(2,1)S(1)}, u32[]{:S(2)}, u32[]{:S(2)}) collective-permute-start(bf16[512,768]{1,0:T(8,128)(2,1)S(1)} %early2.1), channel_id=1, source_target_pairs={{0,4},{1,5},{2,6},{3,7},{4,0},{5,1},{6,2},{7,3},{8,12},{9,13},{10,... | collective-permute-start | bytes 2359304 | tf_op jit(solution)/shard_map/ppermute | solution.py:26
  51.9 23.7 %collective-permute-start.7 = (bf16[512,896]{1,0:T(8,128)(2,1)S(1)}, bf16[512,896]{1,0:T(8,128)(2,1)S(1)}, u32[]{:S(2)}, u32[]{:S(2)}) collective-permute-start(bf16[512,896]{1,0:T(8,128)(2,1)S(1)} %late1.1), channel_id=1, source_target_pairs={{0,1},{1,0},{2,3},{3,2},{4,5},{5,4},{6,7},{7,6},{8,9},{9,8},{10,11... | collective-permute-start | bytes 2752520 | tf_op jit(solution)/shard_map/ppermute | solution.py:26
  54.4 20.9 %collective-permute-start.5 = (bf16[512,768]{1,0:T(8,128)(2,1)S(1)}, bf16[512,768]{1,0:T(8,128)(2,1)S(1)}, u32[]{:S(2)}, u32[]{:S(2)}) collective-permute-start(bf16[512,768]{1,0:T(8,128)(2,1)S(1)} %late0.1), channel_id=1, source_target_pairs={{0,8},{1,9},{2,10},{3,11},{4,12},{5,13},{6,14},{7,15},{8,0},{9,1},... | collective-permute-start | bytes 2359304 | tf_op jit(solution)/shard_map/ppermute | solution.py:26
  57.9 22.1 %collective-permute-start.19 = (bf16[512,896]{1,0:T(8,128)(2,1)S(1)}, bf16[512,896]{1,0:T(8,128)(2,1)S(1)}, u32[]{:S(2)}, u32[]{:S(2)}) collective-permute-start(bf16[512,896]{1,0:T(8,128)(2,1)S(1)} %late4.1), channel_id=1, source_target_pairs={{0,3},{1,2},{2,1},{3,0},{4,7},{5,6},{6,5},{7,4},{8,11},{9,10},{10,... | collective-permute-start | bytes 2752520 | tf_op jit(solution)/shard_map/ppermute | solution.py:26
  62.3 21.9 %collective-permute-start.14 = (bf16[512,896]{1,0:T(8,128)(2,1)S(1)}, bf16[512,896]{1,0:T(8,128)(2,1)S(1)}, u32[]{:S(2)}, u32[]{:S(2)}) collective-permute-start(bf16[512,896]{1,0:T(8,128)(2,1)S(1)} %late3.1), channel_id=1, source_target_pairs={{0,24},{1,25},{2,26},{3,27},{4,28},{5,29},{6,30},{7,31},{8,16},{9,... | collective-permute-start | bytes 2752520 | tf_op jit(solution)/shard_map/ppermute | solution.py:26
  64.4 23.0 %collective-permute-start.10 = (bf16[512,896]{1,0:T(8,128)(2,1)S(1)}, bf16[512,896]{1,0:T(8,128)(2,1)S(1)}, u32[]{:S(2)}, u32[]{:S(2)}) collective-permute-start(bf16[512,896]{1,0:T(8,128)(2,1)S(1)} %late2.1), channel_id=1, source_target_pairs={{0,4},{1,5},{2,6},{3,7},{4,0},{5,1},{6,2},{7,3},{8,12},{9,13},{10,... | collective-permute-start | bytes 2752520 | tf_op jit(solution)/shard_map/ppermute | solution.py:26
  75.6 17.3 %collective-permute-start.8 = (bf16[256,1536]{1,0:T(8,128)(2,1)S(1)}, bf16[256,1536]{1,0:T(8,128)(2,1)S(1)}, u32[]{:S(2)}, u32[]{:S(2)}) collective-permute-start(bf16[256,1536]{1,0:T(8,128)(2,1)S(1)} %get-tuple-element.72), channel_id=1, source_target_pairs={{0,1},{1,0},{2,3},{3,2},{4,5},{5,4},{6,7},{7,6},{8,9},{9,8},{10,11... | collective-permute-start | bytes 2359304 | tf_op jit(solution)/shard_map/ppermute | solution.py:26
  80.3 18.7 %collective-permute-start.24 = (bf16[256,1664]{1,0:T(8,128)(2,1)S(1)}, bf16[256,1664]{1,0:T(8,128)(2,1)S(1)}, u32[]{:S(2)}, u32[]{:S(2)}) collective-permute-start(bf16[256,1664]{1,0:T(8,128)(2,1)S(1)} %get-tuple-element.98), channel_id=1, source_target_pairs={{0,8},{1,9},{2,10},{3,11},{4,12},{5,13},{6,14},{7,15},{8,0},{9,1},... | collective-permute-start | bytes 2555912 | tf_op jit(solution)/shard_map/ppermute | solution.py:26
  84.5 19.6 %collective-permute-start.20 = (bf16[256,1664]{1,0:T(8,128)(2,1)S(1)}, bf16[256,1664]{1,0:T(8,128)(2,1)S(1)}, u32[]{:S(2)}, u32[]{:S(2)}) collective-permute-start(bf16[256,1664]{1,0:T(8,128)(2,1)S(1)} %get-tuple-element.92), channel_id=1, source_target_pairs={{0,3},{1,2},{2,1},{3,0},{4,7},{5,6},{6,5},{7,4},{8,11},{9,10},{10,... | collective-permute-start | bytes 2555912 | tf_op jit(solution)/shard_map/ppermute | solution.py:26
  87.4 18.7 %collective-permute-start.11 = (bf16[256,1664]{1,0:T(8,128)(2,1)S(1)}, bf16[256,1664]{1,0:T(8,128)(2,1)S(1)}, u32[]{:S(2)}, u32[]{:S(2)}) collective-permute-start(bf16[256,1664]{1,0:T(8,128)(2,1)S(1)} %get-tuple-element.78), channel_id=1, source_target_pairs={{0,4},{1,5},{2,6},{3,7},{4,0},{5,1},{6,2},{7,3},{8,12},{9,13},{10,... | collective-permute-start | bytes 2555912 | tf_op jit(solution)/shard_map/ppermute | solution.py:26
  89.4 19.0 %collective-permute-start.15 = (bf16[256,1664]{1,0:T(8,128)(2,1)S(1)}, bf16[256,1664]{1,0:T(8,128)(2,1)S(1)}, u32[]{:S(2)}, u32[]{:S(2)}) collective-permute-start(bf16[256,1664]{1,0:T(8,128)(2,1)S(1)} %get-tuple-element.85), channel_id=1, source_target_pairs={{0,24},{1,25},{2,26},{3,27},{4,28},{5,29},{6,30},{7,31},{8,16},{9,... | collective-permute-start | bytes 2555912 | tf_op jit(solution)/shard_map/ppermute | solution.py:26
  104.4 9.8 %collective-permute-start.25 = (bf16[128,1664]{1,0:T(8,128)(2,1)S(1)}, bf16[128,1664]{1,0:T(8,128)(2,1)S(1)}, u32[]{:S(2)}, u32[]{:S(2)}) collective-permute-start(bf16[128,1664]{1,0:T(8,128)(2,1)S(1)} %slice.216), channel_id=1, source_target_pairs={{0,8},{1,9},{2,10},{3,11},{4,12},{5,13},{6,14},{7,15},{8,0},{9,1},... | collective-permute-start | bytes 1277960 | tf_op jit(solution)/shard_map/ppermute | solution.py:26
  106.0 9.3 %collective-permute-start.28 = (bf16[128,1664]{1,0:T(8,128)(2,1)S(1)}, bf16[128,1664]{1,0:T(8,128)(2,1)S(1)}, u32[]{:S(2)}, u32[]{:S(2)}) collective-permute-start(bf16[128,1664]{1,0:T(8,128)(2,1)S(1)} %slice.215), channel_id=1, source_target_pairs={{0,1},{1,0},{2,3},{3,2},{4,5},{5,4},{6,7},{7,6},{8,9},{9,8},{10,11... | collective-permute-start | bytes 1277960 | tf_op jit(solution)/shard_map/ppermute | solution.py:26
  106.1 8.0 %collective-permute-start.12 = (bf16[128,1536]{1,0:T(8,128)(2,1)S(1)}, bf16[128,1536]{1,0:T(8,128)(2,1)S(1)}, u32[]{:S(2)}, u32[]{:S(2)}) collective-permute-start(bf16[128,1536]{1,0:T(8,128)(2,1)S(1)} %slice.219), channel_id=1, source_target_pairs={{0,4},{1,5},{2,6},{3,7},{4,0},{5,1},{6,2},{7,3},{8,12},{9,13},{10,... | collective-permute-start | bytes 1179656 | tf_op jit(solution)/shard_map/ppermute | solution.py:26
  108.7 10.3 %collective-permute-start.21 = (bf16[128,1664]{1,0:T(8,128)(2,1)S(1)}, bf16[128,1664]{1,0:T(8,128)(2,1)S(1)}, u32[]{:S(2)}, u32[]{:S(2)}) collective-permute-start(bf16[128,1664]{1,0:T(8,128)(2,1)S(1)} %slice.217), channel_id=1, source_target_pairs={{0,3},{1,2},{2,1},{3,0},{4,7},{5,6},{6,5},{7,4},{8,11},{9,10},{10,... | collective-permute-start | bytes 1277960 | tf_op jit(solution)/shard_map/ppermute | solution.py:26
  110.7 10.6 %collective-permute-start.16 = (bf16[128,1664]{1,0:T(8,128)(2,1)S(1)}, bf16[128,1664]{1,0:T(8,128)(2,1)S(1)}, u32[]{:S(2)}, u32[]{:S(2)}) collective-permute-start(bf16[128,1664]{1,0:T(8,128)(2,1)S(1)} %slice.218), channel_id=1, source_target_pairs={{0,24},{1,25},{2,26},{3,27},{4,28},{5,29},{6,30},{7,31},{8,16},{9,... | collective-permute-start | bytes 1277960 | tf_op jit(solution)/shard_map/ppermute | solution.py:26
  115.4 13.4 %collective-permute-start.29 = (bf16[64,1664]{1,0:T(8,128)(2,1)S(1)}, bf16[64,1664]{1,0:T(8,128)(2,1)S(1)}, u32[]{:S(2)}, u32[]{:S(2)}) collective-permute-start(bf16[64,1664]{1,0:T(8,128)(2,1)S(1)} %slice.221), channel_id=1, source_target_pairs={{0,1},{1,0},{2,3},{3,2},{4,5},{5,4},{6,7},{7,6},{8,9},{9,8},{10,11... | collective-permute-start | bytes 638984 | tf_op jit(solution)/shard_map/ppermute | solution.py:26
  117.4 11.5 %collective-permute-start.31 = (bf16[64,1664]{1,0:T(8,128)(2,1)S(1)}, bf16[64,1664]{1,0:T(8,128)(2,1)S(1)}, u32[]{:S(2)}, u32[]{:S(2)}) collective-permute-start(bf16[64,1664]{1,0:T(8,128)(2,1)S(1)} %slice.220), channel_id=1, source_target_pairs={{0,4},{1,5},{2,6},{3,7},{4,0},{5,1},{6,2},{7,3},{8,12},{9,13},{10,... | collective-permute-start | bytes 638984 | tf_op jit(solution)/shard_map/ppermute | solution.py:26
  119.1 10.0 %collective-permute-start.26 = (bf16[64,1664]{1,0:T(8,128)(2,1)S(1)}, bf16[64,1664]{1,0:T(8,128)(2,1)S(1)}, u32[]{:S(2)}, u32[]{:S(2)}) collective-permute-start(bf16[64,1664]{1,0:T(8,128)(2,1)S(1)} %slice.222), channel_id=1, source_target_pairs={{0,8},{1,9},{2,10},{3,11},{4,12},{5,13},{6,14},{7,15},{8,0},{9,1},... | collective-permute-start | bytes 638984 | tf_op jit(solution)/shard_map/ppermute | solution.py:26
  121.3 7.4 %collective-permute-start.17 = (bf16[64,1536]{1,0:T(8,128)(2,1)S(1)}, bf16[64,1536]{1,0:T(8,128)(2,1)S(1)}, u32[]{:S(2)}, u32[]{:S(2)}) collective-permute-start(bf16[64,1536]{1,0:T(8,128)(2,1)S(1)} %slice.224), channel_id=1, source_target_pairs={{0,24},{1,25},{2,26},{3,27},{4,28},{5,29},{6,30},{7,31},{8,16},{9,... | collective-permute-start | bytes 589832 | tf_op jit(solution)/shard_map/ppermute | solution.py:26
  123.5 10.6 %collective-permute-start.22 = (bf16[64,1664]{1,0:T(8,128)(2,1)S(1)}, bf16[64,1664]{1,0:T(8,128)(2,1)S(1)}, u32[]{:S(2)}, u32[]{:S(2)}) collective-permute-start(bf16[64,1664]{1,0:T(8,128)(2,1)S(1)} %slice.223), channel_id=1, source_target_pairs={{0,3},{1,2},{2,1},{3,0},{4,7},{5,6},{6,5},{7,4},{8,11},{9,10},{10,... | collective-permute-start | bytes 638984 | tf_op jit(solution)/shard_map/ppermute | solution.py:26
  129.0 11.1 %collective-permute-start.32 = (bf16[32,1664]{1,0:T(8,128)(2,1)S(1)}, bf16[32,1664]{1,0:T(8,128)(2,1)S(1)}, u32[]{:S(2)}, u32[]{:S(2)}) collective-permute-start(bf16[32,1664]{1,0:T(8,128)(2,1)S(1)} %slice.226), channel_id=1, source_target_pairs={{0,4},{1,5},{2,6},{3,7},{4,0},{5,1},{6,2},{7,3},{8,12},{9,13},{10,... | collective-permute-start | bytes 319496 | tf_op jit(solution)/shard_map/ppermute | solution.py:26
  129.1 11.0 %copy-start.2 = (f32[1,8192]{1,0:T(1,128)S(1)}, f32[1,8192]{1,0:T(1,128)}, u32[]{:S(2)}) copy-start(f32[1,8192]{1,0:T(1,128)} %param.16) | copy-start | bytes 98308
  129.1 10.9 %collective-permute-start.30 = (bf16[32,1664]{1,0:T(8,128)(2,1)S(1)}, bf16[32,1664]{1,0:T(8,128)(2,1)S(1)}, u32[]{:S(2)}, u32[]{:S(2)}) collective-permute-start(bf16[32,1664]{1,0:T(8,128)(2,1)S(1)} %slice.227), channel_id=1, source_target_pairs={{0,1},{1,0},{2,3},{3,2},{4,5},{5,4},{6,7},{7,6},{8,9},{9,8},{10,11... | collective-permute-start | bytes 319496 | tf_op jit(solution)/shard_map/ppermute | solution.py:26
  132.0 8.1 %collective-permute-start.33 = (bf16[32,1664]{1,0:T(8,128)(2,1)S(1)}, bf16[32,1664]{1,0:T(8,128)(2,1)S(1)}, u32[]{:S(2)}, u32[]{:S(2)}) collective-permute-start(bf16[32,1664]{1,0:T(8,128)(2,1)S(1)} %slice.225), channel_id=1, source_target_pairs={{0,24},{1,25},{2,26},{3,27},{4,28},{5,29},{6,30},{7,31},{8,16},{9,... | collective-permute-start | bytes 319496 | tf_op jit(solution)/shard_map/ppermute | solution.py:26
  134.1 5.8 %collective-permute-start.23 = (bf16[32,1536]{1,0:T(8,128)(2,1)S(1)}, bf16[32,1536]{1,0:T(8,128)(2,1)S(1)}, u32[]{:S(2)}, u32[]{:S(2)}) collective-permute-start(bf16[32,1536]{1,0:T(8,128)(2,1)S(1)} %slice.229), channel_id=1, source_target_pairs={{0,3},{1,2},{2,1},{3,0},{4,7},{5,6},{6,5},{7,4},{8,11},{9,10},{10,... | collective-permute-start | bytes 294920 | tf_op jit(solution)/shard_map/ppermute | solution.py:26
  134.2 5.7 %collective-permute-start.27 = (bf16[32,1664]{1,0:T(8,128)(2,1)S(1)}, bf16[32,1664]{1,0:T(8,128)(2,1)S(1)}, u32[]{:S(2)}, u32[]{:S(2)}) collective-permute-start(bf16[32,1664]{1,0:T(8,128)(2,1)S(1)} %slice.228), channel_id=1, source_target_pairs={{0,8},{1,9},{2,10},{3,11},{4,12},{5,13},{6,14},{7,15},{8,0},{9,1},... | collective-permute-start | bytes 319496 | tf_op jit(solution)/shard_map/ppermute | solution.py:26
  140.0 1.0 copy-start.1

commit v9 on v5

--- a/solution.py
+++ b/solution.py
@@ -10,7 +10,7 @@
 BF16, F32 = jnp.bfloat16, jnp.float32
 LINKS = (8, 1, 4, 24, 3)
 STEPS = len(LINKS)
-LANES, TILE = 128, 256
+LANES, TILE = 128, 512
 PARTS = (12, 13, 13, 13, 13)
 EARLY = (6, 6, 6, 6, 6)
 READY = 4

time: 135 us -> 133 us (0.985)
  Pallas kernels: 48.3 us -> 38.4 us
  starting transfers between devices: 44.1 us -> 51.3 us
    pallas_call x15, Pallas kernels: 29.3 us -> 21.7 us  [call_tiny(): pl.pallas_call(kernel, out_shape=out_shape, in_specs=[VMEM] * len(args),...]
    ppermute x34, starting transfers between devices: 44.1 us -> 51.3 us  [xor_swap(): lax.ppermute(value, axis, [(i, i ^ mask) for i in range(lax.axis_size(axi...]
    pallas_call x1, Pallas kernels: 8.27 us -> 5.94 us  [own_part(): pl.pallas_call(functools.partial(own_kernel, spans=spans), out_shape=[plt...]
  transfers between devices with their start and end apart: 34 -> 34, of which waited for: 14 -> 16; matrix products, arithmetic and copies ran while one was open for 4% -> 4% of each run, Pallas kernels for 28% -> 21%
where the time goes in v9:
time: 133 us
  starting transfers between devices  51.3 us (39%)
  Pallas kernels  38.4 us (29%)
  waiting for transfers between devices  36.2 us (27%)
  other arithmetic  2.93 us (2%)
  local copies, waits for them, and re-layouts  2.06 us (2%)
  matrix products  1.34 us (1%)
    ppermute x34, starting transfers between devices, xor_swap(): lax.ppermute(value, axis, [(i, i ^ mask) for i in range(lax.axis_size(axi...  51.3 us
    ppermute x34, waiting for transfers between devices, xor_swap(): lax.ppermute(value, axis, [(i, i ^ mask) for i in range(lax.axis_size(axi...  36.2 us
    pallas_call x15, Pallas kernels, call_tiny(): pl.pallas_call(kernel, out_shape=out_shape, in_specs=[VMEM] * len(args),...  21.7 us
    pallas_call x1, Pallas kernels, encode(): pl.pallas_call(functools.partial(encode_kernel, masks=masks, rows=rows, c...  9.09 us
    pallas_call x1, Pallas kernels, own_part(): pl.pallas_call(functools.partial(own_kernel, spans=spans), out_shape=[plt...  5.94 us
  transfers between devices with their start and end apart: 34, of which 16 were waited for; matrix products, arithmetic and copies ran while one was open for 4% of the time, Pallas kernels for 21%

profile of v9, /device:TPU:0, one launch (start us, length us, event | category | flops | bytes accessed | tf_op | source)
XLA Modules:
  0.0 132.8 jit_solution(7134265977581123433)
XLA Ops:
  0.0 9.1 %encode.1 = (f32[1024,256]{1,0:T(8,128)S(1)}, f32[1024,256]{1,0:T(8,128)S(1)}) custom-call(bf16[1,1024,4096]{2,1,0:T(8,128)(2,1)} %x_hbm.1, bf16[1,4096,512]{2,1,0:T(8,128)(2,1)} %w_hbm.1), custom_call_target="tpu_custom_call" | custom-call | flops 4294967296 | bytes 14680064 | tf_op jit(solution)/shard_map/encode/pallas_call | solution.py:94
  11.0 1.3 %fusion = f32[1,1024]{1,0:T(1,128)S(1)} fusion(s32[1024]{0:T(1024)S(1)} %add.145, s32[1024]{0:T(1024)S(1)} %bitcast.33, s32[2,1024]{1,0:T(2,128)S(1)} %copy-done.4, s32[]{:T(128)S(6)} %select_n.42, s32[2,1024]{1,0:T(2,128)S(1)} %copy-done.5), kind=kOutput, calls=%fused_computation | convolution fusion | flops 13634560 | bytes 20484 | tf_op jit(solution)/shard_map/dot_general | solution.py:349
  13.3 3.3 %collective-permute-start.2 = (bf16[1024,256]{1,0:T(8,128)(2,1)S(1)}, bf16[1024,256]{1,0:T(8,128)(2,1)S(1)}, u32[]{:S(2)}, u32[]{:S(2)}) collective-permute-start(bf16[1024,256]{1,0:T(8,128)(2,1)S(1)} %select_convert_fusion.mine_ref.own_ref), channel_id=1, source_target_pairs={{0,64},{32,96},{64,0},{96,32},{1,65},{33,97},{65,1},{97,33},{2,66}... | collective-permute-start | bytes 1572872 | tf_op jit(solution)/shard_map/ppermute | solution.py:24
  16.6 5.9 %own.1 = (bf16[2,512,8192]{2,1,0:T(8,128)(2,1)S(1)}, f32[512,768]{1,0:T(8,128)S(1)}, f32[512,768]{1,0:T(8,128)S(1)}, f32[512,768]{1,0:T(8,128)S(1)}, f32[512,768]{1,0:T(8,128)S(1)}, /*index=5*/f32[512,768]{1,0:T(8,128)S(1)}) custom-call(bf16[1024,256]{1,0:T(8,128)(2,1)S(1)} %select_convert_fusion.mine_ref.own_ref, ...), custom_call_target="tpu_custom_call" | custom-call | flops 2147483648 | bytes 33554432 | tf_op jit(solution)/shard_map/own/pallas_call | solution.py:204
  22.6 6.2 %collective-permute-done.2.far_ref = bf16[1024,256]{1,0:T(8,128)(2,1)S(1)} collective-permute-done((bf16[1024,256]{1,0:T(8,128)(2,1)S(1)}, bf16[1024,256]{1,0:T(8,128)(2,1)S(1)}, u32[]{:S(2)}, u32[]{:S(2)}) %collective-permute-start.2) | collective-permute-done | bytes 524320 | tf_op jit(solution)/shard_map/ppermute | solution.py:24
  28.8 1.9 %collective-permute-done.3.far_sib_ref = bf16[1024,256]{1,0:T(8,128)(2,1)S(1)} collective-permute-done((bf16[1024,256]{1,0:T(8,128)(2,1)S(1)}, bf16[1024,256]{1,0:T(8,128)(2,1)S(1)}, u32[]{:S(2)}, u32[]{:S(2)}) %collective-permute-start.3) | collective-permute-done | bytes 524320 | tf_op jit(solution)/shard_map/ppermute | solution.py:24
  31.6 2.0 %collective-permute-start.6 = (bf16[512,768]{1,0:T(8,128)(2,1)S(1)}, bf16[512,768]{1,0:T(8,128)(2,1)S(1)}, u32[]{:S(2)}, u32[]{:S(2)}) collective-permute-start(bf16[512,768]{1,0:T(8,128)(2,1)S(1)} %early1.1), channel_id=1, source_target_pairs={{0,1},{1,0},{2,3},{3,2},{4,5},{5,4},{6,7},{7,6},{8,9},{9,8},{10,11... | collective-permute-start | bytes 2359304 | tf_op jit(solution)/shard_map/ppermute | solution.py:24
  34.3 1.6 %collective-permute-start.4 = (bf16[512,768]{1,0:T(8,128)(2,1)S(1)}, bf16[512,768]{1,0:T(8,128)(2,1)S(1)}, u32[]{:S(2)}, u32[]{:S(2)}) collective-permute-start(bf16[512,768]{1,0:T(8,128)(2,1)S(1)} %early0.1), channel_id=1, source_target_pairs={{0,8},{1,9},{2,10},{3,11},{4,12},{5,13},{6,14},{7,15},{8,0},{9,1},... | collective-permute-start | bytes 2359304 | tf_op jit(solution)/shard_map/ppermute | solution.py:24
  36.4 2.6 %collective-permute-start.18 = (bf16[512,768]{1,0:T(8,128)(2,1)S(1)}, bf16[512,768]{1,0:T(8,128)(2,1)S(1)}, u32[]{:S(2)}, u32[]{:S(2)}) collective-permute-start(bf16[512,768]{1,0:T(8,128)(2,1)S(1)} %early4.1), channel_id=1, source_target_pairs={{0,3},{1,2},{2,1},{3,0},{4,7},{5,6},{6,5},{7,4},{8,11},{9,10},{10,... | collective-permute-start | bytes 2359304 | tf_op jit(solution)/shard_map/ppermute | solution.py:24
  39.6 1.7 %collective-permute-start.9 = (bf16[512,768]{1,0:T(8,128)(2,1)S(1)}, bf16[512,768]{1,0:T(8,128)(2,1)S(1)}, u32[]{:S(2)}, u32[]{:S(2)}) collective-permute-start(bf16[512,768]{1,0:T(8,128)(2,1)S(1)} %early2.1), channel_id=1, source_target_pairs={{0,4},{1,5},{2,6},{3,7},{4,0},{5,1},{6,2},{7,3},{8,12},{9,13},{10,... | collective-permute-start | bytes 2359304 | tf_op jit(solution)/shard_map/ppermute | solution.py:24
  41.8 2.4 %collective-permute-start.13 = (bf16[512,768]{1,0:T(8,128)(2,1)S(1)}, bf16[512,768]{1,0:T(8,128)(2,1)S(1)}, u32[]{:S(2)}, u32[]{:S(2)}) collective-permute-start(bf16[512,768]{1,0:T(8,128)(2,1)S(1)} %early3.1), channel_id=1, source_target_pairs={{0,24},{1,25},{2,26},{3,27},{4,28},{5,29},{6,30},{7,31},{8,16},{9,... | collective-permute-start | bytes 2359304 | tf_op jit(solution)/shard_map/ppermute | solution.py:24
  45.2 1.2 late3.1
  46.4 1.3 late2.1
  47.7 1.2 late1.1
  48.9 2.6 %collective-permute-done.6.early_ref = bf16[512,768]{1,0:T(8,128)(2,1)S(1)} collective-permute-done((bf16[512,768]{1,0:T(8,128)(2,1)S(1)}, bf16[512,768]{1,0:T(8,128)(2,1)S(1)}, u32[]{:S(2)}, u32[]{:S(2)}) %collective-permute-start.6) | collective-permute-done | bytes 786464 | tf_op jit(solution)/shard_map/ppermute | solution.py:24
  51.5 1.7 %collective-permute-start.7 = (bf16[512,896]{1,0:T(8,128)(2,1)S(1)}, bf16[512,896]{1,0:T(8,128)(2,1)S(1)}, u32[]{:S(2)}, u32[]{:S(2)}) collective-permute-start(bf16[512,896]{1,0:T(8,128)(2,1)S(1)} %late1.1), channel_id=1, source_target_pairs={{0,1},{1,0},{2,3},{3,2},{4,5},{5,4},{6,7},{7,6},{8,9},{9,8},{10,11... | collective-permute-start | bytes 2752520 | tf_op jit(solution)/shard_map/ppermute | solution.py:24
  53.6 1.5 %collective-permute-start.5 = (bf16[512,768]{1,0:T(8,128)(2,1)S(1)}, bf16[512,768]{1,0:T(8,128)(2,1)S(1)}, u32[]{:S(2)}, u32[]{:S(2)}) collective-permute-start(bf16[512,768]{1,0:T(8,128)(2,1)S(1)} %late0.1), channel_id=1, source_target_pairs={{0,8},{1,9},{2,10},{3,11},{4,12},{5,13},{6,14},{7,15},{8,0},{9,1},... | collective-permute-start | bytes 2359304 | tf_op jit(solution)/shard_map/ppermute | solution.py:24
  55.1 1.2 late4.1
  56.7 2.5 %collective-permute-start.19 = (bf16[512,896]{1,0:T(8,128)(2,1)S(1)}, bf16[512,896]{1,0:T(8,128)(2,1)S(1)}, u32[]{:S(2)}, u32[]{:S(2)}) collective-permute-start(bf16[512,896]{1,0:T(8,128)(2,1)S(1)} %late4.1), channel_id=1, source_target_pairs={{0,3},{1,2},{2,1},{3,0},{4,7},{5,6},{6,5},{7,4},{8,11},{9,10},{10,... | collective-permute-start | bytes 2752520 | tf_op jit(solution)/shard_map/ppermute | solution.py:24
  59.3 1.6 %collective-permute-start.10 = (bf16[512,896]{1,0:T(8,128)(2,1)S(1)}, bf16[512,896]{1,0:T(8,128)(2,1)S(1)}, u32[]{:S(2)}, u32[]{:S(2)}) collective-permute-start(bf16[512,896]{1,0:T(8,128)(2,1)S(1)} %late2.1), channel_id=1, source_target_pairs={{0,4},{1,5},{2,6},{3,7},{4,0},{5,1},{6,2},{7,3},{8,12},{9,13},{10,... | collective-permute-start | bytes 2752520 | tf_op jit(solution)/shard_map/ppermute | solution.py:24
  61.8 2.1 %collective-permute-start.14 = (bf16[512,896]{1,0:T(8,128)(2,1)S(1)}, bf16[512,896]{1,0:T(8,128)(2,1)S(1)}, u32[]{:S(2)}, u32[]{:S(2)}) collective-permute-start(bf16[512,896]{1,0:T(8,128)(2,1)S(1)} %late3.1), channel_id=1, source_target_pairs={{0,24},{1,25},{2,26},{3,27},{4,28},{5,29},{6,30},{7,31},{8,16},{9,... | collective-permute-start | bytes 2752520 | tf_op jit(solution)/shard_map/ppermute | solution.py:24
  63.9 2.2 %keep0.1.keep_ref = f32[512,1536]{1,0:T(8,128)S(1)} custom-call(bf16[1024,1024]{1,0:T(8,128)(2,1)S(1)} %assemble.1.codes_ref, bf16[2,512,8192]{2,1,0:T(8,128)(2,1)S(1)} %get-tuple-element.63.w_ref), custom_call_target="tpu_custom_call" | custom-call | flops 1000 | bytes 1000 | tf_op jit(solution)/shard_map/keep0/pallas_call | solution.py:233
  66.1 2.7 %keep3.1.keep_ref = f32[512,1664]{1,0:T(8,128)S(1)} custom-call(bf16[1024,1024]{1,0:T(8,128)(2,1)S(1)} %assemble.1.codes_ref, bf16[2,512,8192]{2,1,0:T(8,128)(2,1)S(1)} %get-tuple-element.63.w_ref), custom_call_target="tpu_custom_call" | custom-call | flops 1000 | bytes 1000 | tf_op jit(solution)/shard_map/keep3/pallas_call | solution.py:233
  68.7 2.7 %keep2.1.keep_ref = f32[512,1664]{1,0:T(8,128)S(1)} custom-call(bf16[1024,1024]{1,0:T(8,128)(2,1)S(1)} %assemble.1.codes_ref, bf16[2,512,8192]{2,1,0:T(8,128)(2,1)S(1)} %get-tuple-element.63.w_ref), custom_call_target="tpu_custom_call" | custom-call | flops 1000 | bytes 1000 | tf_op jit(solution)/shard_map/keep2/pallas_call | solution.py:233
  71.4 2.6 %keep1.1.keep_ref = f32[512,1664]{1,0:T(8,128)S(1)} custom-call(bf16[1024,1024]{1,0:T(8,128)(2,1)S(1)} %assemble.1.codes_ref, bf16[2,512,8192]{2,1,0:T(8,128)(2,1)S(1)} %get-tuple-element.63.w_ref), custom_call_target="tpu_custom_call" | custom-call | flops 1000 | bytes 1000 | tf_op jit(solution)/shard_map/keep1/pallas_call | solution.py:233
  74.3 1.1 collective-permute-start.8
  75.4 2.7 %keep4.1.keep_ref = f32[512,1664]{1,0:T(8,128)S(1)} custom-call(bf16[1024,1024]{1,0:T(8,128)(2,1)S(1)} %assemble.1.codes_ref, bf16[2,512,8192]{2,1,0:T(8,128)(2,1)S(1)} %get-tuple-element.63.w_ref), custom_call_target="tpu_custom_call" | custom-call | flops 1000 | bytes 1000 | tf_op jit(solution)/shard_map/keep4/pallas_call | solution.py:233
  80.1 1.7 %collective-permute-start.11 = (bf16[256,1664]{1,0:T(8,128)(2,1)S(1)}, bf16[256,1664]{1,0:T(8,128)(2,1)S(1)}, u32[]{:S(2)}, u32[]{:S(2)}) collective-permute-start(bf16[256,1664]{1,0:T(8,128)(2,1)S(1)} %get-tuple-element.80), channel_id=1, source_target_pairs={{0,4},{1,5},{2,6},{3,7},{4,0},{5,1},{6,2},{7,3},{8,12},{9,13},{10,... | collective-permute-start | bytes 2555912 | tf_op jit(solution)/shard_map/ppermute | solution.py:24
  82.0 1.3 %collective-permute-done.14.late_ref = bf16[512,896]{1,0:T(8,128)(2,1)S(1)} collective-permute-done((bf16[512,896]{1,0:T(8,128)(2,1)S(1)}, bf16[512,896]{1,0:T(8,128)(2,1)S(1)}, u32[]{:S(2)}, u32[]{:S(2)}) %collective-permute-start.14) | collective-permute-done | bytes 917536 | tf_op jit(solution)/shard_map/ppermute | solution.py:24
  83.3 2.1 %collective-permute-start.15 = (bf16[256,1664]{1,0:T(8,128)(2,1)S(1)}, bf16[256,1664]{1,0:T(8,128)(2,1)S(1)}, u32[]{:S(2)}, u32[]{:S(2)}) collective-permute-start(bf16[256,1664]{1,0:T(8,128)(2,1)S(1)} %get-tuple-element.88), channel_id=1, source_target_pairs={{0,24},{1,25},{2,26},{3,27},{4,28},{5,29},{6,30},{7,31},{8,16},{9,... | collective-permute-start | bytes 2555912 | tf_op jit(solution)/shard_map/ppermute | solution.py:24
  85.7 2.2 %collective-permute-start.20 = (bf16[256,1664]{1,0:T(8,128)(2,1)S(1)}, bf16[256,1664]{1,0:T(8,128)(2,1)S(1)}, u32[]{:S(2)}, u32[]{:S(2)}) collective-permute-start(bf16[256,1664]{1,0:T(8,128)(2,1)S(1)} %get-tuple-element.96), channel_id=1, source_target_pairs={{0,3},{1,2},{2,1},{3,0},{4,7},{5,6},{6,5},{7,4},{8,11},{9,10},{10,... | collective-permute-start | bytes 2555912 | tf_op jit(solution)/shard_map/ppermute | solution.py:24
  87.9 3.8 %collective-permute-done.8 = bf16[256,1536]{1,0:T(8,128)(2,1)S(1)} collective-permute-done((bf16[256,1536]{1,0:T(8,128)(2,1)S(1)}, bf16[256,1536]{1,0:T(8,128)(2,1)S(1)}, u32[]{:S(2)}, u32[]{:S(2)}) %collective-permute-start.8) | collective-permute-done | bytes 786464 | tf_op jit(solution)/shard_map/ppermute | solution.py:24
  91.9 5.9 %collective-permute-done.24 = bf16[256,1664]{1,0:T(8,128)(2,1)S(1)} collective-permute-done((bf16[256,1664]{1,0:T(8,128)(2,1)S(1)}, bf16[256,1664]{1,0:T(8,128)(2,1)S(1)}, u32[]{:S(2)}, u32[]{:S(2)}) %collective-permute-start.24) | collective-permute-done | bytes 852000 | tf_op jit(solution)/shard_map/ppermute | solution.py:24
  98.8 1.6 %collective-permute-start.12 = (bf16[128,1536]{1,0:T(8,128)(2,1)S(1)}, bf16[128,1536]{1,0:T(8,128)(2,1)S(1)}, u32[]{:S(2)}, u32[]{:S(2)}) collective-permute-start(bf16[128,1536]{1,0:T(8,128)(2,1)S(1)} %slice.219), channel_id=1, source_target_pairs={{0,4},{1,5},{2,6},{3,7},{4,0},{5,1},{6,2},{7,3},{8,12},{9,13},{10,... | collective-permute-start | bytes 1179656 | tf_op jit(solution)/shard_map/ppermute | solution.py:24
  100.6 2.0 %collective-permute-done.15 = bf16[256,1664]{1,0:T(8,128)(2,1)S(1)} collective-permute-done((bf16[256,1664]{1,0:T(8,128)(2,1)S(1)}, bf16[256,1664]{1,0:T(8,128)(2,1)S(1)}, u32[]{:S(2)}, u32[]{:S(2)}) %collective-permute-start.15) | collective-permute-done | bytes 852000 | tf_op jit(solution)/shard_map/ppermute | solution.py:24
  102.8 2.2 %collective-permute-start.16 = (bf16[128,1664]{1,0:T(8,128)(2,1)S(1)}, bf16[128,1664]{1,0:T(8,128)(2,1)S(1)}, u32[]{:S(2)}, u32[]{:S(2)}) collective-permute-start(bf16[128,1664]{1,0:T(8,128)(2,1)S(1)} %slice.218), channel_id=1, source_target_pairs={{0,24},{1,25},{2,26},{3,27},{4,28},{5,29},{6,30},{7,31},{8,16},{9,... | collective-permute-start | bytes 1277960 | tf_op jit(solution)/shard_map/ppermute | solution.py:24
  105.3 2.1 %collective-permute-start.21 = (bf16[128,1664]{1,0:T(8,128)(2,1)S(1)}, bf16[128,1664]{1,0:T(8,128)(2,1)S(1)}, u32[]{:S(2)}, u32[]{:S(2)}) collective-permute-start(bf16[128,1664]{1,0:T(8,128)(2,1)S(1)} %slice.217), channel_id=1, source_target_pairs={{0,3},{1,2},{2,1},{3,0},{4,7},{5,6},{6,5},{7,4},{8,11},{9,10},{10,... | collective-permute-start | bytes 1277960 | tf_op jit(solution)/shard_map/ppermute | solution.py:24
  108.0 1.7 %collective-permute-start.31 = (bf16[64,1664]{1,0:T(8,128)(2,1)S(1)}, bf16[64,1664]{1,0:T(8,128)(2,1)S(1)}, u32[]{:S(2)}, u32[]{:S(2)}) collective-permute-start(bf16[64,1664]{1,0:T(8,128)(2,1)S(1)} %slice.220), channel_id=1, source_target_pairs={{0,4},{1,5},{2,6},{3,7},{4,0},{5,1},{6,2},{7,3},{8,12},{9,13},{10,... | collective-permute-start | bytes 638984 | tf_op jit(solution)/shard_map/ppermute | solution.py:24
  109.7 3.5 %collective-permute-done.16 = bf16[128,1664]{1,0:T(8,128)(2,1)S(1)} collective-permute-done((bf16[128,1664]{1,0:T(8,128)(2,1)S(1)}, bf16[128,1664]{1,0:T(8,128)(2,1)S(1)}, u32[]{:S(2)}, u32[]{:S(2)}) %collective-permute-start.16) | collective-permute-done | bytes 426016 | tf_op jit(solution)/shard_map/ppermute | solution.py:24
  113.2 2.1 %collective-permute-start.17 = (bf16[64,1536]{1,0:T(8,128)(2,1)S(1)}, bf16[64,1536]{1,0:T(8,128)(2,1)S(1)}, u32[]{:S(2)}, u32[]{:S(2)}) collective-permute-start(bf16[64,1536]{1,0:T(8,128)(2,1)S(1)} %slice.224), channel_id=1, source_target_pairs={{0,24},{1,25},{2,26},{3,27},{4,28},{5,29},{6,30},{7,31},{8,16},{9,... | collective-permute-start | bytes 589832 | tf_op jit(solution)/shard_map/ppermute | solution.py:24
  115.5 1.1 collective-permute-start.29
  117.5 1.2 collective-permute-start.22
  118.8 2.5 %collective-permute-done.17 = bf16[64,1536]{1,0:T(8,128)(2,1)S(1)} collective-permute-done((bf16[64,1536]{1,0:T(8,128)(2,1)S(1)}, bf16[64,1536]{1,0:T(8,128)(2,1)S(1)}, u32[]{:S(2)}, u32[]{:S(2)}) %collective-permute-start.17) | collective-permute-done | bytes 196640 | tf_op jit(solution)/shard_map/ppermute | solution.py:24
  121.4 2.2 %collective-permute-start.33 = (bf16[32,1664]{1,0:T(8,128)(2,1)S(1)}, bf16[32,1664]{1,0:T(8,128)(2,1)S(1)}, u32[]{:S(2)}, u32[]{:S(2)}) collective-permute-start(bf16[32,1664]{1,0:T(8,128)(2,1)S(1)} %slice.225), channel_id=1, source_target_pairs={{0,24},{1,25},{2,26},{3,27},{4,28},{5,29},{6,30},{7,31},{8,16},{9,... | collective-permute-start | bytes 319496 | tf_op jit(solution)/shard_map/ppermute | solution.py:24
  124.2 1.1 collective-permute-start.30
  125.3 1.6 %collective-permute-start.23 = (bf16[32,1536]{1,0:T(8,128)(2,1)S(1)}, bf16[32,1536]{1,0:T(8,128)(2,1)S(1)}, u32[]{:S(2)}, u32[]{:S(2)}) collective-permute-start(bf16[32,1536]{1,0:T(8,128)(2,1)S(1)} %slice.229), channel_id=1, source_target_pairs={{0,3},{1,2},{2,1},{3,0},{4,7},{5,6},{6,5},{7,4},{8,11},{9,10},{10,... | collective-permute-start | bytes 294920 | tf_op jit(solution)/shard_map/ppermute | solution.py:24
  127.0 1.0 collective-permute-start.27
  128.0 3.2 %collective-permute-done.23 = bf16[32,1536]{1,0:T(8,128)(2,1)S(1)} collective-permute-done((bf16[32,1536]{1,0:T(8,128)(2,1)S(1)}, bf16[32,1536]{1,0:T(8,128)(2,1)S(1)}, u32[]{:S(2)}, u32[]{:S(2)}) %collective-permute-start.23) | collective-permute-done | bytes 98336 | tf_op jit(solution)/shard_map/ppermute | solution.py:24
  (103 shorter events, 17.4 us)
Async XLA Ops:
  0.0 10.9 %copy-start = (s32[2,1024]{1,0:T(2,128)S(1)}, s32[2,1024]{1,0:T(2,128)}, u32[]{:S(2)}) copy-start(s32[2,1024]{1,0:T(2,128)} %param.17) | copy-start | bytes 24580
  0.0 10.8 %copy-start.6 = (s32[32]{0:T(128)S(1)}, s32[32]{0:T(128)}, u32[]{:S(2)}) copy-start(s32[32]{0:T(128)} %constant.82.clone) | copy-start | bytes 388
  0.0 10.9 %copy-start.4 = (s32[2,1024]{1,0:T(2,128)S(1)}, s32[2,1024]{1,0:T(2,128)}, u32[]{:S(2)}) copy-start(s32[2,1024]{1,0:T(2,128)} %param.19) | copy-start | bytes 24580
  0.0 10.9 %copy-start.5 = (s32[2,1024]{1,0:T(2,128)S(1)}, s32[2,1024]{1,0:T(2,128)}, u32[]{:S(2)}) copy-start(s32[2,1024]{1,0:T(2,128)} %param.18) | copy-start | bytes 24580
  0.0 12.3 %copy-start.3 = (f32[16]{0:T(128)S(1)}, f32[16]{0:T(128)}, u32[]{:S(2)}) copy-start(f32[16]{0:T(128)} %param.20) | copy-start | bytes 196
  9.1 3.3 %collective-permute-start = (f32[1024,256]{1,0:T(8,128)S(1)}, f32[1024,256]{1,0:T(8,128)S(1)}, u32[]{:S(2)}, u32[]{:S(2)}) collective-permute-start(f32[1024,256]{1,0:T(8,128)S(1)} %get-tuple-element.60), channel_id=1, source_target_pairs={{0,32},{32,0},{64,96},{96,64},{1,33},{33,1},{65,97},{97,65},{2,34}... | collective-permute-start | bytes 3145736 | tf_op jit(solution)/shard_map/ppermute | solution.py:24
  12.8 3.8 %collective-permute-start.1 = (bf16[1024,256]{1,0:T(8,128)(2,1)S(1)}, bf16[1024,256]{1,0:T(8,128)(2,1)S(1)}, u32[]{:S(2)}, u32[]{:S(2)}) collective-permute-start(bf16[1024,256]{1,0:T(8,128)(2,1)S(1)} %select_convert_fusion.mine_ref.own_ref), channel_id=1, source_target_pairs={{0,32},{32,0},{64,96},{96,64},{1,33},{33,1},{65,97},{97,65},{2,34}... | collective-permute-start | bytes 1572872 | tf_op jit(solution)/shard_map/ppermute | solution.py:24
  13.3 15.5 %collective-permute-start.2 = (bf16[1024,256]{1,0:T(8,128)(2,1)S(1)}, bf16[1024,256]{1,0:T(8,128)(2,1)S(1)}, u32[]{:S(2)}, u32[]{:S(2)}) collective-permute-start(bf16[1024,256]{1,0:T(8,128)(2,1)S(1)} %select_convert_fusion.mine_ref.own_ref), channel_id=1, source_target_pairs={{0,64},{32,96},{64,0},{96,32},{1,65},{33,97},{65,1},{97,33},{2,66}... | collective-permute-start | bytes 1572872 | tf_op jit(solution)/shard_map/ppermute | solution.py:24
  28.8 1.9 %collective-permute-start.3 = (bf16[1024,256]{1,0:T(8,128)(2,1)S(1)}, bf16[1024,256]{1,0:T(8,128)(2,1)S(1)}, u32[]{:S(2)}, u32[]{:S(2)}) collective-permute-start(bf16[1024,256]{1,0:T(8,128)(2,1)S(1)} %collective-permute-done.2.far_ref), channel_id=1, source_target_pairs={{0,32},{32,0},{64,96},{96,64},{1,33},{33,1},{65,97},{97,65},{2,34}... | collective-permute-start | bytes 1572872 | tf_op jit(solution)/shard_map/ppermute | solution.py:24
  31.6 19.9 %collective-permute-start.6 = (bf16[512,768]{1,0:T(8,128)(2,1)S(1)}, bf16[512,768]{1,0:T(8,128)(2,1)S(1)}, u32[]{:S(2)}, u32[]{:S(2)}) collective-permute-start(bf16[512,768]{1,0:T(8,128)(2,1)S(1)} %early1.1), channel_id=1, source_target_pairs={{0,1},{1,0},{2,3},{3,2},{4,5},{5,4},{6,7},{7,6},{8,9},{9,8},{10,11... | collective-permute-start | bytes 2359304 | tf_op jit(solution)/shard_map/ppermute | solution.py:24
  34.3 19.4 %collective-permute-start.4 = (bf16[512,768]{1,0:T(8,128)(2,1)S(1)}, bf16[512,768]{1,0:T(8,128)(2,1)S(1)}, u32[]{:S(2)}, u32[]{:S(2)}) collective-permute-start(bf16[512,768]{1,0:T(8,128)(2,1)S(1)} %early0.1), channel_id=1, source_target_pairs={{0,8},{1,9},{2,10},{3,11},{4,12},{5,13},{6,14},{7,15},{8,0},{9,1},... | collective-permute-start | bytes 2359304 | tf_op jit(solution)/shard_map/ppermute | solution.py:24
  36.4 20.3 %collective-permute-start.18 = (bf16[512,768]{1,0:T(8,128)(2,1)S(1)}, bf16[512,768]{1,0:T(8,128)(2,1)S(1)}, u32[]{:S(2)}, u32[]{:S(2)}) collective-permute-start(bf16[512,768]{1,0:T(8,128)(2,1)S(1)} %early4.1), channel_id=1, source_target_pairs={{0,3},{1,2},{2,1},{3,0},{4,7},{5,6},{6,5},{7,4},{8,11},{9,10},{10,... | collective-permute-start | bytes 2359304 | tf_op jit(solution)/shard_map/ppermute | solution.py:24
  39.6 19.7 %collective-permute-start.9 = (bf16[512,768]{1,0:T(8,128)(2,1)S(1)}, bf16[512,768]{1,0:T(8,128)(2,1)S(1)}, u32[]{:S(2)}, u32[]{:S(2)}) collective-permute-start(bf16[512,768]{1,0:T(8,128)(2,1)S(1)} %early2.1), channel_id=1, source_target_pairs={{0,4},{1,5},{2,6},{3,7},{4,0},{5,1},{6,2},{7,3},{8,12},{9,13},{10,... | collective-permute-start | bytes 2359304 | tf_op jit(solution)/shard_map/ppermute | solution.py:24
  41.8 19.9 %collective-permute-start.13 = (bf16[512,768]{1,0:T(8,128)(2,1)S(1)}, bf16[512,768]{1,0:T(8,128)(2,1)S(1)}, u32[]{:S(2)}, u32[]{:S(2)}) collective-permute-start(bf16[512,768]{1,0:T(8,128)(2,1)S(1)} %early3.1), channel_id=1, source_target_pairs={{0,24},{1,25},{2,26},{3,27},{4,28},{5,29},{6,30},{7,31},{8,16},{9,... | collective-permute-start | bytes 2359304 | tf_op jit(solution)/shard_map/ppermute | solution.py:24
  51.5 22.8 %collective-permute-start.7 = (bf16[512,896]{1,0:T(8,128)(2,1)S(1)}, bf16[512,896]{1,0:T(8,128)(2,1)S(1)}, u32[]{:S(2)}, u32[]{:S(2)}) collective-permute-start(bf16[512,896]{1,0:T(8,128)(2,1)S(1)} %late1.1), channel_id=1, source_target_pairs={{0,1},{1,0},{2,3},{3,2},{4,5},{5,4},{6,7},{7,6},{8,9},{9,8},{10,11... | collective-permute-start | bytes 2752520 | tf_op jit(solution)/shard_map/ppermute | solution.py:24
  53.6 20.4 %collective-permute-start.5 = (bf16[512,768]{1,0:T(8,128)(2,1)S(1)}, bf16[512,768]{1,0:T(8,128)(2,1)S(1)}, u32[]{:S(2)}, u32[]{:S(2)}) collective-permute-start(bf16[512,768]{1,0:T(8,128)(2,1)S(1)} %late0.1), channel_id=1, source_target_pairs={{0,8},{1,9},{2,10},{3,11},{4,12},{5,13},{6,14},{7,15},{8,0},{9,1},... | collective-permute-start | bytes 2359304 | tf_op jit(solution)/shard_map/ppermute | solution.py:24
  56.7 22.1 %collective-permute-start.19 = (bf16[512,896]{1,0:T(8,128)(2,1)S(1)}, bf16[512,896]{1,0:T(8,128)(2,1)S(1)}, u32[]{:S(2)}, u32[]{:S(2)}) collective-permute-start(bf16[512,896]{1,0:T(8,128)(2,1)S(1)} %late4.1), channel_id=1, source_target_pairs={{0,3},{1,2},{2,1},{3,0},{4,7},{5,6},{6,5},{7,4},{8,11},{9,10},{10,... | collective-permute-start | bytes 2752520 | tf_op jit(solution)/shard_map/ppermute | solution.py:24
  59.3 20.8 %collective-permute-start.10 = (bf16[512,896]{1,0:T(8,128)(2,1)S(1)}, bf16[512,896]{1,0:T(8,128)(2,1)S(1)}, u32[]{:S(2)}, u32[]{:S(2)}) collective-permute-start(bf16[512,896]{1,0:T(8,128)(2,1)S(1)} %late2.1), channel_id=1, source_target_pairs={{0,4},{1,5},{2,6},{3,7},{4,0},{5,1},{6,2},{7,3},{8,12},{9,13},{10,... | collective-permute-start | bytes 2752520 | tf_op jit(solution)/shard_map/ppermute | solution.py:24
  61.8 21.6 %collective-permute-start.14 = (bf16[512,896]{1,0:T(8,128)(2,1)S(1)}, bf16[512,896]{1,0:T(8,128)(2,1)S(1)}, u32[]{:S(2)}, u32[]{:S(2)}) collective-permute-start(bf16[512,896]{1,0:T(8,128)(2,1)S(1)} %late3.1), channel_id=1, source_target_pairs={{0,24},{1,25},{2,26},{3,27},{4,28},{5,29},{6,30},{7,31},{8,16},{9,... | collective-permute-start | bytes 2752520 | tf_op jit(solution)/shard_map/ppermute | solution.py:24
  74.3 17.3 %collective-permute-start.8 = (bf16[256,1536]{1,0:T(8,128)(2,1)S(1)}, bf16[256,1536]{1,0:T(8,128)(2,1)S(1)}, u32[]{:S(2)}, u32[]{:S(2)}) collective-permute-start(bf16[256,1536]{1,0:T(8,128)(2,1)S(1)} %get-tuple-element.74), channel_id=1, source_target_pairs={{0,1},{1,0},{2,3},{3,2},{4,5},{5,4},{6,7},{7,6},{8,9},{9,8},{10,11... | collective-permute-start | bytes 2359304 | tf_op jit(solution)/shard_map/ppermute | solution.py:24
  79.1 18.7 %collective-permute-start.24 = (bf16[256,1664]{1,0:T(8,128)(2,1)S(1)}, bf16[256,1664]{1,0:T(8,128)(2,1)S(1)}, u32[]{:S(2)}, u32[]{:S(2)}) collective-permute-start(bf16[256,1664]{1,0:T(8,128)(2,1)S(1)} %get-tuple-element.102), channel_id=1, source_target_pairs={{0,8},{1,9},{2,10},{3,11},{4,12},{5,13},{6,14},{7,15},{8,0},{9,1},... | collective-permute-start | bytes 2555912 | tf_op jit(solution)/shard_map/ppermute | solution.py:24
  80.1 18.7 %collective-permute-start.11 = (bf16[256,1664]{1,0:T(8,128)(2,1)S(1)}, bf16[256,1664]{1,0:T(8,128)(2,1)S(1)}, u32[]{:S(2)}, u32[]{:S(2)}) collective-permute-start(bf16[256,1664]{1,0:T(8,128)(2,1)S(1)} %get-tuple-element.80), channel_id=1, source_target_pairs={{0,4},{1,5},{2,6},{3,7},{4,0},{5,1},{6,2},{7,3},{8,12},{9,13},{10,... | collective-permute-start | bytes 2555912 | tf_op jit(solution)/shard_map/ppermute | solution.py:24
  83.3 19.2 %collective-permute-start.15 = (bf16[256,1664]{1,0:T(8,128)(2,1)S(1)}, bf16[256,1664]{1,0:T(8,128)(2,1)S(1)}, u32[]{:S(2)}, u32[]{:S(2)}) collective-permute-start(bf16[256,1664]{1,0:T(8,128)(2,1)S(1)} %get-tuple-element.88), channel_id=1, source_target_pairs={{0,24},{1,25},{2,26},{3,27},{4,28},{5,29},{6,30},{7,31},{8,16},{9,... | collective-permute-start | bytes 2555912 | tf_op jit(solution)/shard_map/ppermute | solution.py:24
  85.7 19.3 %collective-permute-start.20 = (bf16[256,1664]{1,0:T(8,128)(2,1)S(1)}, bf16[256,1664]{1,0:T(8,128)(2,1)S(1)}, u32[]{:S(2)}, u32[]{:S(2)}) collective-permute-start(bf16[256,1664]{1,0:T(8,128)(2,1)S(1)} %get-tuple-element.96), channel_id=1, source_target_pairs={{0,3},{1,2},{2,1},{3,0},{4,7},{5,6},{6,5},{7,4},{8,11},{9,10},{10,... | collective-permute-start | bytes 2555912 | tf_op jit(solution)/shard_map/ppermute | solution.py:24
  98.0 9.9 %collective-permute-start.28 = (bf16[128,1664]{1,0:T(8,128)(2,1)S(1)}, bf16[128,1664]{1,0:T(8,128)(2,1)S(1)}, u32[]{:S(2)}, u32[]{:S(2)}) collective-permute-start(bf16[128,1664]{1,0:T(8,128)(2,1)S(1)} %slice.215), channel_id=1, source_target_pairs={{0,1},{1,0},{2,3},{3,2},{4,5},{5,4},{6,7},{7,6},{8,9},{9,8},{10,11... | collective-permute-start | bytes 1277960 | tf_op jit(solution)/shard_map/ppermute | solution.py:24
  98.8 9.0 %collective-permute-start.12 = (bf16[128,1536]{1,0:T(8,128)(2,1)S(1)}, bf16[128,1536]{1,0:T(8,128)(2,1)S(1)}, u32[]{:S(2)}, u32[]{:S(2)}) collective-permute-start(bf16[128,1536]{1,0:T(8,128)(2,1)S(1)} %slice.219), channel_id=1, source_target_pairs={{0,4},{1,5},{2,6},{3,7},{4,0},{5,1},{6,2},{7,3},{8,12},{9,13},{10,... | collective-permute-start | bytes 1179656 | tf_op jit(solution)/shard_map/ppermute | solution.py:24
  102.8 10.4 %collective-permute-start.16 = (bf16[128,1664]{1,0:T(8,128)(2,1)S(1)}, bf16[128,1664]{1,0:T(8,128)(2,1)S(1)}, u32[]{:S(2)}, u32[]{:S(2)}) collective-permute-start(bf16[128,1664]{1,0:T(8,128)(2,1)S(1)} %slice.218), channel_id=1, source_target_pairs={{0,24},{1,25},{2,26},{3,27},{4,28},{5,29},{6,30},{7,31},{8,16},{9,... | collective-permute-start | bytes 1277960 | tf_op jit(solution)/shard_map/ppermute | solution.py:24
  105.2 10.1 %collective-permute-start.25 = (bf16[128,1664]{1,0:T(8,128)(2,1)S(1)}, bf16[128,1664]{1,0:T(8,128)(2,1)S(1)}, u32[]{:S(2)}, u32[]{:S(2)}) collective-permute-start(bf16[128,1664]{1,0:T(8,128)(2,1)S(1)} %slice.216), channel_id=1, source_target_pairs={{0,8},{1,9},{2,10},{3,11},{4,12},{5,13},{6,14},{7,15},{8,0},{9,1},... | collective-permute-start | bytes 1277960 | tf_op jit(solution)/shard_map/ppermute | solution.py:24
  105.3 11.3 %collective-permute-start.21 = (bf16[128,1664]{1,0:T(8,128)(2,1)S(1)}, bf16[128,1664]{1,0:T(8,128)(2,1)S(1)}, u32[]{:S(2)}, u32[]{:S(2)}) collective-permute-start(bf16[128,1664]{1,0:T(8,128)(2,1)S(1)} %slice.217), channel_id=1, source_target_pairs={{0,3},{1,2},{2,1},{3,0},{4,7},{5,6},{6,5},{7,4},{8,11},{9,10},{10,... | collective-permute-start | bytes 1277960 | tf_op jit(solution)/shard_map/ppermute | solution.py:24
  108.0 13.3 %collective-permute-start.31 = (bf16[64,1664]{1,0:T(8,128)(2,1)S(1)}, bf16[64,1664]{1,0:T(8,128)(2,1)S(1)}, u32[]{:S(2)}, u32[]{:S(2)}) collective-permute-start(bf16[64,1664]{1,0:T(8,128)(2,1)S(1)} %slice.220), channel_id=1, source_target_pairs={{0,4},{1,5},{2,6},{3,7},{4,0},{5,1},{6,2},{7,3},{8,12},{9,13},{10,... | collective-permute-start | bytes 638984 | tf_op jit(solution)/shard_map/ppermute | solution.py:24
  113.2 8.0 %collective-permute-start.17 = (bf16[64,1536]{1,0:T(8,128)(2,1)S(1)}, bf16[64,1536]{1,0:T(8,128)(2,1)S(1)}, u32[]{:S(2)}, u32[]{:S(2)}) collective-permute-start(bf16[64,1536]{1,0:T(8,128)(2,1)S(1)} %slice.224), channel_id=1, source_target_pairs={{0,24},{1,25},{2,26},{3,27},{4,28},{5,29},{6,30},{7,31},{8,16},{9,... | collective-permute-start | bytes 589832 | tf_op jit(solution)/shard_map/ppermute | solution.py:24
  115.5 8.1 %collective-permute-start.29 = (bf16[64,1664]{1,0:T(8,128)(2,1)S(1)}, bf16[64,1664]{1,0:T(8,128)(2,1)S(1)}, u32[]{:S(2)}, u32[]{:S(2)}) collective-permute-start(bf16[64,1664]{1,0:T(8,128)(2,1)S(1)} %slice.221), channel_id=1, source_target_pairs={{0,1},{1,0},{2,3},{3,2},{4,5},{5,4},{6,7},{7,6},{8,9},{9,8},{10,11... | collective-permute-start | bytes 638984 | tf_op jit(solution)/shard_map/ppermute | solution.py:24
  116.8 7.4 %collective-permute-start.26 = (bf16[64,1664]{1,0:T(8,128)(2,1)S(1)}, bf16[64,1664]{1,0:T(8,128)(2,1)S(1)}, u32[]{:S(2)}, u32[]{:S(2)}) collective-permute-start(bf16[64,1664]{1,0:T(8,128)(2,1)S(1)} %slice.222), channel_id=1, source_target_pairs={{0,8},{1,9},{2,10},{3,11},{4,12},{5,13},{6,14},{7,15},{8,0},{9,1},... | collective-permute-start | bytes 638984 | tf_op jit(solution)/shard_map/ppermute | solution.py:24
  117.5 7.8 %collective-permute-start.22 = (bf16[64,1664]{1,0:T(8,128)(2,1)S(1)}, bf16[64,1664]{1,0:T(8,128)(2,1)S(1)}, u32[]{:S(2)}, u32[]{:S(2)}) collective-permute-start(bf16[64,1664]{1,0:T(8,128)(2,1)S(1)} %slice.223), channel_id=1, source_target_pairs={{0,3},{1,2},{2,1},{3,0},{4,7},{5,6},{6,5},{7,4},{8,11},{9,10},{10,... | collective-permute-start | bytes 638984 | tf_op jit(solution)/shard_map/ppermute | solution.py:24
  121.4 10.5 %collective-permute-start.33 = (bf16[32,1664]{1,0:T(8,128)(2,1)S(1)}, bf16[32,1664]{1,0:T(8,128)(2,1)S(1)}, u32[]{:S(2)}, u32[]{:S(2)}) collective-permute-start(bf16[32,1664]{1,0:T(8,128)(2,1)S(1)} %slice.225), channel_id=1, source_target_pairs={{0,24},{1,25},{2,26},{3,27},{4,28},{5,29},{6,30},{7,31},{8,16},{9,... | collective-permute-start | bytes 319496 | tf_op jit(solution)/shard_map/ppermute | solution.py:24
  123.6 8.2 %collective-permute-start.32 = (bf16[32,1664]{1,0:T(8,128)(2,1)S(1)}, bf16[32,1664]{1,0:T(8,128)(2,1)S(1)}, u32[]{:S(2)}, u32[]{:S(2)}) collective-permute-start(bf16[32,1664]{1,0:T(8,128)(2,1)S(1)} %slice.226), channel_id=1, source_target_pairs={{0,4},{1,5},{2,6},{3,7},{4,0},{5,1},{6,2},{7,3},{8,12},{9,13},{10,... | collective-permute-start | bytes 319496 | tf_op jit(solution)/shard_map/ppermute | solution.py:24
  124.2 7.7 %copy-start.2 = (f32[1,8192]{1,0:T(1,128)S(1)}, f32[1,8192]{1,0:T(1,128)}, u32[]{:S(2)}) copy-start(f32[1,8192]{1,0:T(1,128)} %param.16) | copy-start | bytes 98308
  124.2 7.6 %collective-permute-start.30 = (bf16[32,1664]{1,0:T(8,128)(2,1)S(1)}, bf16[32,1664]{1,0:T(8,128)(2,1)S(1)}, u32[]{:S(2)}, u32[]{:S(2)}) collective-permute-start(bf16[32,1664]{1,0:T(8,128)(2,1)S(1)} %slice.227), channel_id=1, source_target_pairs={{0,1},{1,0},{2,3},{3,2},{4,5},{5,4},{6,7},{7,6},{8,9},{9,8},{10,11... | collective-permute-start | bytes 319496 | tf_op jit(solution)/shard_map/ppermute | solution.py:24
  125.3 5.8 %collective-permute-start.23 = (bf16[32,1536]{1,0:T(8,128)(2,1)S(1)}, bf16[32,1536]{1,0:T(8,128)(2,1)S(1)}, u32[]{:S(2)}, u32[]{:S(2)}) collective-permute-start(bf16[32,1536]{1,0:T(8,128)(2,1)S(1)} %slice.229), channel_id=1, source_target_pairs={{0,3},{1,2},{2,1},{3,0},{4,7},{5,6},{6,5},{7,4},{8,11},{9,10},{10,... | collective-permute-start | bytes 294920 | tf_op jit(solution)/shard_map/ppermute | solution.py:24
  127.0 4.8 %collective-permute-start.27 = (bf16[32,1664]{1,0:T(8,128)(2,1)S(1)}, bf16[32,1664]{1,0:T(8,128)(2,1)S(1)}, u32[]{:S(2)}, u32[]{:S(2)}) collective-permute-start(bf16[32,1664]{1,0:T(8,128)(2,1)S(1)} %slice.228), channel_id=1, source_target_pairs={{0,8},{1,9},{2,10},{3,11},{4,12},{5,13},{6,14},{7,15},{8,0},{9,1},... | collective-permute-start | bytes 319496 | tf_op jit(solution)/shard_map/ppermute | solution.py:24
  131.8 1.0 copy-start.1
